TPU v7x, 32 devices: a whole 2x2x4 slice. The times are simulated.
32 devices in a mesh: dp: 16 (over z, y, core), mlp: 2 (over x).
Axes of the slice: x: 2, y: 2, z: 4, core: 2. Of those that a mesh axis runs over, the one named last changes fastest.
Arguments:
- tokens: bfloat16 [2, 2048, 2048], P(None, ('dp', 'mlp')), may hold values from -6 to 6
- cotangent: bfloat16 [2, 2048, 2048], P(None, ('dp', 'mlp')), may hold values from -6 to 6
- group_start: int32 [2, 32], P(None, ('dp', 'mlp')), may hold values from 0 to 1, as said below
- pad_mask: int32 [2, 2048], P(None, ('dp', 'mlp')), may hold values from 0 to 1, as said below
- query_weight: bfloat16 [2048, 2048], P(('dp', 'mlp')), may hold values from -0.125 to 0.125
- key_weight: bfloat16 [2048, 2048], P(('dp', 'mlp')), may hold values from -0.125 to 0.125
- value_weight: bfloat16 [2048, 2048], P(('dp', 'mlp')), may hold values from -0.125 to 0.125
- gate_weight: bfloat16 [2048, 2048], P(('dp', 'mlp')), may hold values from -0.125 to 0.125
- beta_weight: bfloat16 [2048, 16], P(('dp', 'mlp')), may hold values from -0.25 to 0.25
- out_weight: bfloat16 [2048, 2048], P(('dp', 'mlp')), may hold values from -0.1875 to 0.1875
- conv_weight: bfloat16 [3, 4, 2048], P(None, None, ('dp', 'mlp')), may hold values from -3 to 3
- mixer_gain: bfloat16 [2048], P(('dp', 'mlp')), may hold values from 0.25 to 1.75
- head_gain: bfloat16 [128], replicated, may hold values from 0.25 to 1.75
- swiglu_gain: bfloat16 [2048], P(('dp', 'mlp')), may hold values from 0.25 to 1.75
- swiglu_gate: bfloat16 [2048, 5632], P('dp', 'mlp'), may hold values from -0.125 to 0.125
- swiglu_up: bfloat16 [2048, 5632], P('dp', 'mlp'), may hold values from -0.125 to 0.125
- swiglu_down: bfloat16 [5632, 2048], P('mlp', 'dp'), may hold values from -0.15625 to 0.15625
Outputs:
- block_out: bfloat16 [2, 2048, 2048], P(None, ('dp', 'mlp'))
- tokens_grad: float32 [2, 2048, 2048], P(None, ('dp', 'mlp'))
- query_grad: float32 [2048, 2048], P(('dp', 'mlp'))
- key_grad: float32 [2048, 2048], P(('dp', 'mlp'))
- value_grad: float32 [2048, 2048], P(('dp', 'mlp'))
- gate_grad: float32 [2048, 2048], P(('dp', 'mlp'))
- beta_grad: float32 [2048, 16], P(('dp', 'mlp'))
- out_grad: float32 [2048, 2048], P(('dp', 'mlp'))
- conv_grad: float32 [3, 4, 2048], P(None, None, ('dp', 'mlp'))
- mixer_gain_grad: float32 [2048], P(('dp', 'mlp'))
- head_gain_grad: float32 [128], replicated
- swiglu_gain_grad: float32 [2048], P(('dp', 'mlp'))
- swiglu_gate_grad: float32 [2048, 5632], P('dp', 'mlp')
- swiglu_up_grad: float32 [2048, 5632], P('dp', 'mlp')
- swiglu_down_grad: float32 [5632, 2048], P('mlp', 'dp')
Inputs may be any that keep to these rules, and one draw needn't show every extreme that they name: group_start is 1 at the first block of 64 tokens of every device's share of a micro-batch, so a document never spans two devices. `pad_mask`: each document's padding lies at its end, within its last block of 64 tokens, and holds 1 to 63 tokens.
All inputs are finite; a program needn't handle non-finite values.
Results may differ from a plain program's by a relative error of at most 0.013.
Values may be sent and summed in bfloat16 or wider, within the bound.
A program may use at most 384 MiB of HBM per device.

v0:
```python
import jax
import jax.numpy as jnp
from jax import lax
from jax.sharding import PartitionSpec as P


def rms_norm(values, scale_gain):
    return (
        values * lax.rsqrt(jnp.mean(values * values, axis=-1, keepdims=True) + 1e-06) * scale_gain
    )


def short_conv(linear, tap_weights, starts):
    length = linear.shape[0]
    block_len = length // starts.shape[0]
    position = jnp.arange(length)
    restart = jnp.repeat(starts, block_len)
    summed = linear * tap_weights[0]
    for offset in range(1, tap_weights.shape[0]):
        shifted = jnp.concatenate(
            [jnp.zeros((offset, linear.shape[1]), linear.dtype), linear[: length - offset]], axis=0
        )
        usable = ((position % block_len >= offset) | (restart == 0)).astype(linear.dtype)
        summed = summed + shifted * tap_weights[offset] * usable[:, None]
    return summed


def outer_product_result(form, first, second):
    return jnp.einsum(form, first, second, precision=lax.Precision.HIGHEST)


def delta_core(queries, keys, values, betas, starts):
    length, head_count, head_width = queries.shape
    value_width = values.shape[2]
    block_count = starts.shape[0]
    block_len = length // block_count

    def blocked(array):
        return array.reshape(block_count, block_len, head_count, -1).transpose(0, 2, 1, 3)

    query_blocks = blocked(queries)
    key_blocks = blocked(keys)
    value_blocks = blocked(values)
    beta_blocks = betas.reshape(block_count, block_len, head_count).transpose(0, 2, 1)[..., None]
    position = jnp.arange(block_len)
    strict = (position[:, None] > position[None, :]).astype(queries.dtype)
    causal = (position[:, None] >= position[None, :]).astype(queries.dtype)
    weighted = key_blocks * beta_blocks
    negative = -outer_product_result("nhik,nhjk->nhij", weighted, key_blocks) * strict
    inverse = jnp.eye(block_len, dtype=queries.dtype) + negative
    power_term = negative
    for doubling in range(5):
        power_term = outer_product_result("nhij,nhjk->nhik", power_term, power_term)
        inverse = inverse + outer_product_result("nhij,nhjk->nhik", inverse, power_term)
    key_mix = outer_product_result("nhij,nhjk->nhik", inverse, weighted)
    value_mix = outer_product_result("nhij,nhjk->nhik", inverse, value_blocks * beta_blocks)
    scores = outer_product_result("nhik,nhjk->nhij", query_blocks, key_blocks) * causal

    def advance(current_state, block_items):
        (
            query_slice,
            key_slice,
            key_mixture_slice,
            value_mixture_slice,
            attention_score_slice,
            restart,
        ) = block_items
        current_state = current_state * (1 - restart).astype(current_state.dtype)
        adjusted_result = value_mixture_slice - outer_product_result(
            "pzd,pde->pze", key_mixture_slice, current_state
        )
        produced_output = outer_product_result(
            "pzd,pde->pze", query_slice, current_state
        ) + outer_product_result("lqz,lzr->lqr", attention_score_slice, adjusted_result)
        current_state = current_state + outer_product_result(
            "ixl,ixr->ilr", key_slice, adjusted_result
        )
        return (current_state, produced_output)

    initial = jnp.zeros((head_count, head_width, value_width), queries.dtype)
    final_state, produced_output = lax.scan(
        advance, initial, (query_blocks, key_blocks, key_mix, value_mix, scores, starts)
    )
    return produced_output.transpose(0, 2, 1, 3).reshape(length, head_count, value_width)


def mixer_core(query_lin, key_lin, value_lin, gate_lin, beta_lin, conv_taps, head_scale, starts):
    length = query_lin.shape[0]
    head_count = beta_lin.shape[1]
    head_width = query_lin.shape[1] // head_count
    queries = jax.nn.silu(short_conv(query_lin, conv_taps[0], starts)).reshape(
        length, head_count, head_width
    )
    keys = jax.nn.silu(short_conv(key_lin, conv_taps[1], starts)).reshape(
        length, head_count, head_width
    )
    values = jax.nn.silu(short_conv(value_lin, conv_taps[2], starts)).reshape(
        length, head_count, head_width
    )
    queries = (
        queries
        * lax.rsqrt(jnp.sum(queries * queries, axis=-1, keepdims=True) + 1e-06)
        * head_width ** (-0.5)
    )
    keys = keys * lax.rsqrt(jnp.sum(keys * keys, axis=-1, keepdims=True) + 1e-06)
    recurrent = delta_core(queries, keys, values, jax.nn.sigmoid(beta_lin), starts)
    normed = (
        recurrent
        * lax.rsqrt(jnp.mean(recurrent * recurrent, axis=-1, keepdims=True) + 1e-05)
        * head_scale
    )
    gated_out = normed * jax.nn.silu(gate_lin.reshape(length, head_count, head_width))
    return gated_out.reshape(length, head_count * head_width)


def swiglu_mix(gate_act, up_act):
    return jax.nn.silu(gate_act) * up_act


def matmul_rows(left, right):
    return jnp.dot(left, right, preferred_element_type=jnp.float32)


def left_product(first, second):
    return jnp.einsum("tf,tg->fg", first, second, preferred_element_type=jnp.float32)


def back_product(gradient, weight):
    return jnp.einsum("tg,fg->tf", gradient, weight, preferred_element_type=jnp.float32)


def add_terms(running, fresh_terms):
    if running is None:
        return fresh_terms
    return tuple((left_term + right_term for left_term, right_term in zip(running, fresh_terms)))


def joined(pieces):
    return jnp.concatenate(pieces, axis=0)


def on_device(
    tokens,
    cotangent,
    group_start,
    pad_mask,
    query_weight,
    key_weight,
    value_weight,
    gate_weight,
    beta_weight,
    out_weight,
    conv_weight,
    mixer_gain,
    head_gain,
    swiglu_gain,
    swiglu_gate,
    swiglu_up,
    swiglu_down,
):
    micro_count = tokens.shape[0]
    head_scale = head_gain.astype(jnp.float32)
    mixer_set = (
        lax.all_gather(query_weight, ("dp", "mlp"), axis=0, tiled=True),
        lax.all_gather(key_weight, ("dp", "mlp"), axis=0, tiled=True),
        lax.all_gather(value_weight, ("dp", "mlp"), axis=0, tiled=True),
        lax.all_gather(gate_weight, ("dp", "mlp"), axis=0, tiled=True),
        lax.all_gather(beta_weight, ("dp", "mlp"), axis=0, tiled=True),
        lax.all_gather(out_weight, ("dp", "mlp"), axis=0, tiled=True),
        lax.all_gather(conv_weight, ("dp", "mlp"), axis=2, tiled=True),
        lax.all_gather(mixer_gain, ("dp", "mlp"), axis=0, tiled=True),
        lax.all_gather(swiglu_gain, ("dp", "mlp"), axis=0, tiled=True),
    )
    swiglu_set = (
        lax.all_gather(swiglu_gate, "dp", axis=0, tiled=True),
        lax.all_gather(swiglu_up, "dp", axis=0, tiled=True),
        lax.all_gather(swiglu_down, "dp", axis=1, tiled=True),
    )
    mixer_sums = None
    swiglu_sums = None
    small_sums = None
    kept_rows = []
    head_sums = jnp.zeros(head_gain.shape, jnp.float32)
    outputs = []
    input_grads = []
    for micro_index in range(micro_count):
        (
            query_full,
            key_full,
            value_full,
            gate_full,
            beta_full,
            out_full,
            conv_full,
            gain_mixer,
            gain_swiglu,
        ) = mixer_set
        gate_half, up_half, down_half = swiglu_set
        inputs = tokens[micro_index].astype(jnp.float32)
        starts = group_start[micro_index]
        normed, norm_back = jax.vjp(rms_norm, inputs, gain_mixer.astype(jnp.float32))
        normed_low = normed.astype(jnp.bfloat16)
        query_lin = matmul_rows(normed_low, query_full)
        key_lin = matmul_rows(normed_low, key_full)
        value_lin = matmul_rows(normed_low, value_full)
        gate_lin = matmul_rows(normed_low, gate_full)
        beta_lin = matmul_rows(normed_low, beta_full)

        def core_at(query_in, key_in, value_in, gate_in, beta_in, conv_in, head_in):
            return mixer_core(
                query_in, key_in, value_in, gate_in, beta_in, conv_in, head_in, starts
            )

        gated_out, core_back = jax.vjp(
            core_at,
            query_lin,
            key_lin,
            value_lin,
            gate_lin,
            beta_lin,
            conv_full.astype(jnp.float32),
            head_scale,
        )
        gated_low = gated_out.astype(jnp.bfloat16)
        residual = inputs + matmul_rows(gated_low, out_full)
        inner, inner_norm_back = jax.vjp(rms_norm, residual, gain_swiglu.astype(jnp.float32))
        inner_low = inner.astype(jnp.bfloat16)
        inner_pair = lax.all_gather(inner_low, "mlp", axis=0, tiled=True)
        gate_act = matmul_rows(inner_pair, gate_half)
        up_act = matmul_rows(inner_pair, up_half)
        hidden, hidden_back = jax.vjp(swiglu_mix, gate_act, up_act)
        hidden_low = hidden.astype(jnp.bfloat16)
        partial_rows = matmul_rows(hidden_low, down_half)
        branch_rows = lax.psum_scatter(
            partial_rows.astype(jnp.bfloat16), "mlp", scatter_dimension=0, tiled=True
        ).astype(jnp.float32)
        outputs.append((residual + branch_rows).astype(jnp.bfloat16))
        out_back = (
            cotangent[micro_index].astype(jnp.float32)
            * pad_mask[micro_index].astype(jnp.float32)[:, None]
        )
        out_back_low = out_back.astype(jnp.bfloat16)
        upstream_pair = lax.all_gather(out_back_low, "mlp", axis=0, tiled=True)
        gate_back, up_back = hidden_back(back_product(upstream_pair, down_half))
        gate_back_low = gate_back.astype(jnp.bfloat16)
        up_back_low = up_back.astype(jnp.bfloat16)
        inner_part = back_product(gate_back_low, gate_half) + back_product(up_back_low, up_half)
        inner_back = lax.psum_scatter(
            inner_part.astype(jnp.bfloat16), "mlp", scatter_dimension=0, tiled=True
        ).astype(jnp.float32)
        residual_part, swiglu_gain_term = inner_norm_back(inner_back)
        residual_back = out_back + residual_part
        mixed_back = residual_back.astype(jnp.bfloat16)
        gated_back = back_product(mixed_back, out_full)
        query_back, key_back, value_back, gate_lin_back, beta_back, conv_term, head_term = (
            core_back(gated_back)
        )
        query_low = query_back.astype(jnp.bfloat16)
        key_low = key_back.astype(jnp.bfloat16)
        value_low = value_back.astype(jnp.bfloat16)
        gate_low = gate_lin_back.astype(jnp.bfloat16)
        beta_low = beta_back.astype(jnp.bfloat16)
        normed_back = (
            back_product(query_low, query_full)
            + back_product(key_low, key_full)
            + back_product(value_low, value_full)
            + back_product(gate_low, gate_full)
            + back_product(beta_low, beta_full)
        )
        input_part, mixer_gain_term = norm_back(normed_back)
        input_grads.append(residual_back + input_part)
        kept_rows.append(
            (
                normed_low,
                query_low,
                key_low,
                value_low,
                gate_low,
                beta_low,
                gated_low,
                mixed_back,
                inner_pair,
                gate_back_low,
                up_back_low,
                hidden_low,
                upstream_pair,
            )
        )
        small_sums = add_terms(small_sums, (conv_term, mixer_gain_term, swiglu_gain_term))
        head_sums = head_sums + head_term
    columns = [joined([row[position] for row in kept_rows]) for position in range(13)]
    normed_all = columns[0]
    gate_term = left_product(columns[8], columns[9])
    up_term = left_product(columns[8], columns[10])
    down_term = left_product(columns[11], columns[12])
    swiglu_sums = (
        lax.psum_scatter(gate_term, "dp", scatter_dimension=0, tiled=True),
        lax.psum_scatter(up_term, "dp", scatter_dimension=0, tiled=True),
        lax.psum_scatter(down_term, "dp", scatter_dimension=1, tiled=True),
    )
    query_term = left_product(normed_all, columns[1])
    key_term = left_product(normed_all, columns[2])
    value_term = left_product(normed_all, columns[3])
    gate_term_mix = left_product(normed_all, columns[4])
    beta_term = left_product(normed_all, columns[5])
    out_term = left_product(columns[6], columns[7])
    mixer_sums = (
        lax.psum_scatter(query_term, ("dp", "mlp"), scatter_dimension=0, tiled=True),
        lax.psum_scatter(key_term, ("dp", "mlp"), scatter_dimension=0, tiled=True),
        lax.psum_scatter(value_term, ("dp", "mlp"), scatter_dimension=0, tiled=True),
        lax.psum_scatter(gate_term_mix, ("dp", "mlp"), scatter_dimension=0, tiled=True),
        lax.psum_scatter(beta_term, ("dp", "mlp"), scatter_dimension=0, tiled=True),
        lax.psum_scatter(out_term, ("dp", "mlp"), scatter_dimension=0, tiled=True),
        lax.psum_scatter(small_sums[0], ("dp", "mlp"), scatter_dimension=2, tiled=True),
        lax.psum_scatter(small_sums[1], ("dp", "mlp"), scatter_dimension=0, tiled=True),
        lax.psum_scatter(small_sums[2], ("dp", "mlp"), scatter_dimension=0, tiled=True),
    )
    head_total = lax.psum(head_sums, ("dp", "mlp"))
    return (
        jnp.stack(outputs),
        jnp.stack(input_grads),
        mixer_sums[0],
        mixer_sums[1],
        mixer_sums[2],
        mixer_sums[3],
        mixer_sums[4],
        mixer_sums[5],
        mixer_sums[6],
        mixer_sums[7],
        head_total,
        mixer_sums[8],
        swiglu_sums[0],
        swiglu_sums[1],
        swiglu_sums[2],
    )


def solution(mesh):
    placed = (
        P(None, ("dp", "mlp"), None),
        P(None, ("dp", "mlp"), None),
        P(None, ("dp", "mlp")),
        P(None, ("dp", "mlp")),
        P(("dp", "mlp"), None),
        P(("dp", "mlp"), None),
        P(("dp", "mlp"), None),
        P(("dp", "mlp"), None),
        P(("dp", "mlp"), None),
        P(("dp", "mlp"), None),
        P(None, None, ("dp", "mlp")),
        P(("dp", "mlp")),
        P(),
        P(("dp", "mlp")),
        P("dp", "mlp"),
        P("dp", "mlp"),
        P("mlp", "dp"),
    )
    return jax.shard_map(
        on_device,
        mesh=mesh,
        in_specs=placed,
        out_specs=(
            P(None, ("dp", "mlp"), None),
            P(None, ("dp", "mlp"), None),
            P(("dp", "mlp"), None),
            P(("dp", "mlp"), None),
            P(("dp", "mlp"), None),
            P(("dp", "mlp"), None),
            P(("dp", "mlp"), None),
            P(("dp", "mlp"), None),
            P(None, None, ("dp", "mlp")),
            P(("dp", "mlp")),
            P(),
            P(("dp", "mlp")),
            P("dp", "mlp"),
            P("dp", "mlp"),
            P("mlp", "dp"),
        ),
        check_vma=False,
    )
```

profile of v0, /device:TPU:0, one launch (start us, length us, event | category | flops | bytes accessed | tf_op | source)
XLA Modules:
  0.0 3746.5 jit_solution(16538072336483097468)
XLA Ops:
  17.6 92.1 %all_gather.50 = bf16[3,4,2048]{1,0,2:T(4,128)(2,1)S(1)} all-gather(bf16[3,4,64]{1,0,2:T(4,128)(2,1)S(1)} %copy.404), channel_id=1, replica_groups=mesh['dp'=16,'mlp'=2] {'dp','mlp'}, dimensions={2}, use_global_device_ids=true | all-gather | bytes 50688 | tf_op jit(solution)/shard_map/all_gather | solution.py:170
  112.5 40.4 %all-reduce.71 = (bf16[2048]{0:T(1024)(128)(2,1)S(1)}, bf16[2048]{0:T(1024)(128)(2,1)S(1)}) all-reduce(bf16[2048]{0:T(1024)(128)(2,1)S(1)} %dynamic-update-slice, bf16[2048]{0:T(1024)(128)(2,1)S(1)} %dynamic-update-slice.1), channel_id=1, replica_groups=mesh['dp'=16,'mlp'=2] {'dp','mlp'}, use_global_device_ids=true, to_apply=%add.66 | all-reduce | flops 4096 | bytes 16384
  154.8 67.6 %all-gather = bf16[32,64,16]{1,2,0:T(8,128)(2,1)S(1)} all-gather(bf16[1,64,16]{1,2,0:T(8,128)(2,1)S(1)} %bitcast.1181), channel_id=1, replica_groups=mesh['dp'=16,'mlp'=2] {'dp','mlp'}, dimensions={0}, use_global_device_ids=true | all-gather | bytes 67584 | tf_op jit(solution)/shard_map/all_gather | solution.py:168
  234.3 113.9 %slice_reduce_fusion.3 = (f32[2048]{0:T(1024)S(1)}, f32[2048]{0:T(1024)S(1)}, f32[2048]{0:T(1024)S(1)}, f32[2048]{0:T(1024)S(1)}, f32[2048]{0:T(1024)S(1)}, /*in...) fusion(f32[3,4,2048]{1,0,2:T(4,128)} %convert_element_type.301), kind=kLoop, calls=%fused_computation.177 | loop fusion | bytes 196608 | tf_op jit(solution)/shard_map/jvp()/slice | solution.py:18
  378.9 11.8 copy.411
  449.4 78.8 %all-gather.20.cloned.1.call-done = bf16[2048,2816]{1,0:T(8,128)(2,1)} async-done(((bf16[128,2816]{1,0:T(8,128)(2,1)}), bf16[2048,2816]{1,0:T(8,128)(2,1)}) %all-gather.20.cloned.1.call-update) | async-done | bytes 11534352 | tf_op jit(solution)/shard_map/all_gather | solution.py:175
  535.4 87.6 %all-gather.22.cloned.1.call-done = bf16[2048,2816]{1,0:T(8,128)(2,1)} async-done(((bf16[128,2816]{1,0:T(8,128)(2,1)}), bf16[2048,2816]{1,0:T(8,128)(2,1)}) %all-gather.22.cloned.1.call-update) | async-done | bytes 11534352 | tf_op jit(solution)/shard_map/all_gather | solution.py:176
  630.3 90.5 %all-gather.24.cloned.1.call-done = bf16[2816,2048]{1,0:T(8,128)(2,1)} async-done(((bf16[2816,128]{1,0:T(8,128)(2,1)}), bf16[2816,2048]{1,0:T(8,128)(2,1)}) %all-gather.24.cloned.1.call-update) | async-done | bytes 11534352 | tf_op jit(solution)/shard_map/all_gather | solution.py:177
  720.8 10.4 multiply_convert_fusion.1
  745.0 12.9 all_gather.63
  784.4 10.9 multiply_convert_fusion
  826.1 13.3 reduce-scatter.21.cloned.1.call-done
  1033.3 9.5 fusion.14
  1044.5 9.8 fusion.18
  1088.0 40.1 %all-reduce.70 = (f32[2048]{0:T(1024)S(1)}, f32[128]{0:T(128)}, f32[2048]{0:T(1024)S(1)}) all-reduce(f32[2048]{0:T(1024)S(1)} %add.647, f32[128]{0:T(128)S(1)} %add.648, f32[2048]{0:T(1024)S(1)} %add.649), channel_id=13, replica_groups=mesh['dp'=16,'mlp'=2] {'dp','mlp'}, use_global_device_ids=true, to_apply=%region_61.62.clone | all-reduce | flops 4224 | bytes 33792
  1135.4 107.9 %reduce-scatter.43.cloned.1.call-done = f32[64,16]{1,0:T(8,128)} async-done(((f32[2048,16]{1,0:T(8,128)}), f32[64,16]{1,0:T(8,128)}) %reduce-scatter.43.cloned.1.call-update) | async-done | bytes 4112
  1244.7 355.1 %reduce-scatter.27.cloned.1.call-done = f32[64,2048]{1,0:T(8,128)} async-done(((f32[2048,2048]{1,0:T(8,128)}), f32[64,2048]{1,0:T(8,128)}) %reduce-scatter.27.cloned.1.call-update) | async-done | bytes 524304 | tf_op jit(solution)/shard_map/reduce_scatter | solution.py:308
  1599.8 361.4 %reduce-scatter.29.cloned.1.call-done = f32[64,2048]{1,0:T(8,128)} async-done(((f32[2048,2048]{1,0:T(8,128)}), f32[64,2048]{1,0:T(8,128)}) %reduce-scatter.29.cloned.1.call-update) | async-done | bytes 524304 | tf_op jit(solution)/shard_map/reduce_scatter | solution.py:309
  1961.2 361.4 %reduce-scatter.31.cloned.1.call-done = f32[64,2048]{1,0:T(8,128)} async-done(((f32[2048,2048]{1,0:T(8,128)}), f32[64,2048]{1,0:T(8,128)}) %reduce-scatter.31.cloned.1.call-update) | async-done | bytes 524304 | tf_op jit(solution)/shard_map/reduce_scatter | solution.py:310
  2322.5 361.4 %reduce-scatter.33.cloned.1.call-done = f32[64,2048]{1,0:T(8,128)} async-done(((f32[2048,2048]{1,0:T(8,128)}), f32[64,2048]{1,0:T(8,128)}) %reduce-scatter.33.cloned.1.call-update) | async-done | bytes 524304 | tf_op jit(solution)/shard_map/reduce_scatter | solution.py:311
  2683.9 361.5 %reduce-scatter.35.cloned.1.call-done = f32[64,2048]{1,0:T(8,128)} async-done(((f32[2048,2048]{1,0:T(8,128)}), f32[64,2048]{1,0:T(8,128)}) %reduce-scatter.35.cloned.1.call-update) | async-done | bytes 524304 | tf_op jit(solution)/shard_map/reduce_scatter | solution.py:313
  3045.4 232.7 %reduce-scatter.37.cloned.1.call-done = f32[128,2816]{1,0:T(8,128)} async-done(((f32[2048,2816]{1,0:T(8,128)}), f32[128,2816]{1,0:T(8,128)}) %reduce-scatter.37.cloned.1.call-update) | async-done | bytes 1441808 | tf_op jit(solution)/shard_map/reduce_scatter | solution.py:297
  3278.1 230.7 %reduce-scatter.39.cloned.1.call-done = f32[128,2816]{1,0:T(8,128)} async-done(((f32[2048,2816]{1,0:T(8,128)}), f32[128,2816]{1,0:T(8,128)}) %reduce-scatter.39.cloned.1.call-update) | async-done | bytes 1441808 | tf_op jit(solution)/shard_map/reduce_scatter | solution.py:298
  3508.8 230.7 %reduce-scatter.41.cloned.1.call-done = f32[2816,128]{1,0:T(8,128)} async-done(((f32[2816,2048]{1,0:T(8,128)}), f32[2816,128]{1,0:T(8,128)}) %reduce-scatter.41.cloned.1.call-update) | async-done | bytes 1441808 | tf_op jit(solution)/shard_map/reduce_scatter | solution.py:299
  (788 shorter events, 433.1 us)
Async XLA Ops:
  7.3 341.0 %all-gather.10.cloned.1.call-start = ((), (), s32[]{:S(2)}) async-start(), calls=%async_computation.14 | async-start | bytes 8650752 | tf_op jit(solution)/shard_map/all_gather | solution.py:164
  8.0 350.6 %all-gather.12.cloned.1.call-start = ((), (), s32[]{:S(2)}) async-start(), calls=%async_computation.15 | async-start | bytes 8650752 | tf_op jit(solution)/shard_map/all_gather | solution.py:165
  8.7 360.0 %all-gather.14.cloned.1.call-start = ((), (), s32[]{:S(2)}) async-start(), calls=%async_computation.16 | async-start | bytes 8650752 | tf_op jit(solution)/shard_map/all_gather | solution.py:166
  9.5 369.5 %all-gather.16.cloned.1.call-start = ((), (), s32[]{:S(2)}) async-start(), calls=%async_computation.17 | async-start | bytes 8650752 | tf_op jit(solution)/shard_map/all_gather | solution.py:167
  10.1 423.1 %all-gather.18.cloned.1.call-start = ((), (), s32[]{:S(2)}) async-start(), calls=%async_computation.18 | async-start | bytes 8650752 | tf_op jit(solution)/shard_map/all_gather | solution.py:169
  10.6 517.6 %all-gather.20.cloned.1.call-start = ((), (), s32[]{:S(2)}) async-start(), calls=%async_computation.19 | async-start | bytes 12255232 | tf_op jit(solution)/shard_map/all_gather | solution.py:175
  11.2 611.8 %all-gather.22.cloned.1.call-start = ((), (), s32[]{:S(2)}) async-start(), calls=%async_computation.20 | async-start | bytes 12255232 | tf_op jit(solution)/shard_map/all_gather | solution.py:176
  12.0 708.8 %all-gather.24.cloned.1.call-start = ((), (), s32[]{:S(2)}) async-start(), calls=%async_computation.21 | async-start | bytes 12255232 | tf_op jit(solution)/shard_map/all_gather | solution.py:177
  12.7 751.2 %reduce-scatter.23.cloned.1.call-start = ((), (), s32[]{:S(2)}) async-start(), calls=%async_computation.24 | async-start | bytes 786432 | tf_op jit(solution)/shard_map/reduce_scatter | solution.py:248
  15.4 360.8 %copy-start.177 = (f32[64]{0:T(128)}, f32[64]{0:T(128)S(1)}, u32[]{:S(2)}) copy-start(f32[64]{0:T(128)S(1)} %get-tuple-element.402) | copy-start | bytes 772
  438.4 401.0 %copy-start.185 = (f32[64]{0:T(128)}, f32[64]{0:T(128)S(1)}, u32[]{:S(2)}) copy-start(f32[64]{0:T(128)S(1)} %fusion.312) | copy-start | bytes 772
  744.9 79.3 %reduce-scatter.25.cloned.1.call-start = ((), (), s32[]{:S(2)}) async-start(), calls=%async_computation.25 | async-start | bytes 786432 | tf_op jit(solution)/shard_map/reduce_scatter | solution.py:248
  809.2 30.2 reduce-scatter.21.cloned.1.call-start
  816.4 312.9 %reduce-scatter.19.cloned.1.call-start = ((), (), s32[]{:S(2)}) async-start(), calls=%async_computation.22 | async-start | bytes 786432 | tf_op jit(solution)/shard_map/reduce_scatter | solution.py:234
  824.1 309.8 %reduce-scatter.45.cloned.1.call-start = ((), (), s32[]{:S(2)}) async-start(), calls=%async_computation.35 | async-start | bytes 1081344
  974.7 268.6 %reduce-scatter.43.cloned.1.call-start = ((), (), s32[]{:S(2)}) async-start(), calls=%async_computation.34 | async-start | bytes 1081344
  976.2 623.6 %reduce-scatter.27.cloned.1.call-start = ((), (), s32[]{:S(2)}) async-start(), calls=%async_computation.26 | async-start | bytes 17301504 | tf_op jit(solution)/shard_map/reduce_scatter | solution.py:308
  984.5 976.7 %reduce-scatter.29.cloned.1.call-start = ((), (), s32[]{:S(2)}) async-start(), calls=%async_computation.27 | async-start | bytes 17301504 | tf_op jit(solution)/shard_map/reduce_scatter | solution.py:309
  993.5 1329.0 %reduce-scatter.31.cloned.1.call-start = ((), (), s32[]{:S(2)}) async-start(), calls=%async_computation.28 | async-start | bytes 17301504 | tf_op jit(solution)/shard_map/reduce_scatter | solution.py:310
  1002.6 1681.3 %reduce-scatter.33.cloned.1.call-start = ((), (), s32[]{:S(2)}) async-start(), calls=%async_computation.29 | async-start | bytes 17301504 | tf_op jit(solution)/shard_map/reduce_scatter | solution.py:311
  1011.8 2033.6 %reduce-scatter.35.cloned.1.call-start = ((), (), s32[]{:S(2)}) async-start(), calls=%async_computation.30 | async-start | bytes 17301504 | tf_op jit(solution)/shard_map/reduce_scatter | solution.py:313
  1021.0 2257.1 %reduce-scatter.37.cloned.1.call-start = ((), (), s32[]{:S(2)}) async-start(), calls=%async_computation.31 | async-start | bytes 24510464 | tf_op jit(solution)/shard_map/reduce_scatter | solution.py:297
  1032.0 2476.8 %reduce-scatter.39.cloned.1.call-start = ((), (), s32[]{:S(2)}) async-start(), calls=%async_computation.32 | async-start | bytes 24510464 | tf_op jit(solution)/shard_map/reduce_scatter | solution.py:298
  1042.9 2696.7 %reduce-scatter.41.cloned.1.call-start = ((), (), s32[]{:S(2)}) async-start(), calls=%async_computation.33 | async-start | bytes 24510464 | tf_op jit(solution)/shard_map/reduce_scatter | solution.py:299
  (218 other events, 5015.2 us)
Sparse Core Ops, SparseCore 0:
  11.1 96.3 all-gather.9
  110.4 80.3 all-gather.11
  193.8 81.4 all-gather.13
  278.1 75.9 all-gather.15
  357.0 76.1 all-gather.17
  435.3 92.8 all-gather.19
  530.5 92.4 all-gather.21
  625.2 95.5 all-gather.23
  745.0 15.6 reduce-scatter.22
  809.3 12.6 reduce-scatter.24
  824.8 14.5 reduce-scatter.20
  841.6 14.5 reduce-scatter.18
  974.9 135.0 reduce-scatter.44
  1112.1 131.1 reduce-scatter.42
  1246.0 353.7 reduce-scatter.26
  1602.5 358.6 reduce-scatter.28
  1963.9 358.6 reduce-scatter.30
  2325.3 358.6 reduce-scatter.32
  2686.8 358.6 reduce-scatter.34
  3050.0 228.1 reduce-scatter.36
  3282.8 225.9 reduce-scatter.38
  3513.5 225.9 reduce-scatter.40
where the time goes:
time: 3750 us
  waiting for transfers between devices  2880 us (77%)
  matrix products  350 us (9%)
  blocking collectives  278 us (7%)
  local copies, waits for them, and re-layouts  170 us (5%)
  other arithmetic  45.8 us (1%)
    reduce_scatter x1, waiting for transfers between devices, on_device(): lax.psum_scatter(out_term, ('dp', 'mlp'), scatter_dimension=0, tiled=True)  362 us
    reduce_scatter x1, waiting for transfers between devices, on_device(): lax.psum_scatter(key_term, ('dp', 'mlp'), scatter_dimension=0, tiled=True)  361 us
    reduce_scatter x1, waiting for transfers between devices, on_device(): lax.psum_scatter(gate_term_mix, ('dp', 'mlp'), scatter_dimension=0, tiled...  361 us
    reduce_scatter x1, waiting for transfers between devices, on_device(): lax.psum_scatter(value_term, ('dp', 'mlp'), scatter_dimension=0, tiled=True)  361 us
    reduce_scatter x1, waiting for transfers between devices, on_device(): lax.psum_scatter(query_term, ('dp', 'mlp'), scatter_dimension=0, tiled=True)  355 us
    reduce_scatter x1, waiting for transfers between devices, on_device(): lax.psum_scatter(gate_term, 'dp', scatter_dimension=0, tiled=True)  233 us
    reduce_scatter x1, waiting for transfers between devices, on_device(): lax.psum_scatter(up_term, 'dp', scatter_dimension=0, tiled=True)  231 us
    reduce_scatter x1, waiting for transfers between devices, on_device(): lax.psum_scatter(down_term, 'dp', scatter_dimension=1, tiled=True)  231 us
  transfers between devices with their start and end apart: 22, of which 14 were waited for; matrix products, arithmetic and copies ran while one was open for 13% of the time, Pallas kernels for 0%

commit v1 on v0

--- a/solution.py
+++ b/solution.py
@@ -133,6 +133,12 @@
     if running is None:
         return fresh_terms
     return tuple((left_term + right_term for left_term, right_term in zip(running, fresh_terms)))
+
+
+def scatter_low(term, axes, dimension):
+    return lax.psum_scatter(
+        term.astype(jnp.bfloat16), axes, scatter_dimension=dimension, tiled=True
+    ).astype(jnp.float32)
 
 
 def joined(pieces):
@@ -159,18 +165,36 @@
     swiglu_down,
 ):
     micro_count = tokens.shape[0]
+    n_all = tokens.shape[2] // query_weight.shape[0]
     head_scale = head_gain.astype(jnp.float32)
     mixer_set = (
         lax.all_gather(query_weight, ("dp", "mlp"), axis=0, tiled=True),
         lax.all_gather(key_weight, ("dp", "mlp"), axis=0, tiled=True),
         lax.all_gather(value_weight, ("dp", "mlp"), axis=0, tiled=True),
         lax.all_gather(gate_weight, ("dp", "mlp"), axis=0, tiled=True),
-        lax.all_gather(beta_weight, ("dp", "mlp"), axis=0, tiled=True),
         lax.all_gather(out_weight, ("dp", "mlp"), axis=0, tiled=True),
-        lax.all_gather(conv_weight, ("dp", "mlp"), axis=2, tiled=True),
-        lax.all_gather(mixer_gain, ("dp", "mlp"), axis=0, tiled=True),
-        lax.all_gather(swiglu_gain, ("dp", "mlp"), axis=0, tiled=True),
-    )
+    )
+    rows = beta_weight.shape[0]
+    small_pack = jnp.concatenate(
+        [
+            conv_weight.reshape(-1),
+            beta_weight.reshape(-1),
+            mixer_gain.reshape(-1),
+            swiglu_gain.reshape(-1),
+        ]
+    )
+    small_all = lax.all_gather(small_pack, ("dp", "mlp"), axis=0, tiled=False)
+    conv_size = conv_weight.size
+    beta_size = beta_weight.size
+    conv_full = (
+        small_all[:, :conv_size]
+        .reshape((n_all,) + conv_weight.shape)
+        .transpose(1, 2, 0, 3)
+        .reshape(conv_weight.shape[0], conv_weight.shape[1], -1)
+    )
+    beta_full = small_all[:, conv_size : conv_size + beta_size].reshape(-1, beta_weight.shape[1])
+    gain_mixer = small_all[:, conv_size + beta_size : conv_size + beta_size + rows].reshape(-1)
+    gain_swiglu = small_all[:, conv_size + beta_size + rows :].reshape(-1)
     swiglu_set = (
         lax.all_gather(swiglu_gate, "dp", axis=0, tiled=True),
         lax.all_gather(swiglu_up, "dp", axis=0, tiled=True),
@@ -184,17 +208,7 @@
     outputs = []
     input_grads = []
     for micro_index in range(micro_count):
-        (
-            query_full,
-            key_full,
-            value_full,
-            gate_full,
-            beta_full,
-            out_full,
-            conv_full,
-            gain_mixer,
-            gain_swiglu,
-        ) = mixer_set
+        query_full, key_full, value_full, gate_full, out_full = mixer_set
         gate_half, up_half, down_half = swiglu_set
         inputs = tokens[micro_index].astype(jnp.float32)
         starts = group_start[micro_index]
@@ -294,9 +308,9 @@
     up_term = left_product(columns[8], columns[10])
     down_term = left_product(columns[11], columns[12])
     swiglu_sums = (
-        lax.psum_scatter(gate_term, "dp", scatter_dimension=0, tiled=True),
-        lax.psum_scatter(up_term, "dp", scatter_dimension=0, tiled=True),
-        lax.psum_scatter(down_term, "dp", scatter_dimension=1, tiled=True),
+        scatter_low(gate_term, "dp", 0),
+        scatter_low(up_term, "dp", 0),
+        scatter_low(down_term, "dp", 1),
     )
     query_term = left_product(normed_all, columns[1])
     key_term = left_product(normed_all, columns[2])
@@ -304,18 +318,39 @@
     gate_term_mix = left_product(normed_all, columns[4])
     beta_term = left_product(normed_all, columns[5])
     out_term = left_product(columns[6], columns[7])
+    big_sums = tuple(
+        scatter_low(term, ("dp", "mlp"), 0)
+        for term in (query_term, key_term, value_term, gate_term_mix, out_term)
+    )
+    conv_sum, mixer_gain_sum, swiglu_gain_sum = small_sums
+    taps = conv_sum.shape[0] * conv_sum.shape[1]
+    small_rows = jnp.concatenate(
+        [
+            conv_sum.reshape(taps, n_all, -1).transpose(1, 0, 2).reshape(n_all, -1),
+            beta_term.reshape(n_all, -1),
+            mixer_gain_sum.reshape(n_all, -1),
+            swiglu_gain_sum.reshape(n_all, -1),
+            jnp.broadcast_to(head_sums[None, :], (n_all, head_sums.shape[0])),
+        ],
+        axis=1,
+    )
+    small_out = lax.psum_scatter(small_rows, ("dp", "mlp"), scatter_dimension=0, tiled=False)
+    conv_owned = small_out[: conv_size].reshape(conv_weight.shape)
+    beta_owned = small_out[conv_size : conv_size + beta_size].reshape(beta_weight.shape)
+    mixer_gain_owned = small_out[conv_size + beta_size : conv_size + beta_size + rows]
+    swiglu_gain_owned = small_out[conv_size + beta_size + rows : conv_size + beta_size + 2 * rows]
+    head_total = small_out[conv_size + beta_size + 2 * rows :]
     mixer_sums = (
-        lax.psum_scatter(query_term, ("dp", "mlp"), scatter_dimension=0, tiled=True),
-        lax.psum_scatter(key_term, ("dp", "mlp"), scatter_dimension=0, tiled=True),
-        lax.psum_scatter(value_term, ("dp", "mlp"), scatter_dimension=0, tiled=True),
-        lax.psum_scatter(gate_term_mix, ("dp", "mlp"), scatter_dimension=0, tiled=True),
-        lax.psum_scatter(beta_term, ("dp", "mlp"), scatter_dimension=0, tiled=True),
-        lax.psum_scatter(out_term, ("dp", "mlp"), scatter_dimension=0, tiled=True),
-        lax.psum_scatter(small_sums[0], ("dp", "mlp"), scatter_dimension=2, tiled=True),
-        lax.psum_scatter(small_sums[1], ("dp", "mlp"), scatter_dimension=0, tiled=True),
-        lax.psum_scatter(small_sums[2], ("dp", "mlp"), scatter_dimension=0, tiled=True),
-    )
-    head_total = lax.psum(head_sums, ("dp", "mlp"))
+        big_sums[0],
+        big_sums[1],
+        big_sums[2],
+        big_sums[3],
+        beta_owned,
+        big_sums[4],
+        conv_owned,
+        mixer_gain_owned,
+        swiglu_gain_owned,
+    )
     return (
         jnp.stack(outputs),
         jnp.stack(input_grads),

time: 3750 us -> 2450 us (0.65)
  waiting for transfers between devices: 2880 us -> 1840 us
  blocking collectives: 278 us -> 112 us
  local copies, waits for them, and re-layouts: 170 us -> 72.5 us
    reduce_scatter x8 -> x7, waiting for transfers between devices: 2490 us -> 1180 us  [scatter_low(): lax.psum_scatter(term.astype(jnp.bfloat16), axes, scatter_dimension=dimen...]
    slice x1, local copies, waits for them, and re-layouts: 114 us -> 0.07 us  [short_conv(): summed = linear * tap_weights[0]]
    all_gather x2 -> x1, blocking collectives: 160 us -> 72.7 us  [on_device(): small_all = lax.all_gather(small_pack, ('dp', 'mlp'), axis=0, tiled=False)]
    unnamed x2 -> x0, blocking collectives: 80.5 us -> none
    all_gather x1, waiting for transfers between devices: 0.01 us -> 68.9 us  [on_device(): lax.all_gather(value_weight, ('dp', 'mlp'), axis=0, tiled=True)]
    all_gather x1, waiting for transfers between devices: 0.01 us -> 68.6 us  [on_device(): lax.all_gather(gate_weight, ('dp', 'mlp'), axis=0, tiled=True)]
    unnamed x24 -> x23, waiting for transfers between devices: 113 us -> 180 us
    all_gather x1, waiting for transfers between devices: 0.01 us -> 48.4 us  [on_device(): lax.all_gather(key_weight, ('dp', 'mlp'), axis=0, tiled=True)]
  transfers between devices with their start and end apart: 22 -> 21, of which waited for: 14 -> 17; matrix products, arithmetic and copies ran while one was open for 13% -> 16% of each run, Pallas kernels for 0% -> 0%
where the time goes in v1:
time: 2450 us; the launch traced here: 2440 us
  waiting for transfers between devices  1840 us (75%)
  matrix products  332 us (14%)
  blocking collectives  112 us (5%)
  local copies, waits for them, and re-layouts  72.5 us (3%)
  other arithmetic  62.9 us (3%)
    reduce_scatter x7, waiting for transfers between devices, scatter_low(): lax.psum_scatter(term.astype(jnp.bfloat16), axes, scatter_dimension=dimen...  1180 us
    unnamed x23, waiting for transfers between devices  180 us
    dot_general x102, matrix products, outer_product_result(): return jnp.einsum(form, first, second, precision=lax.Precision.HIGHEST)  112 us
    dot_general x18, matrix products, back_product(): jnp.einsum('tg,fg->tf', gradient, weight, preferred_element_type=jnp.floa...  91.8 us
    all_gather x1, waiting for transfers between devices, on_device(): lax.all_gather(swiglu_down, 'dp', axis=1, tiled=True)  90.5 us
    all_gather x1, waiting for transfers between devices, on_device(): lax.all_gather(swiglu_up, 'dp', axis=0, tiled=True)  87.6 us
    all_gather x1, waiting for transfers between devices, on_device(): lax.all_gather(swiglu_gate, 'dp', axis=0, tiled=True)  78.8 us
    dot_general x18, matrix products, matmul_rows(): return jnp.dot(left, right, preferred_element_type=jnp.float32)  78.6 us
  transfers between devices with their start and end apart: 21, of which 17 were waited for; matrix products, arithmetic and copies ran while one was open for 16% of the time, Pallas kernels for 0%

profile of v1, /device:TPU:0, one launch (start us, length us, event | category | flops | bytes accessed | tf_op | source)
XLA Modules:
  0.0 2440.3 jit_solution(7829317304273394769)
XLA Ops:
  15.8 72.7 %all-gather.1 = bf16[32,1,1920]{2,1,0:T(2,128)(2,1)S(1)} all-gather(bf16[1,1,1920]{2,1,0:T(2,128)(2,1)S(1)} %reshape.1346), channel_id=2, replica_groups=mesh['dp'=16,'mlp'=2] {'dp','mlp'}, dimensions={0}, use_global_device_ids=true | all-gather | bytes 126720 | tf_op jit(solution)/shard_map/all_gather | solution.py:186
  123.7 48.4 %all-gather.13.cloned.1.call-done = bf16[2048,2048]{1,0:T(8,128)(2,1)} async-done(((bf16[64,2048]{1,0:T(8,128)(2,1)}), bf16[2048,2048]{1,0:T(8,128)(2,1)}) %all-gather.13.cloned.1.call-update) | async-done | bytes 8388624 | tf_op jit(solution)/shard_map/all_gather | solution.py:172
  182.1 68.9 %all-gather.15.cloned.1.call-done = bf16[2048,2048]{1,0:T(8,128)(2,1)} async-done(((bf16[64,2048]{1,0:T(8,128)(2,1)}), bf16[2048,2048]{1,0:T(8,128)(2,1)}) %all-gather.15.cloned.1.call-update) | async-done | bytes 8388624 | tf_op jit(solution)/shard_map/all_gather | solution.py:173
  261.1 68.6 %all-gather.17.cloned.1.call-done = bf16[2048,2048]{1,0:T(8,128)(2,1)} async-done(((bf16[64,2048]{1,0:T(8,128)(2,1)}), bf16[2048,2048]{1,0:T(8,128)(2,1)}) %all-gather.17.cloned.1.call-update) | async-done | bytes 8388624 | tf_op jit(solution)/shard_map/all_gather | solution.py:174
  329.7 12.7 copy.346
  384.5 24.1 all-gather.19.cloned.1.call-done
  415.3 9.7 all_gather.49
  425.0 78.8 %all-gather.21.cloned.1.call-done = bf16[2048,2816]{1,0:T(8,128)(2,1)} async-done(((bf16[128,2816]{1,0:T(8,128)(2,1)}), bf16[2048,2816]{1,0:T(8,128)(2,1)}) %all-gather.21.cloned.1.call-update) | async-done | bytes 11534352 | tf_op jit(solution)/shard_map/all_gather | solution.py:199
  511.0 87.6 %all-gather.23.cloned.1.call-done = bf16[2048,2816]{1,0:T(8,128)(2,1)} async-done(((bf16[128,2816]{1,0:T(8,128)(2,1)}), bf16[2048,2816]{1,0:T(8,128)(2,1)}) %all-gather.23.cloned.1.call-update) | async-done | bytes 11534352 | tf_op jit(solution)/shard_map/all_gather | solution.py:200
  605.8 90.5 %all-gather.25.cloned.1.call-done = bf16[2816,2048]{1,0:T(8,128)(2,1)} async-done(((bf16[2816,128]{1,0:T(8,128)(2,1)}), bf16[2816,2048]{1,0:T(8,128)(2,1)}) %all-gather.25.cloned.1.call-update) | async-done | bytes 11534352 | tf_op jit(solution)/shard_map/all_gather | solution.py:201
  696.3 10.4 multiply_convert_fusion.1
  720.6 12.9 all_gather.55
  759.8 10.9 multiply_convert_fusion
  801.4 13.6 reduce-scatter.17.cloned.1.call-done
  992.7 15.3 copy.462
  1059.6 50.9 %all-reduce.69.cloned.1.call-done = f32[32,2048]{1,0:T(8,128)} async-done(((f32[32,2048]{1,0:T(8,128)}), f32[32,2048]{1,0:T(8,128)}) %all-reduce.69.cloned.1.call-update) | async-done | bytes 262160
  1116.2 123.6 %reduce-scatter.37.cloned.1.call-done = bf16[128,2816]{1,0:T(8,128)(2,1)} async-done(((bf16[2048,2816]{1,0:T(8,128)(2,1)}), bf16[128,2816]{1,0:T(8,128)(2,1)}) %reduce-scatter.37.cloned.1.call-update) | async-done | bytes 720912
  1242.4 127.9 %reduce-scatter.33.cloned.1.call-done = bf16[128,2816]{1,0:T(8,128)(2,1)} async-done(((bf16[2048,2816]{1,0:T(8,128)(2,1)}), bf16[128,2816]{1,0:T(8,128)(2,1)}) %reduce-scatter.33.cloned.1.call-update) | async-done | bytes 720912 | tf_op jit(solution)/shard_map/reduce_scatter | solution.py:139
  1372.7 127.7 %reduce-scatter.35.cloned.1.call-done = bf16[128,2816]{1,0:T(8,128)(2,1)} async-done(((bf16[2048,2816]{1,0:T(8,128)(2,1)}), bf16[128,2816]{1,0:T(8,128)(2,1)}) %reduce-scatter.35.cloned.1.call-update) | async-done | bytes 720912 | tf_op jit(solution)/shard_map/reduce_scatter | solution.py:139
  1502.7 182.9 %reduce-scatter.23.cloned.1.call-done = bf16[64,2048]{1,0:T(8,128)(2,1)} async-done(((bf16[2048,2048]{1,0:T(8,128)(2,1)}), bf16[64,2048]{1,0:T(8,128)(2,1)}) %reduce-scatter.23.cloned.1.call-update) | async-done | bytes 262160 | tf_op jit(solution)/shard_map/reduce_scatter | solution.py:139
  1687.3 184.5 %reduce-scatter.25.cloned.1.call-done = bf16[64,2048]{1,0:T(8,128)(2,1)} async-done(((bf16[2048,2048]{1,0:T(8,128)(2,1)}), bf16[64,2048]{1,0:T(8,128)(2,1)}) %reduce-scatter.25.cloned.1.call-update) | async-done | bytes 262160 | tf_op jit(solution)/shard_map/reduce_scatter | solution.py:139
  1873.7 184.8 %reduce-scatter.27.cloned.1.call-done = bf16[64,2048]{1,0:T(8,128)(2,1)} async-done(((bf16[2048,2048]{1,0:T(8,128)(2,1)}), bf16[64,2048]{1,0:T(8,128)(2,1)}) %reduce-scatter.27.cloned.1.call-update) | async-done | bytes 262160 | tf_op jit(solution)/shard_map/reduce_scatter | solution.py:139
  2060.2 184.5 %reduce-scatter.29.cloned.1.call-done = bf16[64,2048]{1,0:T(8,128)(2,1)} async-done(((bf16[2048,2048]{1,0:T(8,128)(2,1)}), bf16[64,2048]{1,0:T(8,128)(2,1)}) %reduce-scatter.29.cloned.1.call-update) | async-done | bytes 262160 | tf_op jit(solution)/shard_map/reduce_scatter | solution.py:139
  2246.5 184.7 %reduce-scatter.31.cloned.1.call-done = bf16[64,2048]{1,0:T(8,128)(2,1)} async-done(((bf16[2048,2048]{1,0:T(8,128)(2,1)}), bf16[64,2048]{1,0:T(8,128)(2,1)}) %reduce-scatter.31.cloned.1.call-update) | async-done | bytes 262160 | tf_op jit(solution)/shard_map/reduce_scatter | solution.py:139
  (830 shorter events, 441.9 us)
Async XLA Ops:
  7.2 106.5 %all-gather.11.cloned.1.call-start = ((), (), s32[]{:S(2)}) async-start(), calls=%async_computation.12 | async-start | bytes 8650752 | tf_op jit(solution)/shard_map/all_gather | solution.py:171
  7.9 164.2 %all-gather.13.cloned.1.call-start = ((), (), s32[]{:S(2)}) async-start(), calls=%async_computation.13 | async-start | bytes 8650752 | tf_op jit(solution)/shard_map/all_gather | solution.py:172
  8.7 242.3 %all-gather.15.cloned.1.call-start = ((), (), s32[]{:S(2)}) async-start(), calls=%async_computation.14 | async-start | bytes 8650752 | tf_op jit(solution)/shard_map/all_gather | solution.py:173
  9.4 320.3 %all-gather.17.cloned.1.call-start = ((), (), s32[]{:S(2)}) async-start(), calls=%async_computation.15 | async-start | bytes 8650752 | tf_op jit(solution)/shard_map/all_gather | solution.py:174
  10.0 398.6 %all-gather.19.cloned.1.call-start = ((), (), s32[]{:S(2)}) async-start(), calls=%async_computation.16 | async-start | bytes 8650752 | tf_op jit(solution)/shard_map/all_gather | solution.py:175
  10.6 493.2 %all-gather.21.cloned.1.call-start = ((), (), s32[]{:S(2)}) async-start(), calls=%async_computation.17 | async-start | bytes 12255232 | tf_op jit(solution)/shard_map/all_gather | solution.py:199
  11.1 587.4 %all-gather.23.cloned.1.call-start = ((), (), s32[]{:S(2)}) async-start(), calls=%async_computation.18 | async-start | bytes 12255232 | tf_op jit(solution)/shard_map/all_gather | solution.py:200
  11.9 684.4 %all-gather.25.cloned.1.call-start = ((), (), s32[]{:S(2)}) async-start(), calls=%async_computation.19 | async-start | bytes 12255232 | tf_op jit(solution)/shard_map/all_gather | solution.py:201
  12.6 726.8 %reduce-scatter.19.cloned.1.call-start = ((), (), s32[]{:S(2)}) async-start(), calls=%async_computation.22 | async-start | bytes 786432 | tf_op jit(solution)/shard_map/reduce_scatter | solution.py:262
  123.7 221.5 %copy-start.180 = (f32[64,16]{0,1:T(8,128)}, f32[64,16]{0,1:T(8,128)S(1)}, u32[]{:S(2)}) copy-start(f32[64,16]{0,1:T(8,128)S(1)} %copy.341) | copy-start | bytes 12292
  384.5 349.0 %copy-start.110 = (bf16[16,8,8,128]{3,2,1,0:T(8,128)(2,1)}, bf16[16,8,8,128]{3,2,1,0:T(8,128)(2,1)S(1)}, u32[]{:S(2)}) copy-start(bf16[16,8,8,128]{3,2,1,0:T(8,128)(2,1)S(1)} %get-tuple-element.429) | copy-start | bytes 786436
  413.7 401.2 %copy-start.200 = (f32[64]{0:T(128)}, f32[64]{0:T(128)S(1)}, u32[]{:S(2)}) copy-start(f32[64]{0:T(128)S(1)} %fusion.300) | copy-start | bytes 772
  720.5 78.9 %reduce-scatter.21.cloned.1.call-start = ((), (), s32[]{:S(2)}) async-start(), calls=%async_computation.23 | async-start | bytes 786432 | tf_op jit(solution)/shard_map/reduce_scatter | solution.py:262
  784.6 30.3 %reduce-scatter.17.cloned.1.call-start = ((), (), s32[]{:S(2)}) async-start(), calls=%async_computation.21 | async-start | bytes 786432 | tf_op jit(solution)/shard_map/reduce_scatter | solution.py:248
  791.8 263.1 %reduce-scatter.15.cloned.1.call-start = ((), (), s32[]{:S(2)}) async-start(), calls=%async_computation.20 | async-start | bytes 786432 | tf_op jit(solution)/shard_map/reduce_scatter | solution.py:248
  799.4 311.2 %all-reduce.69.cloned.1.call-start = ((), (), s32[]{:S(2)}) async-start(), calls=%async_computation.32 | async-start | bytes 524288
  985.4 254.3 %reduce-scatter.37.cloned.1.call-start = ((), (), s32[]{:S(2)}) async-start(), calls=%async_computation.31 | async-start | bytes 12255232
  1008.0 362.3 %reduce-scatter.33.cloned.1.call-start = ((), (), s32[]{:S(2)}) async-start(), calls=%async_computation.29 | async-start | bytes 12255232 | tf_op jit(solution)/shard_map/reduce_scatter | solution.py:139
  1016.6 483.8 %reduce-scatter.35.cloned.1.call-start = ((), (), s32[]{:S(2)}) async-start(), calls=%async_computation.30 | async-start | bytes 12255232 | tf_op jit(solution)/shard_map/reduce_scatter | solution.py:139
  1024.8 660.8 %reduce-scatter.23.cloned.1.call-start = ((), (), s32[]{:S(2)}) async-start(), calls=%async_computation.24 | async-start | bytes 8650752 | tf_op jit(solution)/shard_map/reduce_scatter | solution.py:139
  1031.4 840.5 %reduce-scatter.25.cloned.1.call-start = ((), (), s32[]{:S(2)}) async-start(), calls=%async_computation.25 | async-start | bytes 8650752 | tf_op jit(solution)/shard_map/reduce_scatter | solution.py:139
  1037.1 1021.3 %reduce-scatter.27.cloned.1.call-start = ((), (), s32[]{:S(2)}) async-start(), calls=%async_computation.26 | async-start | bytes 8650752 | tf_op jit(solution)/shard_map/reduce_scatter | solution.py:139
  1042.8 1201.9 %reduce-scatter.29.cloned.1.call-start = ((), (), s32[]{:S(2)}) async-start(), calls=%async_computation.27 | async-start | bytes 8650752 | tf_op jit(solution)/shard_map/reduce_scatter | solution.py:139
  1048.7 1382.6 %reduce-scatter.31.cloned.1.call-start = ((), (), s32[]{:S(2)}) async-start(), calls=%async_computation.28 | async-start | bytes 8650752 | tf_op jit(solution)/shard_map/reduce_scatter | solution.py:139
  (229 other events, 4657.7 us)
Sparse Core Ops, SparseCore 0:
  11.0 81.1 all-gather.10
  95.2 76.8 all-gather.12
  175.1 75.8 all-gather.14
  253.8 75.8 all-gather.16
  332.6 76.0 all-gather.18
  410.8 92.9 all-gather.20
  506.0 92.4 all-gather.22
  600.7 95.5 all-gather.24
  720.6 15.6 reduce-scatter.18
  784.8 12.6 reduce-scatter.20
  800.3 14.5 reduce-scatter.16
  817.1 14.5 reduce-scatter.14
  985.5 124.9 all-reduce.68
  1114.5 125.2 reduce-scatter.36
  1244.3 126.0 reduce-scatter.32
  1374.3 126.0 reduce-scatter.34
  1502.6 182.9 reduce-scatter.22
  1687.8 184.0 reduce-scatter.24
  1874.3 184.0 reduce-scatter.26
  2060.7 184.0 reduce-scatter.28
  2247.1 184.0 reduce-scatter.30

commit v2 on v0

v2 whole, which is shorter than its diff:
```python
import jax
import jax.numpy as jnp
import numpy as np
from jax import lax
from jax.sharding import Mesh
from jax.sharding import PartitionSpec as P

TP_AXES = ("core", "mlp")
ALL_AXES = ("dq", "core", "mlp")
FSDP_AXES = tuple(name for name in ALL_AXES if name not in TP_AXES)
INNER_AXES = tuple(name for name in TP_AXES if name != "mlp")


def rms_norm(values, scale_gain):
    return (
        values * lax.rsqrt(jnp.mean(values * values, axis=-1, keepdims=True) + 1e-06) * scale_gain
    )


def short_conv(linear, tap_weights, starts):
    length = linear.shape[0]
    block_len = length // starts.shape[0]
    position = jnp.arange(length)
    restart = jnp.repeat(starts, block_len)
    summed = linear * tap_weights[0]
    for offset in range(1, tap_weights.shape[0]):
        shifted = jnp.concatenate(
            [jnp.zeros((offset, linear.shape[1]), linear.dtype), linear[: length - offset]], axis=0
        )
        usable = ((position % block_len >= offset) | (restart == 0)).astype(linear.dtype)
        summed = summed + shifted * tap_weights[offset] * usable[:, None]
    return summed


def outer_product_result(form, first, second):
    return jnp.einsum(form, first, second, precision=lax.Precision.HIGHEST)


def delta_core(queries, keys, values, betas, starts):
    length, head_count, head_width = queries.shape
    value_width = values.shape[2]
    block_count = starts.shape[0]
    block_len = length // block_count

    def blocked(array):
        return array.reshape(block_count, block_len, head_count, -1).transpose(0, 2, 1, 3)

    query_blocks = blocked(queries)
    key_blocks = blocked(keys)
    value_blocks = blocked(values)
    beta_blocks = betas.reshape(block_count, block_len, head_count).transpose(0, 2, 1)[..., None]
    position = jnp.arange(block_len)
    strict = (position[:, None] > position[None, :]).astype(queries.dtype)
    causal = (position[:, None] >= position[None, :]).astype(queries.dtype)
    weighted = key_blocks * beta_blocks
    negative = -outer_product_result("nhik,nhjk->nhij", weighted, key_blocks) * strict
    inverse = jnp.eye(block_len, dtype=queries.dtype) + negative
    power_term = negative
    for doubling in range(5):
        power_term = outer_product_result("nhij,nhjk->nhik", power_term, power_term)
        inverse = inverse + outer_product_result("nhij,nhjk->nhik", inverse, power_term)
    key_mix = outer_product_result("nhij,nhjk->nhik", inverse, weighted)
    value_mix = outer_product_result("nhij,nhjk->nhik", inverse, value_blocks * beta_blocks)
    scores = outer_product_result("nhik,nhjk->nhij", query_blocks, key_blocks) * causal

    def advance(current_state, block_items):
        (
            query_slice,
            key_slice,
            key_mixture_slice,
            value_mixture_slice,
            attention_score_slice,
            restart,
        ) = block_items
        current_state = current_state * (1 - restart).astype(current_state.dtype)
        adjusted_result = value_mixture_slice - outer_product_result(
            "pzd,pde->pze", key_mixture_slice, current_state
        )
        produced_output = outer_product_result(
            "pzd,pde->pze", query_slice, current_state
        ) + outer_product_result("lqz,lzr->lqr", attention_score_slice, adjusted_result)
        current_state = current_state + outer_product_result(
            "ixl,ixr->ilr", key_slice, adjusted_result
        )
        return (current_state, produced_output)

    initial = jnp.zeros((head_count, head_width, value_width), queries.dtype)
    final_state, produced_output = lax.scan(
        advance, initial, (query_blocks, key_blocks, key_mix, value_mix, scores, starts)
    )
    return produced_output.transpose(0, 2, 1, 3).reshape(length, head_count, value_width)


def mixer_core(query_lin, key_lin, value_lin, gate_lin, beta_lin, conv_taps, head_scale, starts):
    length = query_lin.shape[0]
    head_count = beta_lin.shape[1]
    head_width = query_lin.shape[1] // head_count
    queries = jax.nn.silu(short_conv(query_lin, conv_taps[0], starts)).reshape(
        length, head_count, head_width
    )
    keys = jax.nn.silu(short_conv(key_lin, conv_taps[1], starts)).reshape(
        length, head_count, head_width
    )
    values = jax.nn.silu(short_conv(value_lin, conv_taps[2], starts)).reshape(
        length, head_count, head_width
    )
    queries = (
        queries
        * lax.rsqrt(jnp.sum(queries * queries, axis=-1, keepdims=True) + 1e-06)
        * head_width ** (-0.5)
    )
    keys = keys * lax.rsqrt(jnp.sum(keys * keys, axis=-1, keepdims=True) + 1e-06)
    recurrent = delta_core(queries, keys, values, jax.nn.sigmoid(beta_lin), starts)
    normed = (
        recurrent
        * lax.rsqrt(jnp.mean(recurrent * recurrent, axis=-1, keepdims=True) + 1e-05)
        * head_scale
    )
    gated_out = normed * jax.nn.silu(gate_lin.reshape(length, head_count, head_width))
    return gated_out.reshape(length, head_count * head_width)


def swiglu_mix(gate_act, up_act):
    return jax.nn.silu(gate_act) * up_act


def matmul_rows(left, right):
    return jnp.dot(left, right, preferred_element_type=jnp.float32)


def left_product(first, second):
    return jnp.einsum("tf,tg->fg", first, second, preferred_element_type=jnp.float32)


def back_product(gradient, weight):
    return jnp.einsum("tg,fg->tf", gradient, weight, preferred_element_type=jnp.float32)


def tp_gather(value, axis):
    return lax.all_gather(value, TP_AXES, axis=axis, tiled=True)


def tp_scatter_low(value, axis):
    return lax.psum_scatter(
        value.astype(jnp.bfloat16), TP_AXES, scatter_dimension=axis, tiled=True
    ).astype(jnp.float32)


def fsdp_gather(value, axis):
    return lax.all_gather(value, FSDP_AXES, axis=axis, tiled=True)


def fsdp_scatter_low(value, axis):
    return lax.psum_scatter(
        value.astype(jnp.bfloat16), FSDP_AXES, scatter_dimension=axis, tiled=True
    ).astype(jnp.float32)


def exchange(value, axes, split_axis, concat_axis):
    if not axes:
        return value
    return lax.all_to_all(value, axes, split_axis, concat_axis, tiled=True)


def column_weight(owned, tp):
    rows, width = owned.shape
    swapped = exchange(owned.reshape(rows, tp, width // tp), TP_AXES, 1, 0)
    return fsdp_gather(swapped.reshape(rows * tp, width // tp), 0)


def column_grad(partial, tp):
    reduced = fsdp_scatter_low(partial, 0)
    group_rows, cols = reduced.shape
    swapped = exchange(reduced.reshape(tp, group_rows // tp, cols), TP_AXES, 0, 2)
    return swapped.reshape(group_rows // tp, cols * tp)


def heads_to_rows(values, tp, fsdp, rows):
    count = values.shape[0]
    staged = values.reshape(count, 1, fsdp // tp, tp, rows)
    moved = exchange(staged, TP_AXES, 3, 1)
    return moved.reshape(count, fsdp * rows)


def rows_to_heads(values, tp, fsdp, rows):
    count = values.shape[0]
    staged = values.reshape(count, tp, fsdp // tp, 1, rows)
    moved = exchange(staged, TP_AXES, 1, 3)
    return moved.reshape(count, fsdp * rows)


def make_on_device(tp, fsdp, inner):
    def on_device(
        tokens,
        cotangent,
        group_start,
        pad_mask,
        query_weight,
        key_weight,
        value_weight,
        gate_weight,
        beta_weight,
        out_weight,
        conv_weight,
        mixer_gain,
        head_gain,
        swiglu_gain,
        swiglu_gate,
        swiglu_up,
        swiglu_down,
    ):
        micro_count, slot, width = tokens.shape
        n_all = tp * fsdp
        rows = query_weight.shape[0]
        head_count = beta_weight.shape[1]
        heads_here = head_count // tp
        cols_here = width // tp
        position = lax.axis_index(TP_AXES)
        head_scale = head_gain.astype(jnp.float32)

        query_cols = column_weight(query_weight, tp)
        key_cols = column_weight(key_weight, tp)
        value_cols = column_weight(value_weight, tp)
        gate_cols = column_weight(gate_weight, tp)
        out_rows = fsdp_gather(out_weight, 0)

        small_pack = jnp.concatenate(
            [
                conv_weight.reshape(-1),
                beta_weight.reshape(-1),
                mixer_gain.reshape(-1),
                swiglu_gain.reshape(-1),
            ]
        )
        small_all = lax.all_gather(small_pack, ALL_AXES, axis=0, tiled=False)
        conv_size = conv_weight.size
        beta_size = beta_weight.size
        conv_full = (
            small_all[:, :conv_size]
            .reshape((n_all,) + conv_weight.shape)
            .transpose(1, 2, 0, 3)
            .reshape(conv_weight.shape[0], conv_weight.shape[1], -1)
        )
        beta_full = small_all[:, conv_size : conv_size + beta_size].reshape(-1, head_count)
        gain_mixer = small_all[:, conv_size + beta_size : conv_size + beta_size + rows].reshape(-1)
        gain_swiglu = small_all[:, conv_size + beta_size + rows :].reshape(-1)
        conv_here = lax.dynamic_slice_in_dim(
            conv_full.astype(jnp.float32), position * cols_here, cols_here, axis=2
        )
        beta_here = lax.dynamic_slice_in_dim(beta_full, position * heads_here, heads_here, axis=1)

        owned_rows, hidden_half = swiglu_gate.shape
        gate_half = fsdp_gather(
            exchange(swiglu_gate.reshape(owned_rows, inner, hidden_half // inner), INNER_AXES, 1, 0)
            .reshape(owned_rows * inner, hidden_half // inner),
            0,
        )
        up_half = fsdp_gather(
            exchange(swiglu_up.reshape(owned_rows, inner, hidden_half // inner), INNER_AXES, 1, 0)
            .reshape(owned_rows * inner, hidden_half // inner),
            0,
        )
        down_half = fsdp_gather(
            exchange(swiglu_down.reshape(inner, hidden_half // inner, owned_rows), INNER_AXES, 0, 2)
            .reshape(hidden_half // inner, inner * owned_rows),
            1,
        )

        inputs = tokens.astype(jnp.float32).reshape(micro_count * slot, width)
        normed, norm_back = jax.vjp(rms_norm, inputs, gain_mixer.astype(jnp.float32))
        normed_low = normed.astype(jnp.bfloat16)
        group_tokens = micro_count * slot * tp
        normed_group = tp_gather(normed_low.reshape(micro_count, slot, width), 1).reshape(
            group_tokens, width
        )
        starts = tp_gather(group_start, 1).reshape(-1)

        query_lin = matmul_rows(normed_group, query_cols)
        key_lin = matmul_rows(normed_group, key_cols)
        value_lin = matmul_rows(normed_group, value_cols)
        gate_lin = matmul_rows(normed_group, gate_cols)
        beta_lin = matmul_rows(normed_group, beta_here)

        def core_at(query_in, key_in, value_in, gate_in, beta_in, conv_in, head_in):
            return mixer_core(
                query_in, key_in, value_in, gate_in, beta_in, conv_in, head_in, starts
            )

        gated_out, core_back = jax.vjp(
            core_at, query_lin, key_lin, value_lin, gate_lin, beta_lin, conv_here, head_scale
        )
        gated_low = gated_out.astype(jnp.bfloat16)
        gated_rows = heads_to_rows(gated_low, tp, fsdp, rows)
        mixed_partial = matmul_rows(gated_rows, out_rows)
        residual = inputs + tp_scatter_low(
            mixed_partial.reshape(micro_count, slot * tp, width), 1
        ).reshape(micro_count * slot, width)

        inner_norm, inner_norm_back = jax.vjp(rms_norm, residual, gain_swiglu.astype(jnp.float32))
        inner_low = inner_norm.astype(jnp.bfloat16)
        inner_group = tp_gather(inner_low.reshape(micro_count, slot, width), 1).reshape(
            group_tokens, width
        )
        gate_act = matmul_rows(inner_group, gate_half)
        up_act = matmul_rows(inner_group, up_half)
        hidden, hidden_back = jax.vjp(swiglu_mix, gate_act, up_act)
        hidden_low = hidden.astype(jnp.bfloat16)
        partial_rows = matmul_rows(hidden_low, down_half)
        branch_rows = tp_scatter_low(partial_rows.reshape(micro_count, slot * tp, width), 1)
        block_out = (residual.reshape(micro_count, slot, width) + branch_rows).astype(jnp.bfloat16)

        out_back = cotangent.astype(jnp.float32) * pad_mask.astype(jnp.float32)[:, :, None]
        out_back_low = out_back.astype(jnp.bfloat16)
        upstream_group = tp_gather(out_back_low, 1).reshape(group_tokens, width)
        gate_back, up_back = hidden_back(back_product(upstream_group, down_half))
        gate_back_low = gate_back.astype(jnp.bfloat16)
        up_back_low = up_back.astype(jnp.bfloat16)
        inner_part = back_product(gate_back_low, gate_half) + back_product(up_back_low, up_half)
        inner_back = tp_scatter_low(inner_part.reshape(micro_count, slot * tp, width), 1)
        residual_part, swiglu_gain_term = inner_norm_back(
            inner_back.reshape(micro_count * slot, width)
        )
        residual_back = out_back.reshape(micro_count * slot, width) + residual_part
        mixed_back = residual_back.astype(jnp.bfloat16)
        mixed_group = tp_gather(mixed_back.reshape(micro_count, slot, width), 1).reshape(
            group_tokens, width
        )
        gated_back_rows = back_product(mixed_group, out_rows)
        gated_back = rows_to_heads(gated_back_rows, tp, fsdp, rows)
        query_back, key_back, value_back, gate_lin_back, beta_back, conv_term, head_term = (
            core_back(gated_back)
        )
        query_low = query_back.astype(jnp.bfloat16)
        key_low = key_back.astype(jnp.bfloat16)
        value_low = value_back.astype(jnp.bfloat16)
        gate_low = gate_lin_back.astype(jnp.bfloat16)
        beta_low = beta_back.astype(jnp.bfloat16)
        normed_part = (
            back_product(query_low, query_cols)
            + back_product(key_low, key_cols)
            + back_product(value_low, value_cols)
            + back_product(gate_low, gate_cols)
            + back_product(beta_low, beta_here)
        )
        normed_back = tp_scatter_low(normed_part.reshape(micro_count, slot * tp, width), 1)
        input_part, mixer_gain_term = norm_back(normed_back.reshape(micro_count * slot, width))
        tokens_grad = (residual_back + input_part).reshape(micro_count, slot, width)

        swiglu_gate_sum = left_product(inner_group, gate_back_low)
        swiglu_up_sum = left_product(inner_group, up_back_low)
        swiglu_down_sum = left_product(hidden_low, upstream_group)
        gate_grad_rows = fsdp_scatter_low(swiglu_gate_sum, 0)
        swiglu_gate_grad = exchange(
            gate_grad_rows.reshape(inner, owned_rows, hidden_half // inner), INNER_AXES, 0, 2
        ).reshape(owned_rows, hidden_half)
        up_grad_rows = fsdp_scatter_low(swiglu_up_sum, 0)
        swiglu_up_grad = exchange(
            up_grad_rows.reshape(inner, owned_rows, hidden_half // inner), INNER_AXES, 0, 2
        ).reshape(owned_rows, hidden_half)
        down_grad_cols = fsdp_scatter_low(swiglu_down_sum, 1)
        swiglu_down_grad = exchange(
            down_grad_cols.reshape(hidden_half // inner, inner, owned_rows), INNER_AXES, 1, 0
        ).reshape(hidden_half, owned_rows)

        out_grad = fsdp_scatter_low(left_product(gated_rows, mixed_group), 0)
        query_grad = column_grad(left_product(normed_group, query_low), tp)
        key_grad = column_grad(left_product(normed_group, key_low), tp)
        value_grad = column_grad(left_product(normed_group, value_low), tp)
        gate_grad = column_grad(left_product(normed_group, gate_low), tp)
        beta_sum = left_product(normed_group, beta_low)
        beta_wide = lax.dynamic_update_slice_in_dim(
            jnp.zeros((width, head_count), jnp.float32), beta_sum, position * heads_here, axis=1
        )
        conv_wide = lax.dynamic_update_slice_in_dim(
            jnp.zeros(conv_full.shape, jnp.float32), conv_term, position * cols_here, axis=2
        )
        taps = conv_wide.shape[0] * conv_wide.shape[1]
        small_rows = jnp.concatenate(
            [
                conv_wide.reshape(taps, n_all, -1).transpose(1, 0, 2).reshape(n_all, -1),
                beta_wide.reshape(n_all, -1),
                mixer_gain_term.reshape(n_all, -1),
                swiglu_gain_term.reshape(n_all, -1),
                jnp.broadcast_to(head_term[None, :], (n_all, head_term.shape[0])),
            ],
            axis=1,
        )
        small_out = lax.psum_scatter(small_rows, ALL_AXES, scatter_dimension=0, tiled=False)
        conv_grad = small_out[:conv_size].reshape(conv_weight.shape)
        beta_grad = small_out[conv_size : conv_size + beta_size].reshape(beta_weight.shape)
        mixer_gain_grad = small_out[conv_size + beta_size : conv_size + beta_size + rows]
        swiglu_gain_grad = small_out[conv_size + beta_size + rows : conv_size + beta_size + 2 * rows]
        head_total = small_out[conv_size + beta_size + 2 * rows :]
        return (
            block_out,
            tokens_grad,
            query_grad,
            key_grad,
            value_grad,
            gate_grad,
            beta_grad,
            out_grad,
            conv_grad,
            mixer_gain_grad,
            head_total,
            swiglu_gain_grad,
            swiglu_gate_grad,
            swiglu_up_grad,
            swiglu_down_grad,
        )

    return on_device


def solution(mesh):
    n_dp = mesh.shape["dp"]
    n_mlp = mesh.shape["mlp"]
    devices = np.asarray(mesh.devices).reshape(n_dp // 2, 2, n_mlp)
    split_mesh = Mesh(devices, ALL_AXES)
    sizes = dict(zip(ALL_AXES, devices.shape))
    tp = int(np.prod([sizes[name] for name in TP_AXES]))
    fsdp = int(np.prod([sizes[name] for name in FSDP_AXES]))
    inner = int(np.prod([sizes[name] for name in INNER_AXES]))
    rows_axes = ALL_AXES
    swiglu_rows = ("dq", "core")
    placed = (
        P(None, rows_axes, None),
        P(None, rows_axes, None),
        P(None, rows_axes),
        P(None, rows_axes),
        P(rows_axes, None),
        P(rows_axes, None),
        P(rows_axes, None),
        P(rows_axes, None),
        P(rows_axes, None),
        P(rows_axes, None),
        P(None, None, rows_axes),
        P(rows_axes),
        P(),
        P(rows_axes),
        P(swiglu_rows, "mlp"),
        P(swiglu_rows, "mlp"),
        P("mlp", swiglu_rows),
    )
    return jax.shard_map(
        make_on_device(tp, fsdp, inner),
        mesh=split_mesh,
        in_specs=placed,
        out_specs=(
            P(None, rows_axes, None),
            P(None, rows_axes, None),
            P(rows_axes, None),
            P(rows_axes, None),
            P(rows_axes, None),
            P(rows_axes, None),
            P(rows_axes, None),
            P(rows_axes, None),
            P(None, None, rows_axes),
            P(rows_axes),
            P(),
            P(rows_axes),
            P(swiglu_rows, "mlp"),
            P(swiglu_rows, "mlp"),
            P("mlp", swiglu_rows),
        ),
        check_vma=False,
    )
```

time: 3750 us -> 1760 us (0.47)
  waiting for transfers between devices: 2880 us -> 924 us
  blocking collectives: 278 us -> 161 us
  other arithmetic: 45.8 us -> 96.5 us
    reduce_scatter x12, waiting for transfers between devices: 2510 us -> 416 us  [the longest x8 319 us: fsdp_scatter_low(): lax.psum_scatter(value.astype(jnp.bfloat16), FSDP_AXES, scatter_dimension...]
    dot_general x102 -> x138, matrix products: 109 us -> 261 us  [outer_product_result(): return jnp.einsum(form, first, second, precision=lax.Precision.HIGHEST)]
    all_gather x6 -> x2, blocking collectives: 198 us -> 76.4 us  [the longest x1 70.9 us: on_device(): small_all = lax.all_gather(small_pack, ALL_AXES, axis=0, tiled=False)]
    all_gather x8 -> x12, waiting for transfers between devices: 259 us -> 378 us  [the longest x8 334 us: fsdp_gather(): return lax.all_gather(value, FSDP_AXES, axis=axis, tiled=True)]
    slice x1, local copies, waits for them, and re-layouts: 114 us -> 0.71 us  [short_conv(): summed = linear * tap_weights[0]]
    all_to_all x0 -> x10, blocking collectives: none -> 84.6 us  [exchange(): return lax.all_to_all(value, axes, split_axis, concat_axis, tiled=True)]
    unnamed x2 -> x0, blocking collectives: 80.5 us -> none
    dot_general x18 -> x9, matrix products: 92.6 us -> 35.7 us  [back_product(): jnp.einsum('tg,fg->tf', gradient, weight, preferred_element_type=jnp.floa...]
  transfers between devices with their start and end apart: 22 -> 31, of which waited for: 14 -> 21; matrix products, arithmetic and copies ran while one was open for 13% -> 32% of each run, Pallas kernels for 0% -> 0%
where the time goes in v2:
time: 1760 us; the launch traced here: 1750 us
  waiting for transfers between devices  924 us (52%)
  matrix products  383 us (22%)
  blocking collectives  161 us (9%)
  local copies, waits for them, and re-layouts  136 us (8%)
  other arithmetic  96.5 us (5%)
  starting transfers between devices  26.9 us (2%)
    all_gather x8, waiting for transfers between devices, fsdp_gather(): return lax.all_gather(value, FSDP_AXES, axis=axis, tiled=True)  334 us
    reduce_scatter x8, waiting for transfers between devices, fsdp_scatter_low(): lax.psum_scatter(value.astype(jnp.bfloat16), FSDP_AXES, scatter_dimension...  319 us
    dot_general x138, matrix products, outer_product_result(): return jnp.einsum(form, first, second, precision=lax.Precision.HIGHEST)  261 us
    unnamed x26, waiting for transfers between devices  129 us
    reduce_scatter x4, waiting for transfers between devices, tp_scatter_low(): lax.psum_scatter(value.astype(jnp.bfloat16), TP_AXES, scatter_dimension=a...  97.6 us
    all_to_all x10, blocking collectives, exchange(): return lax.all_to_all(value, axes, split_axis, concat_axis, tiled=True)  84.6 us
    all_gather x1, blocking collectives, on_device(): small_all = lax.all_gather(small_pack, ALL_AXES, axis=0, tiled=False)  70.9 us
    dot_general x9, matrix products, matmul_rows(): return jnp.dot(left, right, preferred_element_type=jnp.float32)  45.6 us
  transfers between devices with their start and end apart: 31, of which 21 were waited for; matrix products, arithmetic and copies ran while one was open for 32% of the time, Pallas kernels for 0%

profile of v2, /device:TPU:0, one launch (start us, length us, event | category | flops | bytes accessed | tf_op | source)
XLA Modules:
  0.0 1745.3 jit_solution(1573754460320509798)
XLA Ops:
  10.4 70.9 %all-gather.2 = bf16[32,1,1920]{2,1,0:T(2,128)(2,1)S(1)} all-gather(bf16[1,1,1920]{2,1,0:T(2,128)(2,1)S(1)} %reshape.786), channel_id=2, replica_groups=mesh['dq'=8,'core'=2,'mlp'=2] {'dq','core','mlp'}, dimensions={0}, use_global_device_ids=true | all-gather | bytes 126720 | tf_op jit(solution)/shard_map/all_gather | solution.py:235
  86.7 11.9 all_to_all.240
  140.8 19.3 %all-gather.22.cloned.1.call-done = bf16[2048,512]{1,0:T(8,128)(2,1)} async-done(((bf16[256,512]{1,0:T(8,128)(2,1)}), bf16[2048,512]{1,0:T(8,128)(2,1)}) %all-gather.22.cloned.1.call-update) | async-done | bytes 2097168 | tf_op jit(solution)/shard_map/all_gather | solution.py:150
  163.0 47.0 %all-gather.18.cloned.1.call-done = bf16[2048,512]{1,0:T(8,128)(2,1)} async-done(((bf16[256,512]{1,0:T(8,128)(2,1)}), bf16[2048,512]{1,0:T(8,128)(2,1)}) %all-gather.18.cloned.1.call-update) | async-done | bytes 2097168 | tf_op jit(solution)/shard_map/all_gather | solution.py:150
  244.6 15.2 all-gather.20.cloned.1.call-done
  280.2 78.1 %while.44 = (s32[]{:T(128)}, f32[4,128,128]{2,1,0:T(8,128)S(1)}, f32[8,4,64,128]{3,2,0,1:T(8,128)}, f32[8]{0:T(128)S(1)}, f32[8,4,128,128]{3,2,1,0:T(8,128)}, /*...) while((s32[]{:T(128)}, f32[4,128,128]{2,1,0:T(8,128)S(1)}, ...), condition=%wide.region_4.5_spmd.clone, body=%wide.region_3.4_spmd.clone.sunk | while | flops 176816128 | bytes 3151050 | solution.py:88
  371.9 11.9 all_to_all.244
  401.4 18.0 %reduce-scatter.13.cloned.1.call-done = bf16[2,64,2048]{2,1,0:T(8,128)(2,1)} async-done(((bf16[2,256,2048]{2,1,0:T(8,128)(2,1)}), bf16[2,64,2048]{2,1,0:T(8,128)(2,1)}) %reduce-scatter.13.cloned.1.call-update) | async-done | bytes 524304 | tf_op jit(solution)/shard_map/reduce_scatter | solution.py:144
  445.4 69.7 %all-gather.30.cloned.1.call-done = bf16[2048,1408]{1,0:T(8,128)(2,1)} async-done(((bf16[256,1408]{1,0:T(8,128)(2,1)}), bf16[2048,1408]{1,0:T(8,128)(2,1)}) %all-gather.30.cloned.1.call-update) | async-done | bytes 5767184 | tf_op jit(solution)/shard_map/all_gather | solution.py:150
  515.1 23.0 %all-gather.28.cloned.1.call-done = bf16[2,256,2048]{2,1,0:T(8,128)(2,1)} async-done(((bf16[2,64,2048]{2,1,0:T(8,128)(2,1)}), bf16[2,256,2048]{2,1,0:T(8,128)(2,1)}) %all-gather.28.cloned.1.call-update) | async-done | bytes 2097168 | tf_op jit(solution)/shard_map/all_gather | solution.py:140
  546.4 87.2 %all-gather.32.cloned.1.call-done = bf16[2048,1408]{1,0:T(8,128)(2,1)} async-done(((bf16[256,1408]{1,0:T(8,128)(2,1)}), bf16[2048,1408]{1,0:T(8,128)(2,1)}) %all-gather.32.cloned.1.call-update) | async-done | bytes 5767184 | tf_op jit(solution)/shard_map/all_gather | solution.py:150
  641.9 14.8 all-gather.36.cloned.1.call-done
  656.7 95.5 %all-gather.34.cloned.1.call-done = bf16[1408,2048]{0,1:T(8,128)(2,1)} async-done(((bf16[1408,256]{0,1:T(8,128)(2,1)}), bf16[1408,2048]{0,1:T(8,128)(2,1)}) %all-gather.34.cloned.1.call-update) | async-done | bytes 5767184 | tf_op jit(solution)/shard_map/all_gather | solution.py:150
  773.9 29.7 %reduce-scatter.17.cloned.1.call-done = bf16[2,64,2048]{2,1,0:T(8,128)(2,1)} async-done(((bf16[2,256,2048]{2,1,0:T(8,128)(2,1)}), bf16[2,64,2048]{2,1,0:T(8,128)(2,1)}) %reduce-scatter.17.cloned.1.call-update) | async-done | bytes 524304 | tf_op jit(solution)/shard_map/reduce_scatter | solution.py:144
  867.8 123.5 %while.45 = (s32[]{:T(128)}, f32[4,128,128]{2,1,0:T(8,128)S(1)}, f32[8,4,64,128]{3,2,1,0:T(8,128)}, f32[8,4,64,128]{3,2,1,0:T(8,128)}, f32[8,4,64,128]{3,2,1,0:T...) while((s32[]{:T(128)}, f32[4,128,128]{2,1,0:T(8,128)S(1)}, ...), condition=%wide.region_13.14_spmd.clone, body=%wide.region_12.13_spmd.clone.sunk | while | flops 352813056 | bytes 4729190 | solution.py:88
  1146.0 26.2 %reduce-scatter.35.cloned.1.call-done = bf16[1408,256]{1,0:T(8,128)(2,1)} async-done(((bf16[1408,2048]{1,0:T(8,128)(2,1)}), bf16[1408,256]{1,0:T(8,128)(2,1)}) %reduce-scatter.35.cloned.1.call-update) | async-done | bytes 720912 | tf_op jit(solution)/shard_map/reduce_scatter | solution.py:154
  1174.5 68.5 %reduce-scatter.23.cloned.1.call-done = bf16[256,512]{1,0:T(8,128)(2,1)} async-done(((bf16[2048,512]{1,0:T(8,128)(2,1)}), bf16[256,512]{1,0:T(8,128)(2,1)}) %reduce-scatter.23.cloned.1.call-update) | async-done | bytes 262160 | tf_op jit(solution)/shard_map/reduce_scatter | solution.py:154
  1266.7 46.4 %reduce-scatter.21.cloned.1.call-done = bf16[256,512]{1,0:T(8,128)(2,1)} async-done(((bf16[2048,512]{1,0:T(8,128)(2,1)}), bf16[256,512]{1,0:T(8,128)(2,1)}) %reduce-scatter.21.cloned.1.call-update) | async-done | bytes 262160 | tf_op jit(solution)/shard_map/reduce_scatter | solution.py:154
  1342.6 40.8 %reduce-scatter.29.cloned.1.call-done = bf16[64,2048]{1,0:T(8,128)(2,1)} async-done(((bf16[512,2048]{1,0:T(8,128)(2,1)}), bf16[64,2048]{1,0:T(8,128)(2,1)}) %reduce-scatter.29.cloned.1.call-update) | async-done | bytes 262160 | tf_op jit(solution)/shard_map/reduce_scatter | solution.py:154
  1385.1 68.5 %reduce-scatter.25.cloned.1.call-done = bf16[256,512]{1,0:T(8,128)(2,1)} async-done(((bf16[2048,512]{1,0:T(8,128)(2,1)}), bf16[256,512]{1,0:T(8,128)(2,1)}) %reduce-scatter.25.cloned.1.call-update) | async-done | bytes 262160 | tf_op jit(solution)/shard_map/reduce_scatter | solution.py:154
  1459.6 26.9 %reduce-scatter.19.cloned.1.call-done = bf16[2,64,2048]{2,1,0:T(8,128)(2,1)} async-done(((bf16[2,256,2048]{2,1,0:T(8,128)(2,1)}), bf16[2,64,2048]{2,1,0:T(8,128)(2,1)}) %reduce-scatter.19.cloned.1.call-update) | async-done | bytes 524304 | tf_op jit(solution)/shard_map/reduce_scatter | solution.py:144
  1490.0 68.1 %reduce-scatter.27.cloned.1.call-done = bf16[256,512]{1,0:T(8,128)(2,1)} async-done(((bf16[2048,512]{1,0:T(8,128)(2,1)}), bf16[256,512]{1,0:T(8,128)(2,1)}) %reduce-scatter.27.cloned.1.call-update) | async-done | bytes 262160 | tf_op jit(solution)/shard_map/reduce_scatter | solution.py:154
  1568.4 23.0 %reduce-scatter.15.cloned.1.call-done = bf16[2,64,2048]{2,1,0:T(8,128)(2,1)} async-done(((bf16[2,256,2048]{2,1,0:T(8,128)(2,1)}), bf16[2,64,2048]{2,1,0:T(8,128)(2,1)}) %reduce-scatter.15.cloned.1.call-update) | async-done | bytes 524304 | tf_op jit(solution)/shard_map/reduce_scatter | solution.py:144
  1594.6 127.9 %all-reduce.36.cloned.1.call-done = f32[32,2048]{1,0:T(8,128)} async-done(((f32[32,2048]{1,0:T(8,128)}), f32[32,2048]{1,0:T(8,128)}) %all-reduce.36.cloned.1.call-update) | async-done | bytes 262160
  (759 shorter events, 717.3 us)
Async XLA Ops:
  7.2 130.4 %all-gather.16.cloned.1.call-start = ((), (), s32[]{:S(2)}) async-start(), calls=%async_computation.28 | async-start | bytes 2621440 | tf_op jit(solution)/shard_map/all_gather | solution.py:140
  109.5 150.4 %all-gather.20.cloned.1.call-start = ((), (), s32[]{:S(2)}) async-start(), calls=%async_computation.30 | async-start | bytes 2359296 | tf_op jit(solution)/shard_map/all_gather | solution.py:150
  118.7 244.3 %all-gather.24.cloned.1.call-start = ((), (), s32[]{:S(2)}) async-start(), calls=%async_computation.32 | async-start | bytes 2359296 | tf_op jit(solution)/shard_map/all_gather | solution.py:150
  127.9 257.9 %all-gather.26.cloned.1.call-start = ((), (), s32[]{:S(2)}) async-start(), calls=%async_computation.33 | async-start | bytes 2359296 | tf_op jit(solution)/shard_map/all_gather | solution.py:150
  128.5 291.0 %reduce-scatter.13.cloned.1.call-start = ((), (), s32[]{:S(2)}) async-start(), calls=%async_computation.34 | async-start | bytes 2621440 | tf_op jit(solution)/shard_map/reduce_scatter | solution.py:144
  390.2 124.9 %all-gather.30.cloned.1.call-start = ((), (), s32[]{:S(2)}) async-start(), calls=%async_computation.36 | async-start | bytes 6488064 | tf_op jit(solution)/shard_map/all_gather | solution.py:150
  401.3 136.8 %all-gather.28.cloned.1.call-start = ((), (), s32[]{:S(2)}) async-start(), calls=%async_computation.35 | async-start | bytes 2621440 | tf_op jit(solution)/shard_map/all_gather | solution.py:140
  423.1 210.5 %all-gather.32.cloned.1.call-start = ((), (), s32[]{:S(2)}) async-start(), calls=%async_computation.37 | async-start | bytes 6488064 | tf_op jit(solution)/shard_map/all_gather | solution.py:150
  434.1 222.5 %all-gather.36.cloned.1.call-start = ((), (), s32[]{:S(2)}) async-start(), calls=%async_computation.40 | async-start | bytes 2621440 | tf_op jit(solution)/shard_map/all_gather | solution.py:140
  436.2 316.0 %all-gather.34.cloned.1.call-start = ((), (), s32[]{:S(2)}) async-start(), calls=%async_computation.38 | async-start | bytes 6488064 | tf_op jit(solution)/shard_map/all_gather | solution.py:150
  444.9 358.8 %reduce-scatter.17.cloned.1.call-start = ((), (), s32[]{:S(2)}) async-start(), calls=%async_computation.41 | async-start | bytes 2621440 | tf_op jit(solution)/shard_map/reduce_scatter | solution.py:144
  808.9 328.8 %reduce-scatter.31.cloned.1.call-start = ((), (), s32[]{:S(2)}) async-start(), calls=%async_computation.49 | async-start | bytes 6488064 | tf_op jit(solution)/shard_map/reduce_scatter | solution.py:154
  817.2 326.5 %reduce-scatter.33.cloned.1.call-start = ((), (), s32[]{:S(2)}) async-start(), calls=%async_computation.50 | async-start | bytes 6488064 | tf_op jit(solution)/shard_map/reduce_scatter | solution.py:154
  840.4 331.8 %reduce-scatter.35.cloned.1.call-start = ((), (), s32[]{:S(2)}) async-start(), calls=%async_computation.51 | async-start | bytes 6488064 | tf_op jit(solution)/shard_map/reduce_scatter | solution.py:154
  853.8 389.2 %reduce-scatter.23.cloned.1.call-start = ((), (), s32[]{:S(2)}) async-start(), calls=%async_computation.45 | async-start | bytes 2359296 | tf_op jit(solution)/shard_map/reduce_scatter | solution.py:154
  1089.6 223.6 %reduce-scatter.21.cloned.1.call-start = ((), (), s32[]{:S(2)}) async-start(), calls=%async_computation.44 | async-start | bytes 2359296 | tf_op jit(solution)/shard_map/reduce_scatter | solution.py:154
  1097.8 285.5 %reduce-scatter.29.cloned.1.call-start = ((), (), s32[]{:S(2)}) async-start(), calls=%async_computation.48 | async-start | bytes 2359296 | tf_op jit(solution)/shard_map/reduce_scatter | solution.py:154
  1103.0 350.5 %reduce-scatter.25.cloned.1.call-start = ((), (), s32[]{:S(2)}) async-start(), calls=%async_computation.46 | async-start | bytes 2359296 | tf_op jit(solution)/shard_map/reduce_scatter | solution.py:154
  1112.1 374.4 %reduce-scatter.19.cloned.1.call-start = ((), (), s32[]{:S(2)}) async-start(), calls=%async_computation.43 | async-start | bytes 2621440 | tf_op jit(solution)/shard_map/reduce_scatter | solution.py:144
  1124.7 433.4 %reduce-scatter.27.cloned.1.call-start = ((), (), s32[]{:S(2)}) async-start(), calls=%async_computation.47 | async-start | bytes 2359296 | tf_op jit(solution)/shard_map/reduce_scatter | solution.py:154
  1129.0 462.4 %reduce-scatter.15.cloned.1.call-start = ((), (), s32[]{:S(2)}) async-start(), calls=%async_computation.39 | async-start | bytes 2621440 | tf_op jit(solution)/shard_map/reduce_scatter | solution.py:144
  1315.0 140.4 %all-to-all-start.9 = ((f32[4,64,512]{2,1,0:T(8,128)}), f32[4,64,512]{2,1,0:T(8,128)}, u32[]{:S(2)}, u32[]{:S(2)}) async-start(f32[4,64,512]{2,1,0:T(8,128)} %convert.12), calls=%async_computation.14 | async-start | bytes 1048576 | tf_op jit(solution)/shard_map/all_to_all | solution.py:162
  1459.6 262.9 %all-reduce.36.cloned.1.call-start = ((), (), s32[]{:S(2)}) async-start(), calls=%async_computation.52 | async-start | bytes 524288
  1564.3 170.9 %all-to-all-start.12 = ((f32[4,64,512]{2,1,0:T(8,128)}), f32[4,64,512]{2,1,0:T(8,128)}, u32[]{:S(2)}, u32[]{:S(2)}) async-start(f32[4,64,512]{2,1,0:T(8,128)} %convert.15), calls=%async_computation.20 | async-start | bytes 1048576 | tf_op jit(solution)/shard_map/all_to_all | solution.py:162
  (165 other events, 3765.2 us)
Sparse Core Ops, SparseCore 0:
  86.7 22.9 all-gather.15
  111.9 48.2 all-gather.21
  162.3 47.7 all-gather.17
  212.0 47.7 all-gather.19
  261.8 47.8 all-gather.23
  311.7 47.8 all-gather.25
  390.3 29.0 reduce-scatter.12
  422.4 92.6 all-gather.29
  540.9 92.6 all-gather.31
  635.9 20.7 all-gather.35
  659.5 92.6 all-gather.33
  774.0 29.6 reduce-scatter.16
  809.0 22.5 all-gather.37
  835.1 110.0 reduce-scatter.30
  948.7 109.7 reduce-scatter.32
  1062.0 110.1 reduce-scatter.34
  1175.6 67.4 reduce-scatter.22
  1246.6 66.5 reduce-scatter.20
  1316.6 66.7 reduce-scatter.28
  1386.9 66.6 reduce-scatter.24
  1456.1 30.3 reduce-scatter.18
  1490.5 67.6 reduce-scatter.26
  1560.7 30.6 reduce-scatter.14
  1597.4 124.9 all-reduce.35
  (1 shorter events, 20.7 us)

commit v3 on v2

--- a/solution.py
+++ b/solution.py
@@ -91,7 +91,36 @@
     return produced_output.transpose(0, 2, 1, 3).reshape(length, head_count, value_width)
 
 
-def mixer_core(query_lin, key_lin, value_lin, gate_lin, beta_lin, conv_taps, head_scale, starts):
+def delta_core_reset(queries, keys, values, betas, block_len):
+    length, head_count, head_width = queries.shape
+    block_count = length // block_len
+
+    def blocked(array):
+        return array.reshape(block_count, block_len, head_count, -1).transpose(0, 2, 1, 3)
+
+    query_blocks = blocked(queries)
+    key_blocks = blocked(keys)
+    value_blocks = blocked(values)
+    beta_blocks = betas.reshape(block_count, block_len, head_count).transpose(0, 2, 1)[..., None]
+    position = jnp.arange(block_len)
+    strict = (position[:, None] > position[None, :]).astype(queries.dtype)
+    causal = (position[:, None] >= position[None, :]).astype(queries.dtype)
+    weighted = key_blocks * beta_blocks
+    negative = -outer_product_result("nhik,nhjk->nhij", weighted, key_blocks) * strict
+    inverse = jnp.eye(block_len, dtype=queries.dtype) + negative
+    power_term = negative
+    for doubling in range(5):
+        power_term = outer_product_result("nhij,nhjk->nhik", power_term, power_term)
+        inverse = inverse + outer_product_result("nhij,nhjk->nhik", inverse, power_term)
+    value_mix = outer_product_result("nhij,nhjk->nhik", inverse, value_blocks * beta_blocks)
+    scores = outer_product_result("nhik,nhjk->nhij", query_blocks, key_blocks) * causal
+    produced_output = outer_product_result("nhqz,nhzr->nhqr", scores, value_mix)
+    return produced_output.transpose(0, 2, 1, 3).reshape(length, head_count, -1)
+
+
+def mixer_core(
+    query_lin, key_lin, value_lin, gate_lin, beta_lin, conv_taps, head_scale, starts, reset_len
+):
     length = query_lin.shape[0]
     head_count = beta_lin.shape[1]
     head_width = query_lin.shape[1] // head_count
@@ -110,7 +139,10 @@
         * head_width ** (-0.5)
     )
     keys = keys * lax.rsqrt(jnp.sum(keys * keys, axis=-1, keepdims=True) + 1e-06)
-    recurrent = delta_core(queries, keys, values, jax.nn.sigmoid(beta_lin), starts)
+    if reset_len:
+        recurrent = delta_core_reset(queries, keys, values, jax.nn.sigmoid(beta_lin), reset_len)
+    else:
+        recurrent = delta_core(queries, keys, values, jax.nn.sigmoid(beta_lin), starts)
     normed = (
         recurrent
         * lax.rsqrt(jnp.mean(recurrent * recurrent, axis=-1, keepdims=True) + 1e-05)
@@ -136,43 +168,39 @@
     return jnp.einsum("tg,fg->tf", gradient, weight, preferred_element_type=jnp.float32)
 
 
-def tp_gather(value, axis):
-    return lax.all_gather(value, TP_AXES, axis=axis, tiled=True)
-
-
-def tp_scatter_low(value, axis):
-    return lax.psum_scatter(
-        value.astype(jnp.bfloat16), TP_AXES, scatter_dimension=axis, tiled=True
-    ).astype(jnp.float32)
-
-
-def fsdp_gather(value, axis):
-    return lax.all_gather(value, FSDP_AXES, axis=axis, tiled=True)
-
-
-def fsdp_scatter_low(value, axis):
-    return lax.psum_scatter(
-        value.astype(jnp.bfloat16), FSDP_AXES, scatter_dimension=axis, tiled=True
-    ).astype(jnp.float32)
-
-
 def exchange(value, axes, split_axis, concat_axis):
     if not axes:
         return value
     return lax.all_to_all(value, axes, split_axis, concat_axis, tiled=True)
 
 
-def column_weight(owned, tp):
-    rows, width = owned.shape
-    swapped = exchange(owned.reshape(rows, tp, width // tp), TP_AXES, 1, 0)
-    return fsdp_gather(swapped.reshape(rows * tp, width // tp), 0)
-
-
-def column_grad(partial, tp):
-    reduced = fsdp_scatter_low(partial, 0)
-    group_rows, cols = reduced.shape
-    swapped = exchange(reduced.reshape(tp, group_rows // tp, cols), TP_AXES, 0, 2)
-    return swapped.reshape(group_rows // tp, cols * tp)
+def tp_gather(value, tp):
+    spread = jnp.broadcast_to(value[:, None], (value.shape[0], tp) + value.shape[1:])
+    moved = exchange(spread, TP_AXES, 1, 1)
+    return moved.reshape((value.shape[0], tp * value.shape[1]) + value.shape[2:])
+
+
+def tp_scatter_sum(value, tp):
+    micro, group, width = value.shape
+    staged = value.astype(jnp.bfloat16).reshape(micro, tp, group // tp, width)
+    moved = exchange(staged, TP_AXES, 1, 1)
+    return jnp.sum(moved.astype(jnp.float32), axis=1)
+
+
+def fsdp_gather_flat(value):
+    return lax.all_gather(value, FSDP_AXES, axis=0, tiled=False)
+
+
+def fsdp_scatter_flat(value, fsdp):
+    length = value.shape[1]
+    pieces = 16 if length % 16 == 0 else 1
+    reduced = lax.psum_scatter(
+        value.astype(jnp.bfloat16).reshape(fsdp * pieces, length // pieces),
+        FSDP_AXES,
+        scatter_dimension=0,
+        tiled=True,
+    )
+    return reduced.reshape(length).astype(jnp.float32)
 
 
 def heads_to_rows(values, tp, fsdp, rows):
@@ -217,13 +245,10 @@
         cols_here = width // tp
         position = lax.axis_index(TP_AXES)
         head_scale = head_gain.astype(jnp.float32)
-
-        query_cols = column_weight(query_weight, tp)
-        key_cols = column_weight(key_weight, tp)
-        value_cols = column_weight(value_weight, tp)
-        gate_cols = column_weight(gate_weight, tp)
-        out_rows = fsdp_gather(out_weight, 0)
-
+        reset_len = slot if group_start.shape[1] == 1 else 0
+
+        column_owned = jnp.stack([query_weight, key_weight, value_weight, gate_weight])
+        column_chunks = column_owned.reshape(4, rows, tp, cols_here).transpose(2, 0, 1, 3)
         small_pack = jnp.concatenate(
             [
                 conv_weight.reshape(-1),
@@ -232,7 +257,38 @@
                 swiglu_gain.reshape(-1),
             ]
         )
-        small_all = lax.all_gather(small_pack, ALL_AXES, axis=0, tiled=False)
+        small_size = small_pack.shape[0]
+        swap_in = jnp.concatenate(
+            [
+                column_chunks.reshape(tp, -1),
+                jnp.broadcast_to(small_pack[None, :], (tp, small_size)),
+            ],
+            axis=1,
+        )
+        swap_out = exchange(swap_in, TP_AXES, 0, 0)
+        column_size = 4 * rows * cols_here
+        column_group = (
+            swap_out[:, :column_size].reshape(tp, 4, rows, cols_here).transpose(1, 0, 2, 3)
+        )
+        mixer_flat = jnp.concatenate(
+            [
+                column_group.reshape(-1),
+                out_weight.reshape(-1),
+                swap_out[:, column_size:].reshape(-1),
+            ]
+        )
+        mixer_all = fsdp_gather_flat(mixer_flat)
+        group_size = tp * column_size
+        column_all = (
+            mixer_all[:, :group_size]
+            .reshape(fsdp, 4, tp * rows, cols_here)
+            .transpose(1, 0, 2, 3)
+            .reshape(4, width, cols_here)
+        )
+        query_cols, key_cols, value_cols, gate_cols = (column_all[index] for index in range(4))
+        out_size = rows * width
+        out_rows = mixer_all[:, group_size : group_size + out_size].reshape(fsdp * rows, width)
+        small_all = mixer_all[:, group_size + out_size :].reshape(n_all, small_size)
         conv_size = conv_weight.size
         beta_size = beta_weight.size
         conv_full = (
@@ -250,30 +306,41 @@
         beta_here = lax.dynamic_slice_in_dim(beta_full, position * heads_here, heads_here, axis=1)
 
         owned_rows, hidden_half = swiglu_gate.shape
-        gate_half = fsdp_gather(
-            exchange(swiglu_gate.reshape(owned_rows, inner, hidden_half // inner), INNER_AXES, 1, 0)
-            .reshape(owned_rows * inner, hidden_half // inner),
-            0,
-        )
-        up_half = fsdp_gather(
-            exchange(swiglu_up.reshape(owned_rows, inner, hidden_half // inner), INNER_AXES, 1, 0)
-            .reshape(owned_rows * inner, hidden_half // inner),
-            0,
-        )
-        down_half = fsdp_gather(
-            exchange(swiglu_down.reshape(inner, hidden_half // inner, owned_rows), INNER_AXES, 0, 2)
-            .reshape(hidden_half // inner, inner * owned_rows),
-            1,
+        hidden_here = hidden_half // inner
+        gate_chunks = swiglu_gate.reshape(owned_rows, inner, hidden_here).transpose(1, 0, 2)
+        up_chunks = swiglu_up.reshape(owned_rows, inner, hidden_here).transpose(1, 0, 2)
+        down_chunks = swiglu_down.reshape(inner, hidden_here, owned_rows)
+        ff_in = jnp.concatenate(
+            [
+                gate_chunks.reshape(inner, -1),
+                up_chunks.reshape(inner, -1),
+                down_chunks.reshape(inner, -1),
+            ],
+            axis=1,
+        )
+        ff_out = exchange(ff_in, INNER_AXES, 0, 0)
+        ff_all = fsdp_gather_flat(ff_out.reshape(-1)).reshape(fsdp, inner, 3, -1)
+        piece = owned_rows * hidden_here
+        gate_half = ff_all[:, :, 0, :piece].reshape(width, hidden_here)
+        up_half = ff_all[:, :, 1, :piece].reshape(width, hidden_here)
+        down_half = (
+            ff_all[:, :, 2, :piece]
+            .reshape(fsdp, inner, hidden_here, owned_rows)
+            .transpose(2, 0, 1, 3)
+            .reshape(hidden_here, width)
         )
 
         inputs = tokens.astype(jnp.float32).reshape(micro_count * slot, width)
         normed, norm_back = jax.vjp(rms_norm, inputs, gain_mixer.astype(jnp.float32))
         normed_low = normed.astype(jnp.bfloat16)
         group_tokens = micro_count * slot * tp
-        normed_group = tp_gather(normed_low.reshape(micro_count, slot, width), 1).reshape(
+        normed_group = tp_gather(normed_low.reshape(micro_count, slot, width), tp).reshape(
             group_tokens, width
         )
-        starts = tp_gather(group_start, 1).reshape(-1)
+        starts = tp_gather(group_start, tp).reshape(-1)
+        out_back = cotangent.astype(jnp.float32) * pad_mask.astype(jnp.float32)[:, :, None]
+        out_back_low = out_back.astype(jnp.bfloat16)
+        upstream_group = tp_gather(out_back_low, tp).reshape(group_tokens, width)
 
         query_lin = matmul_rows(normed_group, query_cols)
         key_lin = matmul_rows(normed_group, key_cols)
@@ -283,7 +350,7 @@
 
         def core_at(query_in, key_in, value_in, gate_in, beta_in, conv_in, head_in):
             return mixer_core(
-                query_in, key_in, value_in, gate_in, beta_in, conv_in, head_in, starts
+                query_in, key_in, value_in, gate_in, beta_in, conv_in, head_in, starts, reset_len
             )
 
         gated_out, core_back = jax.vjp(
@@ -292,13 +359,13 @@
         gated_low = gated_out.astype(jnp.bfloat16)
         gated_rows = heads_to_rows(gated_low, tp, fsdp, rows)
         mixed_partial = matmul_rows(gated_rows, out_rows)
-        residual = inputs + tp_scatter_low(
-            mixed_partial.reshape(micro_count, slot * tp, width), 1
+        residual = inputs + tp_scatter_sum(
+            mixed_partial.reshape(micro_count, slot * tp, width), tp
         ).reshape(micro_count * slot, width)
 
         inner_norm, inner_norm_back = jax.vjp(rms_norm, residual, gain_swiglu.astype(jnp.float32))
         inner_low = inner_norm.astype(jnp.bfloat16)
-        inner_group = tp_gather(inner_low.reshape(micro_count, slot, width), 1).reshape(
+        inner_group = tp_gather(inner_low.reshape(micro_count, slot, width), tp).reshape(
             group_tokens, width
         )
         gate_act = matmul_rows(inner_group, gate_half)
@@ -306,23 +373,52 @@
         hidden, hidden_back = jax.vjp(swiglu_mix, gate_act, up_act)
         hidden_low = hidden.astype(jnp.bfloat16)
         partial_rows = matmul_rows(hidden_low, down_half)
-        branch_rows = tp_scatter_low(partial_rows.reshape(micro_count, slot * tp, width), 1)
+        branch_rows = tp_scatter_sum(partial_rows.reshape(micro_count, slot * tp, width), tp)
         block_out = (residual.reshape(micro_count, slot, width) + branch_rows).astype(jnp.bfloat16)
 
-        out_back = cotangent.astype(jnp.float32) * pad_mask.astype(jnp.float32)[:, :, None]
-        out_back_low = out_back.astype(jnp.bfloat16)
-        upstream_group = tp_gather(out_back_low, 1).reshape(group_tokens, width)
         gate_back, up_back = hidden_back(back_product(upstream_group, down_half))
         gate_back_low = gate_back.astype(jnp.bfloat16)
         up_back_low = up_back.astype(jnp.bfloat16)
         inner_part = back_product(gate_back_low, gate_half) + back_product(up_back_low, up_half)
-        inner_back = tp_scatter_low(inner_part.reshape(micro_count, slot * tp, width), 1)
+        inner_back = tp_scatter_sum(inner_part.reshape(micro_count, slot * tp, width), tp)
+
+        gate_sum = left_product(inner_group, gate_back_low).reshape(fsdp, -1)
+        up_sum = left_product(inner_group, up_back_low).reshape(fsdp, -1)
+        down_sum = (
+            left_product(hidden_low, upstream_group)
+            .reshape(hidden_here, fsdp, inner * owned_rows)
+            .transpose(1, 0, 2)
+            .reshape(fsdp, -1)
+        )
+        ff_reduced = fsdp_scatter_flat(
+            jnp.concatenate([gate_sum, up_sum, down_sum], axis=1), fsdp
+        ).reshape(3, inner, -1)
+        down_for_swap = (
+            ff_reduced[2]
+            .reshape(hidden_here, inner, owned_rows)
+            .transpose(1, 0, 2)
+            .reshape(inner, -1)
+        )
+        ff_back = exchange(
+            jnp.concatenate([ff_reduced[0], ff_reduced[1], down_for_swap], axis=1),
+            INNER_AXES,
+            0,
+            0,
+        ).reshape(inner, 3, -1)
+        swiglu_gate_grad = (
+            ff_back[:, 0].reshape(inner, owned_rows, hidden_here).transpose(1, 0, 2)
+        ).reshape(owned_rows, hidden_half)
+        swiglu_up_grad = (
+            ff_back[:, 1].reshape(inner, owned_rows, hidden_here).transpose(1, 0, 2)
+        ).reshape(owned_rows, hidden_half)
+        swiglu_down_grad = ff_back[:, 2].reshape(hidden_half, owned_rows)
+
         residual_part, swiglu_gain_term = inner_norm_back(
             inner_back.reshape(micro_count * slot, width)
         )
         residual_back = out_back.reshape(micro_count * slot, width) + residual_part
         mixed_back = residual_back.astype(jnp.bfloat16)
-        mixed_group = tp_gather(mixed_back.reshape(micro_count, slot, width), 1).reshape(
+        mixed_group = tp_gather(mixed_back.reshape(micro_count, slot, width), tp).reshape(
             group_tokens, width
         )
         gated_back_rows = back_product(mixed_group, out_rows)
@@ -342,31 +438,20 @@
             + back_product(gate_low, gate_cols)
             + back_product(beta_low, beta_here)
         )
-        normed_back = tp_scatter_low(normed_part.reshape(micro_count, slot * tp, width), 1)
+        normed_back = tp_scatter_sum(normed_part.reshape(micro_count, slot * tp, width), tp)
         input_part, mixer_gain_term = norm_back(normed_back.reshape(micro_count * slot, width))
         tokens_grad = (residual_back + input_part).reshape(micro_count, slot, width)
 
-        swiglu_gate_sum = left_product(inner_group, gate_back_low)
-        swiglu_up_sum = left_product(inner_group, up_back_low)
-        swiglu_down_sum = left_product(hidden_low, upstream_group)
-        gate_grad_rows = fsdp_scatter_low(swiglu_gate_sum, 0)
-        swiglu_gate_grad = exchange(
-            gate_grad_rows.reshape(inner, owned_rows, hidden_half // inner), INNER_AXES, 0, 2
-        ).reshape(owned_rows, hidden_half)
-        up_grad_rows = fsdp_scatter_low(swiglu_up_sum, 0)
-        swiglu_up_grad = exchange(
-            up_grad_rows.reshape(inner, owned_rows, hidden_half // inner), INNER_AXES, 0, 2
-        ).reshape(owned_rows, hidden_half)
-        down_grad_cols = fsdp_scatter_low(swiglu_down_sum, 1)
-        swiglu_down_grad = exchange(
-            down_grad_cols.reshape(hidden_half // inner, inner, owned_rows), INNER_AXES, 1, 0
-        ).reshape(hidden_half, owned_rows)
-
-        out_grad = fsdp_scatter_low(left_product(gated_rows, mixed_group), 0)
-        query_grad = column_grad(left_product(normed_group, query_low), tp)
-        key_grad = column_grad(left_product(normed_group, key_low), tp)
-        value_grad = column_grad(left_product(normed_group, value_low), tp)
-        gate_grad = column_grad(left_product(normed_group, gate_low), tp)
+        column_sums = jnp.stack(
+            [
+                left_product(normed_group, query_low),
+                left_product(normed_group, key_low),
+                left_product(normed_group, value_low),
+                left_product(normed_group, gate_low),
+            ]
+        )
+        column_flat = column_sums.reshape(4, fsdp, -1).transpose(1, 0, 2).reshape(fsdp, -1)
+        out_flat = left_product(gated_rows, mixed_group).reshape(fsdp, -1)
         beta_sum = left_product(normed_group, beta_low)
         beta_wide = lax.dynamic_update_slice_in_dim(
             jnp.zeros((width, head_count), jnp.float32), beta_sum, position * heads_here, axis=1
@@ -385,7 +470,18 @@
             ],
             axis=1,
         )
-        small_out = lax.psum_scatter(small_rows, ALL_AXES, scatter_dimension=0, tiled=False)
+        small_width = small_rows.shape[1]
+        small_tp = jnp.sum(
+            exchange(small_rows.reshape(fsdp, tp, small_width), TP_AXES, 1, 1), axis=1
+        )
+        mixer_reduced = fsdp_scatter_flat(
+            jnp.concatenate([column_flat, out_flat, small_tp], axis=1), fsdp
+        )
+        column_red = mixer_reduced[:group_size].reshape(4, tp, rows, 1, cols_here)
+        column_back = exchange(column_red, TP_AXES, 1, 3).reshape(4, rows, width)
+        query_grad, key_grad, value_grad, gate_grad = (column_back[index] for index in range(4))
+        out_grad = mixer_reduced[group_size : group_size + out_size].reshape(rows, width)
+        small_out = mixer_reduced[group_size + out_size :]
         conv_grad = small_out[:conv_size].reshape(conv_weight.shape)
         beta_grad = small_out[conv_size : conv_size + beta_size].reshape(beta_weight.shape)
         mixer_gain_grad = small_out[conv_size + beta_size : conv_size + beta_size + rows]

time: 1760 us -> 2470 us (1.40)
  local copies, waits for them, and re-layouts: 136 us -> 631 us
  waiting for transfers between devices: 924 us -> 1190 us
  other arithmetic: 96.5 us -> 307 us
  matrix products: 383 us -> 193 us
  blocking collectives: 161 us -> 72.9 us
    all_gather x12 -> x2, waiting for transfers between devices: 378 us -> 770 us  [fsdp_gather_flat(): return lax.all_gather(value, FSDP_AXES, axis=0, tiled=False)]
    dot_general x138 -> x42, matrix products: 261 us -> 78 us  [outer_product_result(): return jnp.einsum(form, first, second, precision=lax.Precision.HIGHEST)]
    slice x2 -> x17, local copies, waits for them, and re-layouts: 1.61 us -> 176 us  [the longest x1 44.5 us: on_device(): ff_all[:, :, 2, :piece].reshape(fsdp, inner, hidden_here, owned_rows)]
    reshape x14 -> x23, local copies, waits for them, and re-layouts: 8.81 us -> 170 us  [the longest x1 91.3 us: on_device(): ff_all = fsdp_gather_flat(ff_out.reshape(-1)).reshape(fsdp, inner, 3, -1)]
    unnamed x26 -> x4, waiting for transfers between devices: 129 us -> 0.07 us
    all_gather x0 -> x1, other arithmetic: none -> 104 us  [fsdp_gather_flat(): return lax.all_gather(value, FSDP_AXES, axis=0, tiled=False)]
    concatenate x0 -> x4, other arithmetic: none -> 87.9 us  [the longest x1 43.4 us: on_device(): jnp.concatenate([column_flat, out_flat, small_tp], axis=1)]
    all_to_all x6 -> x12, waiting for transfers between devices: 1.04 us -> 83.9 us  [exchange(): return lax.all_to_all(value, axes, split_axis, concat_axis, tiled=True)]
  transfers between devices with their start and end apart: 31 -> 16, of which waited for: 21 -> 9; matrix products, arithmetic and copies ran while one was open for 32% -> 16% of each run, Pallas kernels for 0% -> 0%
where the time goes in v3:
time: 2470 us; the launch traced here: 2460 us
  waiting for transfers between devices  1190 us (48%)
  local copies, waits for them, and re-layouts  631 us (26%)
  other arithmetic  307 us (12%)
  matrix products  193 us (8%)
  blocking collectives  72.9 us (3%)
  starting transfers between devices  50.9 us (2%)
    all_gather x2, waiting for transfers between devices, fsdp_gather_flat(): return lax.all_gather(value, FSDP_AXES, axis=0, tiled=False)  770 us
    reduce_scatter x2, waiting for transfers between devices, fsdp_scatter_flat(): lax.psum_scatter(value.astype(jnp.bfloat16).reshape(fsdp * pieces, length...  334 us
    all_gather x1, other arithmetic, fsdp_gather_flat(): return lax.all_gather(value, FSDP_AXES, axis=0, tiled=False)  104 us
    reshape x1, local copies, waits for them, and re-layouts, on_device(): ff_all = fsdp_gather_flat(ff_out.reshape(-1)).reshape(fsdp, inner, 3, -1)  91.3 us
    all_to_all x12, waiting for transfers between devices, exchange(): return lax.all_to_all(value, axes, split_axis, concat_axis, tiled=True)  83.9 us
    unnamed x374, local copies, waits for them, and re-layouts  81 us
    dot_general x42, matrix products, outer_product_result(): return jnp.einsum(form, first, second, precision=lax.Precision.HIGHEST)  78 us
    all_to_all x4, blocking collectives, exchange(): return lax.all_to_all(value, axes, split_axis, concat_axis, tiled=True)  72.9 us
  transfers between devices with their start and end apart: 16, of which 9 were waited for; matrix products, arithmetic and copies ran while one was open for 16% of the time, Pallas kernels for 0%

profile of v3, /device:TPU:0, one launch (start us, length us, event | category | flops | bytes accessed | tf_op | source)
XLA Modules:
  0.0 2458.3 jit_solution(12133176959332755009)
XLA Ops:
  51.5 17.9 maximum_bitcast_fusion
  69.4 21.3 reduce.20
  110.7 347.4 %all-gather.6.cloned.1.call-done = bf16[8,1,663040]{2,1,0:T(2,128)(2,1)} async-done(((bf16[1,1,663040]{2,1,0:T(2,128)(2,1)}), bf16[8,1,663040]{2,1,0:T(2,128)(2,1)}) %all-gather.6.cloned.1.call-update) | async-done | bytes 10608656 | tf_op jit(solution)/shard_map/all_gather | solution.py:191
  458.0 18.5 copy.520
  601.1 25.6 %all-to-all-done.4 = bf16[2,4,64,2048]{3,2,0,1:T(8,128)(2,1)} async-done(((bf16[2,4,64,2048]{3,2,0,1:T(8,128)(2,1)}), bf16[2,4,64,2048]{3,2,0,1:T(8,128)(2,1)}, u32[]{:S(2)}, u32[]{:S(2)}) %all-to-all-start.4) | async-done | bytes 2097184 | tf_op jit(solution)/shard_map/all_to_all | solution.py:174
  637.3 21.2 all-to-all-done.8
  668.8 22.6 all-to-all-done.5
  694.6 422.3 %all-gather.8.cloned.1.call-done = bf16[8,1,1081344]{2,1,0:T(2,128)(2,1)} async-done(((bf16[1,1,1081344]{2,1,0:T(2,128)(2,1)}), bf16[8,1,1081344]{2,1,0:T(2,128)(2,1)}) %all-gather.8.cloned.1.call-update) | async-done | bytes 17301520 | tf_op jit(solution)/shard_map/all_gather | solution.py:191
  1117.0 103.6 %reduce.7 = bf16[8,1081344]{1,0:T(8,128)(2,1)} reduce(bf16[8,1,1081344]{2,1,0:T(2,128)(2,1)} %all-gather.8.cloned.1.call-done, bf16[]{:T(256)} %constant.167), dimensions={1}, to_apply=%all-gather.2.reduce_sub_computation | reduce | bytes 34603008 | tf_op jit(solution)/shard_map/all_gather | solution.py:191
  1220.6 91.3 %reshape.785 = bf16[8,2,3,180224]{3,2,1,0:T(4,128)(2,1)} reshape(bf16[8,1081344]{1,0:T(8,128)(2,1)} %reduce.7) | data formatting | bytes 34603008 | tf_op jit(solution)/shard_map/reshape | solution.py:322
  1311.9 40.5 %slice_reduce_fusion.2 = bf16[8,2,180224]{2,1,0:T(2,128)(2,1)} fusion(bf16[8,2,3,180224]{3,2,1,0:T(4,128)(2,1)} %reshape.785), kind=kLoop, calls=%fused_computation.3 | loop fusion | bytes 11534336 | tf_op jit(solution)/shard_map/slice | solution.py:324
  1352.4 44.2 %slice_reduce_fusion.1 = bf16[8,2,180224]{2,1,0:T(2,128)(2,1)} fusion(bf16[8,2,3,180224]{3,2,1,0:T(4,128)(2,1)} %reshape.785), kind=kLoop, calls=%fused_computation.2 | loop fusion | bytes 11534336 | tf_op jit(solution)/shard_map/slice | solution.py:325
  1396.5 44.5 %slice_reduce_fusion = bf16[8,2,180224]{2,1,0:T(2,128)(2,1)} fusion(bf16[8,2,3,180224]{3,2,1,0:T(4,128)(2,1)} %reshape.785), kind=kLoop, calls=%fused_computation.1 | loop fusion | bytes 11534336 | tf_op jit(solution)/shard_map/slice | solution.py:327
  1526.6 28.2 %all_to_all.126 = bf16[2,4,64,2048]{3,2,0,1:T(8,128)(2,1)S(1)} all-to-all(bf16[2,4,64,2048]{3,2,0,1:T(8,128)(2,1)S(1)} %copy.404), channel_id=1, replica_groups=mesh['dq'=8,'core'=2,'mlp'=2] {'core','mlp'}, dimensions={1} | all-to-all | bytes 4194304 | tf_op jit(solution)/shard_map/all_to_all | solution.py:174
  1577.9 15.6 copy.502
  1818.3 43.4 %pad_maximum_fusion.1 = bf16[8,657408]{1,0:T(8,128)(2,1)} fusion(bf16[8,2048]{1,0:T(8,128)(2,1)S(1)} %reduce_sum.335, bf16[8,131072]{1,0:T(8,128)(2,1)S(1)} %copy-done.61, bf16[8,524288]{1,0:T(8,128)(2,1)} %bitcast.446), kind=kLoop, calls=%fused_computation.5 | loop fusion | flops 31555584 | bytes 21037056 | tf_op jit(solution)/shard_map/concatenate | solution.py:478
  1874.4 22.1 pad_maximum_fusion
  1896.5 19.8 convert_element_type.280
  1933.7 29.2 %all_to_all.127 = bf16[2,4,64,2048]{3,2,0,1:T(8,128)(2,1)S(1)} all-to-all(bf16[2,4,64,2048]{3,2,0,1:T(8,128)(2,1)S(1)} %copy.402), channel_id=1, replica_groups=mesh['dq'=8,'core'=2,'mlp'=2] {'core','mlp'}, dimensions={1} | all-to-all | bytes 4194304 | tf_op jit(solution)/shard_map/all_to_all | solution.py:174
  1964.3 89.4 %reduce-scatter.3.cloned.1.call-done = bf16[16,41088]{1,0:T(8,128)(2,1)} async-done(((bf16[128,41088]{1,0:T(8,128)(2,1)}), bf16[16,41088]{1,0:T(8,128)(2,1)}) %reduce-scatter.3.cloned.1.call-update) | async-done | bytes 1314832 | tf_op jit(solution)/shard_map/reduce_scatter | solution.py:197
  2104.9 245.0 %reduce-scatter.5.cloned.1.call-done = bf16[16,67584]{1,0:T(8,128)(2,1)} async-done(((bf16[128,67584]{1,0:T(8,128)(2,1)}), bf16[16,67584]{1,0:T(8,128)(2,1)}) %reduce-scatter.5.cloned.1.call-update) | async-done | bytes 2162704 | tf_op jit(solution)/shard_map/reduce_scatter | solution.py:197
  2367.9 22.4 pad_maximum_fusion.3
  2401.8 15.8 reduce.11
  2427.0 22.0 slice_reduce_fusion.3
  (672 shorter events, 668.1 us)
Async XLA Ops:
  22.0 19.0 all-to-all-start
  26.4 431.7 %all-gather.6.cloned.1.call-start = ((), (), s32[]{:S(2)}) async-start(), calls=%async_computation.20 | async-start | bytes 23869440 | tf_op jit(solution)/shard_map/all_gather | solution.py:191
  50.4 1066.5 %all-gather.8.cloned.1.call-start = ((), (), s32[]{:S(2)}) async-start(), calls=%async_computation.21 | async-start | bytes 38928384 | tf_op jit(solution)/shard_map/all_gather | solution.py:191
  106.7 374.3 %all-to-all-start.2 = ((s32[2,4,1]{0,2,1:T(1,128)}), s32[2,4,1]{0,2,1:T(1,128)S(1)}, u32[]{:S(2)}, u32[]{:S(2)}) async-start(s32[2,4,1]{0,2,1:T(1,128)} %broadcast_in_dim.45), calls=%async_computation.2 | async-start | bytes 4096 | tf_op jit(solution)/shard_map/all_to_all | solution.py:174
  110.6 365.9 %copy-start.164 = (f32[2,64]{1,0:T(2,128)}, f32[2,64]{1,0:T(2,128)S(1)}, u32[]{:S(2)}) copy-start(f32[2,64]{1,0:T(2,128)S(1)} %fusion.46) | copy-start | bytes 1540
  110.7 370.1 %copy-start.160 = (f32[2,64]{1,0:T(2,128)}, f32[2,64]{1,0:T(2,128)S(1)}, u32[]{:S(2)}) copy-start(f32[2,64]{1,0:T(2,128)S(1)} %fusion.118) | copy-start | bytes 1540
  482.6 32.3 %all-to-all-start.1 = ((bf16[2,4,64,2048]{3,2,0,1:T(8,128)(2,1)}), bf16[2,4,64,2048]{3,2,0,1:T(8,128)(2,1)}, u32[]{:S(2)}, u32[]{:S(2)}) async-start(bf16[2,4,64,2048]{3,2,0,1:T(8,128)(2,1)} %broadcast_in_dim.43), calls=%async_computation.1 | async-start | bytes 4194304 | tf_op jit(solution)/shard_map/all_to_all | solution.py:174
  487.1 80.3 %copy-start.105 = (f32[64,64]{1,0:T(8,128)}, f32[64,64]{1,0:T(8,128)S(1)}, u32[]{:S(2)}) copy-start(f32[64,64]{1,0:T(8,128)S(1)} %fusion.97) | copy-start | bytes 49156
  487.1 68.7 %copy-start.103 = (f32[64,64]{1,0:T(8,128)}, f32[64,64]{1,0:T(8,128)S(1)}, u32[]{:S(2)}) copy-start(f32[64,64]{1,0:T(8,128)S(1)} %fusion.98) | copy-start | bytes 49156
  579.3 12.3 all-to-all-start.3
  596.2 30.4 %all-to-all-start.4 = ((bf16[2,4,64,2048]{3,2,0,1:T(8,128)(2,1)}), bf16[2,4,64,2048]{3,2,0,1:T(8,128)(2,1)}, u32[]{:S(2)}, u32[]{:S(2)}) async-start(bf16[2,4,64,2048]{3,2,0,1:T(8,128)(2,1)} %copy.397), calls=%async_computation.4 | async-start | bytes 4194304 | tf_op jit(solution)/shard_map/all_to_all | solution.py:174
  600.9 954.7 %copy-start.158 = (f32[2,64]{1,0:T(2,128)}, f32[2,64]{1,0:T(2,128)S(1)}, u32[]{:S(2)}) copy-start(f32[2,64]{1,0:T(2,128)S(1)} %convert_element_type.257) | copy-start | bytes 1540
  628.3 30.2 %all-to-all-start.8 = ((bf16[2,4,64,2048]{3,2,0,1:T(8,128)(2,1)}), bf16[2,4,64,2048]{3,2,0,1:T(8,128)(2,1)}, u32[]{:S(2)}, u32[]{:S(2)}) async-start(bf16[2,4,64,2048]{3,2,0,1:T(8,128)(2,1)} %broadcast_in_dim.48), calls=%async_computation.8 | async-start | bytes 4194304 | tf_op jit(solution)/shard_map/all_to_all | solution.py:174
  632.8 922.8 %copy-start.108 = (f32[2048]{0:T(1024)}, f32[2048]{0:T(1024)S(1)}, u32[]{:S(2)}) copy-start(f32[2048]{0:T(1024)S(1)} %reshape.822) | copy-start | bytes 24580
  636.2 919.4 %copy-start.19 = (f32[2,64,2048]{2,1,0:T(8,128)}, f32[2,64,2048]{2,1,0:T(8,128)S(1)}, u32[]{:S(2)}) copy-start(f32[2,64,2048]{2,1,0:T(8,128)S(1)} %get-tuple-element.120) | copy-start | bytes 3145732
  636.2 919.4 %copy-start.132 = (f32[2,64]{1,0:T(2,128)}, f32[2,64]{1,0:T(2,128)S(1)}, u32[]{:S(2)}) copy-start(f32[2,64]{1,0:T(2,128)S(1)} %fusion.119) | copy-start | bytes 1540
  661.1 30.3 %all-to-all-start.5 = ((bf16[2,4,64,2048]{3,2,0,1:T(8,128)(2,1)}), bf16[2,4,64,2048]{3,2,0,1:T(8,128)(2,1)}, u32[]{:S(2)}, u32[]{:S(2)}) async-start(bf16[2,4,64,2048]{3,2,0,1:T(8,128)(2,1)} %broadcast_in_dim.47), calls=%async_computation.5 | async-start | bytes 4194304 | tf_op jit(solution)/shard_map/all_to_all | solution.py:174
  1557.8 49.2 %all-to-all-start.10 = ((bf16[2,4,64,2048]{3,2,0,1:T(8,128)(2,1)}), bf16[2,4,64,2048]{3,2,0,1:T(8,128)(2,1)}, u32[]{:S(2)}, u32[]{:S(2)}) async-start(bf16[2,4,64,2048]{3,2,0,1:T(8,128)(2,1)} %broadcast_in_dim.50), calls=%async_computation.10 | async-start | bytes 4194304 | tf_op jit(solution)/shard_map/all_to_all | solution.py:174
  1612.5 25.6 %all-to-all-start.11 = ((f32[512,4,2,1,64]{0,4,2,3,1:T(8,128)}), f32[512,4,2,1,64]{0,4,2,3,1:T(8,128)S(1)}, u32[]{:S(2)}, u32[]{:S(2)}) async-start(f32[512,4,2,1,64]{0,4,2,3,1:T(8,128)} %convolution_bitcast_fusion.1), calls=%async_computation.11 | async-start | bytes 2097152 | tf_op jit(solution)/shard_map/all_to_all | solution.py:174
  1759.5 42.5 %all-to-all-start.12 = ((bf16[2,4,64,2048]{3,2,0,1:T(8,128)(2,1)}), bf16[2,4,64,2048]{3,2,0,1:T(8,128)(2,1)}, u32[]{:S(2)}, u32[]{:S(2)}) async-start(bf16[2,4,64,2048]{3,2,0,1:T(8,128)(2,1)} %copy.441), calls=%async_computation.12 | async-start | bytes 4194304 | tf_op jit(solution)/shard_map/all_to_all | solution.py:174
  1806.3 12.0 all-to-all-start.13
  1810.5 243.2 %reduce-scatter.3.cloned.1.call-start = ((), (), s32[]{:S(2)}) async-start(), calls=%async_computation.18 | async-start | bytes 11833344 | tf_op jit(solution)/shard_map/reduce_scatter | solution.py:197
  1874.3 475.5 %reduce-scatter.5.cloned.1.call-start = ((), (), s32[]{:S(2)}) async-start(), calls=%async_computation.19 | async-start | bytes 19464192 | tf_op jit(solution)/shard_map/reduce_scatter | solution.py:197
  2064.8 32.9 %all-to-all-start.14 = ((f32[4,4,64,1,512]{4,2,0,3,1:T(8,128)}), f32[4,4,64,1,512]{4,2,0,3,1:T(8,128)}, u32[]{:S(2)}, u32[]{:S(2)}) async-start(f32[4,4,64,1,512]{4,2,0,3,1:T(8,128)} %copy.446), calls=%async_computation.15 | async-start | bytes 4194304 | tf_op jit(solution)/shard_map/all_to_all | solution.py:174
  (170 other events, 1102.5 us)
Sparse Core Ops, SparseCore 0:
  50.5 407.4 all-gather.5
  459.6 657.3 all-gather.7
  1874.5 179.2 reduce-scatter.2
  2058.0 291.7 reduce-scatter.4

commit v4 on v2

--- a/solution.py
+++ b/solution.py
@@ -91,7 +91,36 @@
     return produced_output.transpose(0, 2, 1, 3).reshape(length, head_count, value_width)
 
 
-def mixer_core(query_lin, key_lin, value_lin, gate_lin, beta_lin, conv_taps, head_scale, starts):
+def delta_core_reset(queries, keys, values, betas, block_len):
+    length, head_count, head_width = queries.shape
+    block_count = length // block_len
+
+    def blocked(array):
+        return array.reshape(block_count, block_len, head_count, -1).transpose(0, 2, 1, 3)
+
+    query_blocks = blocked(queries)
+    key_blocks = blocked(keys)
+    value_blocks = blocked(values)
+    beta_blocks = betas.reshape(block_count, block_len, head_count).transpose(0, 2, 1)[..., None]
+    position = jnp.arange(block_len)
+    strict = (position[:, None] > position[None, :]).astype(queries.dtype)
+    causal = (position[:, None] >= position[None, :]).astype(queries.dtype)
+    weighted = key_blocks * beta_blocks
+    negative = -outer_product_result("nhik,nhjk->nhij", weighted, key_blocks) * strict
+    inverse = jnp.eye(block_len, dtype=queries.dtype) + negative
+    power_term = negative
+    for doubling in range(5):
+        power_term = outer_product_result("nhij,nhjk->nhik", power_term, power_term)
+        inverse = inverse + outer_product_result("nhij,nhjk->nhik", inverse, power_term)
+    value_mix = outer_product_result("nhij,nhjk->nhik", inverse, value_blocks * beta_blocks)
+    scores = outer_product_result("nhik,nhjk->nhij", query_blocks, key_blocks) * causal
+    produced_output = outer_product_result("nhqz,nhzr->nhqr", scores, value_mix)
+    return produced_output.transpose(0, 2, 1, 3).reshape(length, head_count, -1)
+
+
+def mixer_core(
+    query_lin, key_lin, value_lin, gate_lin, beta_lin, conv_taps, head_scale, starts, reset_len
+):
     length = query_lin.shape[0]
     head_count = beta_lin.shape[1]
     head_width = query_lin.shape[1] // head_count
@@ -110,7 +139,10 @@
         * head_width ** (-0.5)
     )
     keys = keys * lax.rsqrt(jnp.sum(keys * keys, axis=-1, keepdims=True) + 1e-06)
-    recurrent = delta_core(queries, keys, values, jax.nn.sigmoid(beta_lin), starts)
+    if reset_len:
+        recurrent = delta_core_reset(queries, keys, values, jax.nn.sigmoid(beta_lin), reset_len)
+    else:
+        recurrent = delta_core(queries, keys, values, jax.nn.sigmoid(beta_lin), starts)
     normed = (
         recurrent
         * lax.rsqrt(jnp.mean(recurrent * recurrent, axis=-1, keepdims=True) + 1e-05)
@@ -160,19 +192,6 @@
     if not axes:
         return value
     return lax.all_to_all(value, axes, split_axis, concat_axis, tiled=True)
-
-
-def column_weight(owned, tp):
-    rows, width = owned.shape
-    swapped = exchange(owned.reshape(rows, tp, width // tp), TP_AXES, 1, 0)
-    return fsdp_gather(swapped.reshape(rows * tp, width // tp), 0)
-
-
-def column_grad(partial, tp):
-    reduced = fsdp_scatter_low(partial, 0)
-    group_rows, cols = reduced.shape
-    swapped = exchange(reduced.reshape(tp, group_rows // tp, cols), TP_AXES, 0, 2)
-    return swapped.reshape(group_rows // tp, cols * tp)
 
 
 def heads_to_rows(values, tp, fsdp, rows):
@@ -187,6 +206,13 @@
     staged = values.reshape(count, tp, fsdp // tp, 1, rows)
     moved = exchange(staged, TP_AXES, 1, 3)
     return moved.reshape(count, fsdp * rows)
+
+
+def padded_rows(flat, slices, width):
+    extra = -(-flat.shape[0] // (slices * width))
+    extra = -(-extra // 16) * 16
+    filled = jnp.pad(flat, (0, slices * extra * width - flat.shape[0]))
+    return filled.reshape(slices, extra, width)
 
 
 def make_on_device(tp, fsdp, inner):
@@ -215,15 +241,15 @@
         head_count = beta_weight.shape[1]
         heads_here = head_count // tp
         cols_here = width // tp
+        group_rows = tp * rows
         position = lax.axis_index(TP_AXES)
         head_scale = head_gain.astype(jnp.float32)
-
-        query_cols = column_weight(query_weight, tp)
-        key_cols = column_weight(key_weight, tp)
-        value_cols = column_weight(value_weight, tp)
-        gate_cols = column_weight(gate_weight, tp)
-        out_rows = fsdp_gather(out_weight, 0)
-
+        reset_len = slot if group_start.shape[1] == 1 else 0
+
+        column_owned = jnp.stack([query_weight, key_weight, value_weight, gate_weight])
+        column_swapped = exchange(
+            column_owned.reshape(4, rows, tp, cols_here), TP_AXES, 2, 1
+        ).reshape(4, group_rows, cols_here)
         small_pack = jnp.concatenate(
             [
                 conv_weight.reshape(-1),
@@ -232,7 +258,31 @@
                 swiglu_gain.reshape(-1),
             ]
         )
-        small_all = lax.all_gather(small_pack, ALL_AXES, axis=0, tiled=False)
+        small_size = small_pack.shape[0]
+        small_group = exchange(
+            jnp.broadcast_to(small_pack[None, :], (tp, small_size)), TP_AXES, 0, 0
+        )
+        small_rows_in = padded_rows(small_group.reshape(-1), 5, cols_here)
+        extra_in = small_rows_in.shape[1]
+        mixer_stack = jnp.concatenate(
+            [
+                jnp.concatenate(
+                    [column_swapped, out_weight.reshape(1, group_rows, cols_here)], axis=0
+                ),
+                small_rows_in,
+            ],
+            axis=1,
+        )
+        mixer_all = fsdp_gather(mixer_stack, 1).reshape(5, fsdp, group_rows + extra_in, cols_here)
+        weight_all = mixer_all[:, :, :group_rows].reshape(5, width, cols_here)
+        query_cols, key_cols, value_cols, gate_cols = (weight_all[index] for index in range(4))
+        out_rows = weight_all[4].reshape(fsdp * rows, width)
+        small_all = (
+            mixer_all[:, :, group_rows:]
+            .transpose(1, 0, 2, 3)
+            .reshape(fsdp, -1)[:, : tp * small_size]
+            .reshape(n_all, small_size)
+        )
         conv_size = conv_weight.size
         beta_size = beta_weight.size
         conv_full = (
@@ -250,21 +300,15 @@
         beta_here = lax.dynamic_slice_in_dim(beta_full, position * heads_here, heads_here, axis=1)
 
         owned_rows, hidden_half = swiglu_gate.shape
-        gate_half = fsdp_gather(
-            exchange(swiglu_gate.reshape(owned_rows, inner, hidden_half // inner), INNER_AXES, 1, 0)
-            .reshape(owned_rows * inner, hidden_half // inner),
-            0,
-        )
-        up_half = fsdp_gather(
-            exchange(swiglu_up.reshape(owned_rows, inner, hidden_half // inner), INNER_AXES, 1, 0)
-            .reshape(owned_rows * inner, hidden_half // inner),
-            0,
-        )
-        down_half = fsdp_gather(
-            exchange(swiglu_down.reshape(inner, hidden_half // inner, owned_rows), INNER_AXES, 0, 2)
-            .reshape(hidden_half // inner, inner * owned_rows),
-            1,
-        )
+        hidden_here = hidden_half // inner
+        ff_owned = jnp.stack([swiglu_gate, swiglu_up, swiglu_down.T])
+        ff_swapped = exchange(
+            ff_owned.reshape(3, owned_rows, inner, hidden_here), INNER_AXES, 2, 1
+        ).reshape(3, inner * owned_rows, hidden_here)
+        ff_all = fsdp_gather(ff_swapped, 1)
+        gate_half = ff_all[0]
+        up_half = ff_all[1]
+        down_half_t = ff_all[2]
 
         inputs = tokens.astype(jnp.float32).reshape(micro_count * slot, width)
         normed, norm_back = jax.vjp(rms_norm, inputs, gain_mixer.astype(jnp.float32))
@@ -283,7 +327,7 @@
 
         def core_at(query_in, key_in, value_in, gate_in, beta_in, conv_in, head_in):
             return mixer_core(
-                query_in, key_in, value_in, gate_in, beta_in, conv_in, head_in, starts
+                query_in, key_in, value_in, gate_in, beta_in, conv_in, head_in, starts, reset_len
             )
 
         gated_out, core_back = jax.vjp(
@@ -305,18 +349,34 @@
         up_act = matmul_rows(inner_group, up_half)
         hidden, hidden_back = jax.vjp(swiglu_mix, gate_act, up_act)
         hidden_low = hidden.astype(jnp.bfloat16)
-        partial_rows = matmul_rows(hidden_low, down_half)
+        partial_rows = back_product(hidden_low, down_half_t)
         branch_rows = tp_scatter_low(partial_rows.reshape(micro_count, slot * tp, width), 1)
         block_out = (residual.reshape(micro_count, slot, width) + branch_rows).astype(jnp.bfloat16)
 
         out_back = cotangent.astype(jnp.float32) * pad_mask.astype(jnp.float32)[:, :, None]
         out_back_low = out_back.astype(jnp.bfloat16)
         upstream_group = tp_gather(out_back_low, 1).reshape(group_tokens, width)
-        gate_back, up_back = hidden_back(back_product(upstream_group, down_half))
+        gate_back, up_back = hidden_back(matmul_rows(upstream_group, down_half_t))
         gate_back_low = gate_back.astype(jnp.bfloat16)
         up_back_low = up_back.astype(jnp.bfloat16)
         inner_part = back_product(gate_back_low, gate_half) + back_product(up_back_low, up_half)
         inner_back = tp_scatter_low(inner_part.reshape(micro_count, slot * tp, width), 1)
+
+        ff_sums = jnp.stack(
+            [
+                left_product(inner_group, gate_back_low),
+                left_product(inner_group, up_back_low),
+                left_product(upstream_group, hidden_low),
+            ]
+        )
+        ff_reduced = fsdp_scatter_low(ff_sums, 1)
+        ff_back = exchange(
+            ff_reduced.reshape(3, inner, owned_rows, 1, hidden_here), INNER_AXES, 1, 3
+        ).reshape(3, owned_rows, hidden_half)
+        swiglu_gate_grad = ff_back[0]
+        swiglu_up_grad = ff_back[1]
+        swiglu_down_grad = ff_back[2].T
+
         residual_part, swiglu_gain_term = inner_norm_back(
             inner_back.reshape(micro_count * slot, width)
         )
@@ -346,27 +406,15 @@
         input_part, mixer_gain_term = norm_back(normed_back.reshape(micro_count * slot, width))
         tokens_grad = (residual_back + input_part).reshape(micro_count, slot, width)
 
-        swiglu_gate_sum = left_product(inner_group, gate_back_low)
-        swiglu_up_sum = left_product(inner_group, up_back_low)
-        swiglu_down_sum = left_product(hidden_low, upstream_group)
-        gate_grad_rows = fsdp_scatter_low(swiglu_gate_sum, 0)
-        swiglu_gate_grad = exchange(
-            gate_grad_rows.reshape(inner, owned_rows, hidden_half // inner), INNER_AXES, 0, 2
-        ).reshape(owned_rows, hidden_half)
-        up_grad_rows = fsdp_scatter_low(swiglu_up_sum, 0)
-        swiglu_up_grad = exchange(
-            up_grad_rows.reshape(inner, owned_rows, hidden_half // inner), INNER_AXES, 0, 2
-        ).reshape(owned_rows, hidden_half)
-        down_grad_cols = fsdp_scatter_low(swiglu_down_sum, 1)
-        swiglu_down_grad = exchange(
-            down_grad_cols.reshape(hidden_half // inner, inner, owned_rows), INNER_AXES, 1, 0
-        ).reshape(hidden_half, owned_rows)
-
-        out_grad = fsdp_scatter_low(left_product(gated_rows, mixed_group), 0)
-        query_grad = column_grad(left_product(normed_group, query_low), tp)
-        key_grad = column_grad(left_product(normed_group, key_low), tp)
-        value_grad = column_grad(left_product(normed_group, value_low), tp)
-        gate_grad = column_grad(left_product(normed_group, gate_low), tp)
+        mixer_sums = jnp.stack(
+            [
+                left_product(normed_group, query_low),
+                left_product(normed_group, key_low),
+                left_product(normed_group, value_low),
+                left_product(normed_group, gate_low),
+                left_product(gated_rows, mixed_group).reshape(width, cols_here),
+            ]
+        ).reshape(5, fsdp, group_rows, cols_here)
         beta_sum = left_product(normed_group, beta_low)
         beta_wide = lax.dynamic_update_slice_in_dim(
             jnp.zeros((width, head_count), jnp.float32), beta_sum, position * heads_here, axis=1
@@ -375,7 +423,7 @@
             jnp.zeros(conv_full.shape, jnp.float32), conv_term, position * cols_here, axis=2
         )
         taps = conv_wide.shape[0] * conv_wide.shape[1]
-        small_rows = jnp.concatenate(
+        small_terms = jnp.concatenate(
             [
                 conv_wide.reshape(taps, n_all, -1).transpose(1, 0, 2).reshape(n_all, -1),
                 beta_wide.reshape(n_all, -1),
@@ -385,7 +433,22 @@
             ],
             axis=1,
         )
-        small_out = lax.psum_scatter(small_rows, ALL_AXES, scatter_dimension=0, tiled=False)
+        small_width = small_terms.shape[1]
+        small_tp = jnp.sum(
+            exchange(small_terms.reshape(fsdp, tp, small_width), TP_AXES, 1, 1), axis=1
+        )
+        small_block = jax.vmap(lambda flat: padded_rows(flat, 5, cols_here))(small_tp)
+        extra_out = small_block.shape[2]
+        reduce_in = jnp.concatenate([mixer_sums, small_block.transpose(1, 0, 2, 3)], axis=2)
+        mixer_reduced = fsdp_scatter_low(
+            reduce_in.reshape(5, fsdp * (group_rows + extra_out), cols_here), 1
+        )
+        column_back = exchange(
+            mixer_reduced[:4, :group_rows].reshape(4, tp, rows, 1, cols_here), TP_AXES, 1, 3
+        ).reshape(4, rows, width)
+        query_grad, key_grad, value_grad, gate_grad = (column_back[index] for index in range(4))
+        out_grad = mixer_reduced[4, :group_rows].reshape(rows, width)
+        small_out = mixer_reduced[:, group_rows:].reshape(-1)[:small_width]
         conv_grad = small_out[:conv_size].reshape(conv_weight.shape)
         beta_grad = small_out[conv_size : conv_size + beta_size].reshape(beta_weight.shape)
         mixer_gain_grad = small_out[conv_size + beta_size : conv_size + beta_size + rows]

time: 1760 us -> 1590 us (0.903)
  matrix products: 383 us -> 215 us
  blocking collectives: 161 us -> 13 us
  waiting for transfers between devices: 924 us -> 1070 us
  other arithmetic: 96.5 us -> 64 us
  local copies, waits for them, and re-layouts: 136 us -> 164 us
    dot_general x138 -> x42, matrix products: 261 us -> 95.4 us  [outer_product_result(): return jnp.einsum(form, first, second, precision=lax.Precision.HIGHEST)]
    all_gather x8 -> x2, waiting for transfers between devices: 334 us -> 488 us  [fsdp_gather(): return lax.all_gather(value, FSDP_AXES, axis=axis, tiled=True)]
    unnamed x26 -> x12, waiting for transfers between devices: 129 us -> 0.2 us
    reduce_scatter x8 -> x2, waiting for transfers between devices: 319 us -> 422 us  [fsdp_scatter_low(): lax.psum_scatter(value.astype(jnp.bfloat16), FSDP_AXES, scatter_dimension...]
    all_to_all x10 -> x1, blocking collectives: 84.6 us -> 6.67 us  [exchange(): return lax.all_to_all(value, axes, split_axis, concat_axis, tiled=True)]
    all_gather x1 -> x0, blocking collectives: 70.9 us -> none  [on_device(): small_all = lax.all_gather(small_pack, ALL_AXES, axis=0, tiled=False)]
    all_to_all x6 -> x7, waiting for transfers between devices: 1.04 us -> 29.3 us  [exchange(): return lax.all_to_all(value, axes, split_axis, concat_axis, tiled=True)]
    another operation x5 -> x12, local copies, waits for them, and re-layouts: 5.5 us -> 28.3 us
  transfers between devices with their start and end apart: 31 -> 19, of which waited for: 21 -> 15; matrix products, arithmetic and copies ran while one was open for 32% -> 11% of each run, Pallas kernels for 0% -> 0%
where the time goes in v4:
time: 1590 us; the launch traced here: 1580 us
  waiting for transfers between devices  1070 us (67%)
  matrix products  215 us (14%)
  local copies, waits for them, and re-layouts  164 us (10%)
  other arithmetic  64 us (4%)
  starting transfers between devices  30.2 us (2%)
  between operations  16.5 us (1%)
    all_gather x2, waiting for transfers between devices, fsdp_gather(): return lax.all_gather(value, FSDP_AXES, axis=axis, tiled=True)  488 us
    reduce_scatter x2, waiting for transfers between devices, fsdp_scatter_low(): lax.psum_scatter(value.astype(jnp.bfloat16), FSDP_AXES, scatter_dimension...  422 us
    dot_general x42, matrix products, outer_product_result(): return jnp.einsum(form, first, second, precision=lax.Precision.HIGHEST)  95.4 us
    reduce_scatter x4, waiting for transfers between devices, tp_scatter_low(): lax.psum_scatter(value.astype(jnp.bfloat16), TP_AXES, scatter_dimension=a...  79.7 us
    all_gather x4, waiting for transfers between devices, tp_gather(): return lax.all_gather(value, TP_AXES, axis=axis, tiled=True)  55 us
    dot_general x9, matrix products, back_product(): jnp.einsum('tg,fg->tf', gradient, weight, preferred_element_type=jnp.floa...  47.6 us
    dot_general x9, matrix products, matmul_rows(): return jnp.dot(left, right, preferred_element_type=jnp.float32)  41.9 us
  transfers between devices with their start and end apart: 19, of which 15 were waited for; matrix products, arithmetic and copies ran while one was open for 11% of the time, Pallas kernels for 0%

profile of v4, /device:TPU:0, one launch (start us, length us, event | category | flops | bytes accessed | tf_op | source)
XLA Modules:
  0.0 1577.8 jit_solution(17741058359264872058)
XLA Ops:
  27.2 13.9 all-to-all-done
  42.7 159.6 %all-gather.8.cloned.1.call-done = bf16[5,2176,512]{2,1,0:T(8,128)(2,1)} async-done(((bf16[5,272,512]{2,1,0:T(8,128)(2,1)}), bf16[5,2176,512]{2,1,0:T(8,128)(2,1)}) %all-gather.8.cloned.1.call-update) | async-done | bytes 11141136 | tf_op jit(solution)/shard_map/all_gather | solution.py:182
  205.2 6.3 all-gather
  213.5 7.4 fusion.147
  258.6 13.2 convolution_add_fusion.7
  336.2 6.7 all_to_all.101
  344.6 10.9 reduce-scatter.7.cloned.1.call-done
  361.8 328.3 %all-gather.14.cloned.1.call-done = bf16[3,2048,1408]{2,1,0:T(8,128)(2,1)} async-done(((bf16[3,256,1408]{2,1,0:T(8,128)(2,1)}), bf16[3,2048,1408]{2,1,0:T(8,128)(2,1)}) %all-gather.14.cloned.1.call-update) | async-done | bytes 17301520 | tf_op jit(solution)/shard_map/all_gather | solution.py:182
  690.0 24.6 %all-gather.12.cloned.1.call-done = bf16[2,256,2048]{2,1,0:T(8,128)(2,1)} async-done(((bf16[2,64,2048]{2,1,0:T(8,128)(2,1)}), bf16[2,256,2048]{2,1,0:T(8,128)(2,1)}) %all-gather.12.cloned.1.call-update) | async-done | bytes 2097168 | tf_op jit(solution)/shard_map/all_gather | solution.py:172
  714.7 8.4 fusion.8
  729.6 9.7 all-gather.16.cloned.1.call-done
  739.4 10.3 multiply_convert_fusion
  749.7 6.5 fusion.7
  756.3 7.3 add_convert_fusion.1
  763.6 31.5 %reduce-scatter.11.cloned.1.call-done = bf16[2,64,2048]{2,1,0:T(8,128)(2,1)} async-done(((bf16[2,256,2048]{2,1,0:T(8,128)(2,1)}), bf16[2,64,2048]{2,1,0:T(8,128)(2,1)}) %reduce-scatter.11.cloned.1.call-update) | async-done | bytes 524304 | tf_op jit(solution)/shard_map/reduce_scatter | solution.py:176
  804.2 18.4 %all-gather.18.cloned.1.call-done = bf16[2,256,2048]{2,1,0:T(8,128)(2,1)} async-done(((bf16[2,64,2048]{2,1,0:T(8,128)(2,1)}), bf16[2,256,2048]{2,1,0:T(8,128)(2,1)}) %all-gather.18.cloned.1.call-update) | async-done | bytes 2097168 | tf_op jit(solution)/shard_map/all_gather | solution.py:172
  836.7 9.2 all-to-all-done.4
  966.4 8.6 add_convert_fusion
  989.3 7.3 pad_maximum_fusion
  1042.2 10.3 pad_maximum_fusion.1
  1053.8 7.6 fusion.13
  1061.4 242.1 %reduce-scatter.17.cloned.1.call-done = bf16[3,256,1408]{2,1,0:T(8,128)(2,1)} async-done(((bf16[3,2048,1408]{2,1,0:T(8,128)(2,1)}), bf16[3,256,1408]{2,1,0:T(8,128)(2,1)}) %reduce-scatter.17.cloned.1.call-update) | async-done | bytes 2162704 | tf_op jit(solution)/shard_map/reduce_scatter | solution.py:186
  1313.1 180.4 %reduce-scatter.15.cloned.1.call-done = bf16[5,272,512]{2,1,0:T(8,128)(2,1)} async-done(((bf16[5,2176,512]{2,1,0:T(8,128)(2,1)}), bf16[5,272,512]{2,1,0:T(8,128)(2,1)}) %reduce-scatter.15.cloned.1.call-update) | async-done | bytes 1392656 | tf_op jit(solution)/shard_map/reduce_scatter | solution.py:186
  1500.6 37.2 %reduce-scatter.9.cloned.1.call-done = bf16[2,64,2048]{2,1,0:T(8,128)(2,1)} async-done(((bf16[2,256,2048]{2,1,0:T(8,128)(2,1)}), bf16[2,64,2048]{2,1,0:T(8,128)(2,1)}) %reduce-scatter.9.cloned.1.call-update) | async-done | bytes 524304 | tf_op jit(solution)/shard_map/reduce_scatter | solution.py:176
  (503 shorter events, 395.3 us)
Async XLA Ops:
  12.2 10.9 all-to-all-start.1
  23.2 18.0 %all-to-all-start = ((bf16[4,64,4,512]{3,1,0,2:T(8,128)(2,1)}), bf16[4,64,4,512]{3,1,0,2:T(8,128)(2,1)S(1)}, u32[]{:S(2)}, u32[]{:S(2)}) async-start(bf16[4,64,4,512]{3,1,0,2:T(8,128)(2,1)} %copy.394), calls=%async_computation | async-start | bytes 2097152 | tf_op jit(solution)/shard_map/all_to_all | solution.py:194
  26.7 175.6 %all-gather.8.cloned.1.call-start = ((), (), s32[]{:S(2)}) async-start(), calls=%async_computation.14 | async-start | bytes 12533760 | tf_op jit(solution)/shard_map/all_gather | solution.py:182
  42.5 183.6 %all-gather.10.cloned.1.call-start = ((), (), s32[]{:S(2)}) async-start(), calls=%async_computation.15 | async-start | bytes 2621440 | tf_op jit(solution)/shard_map/all_gather | solution.py:172
  42.7 161.2 %copy-start.97 = (f32[2,64]{1,0:T(2,128)}, f32[2,64]{1,0:T(2,128)S(1)}, u32[]{:S(2)}) copy-start(f32[2,64]{1,0:T(2,128)S(1)} %fusion.65) | copy-start | bytes 1540
  42.7 161.5 %copy-start.93 = (f32[2,64]{1,0:T(2,128)}, f32[2,64]{1,0:T(2,128)S(1)}, u32[]{:S(2)}) copy-start(f32[2,64]{1,0:T(2,128)S(1)} %fusion.140) | copy-start | bytes 1540
  304.6 13.0 all-to-all-start.2
  308.7 46.8 %reduce-scatter.7.cloned.1.call-start = ((), (), s32[]{:S(2)}) async-start(), calls=%async_computation.16 | async-start | bytes 2621440 | tf_op jit(solution)/shard_map/reduce_scatter | solution.py:176
  323.9 366.1 %all-gather.14.cloned.1.call-start = ((), (), s32[]{:S(2)}) async-start(), calls=%async_computation.18 | async-start | bytes 19464192 | tf_op jit(solution)/shard_map/all_gather | solution.py:182
  344.5 370.2 %all-gather.12.cloned.1.call-start = ((), (), s32[]{:S(2)}) async-start(), calls=%async_computation.17 | async-start | bytes 2621440 | tf_op jit(solution)/shard_map/all_gather | solution.py:172
  344.6 452.4 %copy-start.71 = (f32[2048]{0:T(1024)}, f32[2048]{0:T(1024)S(1)}, u32[]{:S(2)}) copy-start(f32[2048]{0:T(1024)S(1)} %reshape.745) | copy-start | bytes 24580
  357.0 440.1 %copy-start.77 = (f32[2,64]{1,0:T(2,128)}, f32[2,64]{1,0:T(2,128)S(1)}, u32[]{:S(2)}) copy-start(f32[2,64]{1,0:T(2,128)S(1)} %fusion.141) | copy-start | bytes 1540
  359.2 380.1 %all-gather.16.cloned.1.call-start = ((), (), s32[]{:S(2)}) async-start(), calls=%async_computation.20 | async-start | bytes 2621440 | tf_op jit(solution)/shard_map/all_gather | solution.py:172
  359.3 437.8 %copy-start.91 = (f32[2,64]{1,0:T(2,128)}, f32[2,64]{1,0:T(2,128)S(1)}, u32[]{:S(2)}) copy-start(f32[2,64]{1,0:T(2,128)S(1)} %convert_element_type.225) | copy-start | bytes 1540
  361.3 433.9 %reduce-scatter.11.cloned.1.call-start = ((), (), s32[]{:S(2)}) async-start(), calls=%async_computation.21 | async-start | bytes 2621440 | tf_op jit(solution)/shard_map/reduce_scatter | solution.py:176
  763.6 59.0 %all-gather.18.cloned.1.call-start = ((), (), s32[]{:S(2)}) async-start(), calls=%async_computation.22 | async-start | bytes 2621440 | tf_op jit(solution)/shard_map/all_gather | solution.py:172
  827.1 18.8 %all-to-all-start.4 = ((f32[512,4,2,1,64]{0,4,2,3,1:T(8,128)}), f32[512,4,2,1,64]{0,4,2,3,1:T(8,128)}, u32[]{:S(2)}, u32[]{:S(2)}) async-start(f32[512,4,2,1,64]{0,4,2,3,1:T(8,128)} %convolution_bitcast_fusion.1), calls=%async_computation.7 | async-start | bytes 2097152 | tf_op jit(solution)/shard_map/all_to_all | solution.py:194
  831.3 196.2 %reduce-scatter.13.cloned.1.call-start = ((), (), s32[]{:S(2)}) async-start(), calls=%async_computation.23 | async-start | bytes 2621440 | tf_op jit(solution)/shard_map/reduce_scatter | solution.py:176
  975.1 328.5 %reduce-scatter.17.cloned.1.call-start = ((), (), s32[]{:S(2)}) async-start(), calls=%async_computation.25 | async-start | bytes 19464192 | tf_op jit(solution)/shard_map/reduce_scatter | solution.py:186
  1032.4 9.4 all-to-all-start.5
  1035.8 457.7 %reduce-scatter.15.cloned.1.call-start = ((), (), s32[]{:S(2)}) async-start(), calls=%async_computation.24 | async-start | bytes 12533760 | tf_op jit(solution)/shard_map/reduce_scatter | solution.py:186
  1052.5 485.3 %reduce-scatter.9.cloned.1.call-start = ((), (), s32[]{:S(2)}) async-start(), calls=%async_computation.19 | async-start | bytes 2621440 | tf_op jit(solution)/shard_map/reduce_scatter | solution.py:176
  1307.5 189.1 %all-to-all-start.7 = ((f32[3,2,128,1,1408]{4,2,0,3,1:T(8,128)}), f32[3,2,128,1,1408]{4,2,0,3,1:T(8,128)}, u32[]{:S(2)}, u32[]{:S(2)}) async-start(f32[3,2,128,1,1408]{4,2,0,3,1:T(8,128)} %copy.476), calls=%async_computation.13 | async-start | bytes 8650752 | tf_op jit(solution)/shard_map/all_to_all | solution.py:194
  1496.6 68.5 %all-to-all-start.6 = ((f32[4,4,64,1,512]{4,2,0,3,1:T(8,128)}), f32[4,4,64,1,512]{4,2,0,3,1:T(8,128)S(1)}, u32[]{:S(2)}, u32[]{:S(2)}) async-start(f32[4,4,64,1,512]{4,2,0,3,1:T(8,128)} %copy.471), calls=%async_computation.11 | async-start | bytes 4194304 | tf_op jit(solution)/shard_map/all_to_all | solution.py:194
  (106 other events, 628.6 us)
Sparse Core Ops, SparseCore 0:
  42.6 159.6 all-gather.7
  205.3 20.7 all-gather.9
  324.1 31.4 reduce-scatter.6
  357.0 332.9 all-gather.13
  692.1 22.5 all-gather.11
  716.7 22.5 all-gather.15
  763.7 31.4 reduce-scatter.10
  800.0 22.5 all-gather.17
  975.2 31.4 reduce-scatter.12
  1010.9 292.6 reduce-scatter.16
  1307.2 186.2 reduce-scatter.14
  1495.9 41.9 reduce-scatter.8

commit v5 on v4

--- a/solution.py
+++ b/solution.py
@@ -186,6 +186,26 @@
     return lax.psum_scatter(
         value.astype(jnp.bfloat16), FSDP_AXES, scatter_dimension=axis, tiled=True
     ).astype(jnp.float32)
+
+
+def fsdp_gather_direct(value, fsdp, axis):
+    spread = jnp.broadcast_to(
+        jnp.expand_dims(value, axis + 1), value.shape[: axis + 1] + (fsdp,) + value.shape[axis + 1 :]
+    )
+    spread = jnp.moveaxis(spread, axis + 1, axis)
+    moved = lax.all_to_all(spread, FSDP_AXES, axis, axis, tiled=True)
+    shape = list(value.shape)
+    shape[axis] *= fsdp
+    return moved.reshape(shape)
+
+
+def fsdp_scatter_direct(value, fsdp, axis):
+    shape = list(value.shape)
+    staged = value.astype(jnp.bfloat16).reshape(
+        shape[:axis] + [fsdp, shape[axis] // fsdp] + shape[axis + 1 :]
+    )
+    moved = lax.all_to_all(staged, FSDP_AXES, axis, axis, tiled=True)
+    return jnp.sum(moved.astype(jnp.float32), axis=axis)
 
 
 def exchange(value, axes, split_axis, concat_axis):
@@ -302,10 +322,10 @@
         owned_rows, hidden_half = swiglu_gate.shape
         hidden_here = hidden_half // inner
         ff_owned = jnp.stack([swiglu_gate, swiglu_up, swiglu_down.T])
-        ff_swapped = exchange(
-            ff_owned.reshape(3, owned_rows, inner, hidden_here), INNER_AXES, 2, 1
-        ).reshape(3, inner * owned_rows, hidden_here)
-        ff_all = fsdp_gather(ff_swapped, 1)
+        ff_rows = fsdp_gather_direct(ff_owned, fsdp, 1)
+        ff_all = exchange(
+            ff_rows.reshape(3, fsdp, 1, owned_rows, inner, hidden_here), INNER_AXES, 4, 2
+        ).reshape(3, width, hidden_here)
         gate_half = ff_all[0]
         up_half = ff_all[1]
         down_half_t = ff_all[2]
@@ -356,6 +376,7 @@
         out_back = cotangent.astype(jnp.float32) * pad_mask.astype(jnp.float32)[:, :, None]
         out_back_low = out_back.astype(jnp.bfloat16)
         upstream_group = tp_gather(out_back_low, 1).reshape(group_tokens, width)
+        block_out, upstream_group = lax.optimization_barrier((block_out, upstream_group))
         gate_back, up_back = hidden_back(matmul_rows(upstream_group, down_half_t))
         gate_back_low = gate_back.astype(jnp.bfloat16)
         up_back_low = up_back.astype(jnp.bfloat16)
@@ -369,7 +390,7 @@
                 left_product(upstream_group, hidden_low),
             ]
         )
-        ff_reduced = fsdp_scatter_low(ff_sums, 1)
+        ff_reduced = fsdp_scatter_direct(ff_sums, fsdp, 1)
         ff_back = exchange(
             ff_reduced.reshape(3, inner, owned_rows, 1, hidden_here), INNER_AXES, 1, 3
         ).reshape(3, owned_rows, hidden_half)

time: 1590 us -> 1680 us (1.057)
  local copies, waits for them, and re-layouts: 164 us -> 204 us
  waiting for transfers between devices: 1070 us -> 1110 us
    all_to_all x0 -> x2, waiting for transfers between devices: none -> 758 us  [the longest x1 430 us: fsdp_scatter_direct(): moved = lax.all_to_all(staged, FSDP_AXES, axis, axis, tiled=True)]
    reduce_scatter x2 -> x1, waiting for transfers between devices: 422 us -> 32.8 us  [fsdp_scatter_low(): lax.psum_scatter(value.astype(jnp.bfloat16), FSDP_AXES, scatter_dimension...]
    all_gather x2 -> x1, waiting for transfers between devices: 488 us -> 160 us  [fsdp_gather(): return lax.all_gather(value, FSDP_AXES, axis=axis, tiled=True)]
    all_to_all x4, local copies, waits for them, and re-layouts: 8.86 us -> 28.7 us  [exchange(): return lax.all_to_all(value, axes, split_axis, concat_axis, tiled=True)]
  transfers between devices with their start and end apart: 19 -> 19, of which waited for: 15 -> 12; matrix products, arithmetic and copies ran while one was open for 11% -> 13% of each run, Pallas kernels for 0% -> 0%
where the time goes in v5:
time: 1680 us; the launch traced here: 1670 us
  waiting for transfers between devices  1110 us (66%)
  local copies, waits for them, and re-layouts  204 us (12%)
  matrix products  202 us (12%)
  other arithmetic  73.5 us (4%)
  starting transfers between devices  41.2 us (2%)
  blocking collectives  26.6 us (2%)
    all_to_all x1, waiting for transfers between devices, fsdp_scatter_direct(): moved = lax.all_to_all(staged, FSDP_AXES, axis, axis, tiled=True)  430 us
    all_to_all x1, waiting for transfers between devices, fsdp_gather_direct(): moved = lax.all_to_all(spread, FSDP_AXES, axis, axis, tiled=True)  328 us
    all_gather x1, waiting for transfers between devices, fsdp_gather(): return lax.all_gather(value, FSDP_AXES, axis=axis, tiled=True)  160 us
    reduce_scatter x4, waiting for transfers between devices, tp_scatter_low(): lax.psum_scatter(value.astype(jnp.bfloat16), TP_AXES, scatter_dimension=a...  90.8 us
    dot_general x42, matrix products, outer_product_result(): return jnp.einsum(form, first, second, precision=lax.Precision.HIGHEST)  81.8 us
    dot_general x9, matrix products, back_product(): jnp.einsum('tg,fg->tf', gradient, weight, preferred_element_type=jnp.floa...  44.8 us
    all_gather x4, waiting for transfers between devices, tp_gather(): return lax.all_gather(value, TP_AXES, axis=axis, tiled=True)  40.6 us
    dot_general x9, matrix products, matmul_rows(): return jnp.dot(left, right, preferred_element_type=jnp.float32)  38.1 us
  transfers between devices with their start and end apart: 19, of which 12 were waited for; matrix products, arithmetic and copies ran while one was open for 13% of the time, Pallas kernels for 0%

profile of v5, /device:TPU:0, one launch (start us, length us, event | category | flops | bytes accessed | tf_op | source)
XLA Modules:
  0.0 1673.9 jit_solution(4552552000076115813)
XLA Ops:
  27.2 13.9 all-to-all-done
  42.7 159.6 %all-gather.7.cloned.1.call-done = bf16[5,2176,512]{2,1,0:T(8,128)(2,1)} async-done(((bf16[5,272,512]{2,1,0:T(8,128)(2,1)}), bf16[5,2176,512]{2,1,0:T(8,128)(2,1)}) %all-gather.7.cloned.1.call-update) | async-done | bytes 11141136 | tf_op jit(solution)/shard_map/all_gather | solution.py:182
  216.0 7.5 fusion.134
  306.6 7.1 transpose.127
  330.4 31.8 %reduce-scatter.6.cloned.1.call-done = bf16[2,64,2048]{2,1,0:T(8,128)(2,1)} async-done(((bf16[2,256,2048]{2,1,0:T(8,128)(2,1)}), bf16[2,64,2048]{2,1,0:T(8,128)(2,1)}) %reduce-scatter.6.cloned.1.call-update) | async-done | bytes 524304 | tf_op jit(solution)/shard_map/reduce_scatter | solution.py:176
  366.0 327.7 %all-to-all-done.3 = bf16[3,8,128,2816]{2,3,0,1:T(8,128)(2,1)} async-done(((bf16[3,8,128,2816]{2,3,0,1:T(8,128)(2,1)}), bf16[3,8,128,2816]{2,3,0,1:T(8,128)(2,1)}, u32[]{:S(2)}, u32[]{:S(2)}) %all-to-all-start.3) | async-done | bytes 17301536 | tf_op jit(solution)/shard_map/all_to_all | solution.py:196
  693.7 8.1 copy.437
  701.8 20.1 %all_to_all.111 = bf16[3,8,1,128,2,1408]{3,5,1,0,2,4:T(8,128)(2,1)} all-to-all(bf16[3,8,1,128,2,1408]{3,5,1,0,2,4:T(8,128)(2,1)S(1)} %copy.437), channel_id=1, replica_groups=mesh['dq'=8,'core'=2,'mlp'=2] {'core'}, dimensions={4} | all-to-all | bytes 34603008 | tf_op jit(solution)/shard_map/all_to_all | solution.py:214
  721.8 21.4 %copy.438 = bf16[3,8,1,128,2,1408]{5,3,4,1,0,2:T(8,128)(2,1)} copy(bf16[3,8,1,128,2,1408]{3,5,1,0,2,4:T(8,128)(2,1)} %all_to_all.111) | data formatting | bytes 34603008 | tf_op jit(solution)/shard_map/all_to_all | solution.py:214
  743.2 11.4 fusion.133
  774.8 27.4 %reduce-scatter.8.cloned.1.call-done = bf16[2,64,2048]{2,1,0:T(8,128)(2,1)} async-done(((bf16[2,256,2048]{2,1,0:T(8,128)(2,1)}), bf16[2,64,2048]{2,1,0:T(8,128)(2,1)}) %reduce-scatter.8.cloned.1.call-update) | async-done | bytes 524304 | tf_op jit(solution)/shard_map/reduce_scatter | solution.py:176
  804.6 22.2 %all-gather.13.cloned.1.call-done = bf16[2,256,2048]{2,1,0:T(8,128)(2,1)} async-done(((bf16[2,64,2048]{2,1,0:T(8,128)(2,1)}), bf16[2,256,2048]{2,1,0:T(8,128)(2,1)}) %all-gather.13.cloned.1.call-update) | async-done | bytes 2097168 | tf_op jit(solution)/shard_map/all_gather | solution.py:172
  826.8 9.1 multiply_convert_fusion
  842.5 7.3 add_convert_fusion.1
  849.9 31.5 %reduce-scatter.10.cloned.1.call-done = bf16[2,64,2048]{2,1,0:T(8,128)(2,1)} async-done(((bf16[2,256,2048]{2,1,0:T(8,128)(2,1)}), bf16[2,64,2048]{2,1,0:T(8,128)(2,1)}) %reduce-scatter.10.cloned.1.call-update) | async-done | bytes 524304 | tf_op jit(solution)/shard_map/reduce_scatter | solution.py:176
  890.5 18.4 %all-gather.15.cloned.1.call-done = bf16[2,256,2048]{2,1,0:T(8,128)(2,1)} async-done(((bf16[2,64,2048]{2,1,0:T(8,128)(2,1)}), bf16[2,256,2048]{2,1,0:T(8,128)(2,1)}) %all-gather.15.cloned.1.call-update) | async-done | bytes 2097168 | tf_op jit(solution)/shard_map/all_gather | solution.py:172
  922.9 9.2 all-to-all-done.5
  1045.8 8.5 add_convert_fusion
  1058.4 8.4 convolution_convert_fusion
  1093.9 8.4 pad_maximum_fusion
  1139.3 10.2 pad_maximum_fusion.1
  1149.5 430.0 %all-to-all-done.8 = bf16[3,8,256,1408]{3,2,0,1:T(8,128)(2,1)} async-done(((bf16[3,8,256,1408]{3,2,0,1:T(8,128)(2,1)}), bf16[3,8,256,1408]{3,2,0,1:T(8,128)(2,1)}, u32[]{:S(2)}, u32[]{:S(2)}) %all-to-all-start.8) | async-done | bytes 17301536 | tf_op jit(solution)/shard_map/all_to_all | solution.py:207
  1579.5 7.1 convert_reduce_fusion
  1594.6 32.8 %reduce-scatter.14.cloned.1.call-done = bf16[5,272,512]{2,1,0:T(8,128)(2,1)} async-done(((bf16[5,2176,512]{2,1,0:T(8,128)(2,1)}), bf16[5,272,512]{2,1,0:T(8,128)(2,1)}) %reduce-scatter.14.cloned.1.call-update) | async-done | bytes 1392656 | tf_op jit(solution)/shard_map/reduce_scatter | solution.py:186
  (572 shorter events, 418.1 us)
Async XLA Ops:
  12.2 10.9 all-to-all-start.1
  23.2 18.0 %all-to-all-start = ((bf16[4,64,4,512]{3,1,0,2:T(8,128)(2,1)}), bf16[4,64,4,512]{3,1,0,2:T(8,128)(2,1)S(1)}, u32[]{:S(2)}, u32[]{:S(2)}) async-start(bf16[4,64,4,512]{3,1,0,2:T(8,128)(2,1)} %copy.409), calls=%async_computation | async-start | bytes 2097152 | tf_op jit(solution)/shard_map/all_to_all | solution.py:214
  26.7 175.6 %all-gather.7.cloned.1.call-start = ((), (), s32[]{:S(2)}) async-start(), calls=%async_computation.15 | async-start | bytes 12533760 | tf_op jit(solution)/shard_map/all_gather | solution.py:182
  42.5 184.1 %all-gather.9.cloned.1.call-start = ((), (), s32[]{:S(2)}) async-start(), calls=%async_computation.16 | async-start | bytes 2621440 | tf_op jit(solution)/shard_map/all_gather | solution.py:172
  42.7 159.6 %copy-start.130 = (f32[2,64]{1,0:T(2,128)}, f32[2,64]{1,0:T(2,128)S(1)}, u32[]{:S(2)}) copy-start(f32[2,64]{1,0:T(2,128)S(1)} %fusion.51) | copy-start | bytes 1540
  42.7 161.5 %copy-start.126 = (f32[2,64]{1,0:T(2,128)}, f32[2,64]{1,0:T(2,128)S(1)}, u32[]{:S(2)}) copy-start(f32[2,64]{1,0:T(2,128)S(1)} %fusion.126) | copy-start | bytes 1540
  293.6 13.1 all-to-all-start.2
  313.8 379.9 %all-to-all-start.3 = ((bf16[3,8,128,2816]{2,3,0,1:T(8,128)(2,1)}), bf16[3,8,128,2816]{2,3,0,1:T(8,128)(2,1)}, u32[]{:S(2)}, u32[]{:S(2)}) async-start(bf16[3,8,128,2816]{2,3,0,1:T(8,128)(2,1)} %transpose.127), calls=%async_computation.4 | async-start | bytes 34603008 | tf_op jit(solution)/shard_map/all_to_all | solution.py:196
  319.5 42.7 %reduce-scatter.6.cloned.1.call-start = ((), (), s32[]{:S(2)}) async-start(), calls=%async_computation.17 | async-start | bytes 2621440 | tf_op jit(solution)/shard_map/reduce_scatter | solution.py:176
  330.3 424.3 %all-gather.11.cloned.1.call-start = ((), (), s32[]{:S(2)}) async-start(), calls=%async_computation.18 | async-start | bytes 2621440 | tf_op jit(solution)/shard_map/all_gather | solution.py:172
  330.4 552.9 %copy-start.80 = (f32[2048]{0:T(1024)}, f32[2048]{0:T(1024)S(1)}, u32[]{:S(2)}) copy-start(f32[2048]{0:T(1024)S(1)} %reshape.759) | copy-start | bytes 24580
  363.7 519.6 %copy-start.98 = (f32[2,64]{1,0:T(2,128)}, f32[2,64]{1,0:T(2,128)S(1)}, u32[]{:S(2)}) copy-start(f32[2,64]{1,0:T(2,128)S(1)} %fusion.127) | copy-start | bytes 1540
  365.9 436.3 %reduce-scatter.8.cloned.1.call-start = ((), (), s32[]{:S(2)}) async-start(), calls=%async_computation.19 | async-start | bytes 2621440 | tf_op jit(solution)/shard_map/reduce_scatter | solution.py:176
  772.1 54.7 %all-gather.13.cloned.1.call-start = ((), (), s32[]{:S(2)}) async-start(), calls=%async_computation.20 | async-start | bytes 2621440 | tf_op jit(solution)/shard_map/all_gather | solution.py:172
  772.7 110.6 %copy-start.124 = (f32[2,64]{1,0:T(2,128)}, f32[2,64]{1,0:T(2,128)S(1)}, u32[]{:S(2)}) copy-start(f32[2,64]{1,0:T(2,128)S(1)} %convert_element_type.228) | copy-start | bytes 1540
  774.7 106.7 %reduce-scatter.10.cloned.1.call-start = ((), (), s32[]{:S(2)}) async-start(), calls=%async_computation.21 | async-start | bytes 2621440 | tf_op jit(solution)/shard_map/reduce_scatter | solution.py:176
  849.9 59.0 %all-gather.15.cloned.1.call-start = ((), (), s32[]{:S(2)}) async-start(), calls=%async_computation.22 | async-start | bytes 2621440 | tf_op jit(solution)/shard_map/all_gather | solution.py:172
  913.3 18.8 %all-to-all-start.5 = ((f32[512,4,2,1,64]{0,4,2,3,1:T(8,128)}), f32[512,4,2,1,64]{0,4,2,3,1:T(8,128)}, u32[]{:S(2)}, u32[]{:S(2)}) async-start(f32[512,4,2,1,64]{0,4,2,3,1:T(8,128)} %convolution_bitcast_fusion.1), calls=%async_computation.8 | async-start | bytes 2097152 | tf_op jit(solution)/shard_map/all_to_all | solution.py:214
  917.6 170.2 %reduce-scatter.12.cloned.1.call-start = ((), (), s32[]{:S(2)}) async-start(), calls=%async_computation.23 | async-start | bytes 2621440 | tf_op jit(solution)/shard_map/reduce_scatter | solution.py:176
  1090.5 18.7 %all-to-all-start.6 = ((f32[8,4,2048]{2,0,1:T(8,128)}), f32[8,4,2048]{2,0,1:T(8,128)S(1)}, u32[]{:S(2)}, u32[]{:S(2)}) async-start(f32[8,4,2048]{2,0,1:T(8,128)} %copy.485), calls=%async_computation.10 | async-start | bytes 524288 | tf_op jit(solution)/shard_map/all_to_all | solution.py:214
  1109.2 470.3 %all-to-all-start.8 = ((bf16[3,8,256,1408]{3,2,0,1:T(8,128)(2,1)}), bf16[3,8,256,1408]{3,2,0,1:T(8,128)(2,1)}, u32[]{:S(2)}, u32[]{:S(2)}) async-start(bf16[3,8,256,1408]{3,2,0,1:T(8,128)(2,1)} %copy.493), calls=%async_computation.13 | async-start | bytes 34603008 | tf_op jit(solution)/shard_map/all_to_all | solution.py:207
  1115.0 512.4 %reduce-scatter.14.cloned.1.call-start = ((), (), s32[]{:S(2)}) async-start(), calls=%async_computation.24 | async-start | bytes 12533760 | tf_op jit(solution)/shard_map/reduce_scatter | solution.py:186
  1589.0 41.5 %all-to-all-start.9 = ((f32[3,2,128,1,1408]{4,2,0,3,1:T(8,128)}), f32[3,2,128,1,1408]{4,2,0,3,1:T(8,128)}, u32[]{:S(2)}, u32[]{:S(2)}) async-start(f32[3,2,128,1,1408]{4,2,0,3,1:T(8,128)} %copy.494), calls=%async_computation.14 | async-start | bytes 8650752 | tf_op jit(solution)/shard_map/all_to_all | solution.py:214
  1630.5 30.9 %all-to-all-start.7 = ((f32[4,4,64,1,512]{4,2,0,3,1:T(8,128)}), f32[4,4,64,1,512]{4,2,0,3,1:T(8,128)S(1)}, u32[]{:S(2)}, u32[]{:S(2)}) async-start(f32[4,4,64,1,512]{4,2,0,3,1:T(8,128)} %copy.487), calls=%async_computation.12 | async-start | bytes 4194304 | tf_op jit(solution)/shard_map/all_to_all | solution.py:214
  (138 other events, 899.9 us)
Sparse Core Ops, SparseCore 0:
  42.6 159.6 all-gather.6
  205.3 20.7 all-gather.8
  330.4 31.7 reduce-scatter.5
  366.1 22.5 all-gather.10
  772.2 29.9 reduce-scatter.7
  804.2 22.5 all-gather.12
  850.0 31.4 reduce-scatter.9
  886.2 22.5 all-gather.14
  1054.4 31.4 reduce-scatter.11
  1149.6 477.7 reduce-scatter.13

commit v6 on v4

--- a/solution.py
+++ b/solution.py
@@ -169,13 +169,24 @@
 
 
 def tp_gather(value, axis):
-    return lax.all_gather(value, TP_AXES, axis=axis, tiled=True)
+    tp = lax.psum(1, TP_AXES)
+    spread = jnp.broadcast_to(
+        jnp.expand_dims(value, axis), value.shape[:axis] + (tp,) + value.shape[axis:]
+    )
+    moved = lax.all_to_all(spread, TP_AXES, axis, axis, tiled=True)
+    shape = list(value.shape)
+    shape[axis] *= tp
+    return moved.reshape(shape)
 
 
 def tp_scatter_low(value, axis):
-    return lax.psum_scatter(
-        value.astype(jnp.bfloat16), TP_AXES, scatter_dimension=axis, tiled=True
-    ).astype(jnp.float32)
+    tp = lax.psum(1, TP_AXES)
+    shape = list(value.shape)
+    staged = value.astype(jnp.bfloat16).reshape(
+        shape[:axis] + [tp, shape[axis] // tp] + shape[axis + 1 :]
+    )
+    moved = lax.all_to_all(staged, TP_AXES, axis, axis, tiled=True)
+    return jnp.sum(moved.astype(jnp.float32), axis=axis)
 
 
 def fsdp_gather(value, axis):
@@ -356,6 +367,7 @@
         out_back = cotangent.astype(jnp.float32) * pad_mask.astype(jnp.float32)[:, :, None]
         out_back_low = out_back.astype(jnp.bfloat16)
         upstream_group = tp_gather(out_back_low, 1).reshape(group_tokens, width)
+        block_out, upstream_group = lax.optimization_barrier((block_out, upstream_group))
         gate_back, up_back = hidden_back(matmul_rows(upstream_group, down_half_t))
         gate_back_low = gate_back.astype(jnp.bfloat16)
         up_back_low = up_back.astype(jnp.bfloat16)

time: 1590 us -> 1400 us (0.88)
  waiting for transfers between devices: 1070 us -> 853 us
  blocking collectives: 13 us -> 43.3 us
  starting transfers between devices: 30.2 us -> 59.5 us
  matrix products: 215 us -> 187 us
    all_gather x2, waiting for transfers between devices: 488 us -> 279 us  [fsdp_gather(): return lax.all_gather(value, FSDP_AXES, axis=axis, tiled=True)]
    all_to_all x0 -> x8, waiting for transfers between devices: none -> 117 us  [the longest x5 59.2 us: tp_gather(): moved = lax.all_to_all(spread, TP_AXES, axis, axis, tiled=True)]
    reduce_scatter x4 -> x0, waiting for transfers between devices: 79.7 us -> none  [tp_scatter_low(): lax.psum_scatter(value.astype(jnp.bfloat16), TP_AXES, scatter_dimension=a...]
    all_gather x4 -> x0, waiting for transfers between devices: 55 us -> none  [tp_gather(): return lax.all_gather(value, TP_AXES, axis=axis, tiled=True)]
    all_to_all x0 -> x8, starting transfers between devices: none -> 34.9 us  [the longest x5 21.4 us: tp_gather(): moved = lax.all_to_all(spread, TP_AXES, axis, axis, tiled=True)]
    all_to_all x0 -> x1, blocking collectives: none -> 28.2 us  [tp_scatter_low(): moved = lax.all_to_all(staged, TP_AXES, axis, axis, tiled=True)]
    all_to_all x7 -> x6, waiting for transfers between devices: 29.3 us -> 35.3 us  [exchange(): return lax.all_to_all(value, axes, split_axis, concat_axis, tiled=True)]
  transfers between devices with their start and end apart: 19 -> 18, of which waited for: 15 -> 13; matrix products, arithmetic and copies ran while one was open for 11% -> 16% of each run, Pallas kernels for 0% -> 0%
where the time goes in v6:
time: 1400 us; the launch traced here: 1390 us
  waiting for transfers between devices  853 us (61%)
  matrix products  187 us (13%)
  local copies, waits for them, and re-layouts  171 us (12%)
  starting transfers between devices  59.5 us (4%)
  other arithmetic  58.4 us (4%)
  blocking collectives  43.3 us (3%)
  between operations  16.6 us (1%)
    reduce_scatter x2, waiting for transfers between devices, fsdp_scatter_low(): lax.psum_scatter(value.astype(jnp.bfloat16), FSDP_AXES, scatter_dimension...  422 us
    all_gather x2, waiting for transfers between devices, fsdp_gather(): return lax.all_gather(value, FSDP_AXES, axis=axis, tiled=True)  279 us
    dot_general x42, matrix products, outer_product_result(): return jnp.einsum(form, first, second, precision=lax.Precision.HIGHEST)  81.1 us
    all_to_all x5, waiting for transfers between devices, tp_gather(): moved = lax.all_to_all(spread, TP_AXES, axis, axis, tiled=True)  59.2 us
    all_to_all x3, waiting for transfers between devices, tp_scatter_low(): moved = lax.all_to_all(staged, TP_AXES, axis, axis, tiled=True)  58 us
    dot_general x9, matrix products, back_product(): jnp.einsum('tg,fg->tf', gradient, weight, preferred_element_type=jnp.floa...  36.9 us
    dot_general x9, matrix products, matmul_rows(): return jnp.dot(left, right, preferred_element_type=jnp.float32)  36.5 us
    all_to_all x6, waiting for transfers between devices, exchange(): return lax.all_to_all(value, axes, split_axis, concat_axis, tiled=True)  35.3 us
  transfers between devices with their start and end apart: 18, of which 13 were waited for; matrix products, arithmetic and copies ran while one was open for 16% of the time, Pallas kernels for 0%

profile of v6, /device:TPU:0, one launch (start us, length us, event | category | flops | bytes accessed | tf_op | source)
XLA Modules:
  0.0 1389.2 jit_solution(16409880348774063830)
XLA Ops:
  27.2 13.9 %all-to-all-done = bf16[4,64,4,512]{3,1,0,2:T(8,128)(2,1)S(1)} async-done(((bf16[4,64,4,512]{3,1,0,2:T(8,128)(2,1)}), bf16[4,64,4,512]{3,1,0,2:T(8,128)(2,1)S(1)}, u32[]{:S(2)}, u32[]{:S(2)}) %all-to-all-start) | async-done | bytes 1048608 | tf_op jit(solution)/shard_map/all_to_all | solution.py:205
  48.7 6.8 all_to_all.146
  61.7 140.6 %all-gather.3.cloned.1.call-done = bf16[5,2176,512]{2,1,0:T(8,128)(2,1)} async-done(((bf16[5,272,512]{2,1,0:T(8,128)(2,1)}), bf16[5,2176,512]{2,1,0:T(8,128)(2,1)}) %all-gather.3.cloned.1.call-update) | async-done | bytes 11141136 | tf_op jit(solution)/shard_map/all_gather | solution.py:193
  211.8 7.6 fusion.143
  222.3 14.1 %all-to-all-done.2 = bf16[2,4,64,2048]{3,2,0,1:T(8,128)(2,1)} async-done(((bf16[2,4,64,2048]{3,2,0,1:T(8,128)(2,1)}), bf16[2,4,64,2048]{3,2,0,1:T(8,128)(2,1)}, u32[]{:S(2)}, u32[]{:S(2)}) %all-to-all-start.2) | async-done | bytes 2097184 | tf_op jit(solution)/shard_map/all_to_all | solution.py:176
  325.2 25.7 %all-to-all-done.5 = bf16[2,4,64,2048]{3,2,0,1:T(8,128)(2,1)} async-done(((bf16[2,4,64,2048]{3,2,0,1:T(8,128)(2,1)}), bf16[2,4,64,2048]{3,2,0,1:T(8,128)(2,1)}, u32[]{:S(2)}, u32[]{:S(2)}) %all-to-all-start.5) | async-done | bytes 2097184 | tf_op jit(solution)/shard_map/all_to_all | solution.py:188
  362.7 23.7 %all-to-all-done.6 = bf16[2,4,64,2048]{3,2,0,1:T(8,128)(2,1)} async-done(((bf16[2,4,64,2048]{3,2,0,1:T(8,128)(2,1)}), bf16[2,4,64,2048]{3,2,0,1:T(8,128)(2,1)}, u32[]{:S(2)}, u32[]{:S(2)}) %all-to-all-start.6) | async-done | bytes 2097184 | tf_op jit(solution)/shard_map/all_to_all | solution.py:176
  396.7 138.3 %all-gather.5.cloned.1.call-done = bf16[3,2048,1408]{2,1,0:T(8,128)(2,1)} async-done(((bf16[3,256,1408]{2,1,0:T(8,128)(2,1)}), bf16[3,2048,1408]{2,1,0:T(8,128)(2,1)}) %all-gather.5.cloned.1.call-update) | async-done | bytes 17301520 | tf_op jit(solution)/shard_map/all_gather | solution.py:193
  535.0 6.9 fusion.8
  561.9 22.6 %all-to-all-done.8 = bf16[2,4,64,2048]{3,2,0,1:T(8,128)(2,1)} async-done(((bf16[2,4,64,2048]{3,2,0,1:T(8,128)(2,1)}), bf16[2,4,64,2048]{3,2,0,1:T(8,128)(2,1)}, u32[]{:S(2)}, u32[]{:S(2)}) %all-to-all-start.8) | async-done | bytes 2097184 | tf_op jit(solution)/shard_map/all_to_all | solution.py:188
  588.5 8.0 multiply_convert_fusion
  602.0 5.3 add_convert_fusion.1
  607.4 28.2 %all_to_all.147 = bf16[2,4,64,2048]{3,2,0,1:T(8,128)(2,1)S(1)} all-to-all(bf16[2,4,64,2048]{3,2,0,1:T(8,128)(2,1)S(1)} %copy.439), channel_id=1, replica_groups=mesh['dq'=8,'core'=2,'mlp'=2] {'core','mlp'}, dimensions={1} | all-to-all | bytes 4194304 | tf_op jit(solution)/shard_map/all_to_all | solution.py:188
  647.4 21.4 %all-to-all-done.11 = bf16[2,4,64,2048]{3,2,0,1:T(8,128)(2,1)} async-done(((bf16[2,4,64,2048]{3,2,0,1:T(8,128)(2,1)}), bf16[2,4,64,2048]{3,2,0,1:T(8,128)(2,1)}, u32[]{:S(2)}, u32[]{:S(2)}) %all-to-all-start.11) | async-done | bytes 2097184 | tf_op jit(solution)/shard_map/all_to_all | solution.py:176
  812.7 7.4 add_convert_fusion
  842.2 9.7 all-to-all-done.13
  866.3 10.2 pad_maximum_fusion.1
  876.8 5.6 fusion.2
  889.9 7.4 pad_maximum_fusion
  897.3 167.0 %reduce-scatter.3.cloned.1.call-done = bf16[5,272,512]{2,1,0:T(8,128)(2,1)} async-done(((bf16[5,2176,512]{2,1,0:T(8,128)(2,1)}), bf16[5,272,512]{2,1,0:T(8,128)(2,1)}) %reduce-scatter.3.cloned.1.call-update) | async-done | bytes 1392656 | tf_op jit(solution)/shard_map/reduce_scatter | solution.py:197
  1081.0 16.9 %all-to-all-done.15 = f32[4,4,64,1,512]{4,2,0,3,1:T(8,128)} async-done(((f32[4,4,64,1,512]{4,2,0,3,1:T(8,128)}), f32[4,4,64,1,512]{4,2,0,3,1:T(8,128)}, u32[]{:S(2)}, u32[]{:S(2)}) %all-to-all-start.15) | async-done | bytes 2097184 | tf_op jit(solution)/shard_map/all_to_all | solution.py:205
  1104.8 255.1 %reduce-scatter.5.cloned.1.call-done = bf16[3,256,1408]{2,1,0:T(8,128)(2,1)} async-done(((bf16[3,2048,1408]{2,1,0:T(8,128)(2,1)}), bf16[3,256,1408]{2,1,0:T(8,128)(2,1)}) %reduce-scatter.5.cloned.1.call-update) | async-done | bytes 2162704 | tf_op jit(solution)/shard_map/reduce_scatter | solution.py:197
  1361.8 8.3 all_to_all.148
  1370.0 5.8 copy.496
  (575 shorter events, 416.4 us)
Async XLA Ops:
  12.2 10.9 all-to-all-start.1
  23.2 18.0 %all-to-all-start = ((bf16[4,64,4,512]{3,1,0,2:T(8,128)(2,1)}), bf16[4,64,4,512]{3,1,0,2:T(8,128)(2,1)S(1)}, u32[]{:S(2)}, u32[]{:S(2)}) async-start(bf16[4,64,4,512]{3,1,0,2:T(8,128)(2,1)} %copy.405), calls=%async_computation | async-start | bytes 2097152 | tf_op jit(solution)/shard_map/all_to_all | solution.py:205
  26.7 175.6 %all-gather.3.cloned.1.call-start = ((), (), s32[]{:S(2)}) async-start(), calls=%async_computation.19 | async-start | bytes 12533760 | tf_op jit(solution)/shard_map/all_gather | solution.py:193
  42.5 492.5 %all-gather.5.cloned.1.call-start = ((), (), s32[]{:S(2)}) async-start(), calls=%async_computation.20 | async-start | bytes 19464192 | tf_op jit(solution)/shard_map/all_gather | solution.py:193
  58.2 146.1 %all-to-all-start.3 = ((s32[2,4,1]{0,2,1:T(1,128)}), s32[2,4,1]{0,2,1:T(1,128)S(1)}, u32[]{:S(2)}, u32[]{:S(2)}) async-start(s32[2,4,1]{0,2,1:T(1,128)} %broadcast_in_dim.45), calls=%async_computation.3 | async-start | bytes 4096 | tf_op jit(solution)/shard_map/all_to_all | solution.py:176
  61.7 142.2 %copy-start.125 = (f32[2,64]{1,0:T(2,128)}, f32[2,64]{1,0:T(2,128)S(1)}, u32[]{:S(2)}) copy-start(f32[2,64]{1,0:T(2,128)S(1)} %fusion.61) | copy-start | bytes 1540
  61.7 142.5 %copy-start.123 = (f32[2,64]{1,0:T(2,128)}, f32[2,64]{1,0:T(2,128)S(1)}, u32[]{:S(2)}) copy-start(f32[2,64]{1,0:T(2,128)S(1)} %fusion.136) | copy-start | bytes 1540
  206.0 30.4 %all-to-all-start.2 = ((bf16[2,4,64,2048]{3,2,0,1:T(8,128)(2,1)}), bf16[2,4,64,2048]{3,2,0,1:T(8,128)(2,1)}, u32[]{:S(2)}, u32[]{:S(2)}) async-start(bf16[2,4,64,2048]{3,2,0,1:T(8,128)(2,1)} %broadcast_in_dim.43), calls=%async_computation.2 | async-start | bytes 4194304 | tf_op jit(solution)/shard_map/all_to_all | solution.py:176
  211.1 50.6 %copy-start.95 = (f32[512]{0:T(512)}, f32[512]{0:T(512)S(1)}, u32[]{:S(2)}) copy-start(f32[512]{0:T(512)S(1)} %get-tuple-element.191) | copy-start | bytes 6148
  211.1 50.6 %copy-start.97 = (f32[512]{0:T(512)}, f32[512]{0:T(512)S(1)}, u32[]{:S(2)}) copy-start(f32[512]{0:T(512)S(1)} %get-tuple-element.193) | copy-start | bytes 6148
  211.8 43.8 %copy-start.63 = (bf16[2048,16]{1,0:T(8,128)(2,1)}, bf16[2048,16]{1,0:T(8,128)(2,1)S(1)}, u32[]{:S(2)}) copy-start(bf16[2048,16]{1,0:T(8,128)(2,1)S(1)} %reshape.737) | copy-start | bytes 196612
  301.1 13.1 all-to-all-start.4
  320.7 30.2 %all-to-all-start.5 = ((bf16[2,4,64,2048]{3,2,0,1:T(8,128)(2,1)}), bf16[2,4,64,2048]{3,2,0,1:T(8,128)(2,1)}, u32[]{:S(2)}, u32[]{:S(2)}) async-start(bf16[2,4,64,2048]{3,2,0,1:T(8,128)(2,1)} %copy.431), calls=%async_computation.5 | async-start | bytes 4194304 | tf_op jit(solution)/shard_map/all_to_all | solution.py:188
  356.0 30.4 %all-to-all-start.6 = ((bf16[2,4,64,2048]{3,2,0,1:T(8,128)(2,1)}), bf16[2,4,64,2048]{3,2,0,1:T(8,128)(2,1)}, u32[]{:S(2)}, u32[]{:S(2)}) async-start(bf16[2,4,64,2048]{3,2,0,1:T(8,128)(2,1)} %broadcast_in_dim.47), calls=%async_computation.6 | async-start | bytes 4194304 | tf_op jit(solution)/shard_map/all_to_all | solution.py:176
  389.1 165.2 %all-to-all-start.9 = ((bf16[2,4,64,2048]{3,2,0,1:T(8,128)(2,1)}), bf16[2,4,64,2048]{3,2,0,1:T(8,128)(2,1)}, u32[]{:S(2)}, u32[]{:S(2)}) async-start(bf16[2,4,64,2048]{3,2,0,1:T(8,128)(2,1)} %broadcast_in_dim.48), calls=%async_computation.9 | async-start | bytes 4194304 | tf_op jit(solution)/shard_map/all_to_all | solution.py:176
  554.3 30.2 %all-to-all-start.8 = ((bf16[2,4,64,2048]{3,2,0,1:T(8,128)(2,1)}), bf16[2,4,64,2048]{3,2,0,1:T(8,128)(2,1)}, u32[]{:S(2)}, u32[]{:S(2)}) async-start(bf16[2,4,64,2048]{3,2,0,1:T(8,128)(2,1)} %copy.437), calls=%async_computation.8 | async-start | bytes 4194304 | tf_op jit(solution)/shard_map/all_to_all | solution.py:188
  638.6 30.2 %all-to-all-start.11 = ((bf16[2,4,64,2048]{3,2,0,1:T(8,128)(2,1)}), bf16[2,4,64,2048]{3,2,0,1:T(8,128)(2,1)}, u32[]{:S(2)}, u32[]{:S(2)}) async-start(bf16[2,4,64,2048]{3,2,0,1:T(8,128)(2,1)} %broadcast_in_dim.50), calls=%async_computation.11 | async-start | bytes 4194304 | tf_op jit(solution)/shard_map/all_to_all | solution.py:176
  674.2 22.5 %all-to-all-start.12 = ((f32[512,4,2,1,64]{0,4,2,3,1:T(8,128)}), f32[512,4,2,1,64]{0,4,2,3,1:T(8,128)}, u32[]{:S(2)}, u32[]{:S(2)}) async-start(f32[512,4,2,1,64]{0,4,2,3,1:T(8,128)} %convolution_bitcast_fusion.1), calls=%async_computation.12 | async-start | bytes 2097152 | tf_op jit(solution)/shard_map/all_to_all | solution.py:205
  707.1 40.2 %copy-start.49 = (f32[8,4,64,64]{3,2,1,0:T(8,128)}, f32[8,4,64,64]{3,2,1,0:T(8,128)S(1)}, u32[]{:S(2)}) copy-start(f32[8,4,64,64]{3,2,1,0:T(8,128)S(1)} %convolution_multiply_fusion) | copy-start | bytes 1572868
  821.6 30.3 %all-to-all-start.13 = ((bf16[2,4,64,2048]{3,2,0,1:T(8,128)(2,1)}), bf16[2,4,64,2048]{3,2,0,1:T(8,128)(2,1)}, u32[]{:S(2)}, u32[]{:S(2)}) async-start(bf16[2,4,64,2048]{3,2,0,1:T(8,128)(2,1)} %copy.476), calls=%async_computation.13 | async-start | bytes 4194304 | tf_op jit(solution)/shard_map/all_to_all | solution.py:188
  856.5 9.4 all-to-all-start.14
  860.0 204.3 %reduce-scatter.3.cloned.1.call-start = ((), (), s32[]{:S(2)}) async-start(), calls=%async_computation.21 | async-start | bytes 12533760 | tf_op jit(solution)/shard_map/reduce_scatter | solution.py:197
  876.5 483.3 %reduce-scatter.5.cloned.1.call-start = ((), (), s32[]{:S(2)}) async-start(), calls=%async_computation.22 | async-start | bytes 19464192 | tf_op jit(solution)/shard_map/reduce_scatter | solution.py:197
  1067.4 30.5 %all-to-all-start.15 = ((f32[4,4,64,1,512]{4,2,0,3,1:T(8,128)}), f32[4,4,64,1,512]{4,2,0,3,1:T(8,128)}, u32[]{:S(2)}, u32[]{:S(2)}) async-start(f32[4,4,64,1,512]{4,2,0,3,1:T(8,128)} %copy.490), calls=%async_computation.16 | async-start | bytes 4194304 | tf_op jit(solution)/shard_map/all_to_all | solution.py:205
  (136 other events, 756.7 us)
Sparse Core Ops, SparseCore 0:
  42.6 159.6 all-gather.2
  203.8 331.1 all-gather.4
  876.6 187.5 reduce-scatter.2
  1068.0 291.7 reduce-scatter.4

commit v7 on v6

--- a/solution.py
+++ b/solution.py
@@ -381,13 +381,9 @@
                 left_product(upstream_group, hidden_low),
             ]
         )
-        ff_reduced = fsdp_scatter_low(ff_sums, 1)
-        ff_back = exchange(
-            ff_reduced.reshape(3, inner, owned_rows, 1, hidden_here), INNER_AXES, 1, 3
-        ).reshape(3, owned_rows, hidden_half)
-        swiglu_gate_grad = ff_back[0]
-        swiglu_up_grad = ff_back[1]
-        swiglu_down_grad = ff_back[2].T
+        ff_sums_low = ff_sums.astype(jnp.bfloat16)
+        ff_sums_low, inner_back = lax.optimization_barrier((ff_sums_low, inner_back))
+        ff_reduced = fsdp_scatter_low(ff_sums_low, 1)
 
         residual_part, swiglu_gain_term = inner_norm_back(
             inner_back.reshape(micro_count * slot, width)
@@ -452,6 +448,13 @@
         small_block = jax.vmap(lambda flat: padded_rows(flat, 5, cols_here))(small_tp)
         extra_out = small_block.shape[2]
         reduce_in = jnp.concatenate([mixer_sums, small_block.transpose(1, 0, 2, 3)], axis=2)
+        ff_reduced, reduce_in = lax.optimization_barrier((ff_reduced, reduce_in))
+        ff_back = exchange(
+            ff_reduced.reshape(3, inner, owned_rows, 1, hidden_here), INNER_AXES, 1, 3
+        ).reshape(3, owned_rows, hidden_half)
+        swiglu_gate_grad = ff_back[0]
+        swiglu_up_grad = ff_back[1]
+        swiglu_down_grad = ff_back[2].T
         mixer_reduced = fsdp_scatter_low(
             reduce_in.reshape(5, fsdp * (group_rows + extra_out), cols_here), 1
         )

time: 1400 us -> 1190 us (0.85)
  waiting for transfers between devices: 853 us -> 663 us
  blocking collectives: 43.3 us -> 6.83 us
  other arithmetic: 58.4 us -> 77.6 us
  matrix products: 187 us -> 169 us
    reduce_scatter x2, waiting for transfers between devices: 422 us -> 235 us  [fsdp_scatter_low(): lax.psum_scatter(value.astype(jnp.bfloat16), FSDP_AXES, scatter_dimension...]
    all_to_all x1 -> x0, blocking collectives: 28.2 us -> none  [tp_scatter_low(): moved = lax.all_to_all(staged, TP_AXES, axis, axis, tiled=True)]
    dot_general x9, matrix products: 36.9 us -> 21.6 us  [back_product(): jnp.einsum('tg,fg->tf', gradient, weight, preferred_element_type=jnp.floa...]
    all_to_all x6 -> x7, waiting for transfers between devices: 35.3 us -> 26.4 us  [exchange(): return lax.all_to_all(value, axes, split_axis, concat_axis, tiled=True)]
    all_to_all x6 -> x7, starting transfers between devices: 24.3 us -> 30.3 us  [exchange(): return lax.all_to_all(value, axes, split_axis, concat_axis, tiled=True)]
    all_to_all x3 -> x4, waiting for transfers between devices: 58 us -> 63.3 us  [tp_scatter_low(): moved = lax.all_to_all(staged, TP_AXES, axis, axis, tiled=True)]
    unnamed x300 -> x324, local copies, waits for them, and re-layouts: 29.6 us -> 28.5 us
  transfers between devices with their start and end apart: 18 -> 20, of which waited for: 13 -> 15; matrix products, arithmetic and copies ran while one was open for 16% -> 30% of each run, Pallas kernels for 0% -> 0%
where the time goes in v7:
time: 1190 us
  waiting for transfers between devices  663 us (56%)
  local copies, waits for them, and re-layouts  180 us (15%)
  matrix products  169 us (14%)
  other arithmetic  77.6 us (7%)
  starting transfers between devices  71.1 us (6%)
  between operations  16.6 us (1%)
    all_gather x2, waiting for transfers between devices, fsdp_gather(): return lax.all_gather(value, FSDP_AXES, axis=axis, tiled=True)  277 us
    reduce_scatter x2, waiting for transfers between devices, fsdp_scatter_low(): lax.psum_scatter(value.astype(jnp.bfloat16), FSDP_AXES, scatter_dimension...  235 us
    dot_general x42, matrix products, outer_product_result(): return jnp.einsum(form, first, second, precision=lax.Precision.HIGHEST)  79.8 us
    all_to_all x4, waiting for transfers between devices, tp_scatter_low(): moved = lax.all_to_all(staged, TP_AXES, axis, axis, tiled=True)  63.3 us
    all_to_all x5, waiting for transfers between devices, tp_gather(): moved = lax.all_to_all(spread, TP_AXES, axis, axis, tiled=True)  62 us
    dot_general x9, matrix products, left_product(): jnp.einsum('tf,tg->fg', first, second, preferred_element_type=jnp.float32)  34.1 us
    dot_general x9, matrix products, matmul_rows(): return jnp.dot(left, right, preferred_element_type=jnp.float32)  33.7 us
    all_to_all x7, starting transfers between devices, exchange(): return lax.all_to_all(value, axes, split_axis, concat_axis, tiled=True)  30.3 us
  transfers between devices with their start and end apart: 20, of which 15 were waited for; matrix products, arithmetic and copies ran while one was open for 30% of the time, Pallas kernels for 0%

profile of v7, /device:TPU:0, one launch (start us, length us, event | category | flops | bytes accessed | tf_op | source)
XLA Modules:
  0.0 1185.2 jit_solution(5688303575806130555)
XLA Ops:
  27.2 13.9 %all-to-all-done = bf16[4,64,4,512]{3,1,0,2:T(8,128)(2,1)S(1)} async-done(((bf16[4,64,4,512]{3,1,0,2:T(8,128)(2,1)}), bf16[4,64,4,512]{3,1,0,2:T(8,128)(2,1)S(1)}, u32[]{:S(2)}, u32[]{:S(2)}) %all-to-all-start) | async-done | bytes 1048608 | tf_op jit(solution)/shard_map/all_to_all | solution.py:205
  48.6 6.8 all_to_all.146
  61.7 140.6 %all-gather.3.cloned.1.call-done = bf16[5,2176,512]{2,1,0:T(8,128)(2,1)} async-done(((bf16[5,272,512]{2,1,0:T(8,128)(2,1)}), bf16[5,2176,512]{2,1,0:T(8,128)(2,1)}) %all-gather.3.cloned.1.call-update) | async-done | bytes 11141136 | tf_op jit(solution)/shard_map/all_gather | solution.py:193
  213.1 7.4 fusion.143
  223.5 13.4 %all-to-all-done.2 = bf16[2,4,64,2048]{3,2,0,1:T(8,128)(2,1)} async-done(((bf16[2,4,64,2048]{3,2,0,1:T(8,128)(2,1)}), bf16[2,4,64,2048]{3,2,0,1:T(8,128)(2,1)}, u32[]{:S(2)}, u32[]{:S(2)}) %all-to-all-start.2) | async-done | bytes 2097184 | tf_op jit(solution)/shard_map/all_to_all | solution.py:176
  312.5 6.3 all-to-all-done.4
  329.2 25.7 %all-to-all-done.5 = bf16[2,4,64,2048]{3,2,0,1:T(8,128)(2,1)} async-done(((bf16[2,4,64,2048]{3,2,0,1:T(8,128)(2,1)}), bf16[2,4,64,2048]{3,2,0,1:T(8,128)(2,1)}, u32[]{:S(2)}, u32[]{:S(2)}) %all-to-all-start.5) | async-done | bytes 2097184 | tf_op jit(solution)/shard_map/all_to_all | solution.py:188
  363.8 25.6 %all-to-all-done.6 = bf16[2,4,64,2048]{3,2,0,1:T(8,128)(2,1)} async-done(((bf16[2,4,64,2048]{3,2,0,1:T(8,128)(2,1)}), bf16[2,4,64,2048]{3,2,0,1:T(8,128)(2,1)}, u32[]{:S(2)}, u32[]{:S(2)}) %all-to-all-start.6) | async-done | bytes 2097184 | tf_op jit(solution)/shard_map/all_to_all | solution.py:176
  398.6 136.4 %all-gather.5.cloned.1.call-done = bf16[3,2048,1408]{2,1,0:T(8,128)(2,1)} async-done(((bf16[3,256,1408]{2,1,0:T(8,128)(2,1)}), bf16[3,2048,1408]{2,1,0:T(8,128)(2,1)}) %all-gather.5.cloned.1.call-update) | async-done | bytes 17301520 | tf_op jit(solution)/shard_map/all_gather | solution.py:193
  535.0 6.9 fusion.8
  562.2 22.6 %all-to-all-done.8 = bf16[2,4,64,2048]{3,2,0,1:T(8,128)(2,1)} async-done(((bf16[2,4,64,2048]{3,2,0,1:T(8,128)(2,1)}), bf16[2,4,64,2048]{3,2,0,1:T(8,128)(2,1)}, u32[]{:S(2)}, u32[]{:S(2)}) %all-to-all-start.8) | async-done | bytes 2097184 | tf_op jit(solution)/shard_map/all_to_all | solution.py:188
  588.8 5.3 fusion.2
  594.1 7.1 fusion.18
  601.3 5.3 fusion
  606.6 5.4 fusion.1
  627.8 14.3 %pad_maximum_fusion.1 = bf16[3,2048,1408]{2,1,0:T(8,128)(2,1)} fusion(bf16[1,2048,1408]{2,1,0:T(8,128)(2,1)} %fusion.2, bf16[1,2048,1408]{2,1,0:T(8,128)(2,1)} %fusion.1, bf16[1,2048,1408]{2,1,0:T(8,128)(2,1)} %fusion), kind=kLoop, calls=%fused_computation.1 | loop fusion | flops 17301504 | bytes 34603008 | tf_op jit(solution)/shard_map/stack | solution.py:377
  642.1 11.4 all-to-all-done.10
  666.4 23.1 %all-to-all-done.11 = bf16[2,4,64,2048]{3,2,0,1:T(8,128)(2,1)} async-done(((bf16[2,4,64,2048]{3,2,0,1:T(8,128)(2,1)}), bf16[2,4,64,2048]{3,2,0,1:T(8,128)(2,1)}, u32[]{:S(2)}, u32[]{:S(2)}) %all-to-all-start.11) | async-done | bytes 2097184 | tf_op jit(solution)/shard_map/all_to_all | solution.py:176
  843.1 5.5 dynamic_update_slice.7
  878.7 10.2 pad_maximum_fusion
  888.9 58.6 %reduce-scatter.3.cloned.1.call-done = bf16[3,256,1408]{2,1,0:T(8,128)(2,1)} async-done(((bf16[3,2048,1408]{2,1,0:T(8,128)(2,1)}), bf16[3,256,1408]{2,1,0:T(8,128)(2,1)}) %reduce-scatter.3.cloned.1.call-update) | async-done | bytes 2162704 | tf_op jit(solution)/shard_map/reduce_scatter | solution.py:197
  956.1 5.7 all-to-all-start.16
  961.8 176.0 %reduce-scatter.5.cloned.1.call-done = bf16[5,272,512]{2,1,0:T(8,128)(2,1)} async-done(((bf16[5,2176,512]{2,1,0:T(8,128)(2,1)}), bf16[5,272,512]{2,1,0:T(8,128)(2,1)}) %reduce-scatter.5.cloned.1.call-update) | async-done | bytes 1392656 | tf_op jit(solution)/shard_map/reduce_scatter | solution.py:197
  1148.7 5.8 copy.496
  (602 shorter events, 429.3 us)
Async XLA Ops:
  12.2 10.9 all-to-all-start.1
  23.2 18.0 %all-to-all-start = ((bf16[4,64,4,512]{3,1,0,2:T(8,128)(2,1)}), bf16[4,64,4,512]{3,1,0,2:T(8,128)(2,1)S(1)}, u32[]{:S(2)}, u32[]{:S(2)}) async-start(bf16[4,64,4,512]{3,1,0,2:T(8,128)(2,1)} %copy.405), calls=%async_computation | async-start | bytes 2097152 | tf_op jit(solution)/shard_map/all_to_all | solution.py:205
  26.7 175.6 %all-gather.3.cloned.1.call-start = ((), (), s32[]{:S(2)}) async-start(), calls=%async_computation.19 | async-start | bytes 12533760 | tf_op jit(solution)/shard_map/all_gather | solution.py:193
  42.5 492.6 %all-gather.5.cloned.1.call-start = ((), (), s32[]{:S(2)}) async-start(), calls=%async_computation.20 | async-start | bytes 19464192 | tf_op jit(solution)/shard_map/all_gather | solution.py:193
  58.2 146.1 %all-to-all-start.3 = ((s32[2,4,1]{0,2,1:T(1,128)}), s32[2,4,1]{0,2,1:T(1,128)S(1)}, u32[]{:S(2)}, u32[]{:S(2)}) async-start(s32[2,4,1]{0,2,1:T(1,128)} %broadcast_in_dim.45), calls=%async_computation.3 | async-start | bytes 4096 | tf_op jit(solution)/shard_map/all_to_all | solution.py:176
  61.7 142.2 %copy-start.134 = (f32[2,64]{1,0:T(2,128)}, f32[2,64]{1,0:T(2,128)S(1)}, u32[]{:S(2)}) copy-start(f32[2,64]{1,0:T(2,128)S(1)} %fusion.61) | copy-start | bytes 1540
  61.7 142.5 %copy-start.130 = (f32[2,64]{1,0:T(2,128)}, f32[2,64]{1,0:T(2,128)S(1)}, u32[]{:S(2)}) copy-start(f32[2,64]{1,0:T(2,128)S(1)} %fusion.136) | copy-start | bytes 1540
  205.9 30.9 %all-to-all-start.2 = ((bf16[2,4,64,2048]{3,2,0,1:T(8,128)(2,1)}), bf16[2,4,64,2048]{3,2,0,1:T(8,128)(2,1)}, u32[]{:S(2)}, u32[]{:S(2)}) async-start(bf16[2,4,64,2048]{3,2,0,1:T(8,128)(2,1)} %broadcast_in_dim.43), calls=%async_computation.2 | async-start | bytes 4194304 | tf_op jit(solution)/shard_map/all_to_all | solution.py:176
  211.2 69.9 %copy-start.86 = (f32[64,64]{1,0:T(8,128)}, f32[64,64]{1,0:T(8,128)S(1)}, u32[]{:S(2)}) copy-start(f32[64,64]{1,0:T(8,128)S(1)} %fusion.116) | copy-start | bytes 49156
  305.8 13.0 %all-to-all-start.4 = ((bf16[512,1,2,4,64]{0,4,2,1,3:T(8,128)(2,1)}), bf16[512,1,2,4,64]{0,4,2,1,3:T(8,128)(2,1)}, u32[]{:S(2)}, u32[]{:S(2)}) async-start(bf16[512,1,2,4,64]{0,4,2,1,3:T(8,128)(2,1)} %copy.429), calls=%async_computation.4 | async-start | bytes 1048576 | tf_op jit(solution)/shard_map/all_to_all | solution.py:205
  324.3 30.6 %all-to-all-start.5 = ((bf16[2,4,64,2048]{3,2,0,1:T(8,128)(2,1)}), bf16[2,4,64,2048]{3,2,0,1:T(8,128)(2,1)}, u32[]{:S(2)}, u32[]{:S(2)}) async-start(bf16[2,4,64,2048]{3,2,0,1:T(8,128)(2,1)} %copy.431), calls=%async_computation.5 | async-start | bytes 4194304 | tf_op jit(solution)/shard_map/all_to_all | solution.py:188
  357.3 298.6 %copy-start.16 = (f32[2,64,2048]{2,1,0:T(8,128)}, f32[2,64,2048]{2,1,0:T(8,128)S(1)}, u32[]{:S(2)}) copy-start(f32[2,64,2048]{2,1,0:T(8,128)S(1)} %get-tuple-element.130) | copy-start | bytes 3145732
  359.0 30.4 %all-to-all-start.6 = ((bf16[2,4,64,2048]{3,2,0,1:T(8,128)(2,1)}), bf16[2,4,64,2048]{3,2,0,1:T(8,128)(2,1)}, u32[]{:S(2)}, u32[]{:S(2)}) async-start(bf16[2,4,64,2048]{3,2,0,1:T(8,128)(2,1)} %broadcast_in_dim.47), calls=%async_computation.6 | async-start | bytes 4194304 | tf_op jit(solution)/shard_map/all_to_all | solution.py:176
  391.0 163.4 %all-to-all-start.9 = ((bf16[2,4,64,2048]{3,2,0,1:T(8,128)(2,1)}), bf16[2,4,64,2048]{3,2,0,1:T(8,128)(2,1)}, u32[]{:S(2)}, u32[]{:S(2)}) async-start(bf16[2,4,64,2048]{3,2,0,1:T(8,128)(2,1)} %broadcast_in_dim.48), calls=%async_computation.9 | async-start | bytes 4194304 | tf_op jit(solution)/shard_map/all_to_all | solution.py:176
  554.4 30.4 %all-to-all-start.8 = ((bf16[2,4,64,2048]{3,2,0,1:T(8,128)(2,1)}), bf16[2,4,64,2048]{3,2,0,1:T(8,128)(2,1)}, u32[]{:S(2)}, u32[]{:S(2)}) async-start(bf16[2,4,64,2048]{3,2,0,1:T(8,128)(2,1)} %copy.437), calls=%async_computation.8 | async-start | bytes 4194304 | tf_op jit(solution)/shard_map/all_to_all | solution.py:188
  623.3 30.2 %all-to-all-start.10 = ((bf16[2,4,64,2048]{3,2,0,1:T(8,128)(2,1)}), bf16[2,4,64,2048]{3,2,0,1:T(8,128)(2,1)}, u32[]{:S(2)}, u32[]{:S(2)}) async-start(bf16[2,4,64,2048]{3,2,0,1:T(8,128)(2,1)} %copy.439), calls=%async_computation.10 | async-start | bytes 4194304 | tf_op jit(solution)/shard_map/all_to_all | solution.py:188
  627.7 319.8 %reduce-scatter.3.cloned.1.call-start = ((), (), s32[]{:S(2)}) async-start(), calls=%async_computation.21 | async-start | bytes 19464192 | tf_op jit(solution)/shard_map/reduce_scatter | solution.py:197
  659.0 30.5 %all-to-all-start.11 = ((bf16[2,4,64,2048]{3,2,0,1:T(8,128)(2,1)}), bf16[2,4,64,2048]{3,2,0,1:T(8,128)(2,1)}, u32[]{:S(2)}, u32[]{:S(2)}) async-start(bf16[2,4,64,2048]{3,2,0,1:T(8,128)(2,1)} %broadcast_in_dim.50), calls=%async_computation.11 | async-start | bytes 4194304 | tf_op jit(solution)/shard_map/all_to_all | solution.py:176
  694.8 19.8 %all-to-all-start.12 = ((f32[512,4,2,1,64]{0,4,2,3,1:T(8,128)}), f32[512,4,2,1,64]{0,4,2,3,1:T(8,128)}, u32[]{:S(2)}, u32[]{:S(2)}) async-start(f32[512,4,2,1,64]{0,4,2,3,1:T(8,128)} %convolution_bitcast_fusion.1), calls=%async_computation.12 | async-start | bytes 2097152 | tf_op jit(solution)/shard_map/all_to_all | solution.py:205
  834.3 30.4 %all-to-all-start.13 = ((bf16[2,4,64,2048]{3,2,0,1:T(8,128)(2,1)}), bf16[2,4,64,2048]{3,2,0,1:T(8,128)(2,1)}, u32[]{:S(2)}, u32[]{:S(2)}) async-start(bf16[2,4,64,2048]{3,2,0,1:T(8,128)(2,1)} %copy.476), calls=%async_computation.13 | async-start | bytes 4194304 | tf_op jit(solution)/shard_map/all_to_all | solution.py:188
  868.9 9.4 all-to-all-start.14
  872.3 265.4 %reduce-scatter.5.cloned.1.call-start = ((), (), s32[]{:S(2)}) async-start(), calls=%async_computation.22 | async-start | bytes 12533760 | tf_op jit(solution)/shard_map/reduce_scatter | solution.py:197
  956.1 184.8 %all-to-all-start.16 = ((f32[3,2,128,1,1408]{4,2,0,3,1:T(8,128)}), f32[3,2,128,1,1408]{4,2,0,3,1:T(8,128)}, u32[]{:S(2)}, u32[]{:S(2)}) async-start(f32[3,2,128,1,1408]{4,2,0,3,1:T(8,128)} %copy.495), calls=%async_computation.18 | async-start | bytes 8650752 | tf_op jit(solution)/shard_map/all_to_all | solution.py:205
  1140.9 30.7 %all-to-all-start.15 = ((f32[4,4,64,1,512]{4,2,0,3,1:T(8,128)}), f32[4,4,64,1,512]{4,2,0,3,1:T(8,128)}, u32[]{:S(2)}, u32[]{:S(2)}) async-start(f32[4,4,64,1,512]{4,2,0,3,1:T(8,128)} %copy.490), calls=%async_computation.17 | async-start | bytes 4194304 | tf_op jit(solution)/shard_map/all_to_all | solution.py:205
  (150 other events, 1044.6 us)
Sparse Core Ops, SparseCore 0:
  42.6 159.6 all-gather.2
  203.8 331.1 all-gather.4
  655.7 291.7 reduce-scatter.2
  951.6 186.1 reduce-scatter.4

commit v8 on v7

--- a/solution.py
+++ b/solution.py
@@ -312,14 +312,16 @@
 
         owned_rows, hidden_half = swiglu_gate.shape
         hidden_here = hidden_half // inner
-        ff_owned = jnp.stack([swiglu_gate, swiglu_up, swiglu_down.T])
-        ff_swapped = exchange(
-            ff_owned.reshape(3, owned_rows, inner, hidden_here), INNER_AXES, 2, 1
-        ).reshape(3, inner * owned_rows, hidden_here)
-        ff_all = fsdp_gather(ff_swapped, 1)
-        gate_half = ff_all[0]
-        up_half = ff_all[1]
-        down_half_t = ff_all[2]
+        ff_owned = jnp.stack([swiglu_gate, swiglu_up, swiglu_down.T]).reshape(
+            3, owned_rows, inner, hidden_here
+        )
+        lanes = hidden_here // 128 if hidden_here % 128 == 0 else 0
+        first = (lanes + 1) // 2 * 128 if lanes > 1 else hidden_here // 2
+        bounds = ((0, first), (first, hidden_here - first))
+        ff_chunks = []
+        for offset, size in bounds:
+            swapped = exchange(ff_owned[..., offset : offset + size], INNER_AXES, 2, 1)
+            ff_chunks.append(fsdp_gather(swapped.reshape(3, inner * owned_rows, size), 1))
 
         inputs = tokens.astype(jnp.float32).reshape(micro_count * slot, width)
         normed, norm_back = jax.vjp(rms_norm, inputs, gain_mixer.astype(jnp.float32))
@@ -356,34 +358,39 @@
         inner_group = tp_gather(inner_low.reshape(micro_count, slot, width), 1).reshape(
             group_tokens, width
         )
-        gate_act = matmul_rows(inner_group, gate_half)
-        up_act = matmul_rows(inner_group, up_half)
-        hidden, hidden_back = jax.vjp(swiglu_mix, gate_act, up_act)
-        hidden_low = hidden.astype(jnp.bfloat16)
-        partial_rows = back_product(hidden_low, down_half_t)
-        branch_rows = tp_scatter_low(partial_rows.reshape(micro_count, slot * tp, width), 1)
-        block_out = (residual.reshape(micro_count, slot, width) + branch_rows).astype(jnp.bfloat16)
-
         out_back = cotangent.astype(jnp.float32) * pad_mask.astype(jnp.float32)[:, :, None]
         out_back_low = out_back.astype(jnp.bfloat16)
         upstream_group = tp_gather(out_back_low, 1).reshape(group_tokens, width)
-        block_out, upstream_group = lax.optimization_barrier((block_out, upstream_group))
-        gate_back, up_back = hidden_back(matmul_rows(upstream_group, down_half_t))
-        gate_back_low = gate_back.astype(jnp.bfloat16)
-        up_back_low = up_back.astype(jnp.bfloat16)
-        inner_part = back_product(gate_back_low, gate_half) + back_product(up_back_low, up_half)
+        partial_rows = None
+        inner_part = None
+        ff_reduced = []
+        for index, chunk_weights in enumerate(ff_chunks):
+            if index > 0:
+                sums_low, chunk_weights = lax.optimization_barrier((sums_low, chunk_weights))
+            gate_piece, up_piece, down_piece_t = chunk_weights[0], chunk_weights[1], chunk_weights[2]
+            gate_act = matmul_rows(inner_group, gate_piece)
+            up_act = matmul_rows(inner_group, up_piece)
+            hidden, hidden_back = jax.vjp(swiglu_mix, gate_act, up_act)
+            hidden_low = hidden.astype(jnp.bfloat16)
+            piece_rows = back_product(hidden_low, down_piece_t)
+            partial_rows = piece_rows if partial_rows is None else partial_rows + piece_rows
+            gate_back, up_back = hidden_back(matmul_rows(upstream_group, down_piece_t))
+            gate_back_low = gate_back.astype(jnp.bfloat16)
+            up_back_low = up_back.astype(jnp.bfloat16)
+            piece_part = back_product(gate_back_low, gate_piece) + back_product(up_back_low, up_piece)
+            inner_part = piece_part if inner_part is None else inner_part + piece_part
+            sums_low = jnp.stack(
+                [
+                    left_product(inner_group, gate_back_low),
+                    left_product(inner_group, up_back_low),
+                    left_product(upstream_group, hidden_low),
+                ]
+            ).astype(jnp.bfloat16)
+            ff_reduced.append(fsdp_scatter_low(sums_low, 1))
+        branch_rows = tp_scatter_low(partial_rows.reshape(micro_count, slot * tp, width), 1)
+        block_out = (residual.reshape(micro_count, slot, width) + branch_rows).astype(jnp.bfloat16)
         inner_back = tp_scatter_low(inner_part.reshape(micro_count, slot * tp, width), 1)
-
-        ff_sums = jnp.stack(
-            [
-                left_product(inner_group, gate_back_low),
-                left_product(inner_group, up_back_low),
-                left_product(upstream_group, hidden_low),
-            ]
-        )
-        ff_sums_low = ff_sums.astype(jnp.bfloat16)
-        ff_sums_low, inner_back = lax.optimization_barrier((ff_sums_low, inner_back))
-        ff_reduced = fsdp_scatter_low(ff_sums_low, 1)
+        block_out, inner_back = lax.optimization_barrier((block_out, inner_back))
 
         residual_part, swiglu_gain_term = inner_norm_back(
             inner_back.reshape(micro_count * slot, width)
@@ -449,8 +456,14 @@
         extra_out = small_block.shape[2]
         reduce_in = jnp.concatenate([mixer_sums, small_block.transpose(1, 0, 2, 3)], axis=2)
         ff_reduced, reduce_in = lax.optimization_barrier((ff_reduced, reduce_in))
-        ff_back = exchange(
-            ff_reduced.reshape(3, inner, owned_rows, 1, hidden_here), INNER_AXES, 1, 3
+        ff_back = jnp.concatenate(
+            [
+                exchange(
+                    piece.reshape(3, inner, owned_rows, 1, size), INNER_AXES, 1, 3
+                ).reshape(3, owned_rows, inner, size)
+                for piece, (offset, size) in zip(ff_reduced, bounds)
+            ],
+            axis=3,
         ).reshape(3, owned_rows, hidden_half)
         swiglu_gate_grad = ff_back[0]
         swiglu_up_grad = ff_back[1]

time: 1190 us -> 1040 us (0.87)
  waiting for transfers between devices: 663 us -> 501 us
  matrix products: 169 us -> 182 us
    all_gather x2 -> x3, waiting for transfers between devices: 277 us -> 165 us  [fsdp_gather(): return lax.all_gather(value, FSDP_AXES, axis=axis, tiled=True)]
    reduce_scatter x2 -> x3, waiting for transfers between devices: 235 us -> 175 us  [fsdp_scatter_low(): lax.psum_scatter(value.astype(jnp.bfloat16), FSDP_AXES, scatter_dimension...]
    all_to_all x5, waiting for transfers between devices: 62 us -> 76.1 us  [tp_gather(): moved = lax.all_to_all(spread, TP_AXES, axis, axis, tiled=True)]
    dot_general x9 -> x12, matrix products: 21.6 us -> 32.2 us  [back_product(): jnp.einsum('tg,fg->tf', gradient, weight, preferred_element_type=jnp.floa...]
    dot_general x9 -> x12, matrix products: 33.7 us -> 38 us  [matmul_rows(): return jnp.dot(left, right, preferred_element_type=jnp.float32)]
    dot_general x9 -> x12, matrix products: 34.1 us -> 30.6 us  [left_product(): jnp.einsum('tf,tg->fg', first, second, preferred_element_type=jnp.float32)]
    unnamed x324 -> x320, local copies, waits for them, and re-layouts: 28.5 us -> 27.8 us
  transfers between devices with their start and end apart: 20 -> 22, of which waited for: 15 -> 15; matrix products, arithmetic and copies ran while one was open for 30% -> 37% of each run, Pallas kernels for 0% -> 0%
where the time goes in v8:
time: 1040 us; the launch traced here: 1030 us
  waiting for transfers between devices  501 us (48%)
  matrix products  182 us (18%)
  local copies, waits for them, and re-layouts  176 us (17%)
  other arithmetic  73.1 us (7%)
  starting transfers between devices  67.8 us (7%)
  blocking collectives  17.8 us (2%)
  between operations  17.2 us (2%)
    reduce_scatter x3, waiting for transfers between devices, fsdp_scatter_low(): lax.psum_scatter(value.astype(jnp.bfloat16), FSDP_AXES, scatter_dimension...  175 us
    all_gather x3, waiting for transfers between devices, fsdp_gather(): return lax.all_gather(value, FSDP_AXES, axis=axis, tiled=True)  165 us
    dot_general x42, matrix products, outer_product_result(): return jnp.einsum(form, first, second, precision=lax.Precision.HIGHEST)  81.4 us
    all_to_all x5, waiting for transfers between devices, tp_gather(): moved = lax.all_to_all(spread, TP_AXES, axis, axis, tiled=True)  76.1 us
    all_to_all x4, waiting for transfers between devices, tp_scatter_low(): moved = lax.all_to_all(staged, TP_AXES, axis, axis, tiled=True)  58.7 us
    dot_general x12, matrix products, matmul_rows(): return jnp.dot(left, right, preferred_element_type=jnp.float32)  38 us
    dot_general x12, matrix products, back_product(): jnp.einsum('tg,fg->tf', gradient, weight, preferred_element_type=jnp.floa...  32.2 us
    dot_general x12, matrix products, left_product(): jnp.einsum('tf,tg->fg', first, second, preferred_element_type=jnp.float32)  30.6 us
  transfers between devices with their start and end apart: 22, of which 15 were waited for; matrix products, arithmetic and copies ran while one was open for 37% of the time, Pallas kernels for 0%

profile of v8, /device:TPU:0, one launch (start us, length us, event | category | flops | bytes accessed | tf_op | source)
XLA Modules:
  0.0 1034.7 jit_solution(461895796433954143)
XLA Ops:
  27.2 13.9 %all-to-all-done = bf16[4,64,4,512]{3,1,0,2:T(8,128)(2,1)S(1)} async-done(((bf16[4,64,4,512]{3,1,0,2:T(8,128)(2,1)}), bf16[4,64,4,512]{3,1,0,2:T(8,128)(2,1)S(1)}, u32[]{:S(2)}, u32[]{:S(2)}) %all-to-all-start) | async-done | bytes 1048608 | tf_op jit(solution)/shard_map/all_to_all | solution.py:205
  44.8 4.7 all_to_all.176
  51.0 4.7 all_to_all.177
  61.1 141.2 %all-gather.4.cloned.1.call-done = bf16[5,2176,512]{2,1,0:T(8,128)(2,1)} async-done(((bf16[5,272,512]{2,1,0:T(8,128)(2,1)}), bf16[5,2176,512]{2,1,0:T(8,128)(2,1)}) %all-gather.4.cloned.1.call-update) | async-done | bytes 11141136 | tf_op jit(solution)/shard_map/all_gather | solution.py:193
  205.9 4.8 all-to-all-start.2
  212.7 7.6 fusion.161
  223.3 13.2 %all-to-all-done.2 = bf16[2,4,64,2048]{3,2,0,1:T(8,128)(2,1)} async-done(((bf16[2,4,64,2048]{3,2,0,1:T(8,128)(2,1)}), bf16[2,4,64,2048]{3,2,0,1:T(8,128)(2,1)}, u32[]{:S(2)}, u32[]{:S(2)}) %all-to-all-start.2) | async-done | bytes 2097184 | tf_op jit(solution)/shard_map/all_to_all | solution.py:176
  308.8 6.3 all-to-all-done.4
  326.4 23.6 %all-to-all-done.5 = bf16[2,4,64,2048]{3,2,0,1:T(8,128)(2,1)S(1)} async-done(((bf16[2,4,64,2048]{3,2,0,1:T(8,128)(2,1)}), bf16[2,4,64,2048]{3,2,0,1:T(8,128)(2,1)S(1)}, u32[]{:S(2)}, u32[]{:S(2)}) %all-to-all-start.5) | async-done | bytes 2097184 | tf_op jit(solution)/shard_map/all_to_all | solution.py:188
  353.1 4.6 all-to-all-start.8
  360.4 23.1 %all-to-all-done.8 = bf16[2,4,64,2048]{3,2,0,1:T(8,128)(2,1)} async-done(((bf16[2,4,64,2048]{3,2,0,1:T(8,128)(2,1)}), bf16[2,4,64,2048]{3,2,0,1:T(8,128)(2,1)}, u32[]{:S(2)}, u32[]{:S(2)}) %all-to-all-start.8) | async-done | bytes 2097184 | tf_op jit(solution)/shard_map/all_to_all | solution.py:176
  393.1 5.5 fusion.10
  398.6 16.7 %all-to-all-done.6 = bf16[2,4,64,2048]{3,2,0,1:T(8,128)(2,1)} async-done(((bf16[2,4,64,2048]{3,2,0,1:T(8,128)(2,1)}), bf16[2,4,64,2048]{3,2,0,1:T(8,128)(2,1)}, u32[]{:S(2)}, u32[]{:S(2)}) %all-to-all-start.6) | async-done | bytes 2097184 | tf_op jit(solution)/shard_map/all_to_all | solution.py:176
  431.6 4.7 pad_maximum_fusion.1
  436.2 23.9 %all-gather.8.cloned.1.call-done = bf16[3,2048,640]{2,1,0:T(8,128)(2,1)} async-done(((bf16[3,256,640]{2,1,0:T(8,128)(2,1)}), bf16[3,2048,640]{2,1,0:T(8,128)(2,1)}) %all-gather.8.cloned.1.call-update) | async-done | bytes 7864336 | tf_op jit(solution)/shard_map/all_gather | solution.py:193
  512.8 9.0 all-to-all-done.10
  528.4 23.7 %all-to-all-done.11 = bf16[2,4,64,2048]{3,2,0,1:T(8,128)(2,1)} async-done(((bf16[2,4,64,2048]{3,2,0,1:T(8,128)(2,1)}), bf16[2,4,64,2048]{3,2,0,1:T(8,128)(2,1)}, u32[]{:S(2)}, u32[]{:S(2)}) %all-to-all-start.11) | async-done | bytes 2097184 | tf_op jit(solution)/shard_map/all_to_all | solution.py:188
  564.8 23.1 %all-to-all-done.12 = bf16[2,4,64,2048]{3,2,0,1:T(8,128)(2,1)} async-done(((bf16[2,4,64,2048]{3,2,0,1:T(8,128)(2,1)}), bf16[2,4,64,2048]{3,2,0,1:T(8,128)(2,1)}, u32[]{:S(2)}, u32[]{:S(2)}) %all-to-all-start.12) | async-done | bytes 2097184 | tf_op jit(solution)/shard_map/all_to_all | solution.py:176
  682.0 4.9 bitcast_multiply_fusion
  743.1 5.6 dynamic_update_slice.7
  778.6 10.1 pad_maximum_fusion
  801.7 175.4 %reduce-scatter.8.cloned.1.call-done = bf16[5,272,512]{2,1,0:T(8,128)(2,1)} async-done(((bf16[5,2176,512]{2,1,0:T(8,128)(2,1)}), bf16[5,272,512]{2,1,0:T(8,128)(2,1)}) %reduce-scatter.8.cloned.1.call-update) | async-done | bytes 1392656 | tf_op jit(solution)/shard_map/reduce_scatter | solution.py:197
  981.6 8.4 all_to_all.178
  990.0 5.0 all-to-all-start.16
  (622 shorter events, 453.9 us)
Async XLA Ops:
  12.2 10.9 %all-to-all-start.1 = ((bf16[4,2,960]{2,1,0:T(2,128)(2,1)}), bf16[4,2,960]{2,1,0:T(2,128)(2,1)S(1)}, u32[]{:S(2)}, u32[]{:S(2)}) async-start(bf16[4,2,960]{2,1,0:T(2,128)(2,1)} %reshape.796), calls=%async_computation.1 | async-start | bytes 32768 | tf_op jit(solution)/shard_map/all_to_all | solution.py:205
  23.2 18.0 %all-to-all-start = ((bf16[4,64,4,512]{3,1,0,2:T(8,128)(2,1)}), bf16[4,64,4,512]{3,1,0,2:T(8,128)(2,1)S(1)}, u32[]{:S(2)}, u32[]{:S(2)}) async-start(bf16[4,64,4,512]{3,1,0,2:T(8,128)(2,1)} %copy.412), calls=%async_computation | async-start | bytes 2097152 | tf_op jit(solution)/shard_map/all_to_all | solution.py:205
  26.7 175.6 %all-gather.4.cloned.1.call-start = ((), (), s32[]{:S(2)}) async-start(), calls=%async_computation.22 | async-start | bytes 12533760 | tf_op jit(solution)/shard_map/all_gather | solution.py:193
  42.5 350.7 %all-gather.6.cloned.1.call-start = ((), (), s32[]{:S(2)}) async-start(), calls=%async_computation.23 | async-start | bytes 10616832 | tf_op jit(solution)/shard_map/all_gather | solution.py:193
  56.3 148.1 %all-to-all-start.3 = ((s32[2,4,1]{0,2,1:T(1,128)}), s32[2,4,1]{0,2,1:T(1,128)S(1)}, u32[]{:S(2)}, u32[]{:S(2)}) async-start(s32[2,4,1]{0,2,1:T(1,128)} %broadcast_in_dim.45), calls=%async_computation.3 | async-start | bytes 4096 | tf_op jit(solution)/shard_map/all_to_all | solution.py:176
  59.5 400.6 %all-gather.8.cloned.1.call-start = ((), (), s32[]{:S(2)}) async-start(), calls=%async_computation.24 | async-start | bytes 8847360 | tf_op jit(solution)/shard_map/all_gather | solution.py:193
  61.1 143.1 %copy-start.133 = (f32[2,64]{1,0:T(2,128)}, f32[2,64]{1,0:T(2,128)S(1)}, u32[]{:S(2)}) copy-start(f32[2,64]{1,0:T(2,128)S(1)} %fusion.154) | copy-start | bytes 1540
  205.9 30.5 %all-to-all-start.2 = ((bf16[2,4,64,2048]{3,2,0,1:T(8,128)(2,1)}), bf16[2,4,64,2048]{3,2,0,1:T(8,128)(2,1)}, u32[]{:S(2)}, u32[]{:S(2)}) async-start(bf16[2,4,64,2048]{3,2,0,1:T(8,128)(2,1)} %broadcast_in_dim.43), calls=%async_computation.2 | async-start | bytes 4194304 | tf_op jit(solution)/shard_map/all_to_all | solution.py:176
  302.0 13.1 %all-to-all-start.4 = ((bf16[512,1,2,4,64]{0,4,2,1,3:T(8,128)(2,1)}), bf16[512,1,2,4,64]{0,4,2,1,3:T(8,128)(2,1)}, u32[]{:S(2)}, u32[]{:S(2)}) async-start(bf16[512,1,2,4,64]{0,4,2,1,3:T(8,128)(2,1)} %copy.436), calls=%async_computation.4 | async-start | bytes 1048576 | tf_op jit(solution)/shard_map/all_to_all | solution.py:205
  320.6 29.4 %all-to-all-start.5 = ((bf16[2,4,64,2048]{3,2,0,1:T(8,128)(2,1)}), bf16[2,4,64,2048]{3,2,0,1:T(8,128)(2,1)S(1)}, u32[]{:S(2)}, u32[]{:S(2)}) async-start(bf16[2,4,64,2048]{3,2,0,1:T(8,128)(2,1)} %copy.438), calls=%async_computation.5 | async-start | bytes 4194304 | tf_op jit(solution)/shard_map/all_to_all | solution.py:188
  353.1 30.4 %all-to-all-start.8 = ((bf16[2,4,64,2048]{3,2,0,1:T(8,128)(2,1)}), bf16[2,4,64,2048]{3,2,0,1:T(8,128)(2,1)}, u32[]{:S(2)}, u32[]{:S(2)}) async-start(bf16[2,4,64,2048]{3,2,0,1:T(8,128)(2,1)} %broadcast_in_dim.48), calls=%async_computation.8 | async-start | bytes 4194304 | tf_op jit(solution)/shard_map/all_to_all | solution.py:176
  360.2 195.3 %copy-start.16 = (f32[2,64,2048]{2,1,0:T(8,128)}, f32[2,64,2048]{2,1,0:T(8,128)S(1)}, u32[]{:S(2)}) copy-start(f32[2,64,2048]{2,1,0:T(8,128)S(1)} %get-tuple-element.130) | copy-start | bytes 3145732
  385.1 30.2 %all-to-all-start.6 = ((bf16[2,4,64,2048]{3,2,0,1:T(8,128)(2,1)}), bf16[2,4,64,2048]{3,2,0,1:T(8,128)(2,1)}, u32[]{:S(2)}, u32[]{:S(2)}) async-start(bf16[2,4,64,2048]{3,2,0,1:T(8,128)(2,1)} %broadcast_in_dim.47), calls=%async_computation.6 | async-start | bytes 4194304 | tf_op jit(solution)/shard_map/all_to_all | solution.py:176
  389.5 399.2 %reduce-scatter.6.cloned.1.call-start = ((), (), s32[]{:S(2)}) async-start(), calls=%async_computation.26 | async-start | bytes 8847360 | tf_op jit(solution)/shard_map/reduce_scatter | solution.py:197
  491.5 30.2 %all-to-all-start.10 = ((bf16[2,4,64,2048]{3,2,0,1:T(8,128)(2,1)}), bf16[2,4,64,2048]{3,2,0,1:T(8,128)(2,1)}, u32[]{:S(2)}, u32[]{:S(2)}) async-start(bf16[2,4,64,2048]{3,2,0,1:T(8,128)(2,1)} %copy.447), calls=%async_computation.10 | async-start | bytes 4194304 | tf_op jit(solution)/shard_map/all_to_all | solution.py:188
  521.7 30.3 %all-to-all-start.11 = ((bf16[2,4,64,2048]{3,2,0,1:T(8,128)(2,1)}), bf16[2,4,64,2048]{3,2,0,1:T(8,128)(2,1)}, u32[]{:S(2)}, u32[]{:S(2)}) async-start(bf16[2,4,64,2048]{3,2,0,1:T(8,128)(2,1)} %copy.448), calls=%async_computation.11 | async-start | bytes 4194304 | tf_op jit(solution)/shard_map/all_to_all | solution.py:188
  557.6 30.3 %all-to-all-start.12 = ((bf16[2,4,64,2048]{3,2,0,1:T(8,128)(2,1)}), bf16[2,4,64,2048]{3,2,0,1:T(8,128)(2,1)}, u32[]{:S(2)}, u32[]{:S(2)}) async-start(bf16[2,4,64,2048]{3,2,0,1:T(8,128)(2,1)} %broadcast_in_dim.50), calls=%async_computation.12 | async-start | bytes 4194304 | tf_op jit(solution)/shard_map/all_to_all | solution.py:176
  593.4 22.0 %all-to-all-start.13 = ((f32[512,4,2,1,64]{0,4,2,3,1:T(8,128)}), f32[512,4,2,1,64]{0,4,2,3,1:T(8,128)}, u32[]{:S(2)}, u32[]{:S(2)}) async-start(f32[512,4,2,1,64]{0,4,2,3,1:T(8,128)} %convolution_bitcast_fusion.1), calls=%async_computation.13 | async-start | bytes 2097152 | tf_op jit(solution)/shard_map/all_to_all | solution.py:205
  597.6 193.7 %reduce-scatter.4.cloned.1.call-start = ((), (), s32[]{:S(2)}) async-start(), calls=%async_computation.25 | async-start | bytes 10616832 | tf_op jit(solution)/shard_map/reduce_scatter | solution.py:197
  734.3 30.3 %all-to-all-start.14 = ((bf16[2,4,64,2048]{3,2,0,1:T(8,128)(2,1)}), bf16[2,4,64,2048]{3,2,0,1:T(8,128)(2,1)}, u32[]{:S(2)}, u32[]{:S(2)}) async-start(bf16[2,4,64,2048]{3,2,0,1:T(8,128)(2,1)} %copy.485), calls=%async_computation.14 | async-start | bytes 4194304 | tf_op jit(solution)/shard_map/all_to_all | solution.py:188
  768.9 9.4 all-to-all-start.15
  772.3 204.8 %reduce-scatter.8.cloned.1.call-start = ((), (), s32[]{:S(2)}) async-start(), calls=%async_computation.27 | async-start | bytes 12533760 | tf_op jit(solution)/shard_map/reduce_scatter | solution.py:197
  794.5 185.7 %all-to-all-start.17 = ((f32[3,2,128,1,768]{4,2,0,3,1:T(8,128)}), f32[3,2,128,1,768]{4,2,0,3,1:T(8,128)S(1)}, u32[]{:S(2)}, u32[]{:S(2)}) async-start(f32[3,2,128,1,768]{4,2,0,3,1:T(8,128)} %copy.504), calls=%async_computation.20 | async-start | bytes 4718592 | tf_op jit(solution)/shard_map/all_to_all | solution.py:205
  990.0 30.7 %all-to-all-start.16 = ((f32[4,4,64,1,512]{4,2,0,3,1:T(8,128)}), f32[4,4,64,1,512]{4,2,0,3,1:T(8,128)}, u32[]{:S(2)}, u32[]{:S(2)}) async-start(f32[4,4,64,1,512]{4,2,0,3,1:T(8,128)} %copy.499), calls=%async_computation.19 | async-start | bytes 4194304 | tf_op jit(solution)/shard_map/all_to_all | solution.py:205
  (150 other events, 1084.8 us)
Sparse Core Ops, SparseCore 0:
  42.6 159.6 all-gather.3
  205.0 136.2 all-gather.5
  343.5 116.5 all-gather.7
  482.1 138.1 reduce-scatter.5
  623.8 162.5 reduce-scatter.3
  793.0 184.0 reduce-scatter.7

commit v9 on v8

--- a/solution.py
+++ b/solution.py
@@ -196,7 +196,7 @@
 def fsdp_scatter_low(value, axis):
     return lax.psum_scatter(
         value.astype(jnp.bfloat16), FSDP_AXES, scatter_dimension=axis, tiled=True
-    ).astype(jnp.float32)
+    )
 
 
 def exchange(value, axes, split_axis, concat_axis):
@@ -257,10 +257,6 @@
         head_scale = head_gain.astype(jnp.float32)
         reset_len = slot if group_start.shape[1] == 1 else 0
 
-        column_owned = jnp.stack([query_weight, key_weight, value_weight, gate_weight])
-        column_swapped = exchange(
-            column_owned.reshape(4, rows, tp, cols_here), TP_AXES, 2, 1
-        ).reshape(4, group_rows, cols_here)
         small_pack = jnp.concatenate(
             [
                 conv_weight.reshape(-1),
@@ -270,8 +266,21 @@
             ]
         )
         small_size = small_pack.shape[0]
-        small_group = exchange(
-            jnp.broadcast_to(small_pack[None, :], (tp, small_size)), TP_AXES, 0, 0
+        small_lines = -(-small_size // (4 * cols_here))
+        small_copy = jnp.pad(small_pack, (0, 4 * small_lines * cols_here - small_size))
+        small_copy = jnp.broadcast_to(
+            small_copy.reshape(4, small_lines, 1, cols_here), (4, small_lines, tp, cols_here)
+        )
+        column_owned = jnp.stack([query_weight, key_weight, value_weight, gate_weight])
+        swap_in = jnp.concatenate(
+            [column_owned.reshape(4, rows, tp, cols_here), small_copy], axis=1
+        )
+        swap_out = exchange(swap_in, TP_AXES, 2, 1).reshape(4, tp, rows + small_lines, cols_here)
+        column_swapped = swap_out[:, :, :rows].reshape(4, group_rows, cols_here)
+        small_group = (
+            swap_out[:, :, rows:]
+            .transpose(1, 0, 2, 3)
+            .reshape(tp, -1)[:, :small_size]
         )
         small_rows_in = padded_rows(small_group.reshape(-1), 5, cols_here)
         extra_in = small_rows_in.shape[1]
@@ -417,6 +426,16 @@
             + back_product(gate_low, gate_cols)
             + back_product(beta_low, beta_here)
         )
+        ff_back = jnp.concatenate(
+            [
+                exchange(
+                    piece.reshape(3, inner, owned_rows, 1, size), INNER_AXES, 1, 3
+                ).reshape(3, owned_rows, inner, size)
+                for piece, (offset, size) in zip(ff_reduced, bounds)
+            ],
+            axis=3,
+        ).reshape(3, owned_rows, hidden_half).astype(jnp.float32)
+        ff_back, normed_part = lax.optimization_barrier((ff_back, normed_part))
         normed_back = tp_scatter_low(normed_part.reshape(micro_count, slot * tp, width), 1)
         input_part, mixer_gain_term = norm_back(normed_back.reshape(micro_count * slot, width))
         tokens_grad = (residual_back + input_part).reshape(micro_count, slot, width)
@@ -455,16 +474,7 @@
         small_block = jax.vmap(lambda flat: padded_rows(flat, 5, cols_here))(small_tp)
         extra_out = small_block.shape[2]
         reduce_in = jnp.concatenate([mixer_sums, small_block.transpose(1, 0, 2, 3)], axis=2)
-        ff_reduced, reduce_in = lax.optimization_barrier((ff_reduced, reduce_in))
-        ff_back = jnp.concatenate(
-            [
-                exchange(
-                    piece.reshape(3, inner, owned_rows, 1, size), INNER_AXES, 1, 3
-                ).reshape(3, owned_rows, inner, size)
-                for piece, (offset, size) in zip(ff_reduced, bounds)
-            ],
-            axis=3,
-        ).reshape(3, owned_rows, hidden_half)
+        ff_back, reduce_in = lax.optimization_barrier((ff_back, reduce_in))
         swiglu_gate_grad = ff_back[0]
         swiglu_up_grad = ff_back[1]
         swiglu_down_grad = ff_back[2].T
@@ -473,10 +483,10 @@
         )
         column_back = exchange(
             mixer_reduced[:4, :group_rows].reshape(4, tp, rows, 1, cols_here), TP_AXES, 1, 3
-        ).reshape(4, rows, width)
+        ).reshape(4, rows, width).astype(jnp.float32)
         query_grad, key_grad, value_grad, gate_grad = (column_back[index] for index in range(4))
-        out_grad = mixer_reduced[4, :group_rows].reshape(rows, width)
-        small_out = mixer_reduced[:, group_rows:].reshape(-1)[:small_width]
+        out_grad = mixer_reduced[4, :group_rows].reshape(rows, width).astype(jnp.float32)
+        small_out = mixer_reduced[:, group_rows:].reshape(-1)[:small_width].astype(jnp.float32)
         conv_grad = small_out[:conv_size].reshape(conv_weight.shape)
         beta_grad = small_out[conv_size : conv_size + beta_size].reshape(beta_weight.shape)
         mixer_gain_grad = small_out[conv_size + beta_size : conv_size + beta_size + rows]

time: 1040 us -> 1080 us (1.038)
  waiting for transfers between devices: 501 us -> 554 us
    reduce_scatter x3, waiting for transfers between devices: 175 us -> 218 us  [fsdp_scatter_low(): lax.psum_scatter(value.astype(jnp.bfloat16), FSDP_AXES, scatter_dimension...]
    all_to_all x7 -> x6, waiting for transfers between devices: 25.7 us -> 32.5 us  [exchange(): return lax.all_to_all(value, axes, split_axis, concat_axis, tiled=True)]
    all_to_all x7 -> x6, starting transfers between devices: 28.7 us -> 23.9 us  [exchange(): return lax.all_to_all(value, axes, split_axis, concat_axis, tiled=True)]
    unnamed x320 -> x318, local copies, waits for them, and re-layouts: 27.8 us -> 24.8 us
  transfers between devices with their start and end apart: 22 -> 21, of which waited for: 15 -> 16; matrix products, arithmetic and copies ran while one was open for 37% -> 32% of each run, Pallas kernels for 0% -> 0%
where the time goes in v9:
time: 1080 us; the launch traced here: 1070 us
  waiting for transfers between devices  554 us (51%)
  matrix products  182 us (17%)
  local copies, waits for them, and re-layouts  171 us (16%)
  other arithmetic  68.2 us (6%)
  starting transfers between devices  63.5 us (6%)
  between operations  17.2 us (2%)
  blocking collectives  15.1 us (1%)
    reduce_scatter x3, waiting for transfers between devices, fsdp_scatter_low(): lax.psum_scatter(value.astype(jnp.bfloat16), FSDP_AXES, scatter_dimension...  218 us
    all_gather x3, waiting for transfers between devices, fsdp_gather(): return lax.all_gather(value, FSDP_AXES, axis=axis, tiled=True)  165 us
    dot_general x42, matrix products, outer_product_result(): return jnp.einsum(form, first, second, precision=lax.Precision.HIGHEST)  81.2 us
    all_to_all x5, waiting for transfers between devices, tp_gather(): moved = lax.all_to_all(spread, TP_AXES, axis, axis, tiled=True)  76.1 us
    all_to_all x4, waiting for transfers between devices, tp_scatter_low(): moved = lax.all_to_all(staged, TP_AXES, axis, axis, tiled=True)  62 us
    dot_general x12, matrix products, matmul_rows(): return jnp.dot(left, right, preferred_element_type=jnp.float32)  38 us
    dot_general x12, matrix products, back_product(): jnp.einsum('tg,fg->tf', gradient, weight, preferred_element_type=jnp.floa...  33.6 us
    all_to_all x6, waiting for transfers between devices, exchange(): return lax.all_to_all(value, axes, split_axis, concat_axis, tiled=True)  32.5 us
  transfers between devices with their start and end apart: 21, of which 16 were waited for; matrix products, arithmetic and copies ran while one was open for 32% of the time, Pallas kernels for 0%

profile of v9, /device:TPU:0, one launch (start us, length us, event | category | flops | bytes accessed | tf_op | source)
XLA Modules:
  0.0 1070.4 jit_solution(7379735180693426736)
XLA Ops:
  21.7 14.5 %all-to-all-done = bf16[4,65,4,512]{3,0,1,2:T(4,128)(2,1)S(1)} async-done(((bf16[4,65,4,512]{3,0,1,2:T(4,128)(2,1)}), bf16[4,65,4,512]{3,0,1,2:T(4,128)(2,1)S(1)}, u32[]{:S(2)}, u32[]{:S(2)}) %all-to-all-start) | async-done | bytes 1064992 | tf_op jit(solution)/shard_map/all_to_all | solution.py:205
  56.5 141.4 %all-gather.4.cloned.1.call-done = bf16[5,2176,512]{2,1,0:T(8,128)(2,1)} async-done(((bf16[5,272,512]{2,1,0:T(8,128)(2,1)}), bf16[5,2176,512]{2,1,0:T(8,128)(2,1)}) %all-gather.4.cloned.1.call-update) | async-done | bytes 11141136 | tf_op jit(solution)/shard_map/all_gather | solution.py:193
  201.6 5.1 all-to-all-start.1
  208.7 7.6 fusion.159
  219.2 13.3 %all-to-all-done.1 = bf16[2,4,64,2048]{3,2,0,1:T(8,128)(2,1)} async-done(((bf16[2,4,64,2048]{3,2,0,1:T(8,128)(2,1)}), bf16[2,4,64,2048]{3,2,0,1:T(8,128)(2,1)}, u32[]{:S(2)}, u32[]{:S(2)}) %all-to-all-start.1) | async-done | bytes 2097184 | tf_op jit(solution)/shard_map/all_to_all | solution.py:176
  304.4 6.3 all-to-all-done.3
  322.0 23.6 %all-to-all-done.4 = bf16[2,4,64,2048]{3,2,0,1:T(8,128)(2,1)S(1)} async-done(((bf16[2,4,64,2048]{3,2,0,1:T(8,128)(2,1)}), bf16[2,4,64,2048]{3,2,0,1:T(8,128)(2,1)S(1)}, u32[]{:S(2)}, u32[]{:S(2)}) %all-to-all-start.4) | async-done | bytes 2097184 | tf_op jit(solution)/shard_map/all_to_all | solution.py:188
  348.7 4.8 all-to-all-start.7
  356.2 23.1 %all-to-all-done.7 = bf16[2,4,64,2048]{3,2,0,1:T(8,128)(2,1)} async-done(((bf16[2,4,64,2048]{3,2,0,1:T(8,128)(2,1)}), bf16[2,4,64,2048]{3,2,0,1:T(8,128)(2,1)}, u32[]{:S(2)}, u32[]{:S(2)}) %all-to-all-start.7) | async-done | bytes 2097184 | tf_op jit(solution)/shard_map/all_to_all | solution.py:176
  388.9 5.5 fusion.10
  394.4 16.7 %all-to-all-done.5 = bf16[2,4,64,2048]{3,2,0,1:T(8,128)(2,1)} async-done(((bf16[2,4,64,2048]{3,2,0,1:T(8,128)(2,1)}), bf16[2,4,64,2048]{3,2,0,1:T(8,128)(2,1)}, u32[]{:S(2)}, u32[]{:S(2)}) %all-to-all-start.5) | async-done | bytes 2097184 | tf_op jit(solution)/shard_map/all_to_all | solution.py:176
  432.0 23.8 %all-gather.8.cloned.1.call-done = bf16[3,2048,640]{2,1,0:T(8,128)(2,1)} async-done(((bf16[3,256,640]{2,1,0:T(8,128)(2,1)}), bf16[3,2048,640]{2,1,0:T(8,128)(2,1)}) %all-gather.8.cloned.1.call-update) | async-done | bytes 7864336 | tf_op jit(solution)/shard_map/all_gather | solution.py:193
  508.5 8.9 all-to-all-done.9
  524.0 23.7 %all-to-all-done.10 = bf16[2,4,64,2048]{3,2,0,1:T(8,128)(2,1)} async-done(((bf16[2,4,64,2048]{3,2,0,1:T(8,128)(2,1)}), bf16[2,4,64,2048]{3,2,0,1:T(8,128)(2,1)}, u32[]{:S(2)}, u32[]{:S(2)}) %all-to-all-start.10) | async-done | bytes 2097184 | tf_op jit(solution)/shard_map/all_to_all | solution.py:188
  560.6 23.1 %all-to-all-done.13 = bf16[2,4,64,2048]{3,2,0,1:T(8,128)(2,1)} async-done(((bf16[2,4,64,2048]{3,2,0,1:T(8,128)(2,1)}), bf16[2,4,64,2048]{3,2,0,1:T(8,128)(2,1)}, u32[]{:S(2)}, u32[]{:S(2)}) %all-to-all-start.13) | async-done | bytes 2097184 | tf_op jit(solution)/shard_map/all_to_all | solution.py:176
  677.6 4.9 bitcast_multiply_fusion
  738.6 43.3 %reduce-scatter.4.cloned.1.call-done = bf16[3,256,768]{2,1,0:T(8,128)(2,1)} async-done(((bf16[3,2048,768]{2,1,0:T(8,128)(2,1)}), bf16[3,256,768]{2,1,0:T(8,128)(2,1)}) %reduce-scatter.4.cloned.1.call-update) | async-done | bytes 1179664 | tf_op jit(solution)/shard_map/reduce_scatter | solution.py:197
  784.2 5.8 all_to_all.166
  801.0 5.4 dynamic_update_slice.7
  819.9 5.8 all-to-all-done.15
  839.7 10.4 pad_maximum_fusion
  854.7 5.0 slice_bitcast_fusion.9
  861.2 174.4 %reduce-scatter.8.cloned.1.call-done = bf16[5,272,512]{2,1,0:T(8,128)(2,1)} async-done(((bf16[5,2176,512]{2,1,0:T(8,128)(2,1)}), bf16[5,272,512]{2,1,0:T(8,128)(2,1)}) %reduce-scatter.8.cloned.1.call-update) | async-done | bytes 1392656 | tf_op jit(solution)/shard_map/reduce_scatter | solution.py:197
  1047.6 10.0 all-to-all-done.17
  (621 shorter events, 446.9 us)
Async XLA Ops:
  17.3 18.8 %all-to-all-start = ((bf16[4,65,4,512]{3,0,1,2:T(4,128)(2,1)}), bf16[4,65,4,512]{3,0,1,2:T(4,128)(2,1)S(1)}, u32[]{:S(2)}, u32[]{:S(2)}) async-start(bf16[4,65,4,512]{3,0,1,2:T(4,128)(2,1)} %copy.509), calls=%async_computation | async-start | bytes 2129920 | tf_op jit(solution)/shard_map/all_to_all | solution.py:205
  21.5 176.5 %all-gather.4.cloned.1.call-start = ((), (), s32[]{:S(2)}) async-start(), calls=%async_computation.21 | async-start | bytes 12533760 | tf_op jit(solution)/shard_map/all_gather | solution.py:193
  37.9 351.0 %all-gather.6.cloned.1.call-start = ((), (), s32[]{:S(2)}) async-start(), calls=%async_computation.22 | async-start | bytes 10616832 | tf_op jit(solution)/shard_map/all_gather | solution.py:193
  51.7 148.3 %all-to-all-start.2 = ((s32[2,4,1]{0,2,1:T(1,128)}), s32[2,4,1]{0,2,1:T(1,128)S(1)}, u32[]{:S(2)}, u32[]{:S(2)}) async-start(s32[2,4,1]{0,2,1:T(1,128)} %broadcast_in_dim.48), calls=%async_computation.2 | async-start | bytes 4096 | tf_op jit(solution)/shard_map/all_to_all | solution.py:176
  55.0 400.9 %all-gather.8.cloned.1.call-start = ((), (), s32[]{:S(2)}) async-start(), calls=%async_computation.23 | async-start | bytes 8847360 | tf_op jit(solution)/shard_map/all_gather | solution.py:193
  56.5 143.0 %copy-start.137 = (f32[2,64]{1,0:T(2,128)}, f32[2,64]{1,0:T(2,128)S(1)}, u32[]{:S(2)}) copy-start(f32[2,64]{1,0:T(2,128)S(1)} %fusion.77) | copy-start | bytes 1540
  56.5 143.3 %copy-start.133 = (f32[2,64]{1,0:T(2,128)}, f32[2,64]{1,0:T(2,128)S(1)}, u32[]{:S(2)}) copy-start(f32[2,64]{1,0:T(2,128)S(1)} %fusion.152) | copy-start | bytes 1540
  201.6 30.9 %all-to-all-start.1 = ((bf16[2,4,64,2048]{3,2,0,1:T(8,128)(2,1)}), bf16[2,4,64,2048]{3,2,0,1:T(8,128)(2,1)}, u32[]{:S(2)}, u32[]{:S(2)}) async-start(bf16[2,4,64,2048]{3,2,0,1:T(8,128)(2,1)} %broadcast_in_dim.46), calls=%async_computation.1 | async-start | bytes 4194304 | tf_op jit(solution)/shard_map/all_to_all | solution.py:176
  297.7 13.1 %all-to-all-start.3 = ((bf16[512,1,2,4,64]{0,4,2,1,3:T(8,128)(2,1)}), bf16[512,1,2,4,64]{0,4,2,1,3:T(8,128)(2,1)}, u32[]{:S(2)}, u32[]{:S(2)}) async-start(bf16[512,1,2,4,64]{0,4,2,1,3:T(8,128)(2,1)} %copy.533), calls=%async_computation.3 | async-start | bytes 1048576 | tf_op jit(solution)/shard_map/all_to_all | solution.py:205
  316.2 29.4 %all-to-all-start.4 = ((bf16[2,4,64,2048]{3,2,0,1:T(8,128)(2,1)}), bf16[2,4,64,2048]{3,2,0,1:T(8,128)(2,1)S(1)}, u32[]{:S(2)}, u32[]{:S(2)}) async-start(bf16[2,4,64,2048]{3,2,0,1:T(8,128)(2,1)} %copy.535), calls=%async_computation.4 | async-start | bytes 4194304 | tf_op jit(solution)/shard_map/all_to_all | solution.py:188
  348.7 30.6 %all-to-all-start.7 = ((bf16[2,4,64,2048]{3,2,0,1:T(8,128)(2,1)}), bf16[2,4,64,2048]{3,2,0,1:T(8,128)(2,1)}, u32[]{:S(2)}, u32[]{:S(2)}) async-start(bf16[2,4,64,2048]{3,2,0,1:T(8,128)(2,1)} %broadcast_in_dim.51), calls=%async_computation.7 | async-start | bytes 4194304 | tf_op jit(solution)/shard_map/all_to_all | solution.py:176
  356.0 195.1 %copy-start.16 = (f32[2,64,2048]{2,1,0:T(8,128)}, f32[2,64,2048]{2,1,0:T(8,128)S(1)}, u32[]{:S(2)}) copy-start(f32[2,64,2048]{2,1,0:T(8,128)S(1)} %get-tuple-element.147) | copy-start | bytes 3145732
  380.8 30.2 %all-to-all-start.5 = ((bf16[2,4,64,2048]{3,2,0,1:T(8,128)(2,1)}), bf16[2,4,64,2048]{3,2,0,1:T(8,128)(2,1)}, u32[]{:S(2)}, u32[]{:S(2)}) async-start(bf16[2,4,64,2048]{3,2,0,1:T(8,128)(2,1)} %broadcast_in_dim.50), calls=%async_computation.5 | async-start | bytes 4194304 | tf_op jit(solution)/shard_map/all_to_all | solution.py:176
  385.3 346.6 %reduce-scatter.6.cloned.1.call-start = ((), (), s32[]{:S(2)}) async-start(), calls=%async_computation.25 | async-start | bytes 8847360 | tf_op jit(solution)/shard_map/reduce_scatter | solution.py:197
  487.1 30.2 %all-to-all-start.9 = ((bf16[2,4,64,2048]{3,2,0,1:T(8,128)(2,1)}), bf16[2,4,64,2048]{3,2,0,1:T(8,128)(2,1)}, u32[]{:S(2)}, u32[]{:S(2)}) async-start(bf16[2,4,64,2048]{3,2,0,1:T(8,128)(2,1)} %copy.544), calls=%async_computation.9 | async-start | bytes 4194304 | tf_op jit(solution)/shard_map/all_to_all | solution.py:188
  517.4 30.3 %all-to-all-start.10 = ((bf16[2,4,64,2048]{3,2,0,1:T(8,128)(2,1)}), bf16[2,4,64,2048]{3,2,0,1:T(8,128)(2,1)}, u32[]{:S(2)}, u32[]{:S(2)}) async-start(bf16[2,4,64,2048]{3,2,0,1:T(8,128)(2,1)} %copy.545), calls=%async_computation.10 | async-start | bytes 4194304 | tf_op jit(solution)/shard_map/all_to_all | solution.py:188
  553.3 30.3 %all-to-all-start.13 = ((bf16[2,4,64,2048]{3,2,0,1:T(8,128)(2,1)}), bf16[2,4,64,2048]{3,2,0,1:T(8,128)(2,1)}, u32[]{:S(2)}, u32[]{:S(2)}) async-start(bf16[2,4,64,2048]{3,2,0,1:T(8,128)(2,1)} %broadcast_in_dim.53), calls=%async_computation.15 | async-start | bytes 4194304 | tf_op jit(solution)/shard_map/all_to_all | solution.py:176
  557.9 224.0 %reduce-scatter.4.cloned.1.call-start = ((), (), s32[]{:S(2)}) async-start(), calls=%async_computation.24 | async-start | bytes 10616832 | tf_op jit(solution)/shard_map/reduce_scatter | solution.py:197
  589.0 21.9 %all-to-all-start.14 = ((f32[512,4,2,1,64]{0,4,2,3,1:T(8,128)}), f32[512,4,2,1,64]{0,4,2,3,1:T(8,128)}, u32[]{:S(2)}, u32[]{:S(2)}) async-start(f32[512,4,2,1,64]{0,4,2,3,1:T(8,128)} %convolution_bitcast_fusion.1), calls=%async_computation.16 | async-start | bytes 2097152 | tf_op jit(solution)/shard_map/all_to_all | solution.py:205
  734.2 50.0 %all-to-all-start.12 = ((bf16[3,2,128,1,640]{4,2,0,3,1:T(8,128)(2,1)}), bf16[3,2,128,1,640]{4,2,0,3,1:T(8,128)(2,1)}, u32[]{:S(2)}, u32[]{:S(2)}) async-start(bf16[3,2,128,1,640]{4,2,0,3,1:T(8,128)(2,1)} %copy.547), calls=%async_computation.14 | async-start | bytes 1966080 | tf_op jit(solution)/shard_map/all_to_all | solution.py:205
  795.5 30.2 %all-to-all-start.15 = ((bf16[2,4,64,2048]{3,2,0,1:T(8,128)(2,1)}), bf16[2,4,64,2048]{3,2,0,1:T(8,128)(2,1)}, u32[]{:S(2)}, u32[]{:S(2)}) async-start(bf16[2,4,64,2048]{3,2,0,1:T(8,128)(2,1)} %copy.585), calls=%async_computation.17 | async-start | bytes 4194304 | tf_op jit(solution)/shard_map/all_to_all | solution.py:188
  829.9 9.4 all-to-all-start.16
  833.4 202.3 %reduce-scatter.8.cloned.1.call-start = ((), (), s32[]{:S(2)}) async-start(), calls=%async_computation.26 | async-start | bytes 12533760 | tf_op jit(solution)/shard_map/reduce_scatter | solution.py:197
  1039.7 17.9 %all-to-all-start.17 = ((bf16[4,4,64,1,512]{4,2,0,3,1:T(8,128)(2,1)}), bf16[4,4,64,1,512]{4,2,0,3,1:T(8,128)(2,1)S(1)}, u32[]{:S(2)}, u32[]{:S(2)}) async-start(bf16[4,4,64,1,512]{4,2,0,3,1:T(8,128)(2,1)} %copy.599), calls=%async_computation.20 | async-start | bytes 2097152 | tf_op jit(solution)/shard_map/all_to_all | solution.py:205
  (149 other events, 942.8 us)
Sparse Core Ops, SparseCore 0:
  38.0 159.8 all-gather.3
  200.7 136.2 all-gather.5
  339.2 116.5 all-gather.7
  477.8 138.1 reduce-scatter.5
  619.4 162.3 reduce-scatter.3
  850.2 185.4 reduce-scatter.7

commit v10 on v9

--- a/solution.py
+++ b/solution.py
@@ -419,13 +419,17 @@
         value_low = value_back.astype(jnp.bfloat16)
         gate_low = gate_lin_back.astype(jnp.bfloat16)
         beta_low = beta_back.astype(jnp.bfloat16)
-        normed_part = (
-            back_product(query_low, query_cols)
-            + back_product(key_low, key_cols)
-            + back_product(value_low, value_cols)
-            + back_product(gate_low, gate_cols)
-            + back_product(beta_low, beta_here)
-        )
+        mixer_sums = jnp.stack(
+            [
+                left_product(normed_group, query_low),
+                left_product(normed_group, key_low),
+                left_product(normed_group, value_low),
+                left_product(normed_group, gate_low),
+                left_product(gated_rows, mixed_group).reshape(width, cols_here),
+            ]
+        )
+        ff_reduced, mixer_sums = lax.optimization_barrier((ff_reduced, mixer_sums))
+        mixer_reduced = fsdp_scatter_low(mixer_sums, 1)
         ff_back = jnp.concatenate(
             [
                 exchange(
@@ -435,20 +439,21 @@
             ],
             axis=3,
         ).reshape(3, owned_rows, hidden_half).astype(jnp.float32)
-        ff_back, normed_part = lax.optimization_barrier((ff_back, normed_part))
+        swiglu_gate_grad = ff_back[0]
+        swiglu_up_grad = ff_back[1]
+        swiglu_down_grad = ff_back[2].T
+
+        normed_part = (
+            back_product(query_low, query_cols)
+            + back_product(key_low, key_cols)
+            + back_product(value_low, value_cols)
+            + back_product(gate_low, gate_cols)
+            + back_product(beta_low, beta_here)
+        )
         normed_back = tp_scatter_low(normed_part.reshape(micro_count, slot * tp, width), 1)
         input_part, mixer_gain_term = norm_back(normed_back.reshape(micro_count * slot, width))
         tokens_grad = (residual_back + input_part).reshape(micro_count, slot, width)
 
-        mixer_sums = jnp.stack(
-            [
-                left_product(normed_group, query_low),
-                left_product(normed_group, key_low),
-                left_product(normed_group, value_low),
-                left_product(normed_group, gate_low),
-                left_product(gated_rows, mixed_group).reshape(width, cols_here),
-            ]
-        ).reshape(5, fsdp, group_rows, cols_here)
         beta_sum = left_product(normed_group, beta_low)
         beta_wide = lax.dynamic_update_slice_in_dim(
             jnp.zeros((width, head_count), jnp.float32), beta_sum, position * heads_here, axis=1
@@ -468,25 +473,12 @@
             axis=1,
         )
         small_width = small_terms.shape[1]
-        small_tp = jnp.sum(
-            exchange(small_terms.reshape(fsdp, tp, small_width), TP_AXES, 1, 1), axis=1
-        )
-        small_block = jax.vmap(lambda flat: padded_rows(flat, 5, cols_here))(small_tp)
-        extra_out = small_block.shape[2]
-        reduce_in = jnp.concatenate([mixer_sums, small_block.transpose(1, 0, 2, 3)], axis=2)
-        ff_back, reduce_in = lax.optimization_barrier((ff_back, reduce_in))
-        swiglu_gate_grad = ff_back[0]
-        swiglu_up_grad = ff_back[1]
-        swiglu_down_grad = ff_back[2].T
-        mixer_reduced = fsdp_scatter_low(
-            reduce_in.reshape(5, fsdp * (group_rows + extra_out), cols_here), 1
-        )
+        small_out = jnp.sum(exchange(small_terms, ALL_AXES, 0, 0), axis=0)
         column_back = exchange(
-            mixer_reduced[:4, :group_rows].reshape(4, tp, rows, 1, cols_here), TP_AXES, 1, 3
+            mixer_reduced[:4].reshape(4, tp, rows, 1, cols_here), TP_AXES, 1, 3
         ).reshape(4, rows, width).astype(jnp.float32)
         query_grad, key_grad, value_grad, gate_grad = (column_back[index] for index in range(4))
-        out_grad = mixer_reduced[4, :group_rows].reshape(rows, width).astype(jnp.float32)
-        small_out = mixer_reduced[:, group_rows:].reshape(-1)[:small_width].astype(jnp.float32)
+        out_grad = mixer_reduced[4].reshape(rows, width).astype(jnp.float32)
         conv_grad = small_out[:conv_size].reshape(conv_weight.shape)
         beta_grad = small_out[conv_size : conv_size + beta_size].reshape(beta_weight.shape)
         mixer_gain_grad = small_out[conv_size + beta_size : conv_size + beta_size + rows]

time: 1080 us -> 1010 us (0.935)
  waiting for transfers between devices: 554 us -> 516 us
  local copies, waits for them, and re-layouts: 171 us -> 159 us
    reduce_scatter x3, waiting for transfers between devices: 218 us -> 153 us  [fsdp_scatter_low(): lax.psum_scatter(value.astype(jnp.bfloat16), FSDP_AXES, scatter_dimension...]
    all_to_all x6 -> x7, waiting for transfers between devices: 32.5 us -> 49.2 us  [exchange(): return lax.all_to_all(value, axes, split_axis, concat_axis, tiled=True)]
    all_to_all x4, waiting for transfers between devices: 62 us -> 74.2 us  [tp_scatter_low(): moved = lax.all_to_all(staged, TP_AXES, axis, axis, tiled=True)]
    all_to_all x6 -> x7, starting transfers between devices: 23.9 us -> 27.1 us  [exchange(): return lax.all_to_all(value, axes, split_axis, concat_axis, tiled=True)]
    unnamed x318 -> x323, local copies, waits for them, and re-layouts: 24.8 us -> 26 us
  transfers between devices with their start and end apart: 21 -> 22, of which waited for: 16 -> 19; matrix products, arithmetic and copies ran while one was open for 32% -> 34% of each run, Pallas kernels for 0% -> 0%
where the time goes in v10:
time: 1010 us; the launch traced here: 1000 us
  waiting for transfers between devices  516 us (51%)
  matrix products  177 us (18%)
  local copies, waits for them, and re-layouts  159 us (16%)
  starting transfers between devices  66.6 us (7%)
  other arithmetic  59.7 us (6%)
  between operations  17.1 us (2%)
    all_gather x3, waiting for transfers between devices, fsdp_gather(): return lax.all_gather(value, FSDP_AXES, axis=axis, tiled=True)  165 us
    reduce_scatter x3, waiting for transfers between devices, fsdp_scatter_low(): lax.psum_scatter(value.astype(jnp.bfloat16), FSDP_AXES, scatter_dimension...  153 us
    dot_general x42, matrix products, outer_product_result(): return jnp.einsum(form, first, second, precision=lax.Precision.HIGHEST)  79 us
    all_to_all x5, waiting for transfers between devices, tp_gather(): moved = lax.all_to_all(spread, TP_AXES, axis, axis, tiled=True)  74.4 us
    all_to_all x4, waiting for transfers between devices, tp_scatter_low(): moved = lax.all_to_all(staged, TP_AXES, axis, axis, tiled=True)  74.2 us
    all_to_all x7, waiting for transfers between devices, exchange(): return lax.all_to_all(value, axes, split_axis, concat_axis, tiled=True)  49.2 us
    dot_general x12, matrix products, matmul_rows(): return jnp.dot(left, right, preferred_element_type=jnp.float32)  38 us
    dot_general x12, matrix products, back_product(): jnp.einsum('tg,fg->tf', gradient, weight, preferred_element_type=jnp.floa...  33.9 us
  transfers between devices with their start and end apart: 22, of which 19 were waited for; matrix products, arithmetic and copies ran while one was open for 34% of the time, Pallas kernels for 0%

profile of v10, /device:TPU:0, one launch (start us, length us, event | category | flops | bytes accessed | tf_op | source)
XLA Modules:
  0.0 1004.6 jit_solution(6882034867024832371)
XLA Ops:
  21.7 14.5 %all-to-all-done = bf16[4,65,4,512]{3,0,1,2:T(4,128)(2,1)S(1)} async-done(((bf16[4,65,4,512]{3,0,1,2:T(4,128)(2,1)}), bf16[4,65,4,512]{3,0,1,2:T(4,128)(2,1)S(1)}, u32[]{:S(2)}, u32[]{:S(2)}) %all-to-all-start) | async-done | bytes 1064992 | tf_op jit(solution)/shard_map/all_to_all | solution.py:205
  40.2 4.7 all_to_all.168
  46.5 4.7 all_to_all.169
  56.5 141.4 %all-gather.4.cloned.1.call-done = bf16[5,2176,512]{2,1,0:T(8,128)(2,1)} async-done(((bf16[5,272,512]{2,1,0:T(8,128)(2,1)}), bf16[5,2176,512]{2,1,0:T(8,128)(2,1)}) %all-gather.4.cloned.1.call-update) | async-done | bytes 11141136 | tf_op jit(solution)/shard_map/all_gather | solution.py:193
  201.7 5.1 all-to-all-start.1
  208.7 7.5 fusion.156
  219.2 13.3 %all-to-all-done.1 = bf16[2,4,64,2048]{3,2,0,1:T(8,128)(2,1)} async-done(((bf16[2,4,64,2048]{3,2,0,1:T(8,128)(2,1)}), bf16[2,4,64,2048]{3,2,0,1:T(8,128)(2,1)}, u32[]{:S(2)}, u32[]{:S(2)}) %all-to-all-start.1) | async-done | bytes 2097184 | tf_op jit(solution)/shard_map/all_to_all | solution.py:176
  304.6 6.3 all-to-all-done.3
  322.1 23.6 %all-to-all-done.4 = bf16[2,4,64,2048]{3,2,0,1:T(8,128)(2,1)S(1)} async-done(((bf16[2,4,64,2048]{3,2,0,1:T(8,128)(2,1)}), bf16[2,4,64,2048]{3,2,0,1:T(8,128)(2,1)S(1)}, u32[]{:S(2)}, u32[]{:S(2)}) %all-to-all-start.4) | async-done | bytes 2097184 | tf_op jit(solution)/shard_map/all_to_all | solution.py:188
  348.8 4.9 all-to-all-start.7
  356.3 23.1 %all-to-all-done.7 = bf16[2,4,64,2048]{3,2,0,1:T(8,128)(2,1)} async-done(((bf16[2,4,64,2048]{3,2,0,1:T(8,128)(2,1)}), bf16[2,4,64,2048]{3,2,0,1:T(8,128)(2,1)}, u32[]{:S(2)}, u32[]{:S(2)}) %all-to-all-start.7) | async-done | bytes 2097184 | tf_op jit(solution)/shard_map/all_to_all | solution.py:176
  389.2 5.5 fusion.10
  394.7 16.5 %all-to-all-done.5 = bf16[2,4,64,2048]{3,2,0,1:T(8,128)(2,1)} async-done(((bf16[2,4,64,2048]{3,2,0,1:T(8,128)(2,1)}), bf16[2,4,64,2048]{3,2,0,1:T(8,128)(2,1)}, u32[]{:S(2)}, u32[]{:S(2)}) %all-to-all-start.5) | async-done | bytes 2097184 | tf_op jit(solution)/shard_map/all_to_all | solution.py:176
  427.5 4.7 pad_maximum_fusion
  432.2 23.6 %all-gather.8.cloned.1.call-done = bf16[3,2048,640]{2,1,0:T(8,128)(2,1)} async-done(((bf16[3,256,640]{2,1,0:T(8,128)(2,1)}), bf16[3,2048,640]{2,1,0:T(8,128)(2,1)}) %all-gather.8.cloned.1.call-update) | async-done | bytes 7864336 | tf_op jit(solution)/shard_map/all_gather | solution.py:193
  508.1 9.0 all-to-all-done.9
  523.7 23.7 %all-to-all-done.10 = bf16[2,4,64,2048]{3,2,0,1:T(8,128)(2,1)} async-done(((bf16[2,4,64,2048]{3,2,0,1:T(8,128)(2,1)}), bf16[2,4,64,2048]{3,2,0,1:T(8,128)(2,1)}, u32[]{:S(2)}, u32[]{:S(2)}) %all-to-all-start.10) | async-done | bytes 2097184 | tf_op jit(solution)/shard_map/all_to_all | solution.py:188
  561.8 21.5 %all-to-all-done.11 = bf16[2,4,64,2048]{3,2,0,1:T(8,128)(2,1)} async-done(((bf16[2,4,64,2048]{3,2,0,1:T(8,128)(2,1)}), bf16[2,4,64,2048]{3,2,0,1:T(8,128)(2,1)}, u32[]{:S(2)}, u32[]{:S(2)}) %all-to-all-start.11) | async-done | bytes 2097184 | tf_op jit(solution)/shard_map/all_to_all | solution.py:176
  601.8 5.7 all-to-all-done.12
  727.1 54.6 %reduce-scatter.4.cloned.1.call-done = bf16[3,256,768]{2,1,0:T(8,128)(2,1)} async-done(((bf16[3,2048,768]{2,1,0:T(8,128)(2,1)}), bf16[3,256,768]{2,1,0:T(8,128)(2,1)}) %reduce-scatter.4.cloned.1.call-update) | async-done | bytes 1179664 | tf_op jit(solution)/shard_map/reduce_scatter | solution.py:197
  806.4 17.9 %all-to-all-done.13 = bf16[2,4,64,2048]{3,2,0,1:T(8,128)(2,1)} async-done(((bf16[2,4,64,2048]{3,2,0,1:T(8,128)(2,1)}), bf16[2,4,64,2048]{3,2,0,1:T(8,128)(2,1)}, u32[]{:S(2)}, u32[]{:S(2)}) %all-to-all-start.13) | async-done | bytes 2097184 | tf_op jit(solution)/shard_map/all_to_all | solution.py:188
  838.3 13.6 %all-to-all-done.15 = f32[32,1,2048]{2,1,0:T(1,128)S(1)} async-done(((f32[32,1,2048]{2,1,0:T(1,128)}), f32[32,1,2048]{2,1,0:T(1,128)S(1)}, u32[]{:S(2)}, u32[]{:S(2)}) %all-to-all-start.15) | async-done | bytes 262176 | tf_op jit(solution)/shard_map/all_to_all | solution.py:205
  871.3 98.2 %reduce-scatter.8.cloned.1.call-done = bf16[5,256,512]{2,1,0:T(8,128)(2,1)} async-done(((bf16[5,2048,512]{2,1,0:T(8,128)(2,1)}), bf16[5,256,512]{2,1,0:T(8,128)(2,1)}) %reduce-scatter.8.cloned.1.call-update) | async-done | bytes 1310736 | tf_op jit(solution)/shard_map/reduce_scatter | solution.py:197
  983.9 6.7 all-to-all-done.14
  (623 shorter events, 437.3 us)
Async XLA Ops:
  17.3 18.8 %all-to-all-start = ((bf16[4,65,4,512]{3,0,1,2:T(4,128)(2,1)}), bf16[4,65,4,512]{3,0,1,2:T(4,128)(2,1)S(1)}, u32[]{:S(2)}, u32[]{:S(2)}) async-start(bf16[4,65,4,512]{3,0,1,2:T(4,128)(2,1)} %copy.472), calls=%async_computation | async-start | bytes 2129920 | tf_op jit(solution)/shard_map/all_to_all | solution.py:205
  21.5 176.5 %all-gather.4.cloned.1.call-start = ((), (), s32[]{:S(2)}) async-start(), calls=%async_computation.21 | async-start | bytes 12533760 | tf_op jit(solution)/shard_map/all_gather | solution.py:193
  37.9 351.3 %all-gather.6.cloned.1.call-start = ((), (), s32[]{:S(2)}) async-start(), calls=%async_computation.22 | async-start | bytes 10616832 | tf_op jit(solution)/shard_map/all_gather | solution.py:193
  51.7 148.3 %all-to-all-start.2 = ((s32[2,4,1]{0,2,1:T(1,128)}), s32[2,4,1]{0,2,1:T(1,128)S(1)}, u32[]{:S(2)}, u32[]{:S(2)}) async-start(s32[2,4,1]{0,2,1:T(1,128)} %broadcast_in_dim.48), calls=%async_computation.2 | async-start | bytes 4096 | tf_op jit(solution)/shard_map/all_to_all | solution.py:176
  55.0 400.9 %all-gather.8.cloned.1.call-start = ((), (), s32[]{:S(2)}) async-start(), calls=%async_computation.23 | async-start | bytes 8847360 | tf_op jit(solution)/shard_map/all_gather | solution.py:193
  201.7 30.8 %all-to-all-start.1 = ((bf16[2,4,64,2048]{3,2,0,1:T(8,128)(2,1)}), bf16[2,4,64,2048]{3,2,0,1:T(8,128)(2,1)}, u32[]{:S(2)}, u32[]{:S(2)}) async-start(bf16[2,4,64,2048]{3,2,0,1:T(8,128)(2,1)} %broadcast_in_dim.46), calls=%async_computation.1 | async-start | bytes 4194304 | tf_op jit(solution)/shard_map/all_to_all | solution.py:176
  297.8 13.0 %all-to-all-start.3 = ((bf16[512,1,2,4,64]{0,4,2,1,3:T(8,128)(2,1)}), bf16[512,1,2,4,64]{0,4,2,1,3:T(8,128)(2,1)}, u32[]{:S(2)}, u32[]{:S(2)}) async-start(bf16[512,1,2,4,64]{0,4,2,1,3:T(8,128)(2,1)} %copy.496), calls=%async_computation.3 | async-start | bytes 1048576 | tf_op jit(solution)/shard_map/all_to_all | solution.py:205
  316.4 29.4 %all-to-all-start.4 = ((bf16[2,4,64,2048]{3,2,0,1:T(8,128)(2,1)}), bf16[2,4,64,2048]{3,2,0,1:T(8,128)(2,1)S(1)}, u32[]{:S(2)}, u32[]{:S(2)}) async-start(bf16[2,4,64,2048]{3,2,0,1:T(8,128)(2,1)} %copy.498), calls=%async_computation.4 | async-start | bytes 4194304 | tf_op jit(solution)/shard_map/all_to_all | solution.py:188
  320.1 230.8 %copy-start.138 = (f32[2,64]{1,0:T(2,128)}, f32[2,64]{1,0:T(2,128)S(1)}, u32[]{:S(2)}) copy-start(f32[2,64]{1,0:T(2,128)S(1)} %convert_element_type.256) | copy-start | bytes 1540
  348.8 30.6 %all-to-all-start.7 = ((bf16[2,4,64,2048]{3,2,0,1:T(8,128)(2,1)}), bf16[2,4,64,2048]{3,2,0,1:T(8,128)(2,1)}, u32[]{:S(2)}, u32[]{:S(2)}) async-start(bf16[2,4,64,2048]{3,2,0,1:T(8,128)(2,1)} %broadcast_in_dim.51), calls=%async_computation.7 | async-start | bytes 4194304 | tf_op jit(solution)/shard_map/all_to_all | solution.py:176
  356.2 194.7 %copy-start.113 = (f32[2,64]{1,0:T(2,128)}, f32[2,64]{1,0:T(2,128)S(1)}, u32[]{:S(2)}) copy-start(f32[2,64]{1,0:T(2,128)S(1)} %fusion.150) | copy-start | bytes 1540
  381.0 30.2 %all-to-all-start.5 = ((bf16[2,4,64,2048]{3,2,0,1:T(8,128)(2,1)}), bf16[2,4,64,2048]{3,2,0,1:T(8,128)(2,1)}, u32[]{:S(2)}, u32[]{:S(2)}) async-start(bf16[2,4,64,2048]{3,2,0,1:T(8,128)(2,1)} %broadcast_in_dim.50), calls=%async_computation.5 | async-start | bytes 4194304 | tf_op jit(solution)/shard_map/all_to_all | solution.py:176
  385.5 341.7 %reduce-scatter.6.cloned.1.call-start = ((), (), s32[]{:S(2)}) async-start(), calls=%async_computation.25 | async-start | bytes 8847360 | tf_op jit(solution)/shard_map/reduce_scatter | solution.py:197
  486.9 30.2 %all-to-all-start.9 = ((bf16[2,4,64,2048]{3,2,0,1:T(8,128)(2,1)}), bf16[2,4,64,2048]{3,2,0,1:T(8,128)(2,1)}, u32[]{:S(2)}, u32[]{:S(2)}) async-start(bf16[2,4,64,2048]{3,2,0,1:T(8,128)(2,1)} %copy.507), calls=%async_computation.9 | async-start | bytes 4194304 | tf_op jit(solution)/shard_map/all_to_all | solution.py:188
  517.1 30.3 %all-to-all-start.10 = ((bf16[2,4,64,2048]{3,2,0,1:T(8,128)(2,1)}), bf16[2,4,64,2048]{3,2,0,1:T(8,128)(2,1)}, u32[]{:S(2)}, u32[]{:S(2)}) async-start(bf16[2,4,64,2048]{3,2,0,1:T(8,128)(2,1)} %copy.508), calls=%async_computation.10 | async-start | bytes 4194304 | tf_op jit(solution)/shard_map/all_to_all | solution.py:188
  553.1 30.2 %all-to-all-start.11 = ((bf16[2,4,64,2048]{3,2,0,1:T(8,128)(2,1)}), bf16[2,4,64,2048]{3,2,0,1:T(8,128)(2,1)}, u32[]{:S(2)}, u32[]{:S(2)}) async-start(bf16[2,4,64,2048]{3,2,0,1:T(8,128)(2,1)} %broadcast_in_dim.53), calls=%async_computation.11 | async-start | bytes 4194304 | tf_op jit(solution)/shard_map/all_to_all | solution.py:176
  557.5 224.2 %reduce-scatter.4.cloned.1.call-start = ((), (), s32[]{:S(2)}) async-start(), calls=%async_computation.24 | async-start | bytes 10616832 | tf_op jit(solution)/shard_map/reduce_scatter | solution.py:197
  588.6 18.9 %all-to-all-start.12 = ((f32[512,4,2,1,64]{0,4,2,3,1:T(8,128)}), f32[512,4,2,1,64]{0,4,2,3,1:T(8,128)}, u32[]{:S(2)}, u32[]{:S(2)}) async-start(f32[512,4,2,1,64]{0,4,2,3,1:T(8,128)} %convolution_bitcast_fusion.1), calls=%async_computation.12 | async-start | bytes 2097152 | tf_op jit(solution)/shard_map/all_to_all | solution.py:205
  593.0 376.5 %reduce-scatter.8.cloned.1.call-start = ((), (), s32[]{:S(2)}) async-start(), calls=%async_computation.26 | async-start | bytes 11796480 | tf_op jit(solution)/shard_map/reduce_scatter | solution.py:197
  794.1 30.2 %all-to-all-start.13 = ((bf16[2,4,64,2048]{3,2,0,1:T(8,128)(2,1)}), bf16[2,4,64,2048]{3,2,0,1:T(8,128)(2,1)}, u32[]{:S(2)}, u32[]{:S(2)}) async-start(bf16[2,4,64,2048]{3,2,0,1:T(8,128)(2,1)} %copy.545), calls=%async_computation.13 | async-start | bytes 4194304 | tf_op jit(solution)/shard_map/all_to_all | solution.py:188
  831.7 20.2 %all-to-all-start.15 = ((f32[32,1,2048]{2,1,0:T(1,128)}), f32[32,1,2048]{2,1,0:T(1,128)S(1)}, u32[]{:S(2)}, u32[]{:S(2)}) async-start(f32[32,1,2048]{2,1,0:T(1,128)} %copy.554), calls=%async_computation.18 | async-start | bytes 524288 | tf_op jit(solution)/shard_map/all_to_all | solution.py:205
  857.0 5.8 all-to-all-start.16
  862.8 5.6 all-to-all-start.17
  971.8 18.8 %all-to-all-start.14 = ((bf16[4,4,64,1,512]{4,2,0,3,1:T(8,128)(2,1)}), bf16[4,4,64,1,512]{4,2,0,3,1:T(8,128)(2,1)}, u32[]{:S(2)}, u32[]{:S(2)}) async-start(bf16[4,4,64,1,512]{4,2,0,3,1:T(8,128)(2,1)} %copy.546), calls=%async_computation.17 | async-start | bytes 2097152 | tf_op jit(solution)/shard_map/all_to_all | solution.py:205
  (154 other events, 1495.5 us)
Sparse Core Ops, SparseCore 0:
  38.0 159.8 all-gather.3
  200.7 136.2 all-gather.5
  339.2 116.5 all-gather.7
  477.5 138.1 reduce-scatter.5
  619.2 162.5 reduce-scatter.3
  785.2 184.2 reduce-scatter.7

commit v11 on v10

--- a/solution.py
+++ b/solution.py
@@ -257,6 +257,13 @@
         head_scale = head_gain.astype(jnp.float32)
         reset_len = slot if group_start.shape[1] == 1 else 0
 
+        out_rows = fsdp_gather(out_weight, 0)
+        column_owned = jnp.stack([query_weight, key_weight, value_weight, gate_weight])
+        column_swapped = exchange(
+            column_owned.reshape(4, rows, tp, cols_here), TP_AXES, 2, 1
+        ).reshape(4, group_rows, cols_here)
+        column_all = fsdp_gather(column_swapped, 1)
+        query_cols, key_cols, value_cols, gate_cols = (column_all[index] for index in range(4))
         small_pack = jnp.concatenate(
             [
                 conv_weight.reshape(-1),
@@ -266,42 +273,8 @@
             ]
         )
         small_size = small_pack.shape[0]
-        small_lines = -(-small_size // (4 * cols_here))
-        small_copy = jnp.pad(small_pack, (0, 4 * small_lines * cols_here - small_size))
-        small_copy = jnp.broadcast_to(
-            small_copy.reshape(4, small_lines, 1, cols_here), (4, small_lines, tp, cols_here)
-        )
-        column_owned = jnp.stack([query_weight, key_weight, value_weight, gate_weight])
-        swap_in = jnp.concatenate(
-            [column_owned.reshape(4, rows, tp, cols_here), small_copy], axis=1
-        )
-        swap_out = exchange(swap_in, TP_AXES, 2, 1).reshape(4, tp, rows + small_lines, cols_here)
-        column_swapped = swap_out[:, :, :rows].reshape(4, group_rows, cols_here)
-        small_group = (
-            swap_out[:, :, rows:]
-            .transpose(1, 0, 2, 3)
-            .reshape(tp, -1)[:, :small_size]
-        )
-        small_rows_in = padded_rows(small_group.reshape(-1), 5, cols_here)
-        extra_in = small_rows_in.shape[1]
-        mixer_stack = jnp.concatenate(
-            [
-                jnp.concatenate(
-                    [column_swapped, out_weight.reshape(1, group_rows, cols_here)], axis=0
-                ),
-                small_rows_in,
-            ],
-            axis=1,
-        )
-        mixer_all = fsdp_gather(mixer_stack, 1).reshape(5, fsdp, group_rows + extra_in, cols_here)
-        weight_all = mixer_all[:, :, :group_rows].reshape(5, width, cols_here)
-        query_cols, key_cols, value_cols, gate_cols = (weight_all[index] for index in range(4))
-        out_rows = weight_all[4].reshape(fsdp * rows, width)
-        small_all = (
-            mixer_all[:, :, group_rows:]
-            .transpose(1, 0, 2, 3)
-            .reshape(fsdp, -1)[:, : tp * small_size]
-            .reshape(n_all, small_size)
+        small_all = exchange(
+            jnp.broadcast_to(small_pack[None, :], (n_all, small_size)), ALL_AXES, 0, 0
         )
         conv_size = conv_weight.size
         beta_size = beta_weight.size

time: 1010 us -> 1020 us (level)
  blocking collectives: 9.34 us -> 41.7 us
  local copies, waits for them, and re-layouts: 159 us -> 137 us
    all_to_all x2 -> x3, blocking collectives: 9.34 us -> 35.6 us  [exchange(): return lax.all_to_all(value, axes, split_axis, concat_axis, tiled=True)]
    all_to_all x7, waiting for transfers between devices: 49.2 us -> 36.7 us  [exchange(): return lax.all_to_all(value, axes, split_axis, concat_axis, tiled=True)]
    all_gather x3 -> x4, waiting for transfers between devices: 165 us -> 177 us  [fsdp_gather(): return lax.all_gather(value, FSDP_AXES, axis=axis, tiled=True)]
    all_to_all x5 -> x4, starting transfers between devices: 22.1 us -> 17.4 us  [tp_gather(): moved = lax.all_to_all(spread, TP_AXES, axis, axis, tiled=True)]
    unnamed x323 -> x321, local copies, waits for them, and re-layouts: 26 us -> 21.8 us
    all_to_all x5 -> x4, waiting for transfers between devices: 74.4 us -> 70.6 us  [tp_gather(): moved = lax.all_to_all(spread, TP_AXES, axis, axis, tiled=True)]
  transfers between devices with their start and end apart: 22 -> 22, of which waited for: 19 -> 19; matrix products, arithmetic and copies ran while one was open for 34% -> 32% of each run, Pallas kernels for 0% -> 0%
where the time goes in v11:
time: 1020 us
  waiting for transfers between devices  517 us (51%)
  matrix products  180 us (18%)
  local copies, waits for them, and re-layouts  137 us (13%)
  starting transfers between devices  62.7 us (6%)
  other arithmetic  59.9 us (6%)
  blocking collectives  41.7 us (4%)
  between operations  17.2 us (2%)
    all_gather x4, waiting for transfers between devices, fsdp_gather(): return lax.all_gather(value, FSDP_AXES, axis=axis, tiled=True)  177 us
    reduce_scatter x3, waiting for transfers between devices, fsdp_scatter_low(): lax.psum_scatter(value.astype(jnp.bfloat16), FSDP_AXES, scatter_dimension...  161 us
    dot_general x42, matrix products, outer_product_result(): return jnp.einsum(form, first, second, precision=lax.Precision.HIGHEST)  77.7 us
    all_to_all x4, waiting for transfers between devices, tp_gather(): moved = lax.all_to_all(spread, TP_AXES, axis, axis, tiled=True)  70.6 us
    all_to_all x4, waiting for transfers between devices, tp_scatter_low(): moved = lax.all_to_all(staged, TP_AXES, axis, axis, tiled=True)  70 us
    dot_general x12, matrix products, matmul_rows(): return jnp.dot(left, right, preferred_element_type=jnp.float32)  40 us
    all_to_all x7, waiting for transfers between devices, exchange(): return lax.all_to_all(value, axes, split_axis, concat_axis, tiled=True)  36.7 us
    dot_general x12, matrix products, back_product(): jnp.einsum('tg,fg->tf', gradient, weight, preferred_element_type=jnp.floa...  35.6 us
  transfers between devices with their start and end apart: 22, of which 19 were waited for; matrix products, arithmetic and copies ran while one was open for 32% of the time, Pallas kernels for 0%

profile of v11, /device:TPU:0, one launch (start us, length us, event | category | flops | bytes accessed | tf_op | source)
XLA Modules:
  0.0 1015.3 jit_solution(7528081344081572573)
XLA Ops:
  13.0 18.5 %all_to_all.177 = bf16[4,64,4,512]{3,1,0,2:T(8,128)(2,1)S(1)} all-to-all(bf16[4,64,4,512]{3,1,0,2:T(8,128)(2,1)S(1)} %copy.376), channel_id=1, replica_groups=mesh['dq'=8,'core'=2,'mlp'=2] {'core','mlp'}, dimensions={2} | all-to-all | bytes 2097152 | tf_op jit(solution)/shard_map/all_to_all | solution.py:205
  34.5 5.5 all_to_all.178
  45.8 4.9 all-to-all-start
  52.1 9.8 all-to-all-done
  68.0 6.1 all_to_all.179
  83.4 22.4 %all-to-all-done.1 = bf16[2,4,64,2048]{3,2,0,1:T(8,128)(2,1)} async-done(((bf16[2,4,64,2048]{3,2,0,1:T(8,128)(2,1)}), bf16[2,4,64,2048]{3,2,0,1:T(8,128)(2,1)}, u32[]{:S(2)}, u32[]{:S(2)}) %all-to-all-start.1) | async-done | bytes 2097184 | tf_op jit(solution)/shard_map/all_to_all | solution.py:176
  108.5 52.2 %all-gather.5.cloned.1.call-done = bf16[4,2048,512]{2,1,0:T(8,128)(2,1)} async-done(((bf16[4,256,512]{2,1,0:T(8,128)(2,1)}), bf16[4,2048,512]{2,1,0:T(8,128)(2,1)}) %all-gather.5.cloned.1.call-update) | async-done | bytes 8388624 | tf_op jit(solution)/shard_map/all_gather | solution.py:193
  228.6 11.6 %all_to_all.180 = bf16[512,1,2,4,64]{0,4,2,1,3:T(8,128)(2,1)S(1)} all-to-all(bf16[512,1,2,4,64]{0,4,2,1,3:T(8,128)(2,1)S(1)} %copy.397), channel_id=1, replica_groups=mesh['dq'=8,'core'=2,'mlp'=2] {'core','mlp'}, dimensions={3} | all-to-all | bytes 1048576 | tf_op jit(solution)/shard_map/all_to_all | solution.py:205
  250.5 23.6 %all-to-all-done.5 = bf16[2,4,64,2048]{3,2,0,1:T(8,128)(2,1)S(1)} async-done(((bf16[2,4,64,2048]{3,2,0,1:T(8,128)(2,1)}), bf16[2,4,64,2048]{3,2,0,1:T(8,128)(2,1)S(1)}, u32[]{:S(2)}, u32[]{:S(2)}) %all-to-all-start.5) | async-done | bytes 2097184 | tf_op jit(solution)/shard_map/all_to_all | solution.py:188
  277.1 4.8 all-to-all-start.8
  284.7 23.1 %all-to-all-done.8 = bf16[2,4,64,2048]{3,2,0,1:T(8,128)(2,1)} async-done(((bf16[2,4,64,2048]{3,2,0,1:T(8,128)(2,1)}), bf16[2,4,64,2048]{3,2,0,1:T(8,128)(2,1)}, u32[]{:S(2)}, u32[]{:S(2)}) %all-to-all-start.8) | async-done | bytes 2097184 | tf_op jit(solution)/shard_map/all_to_all | solution.py:176
  317.0 32.7 %all-gather.9.cloned.1.call-done = bf16[3,2048,768]{2,1,0:T(8,128)(2,1)} async-done(((bf16[3,256,768]{2,1,0:T(8,128)(2,1)}), bf16[3,2048,768]{2,1,0:T(8,128)(2,1)}) %all-gather.9.cloned.1.call-update) | async-done | bytes 9437200 | tf_op jit(solution)/shard_map/all_gather | solution.py:193
  349.7 5.5 fusion.10
  356.9 4.7 fusion.9
  376.3 92.0 %all-gather.11.cloned.1.call-done = bf16[3,2048,640]{2,1,0:T(8,128)(2,1)} async-done(((bf16[3,256,640]{2,1,0:T(8,128)(2,1)}), bf16[3,2048,640]{2,1,0:T(8,128)(2,1)}) %all-gather.11.cloned.1.call-update) | async-done | bytes 7864336 | tf_op jit(solution)/shard_map/all_gather | solution.py:193
  520.8 8.9 all-to-all-done.10
  536.4 23.7 %all-to-all-done.11 = bf16[2,4,64,2048]{3,2,0,1:T(8,128)(2,1)} async-done(((bf16[2,4,64,2048]{3,2,0,1:T(8,128)(2,1)}), bf16[2,4,64,2048]{3,2,0,1:T(8,128)(2,1)}, u32[]{:S(2)}, u32[]{:S(2)}) %all-to-all-start.11) | async-done | bytes 2097184 | tf_op jit(solution)/shard_map/all_to_all | solution.py:188
  570.0 25.1 %all-to-all-done.12 = bf16[2,4,64,2048]{3,2,0,1:T(8,128)(2,1)S(1)} async-done(((bf16[2,4,64,2048]{3,2,0,1:T(8,128)(2,1)}), bf16[2,4,64,2048]{3,2,0,1:T(8,128)(2,1)S(1)}, u32[]{:S(2)}, u32[]{:S(2)}) %all-to-all-start.12) | async-done | bytes 2097184 | tf_op jit(solution)/shard_map/all_to_all | solution.py:176
  612.9 5.7 all-to-all-done.13
  729.0 65.4 %reduce-scatter.4.cloned.1.call-done = bf16[3,256,768]{2,1,0:T(8,128)(2,1)} async-done(((bf16[3,2048,768]{2,1,0:T(8,128)(2,1)}), bf16[3,256,768]{2,1,0:T(8,128)(2,1)}) %reduce-scatter.4.cloned.1.call-update) | async-done | bytes 1179664 | tf_op jit(solution)/shard_map/reduce_scatter | solution.py:197
  814.8 7.7 dynamic_update_slice.7
  824.3 13.8 %all-to-all-done.14 = bf16[2,4,64,2048]{3,2,0,1:T(8,128)(2,1)} async-done(((bf16[2,4,64,2048]{3,2,0,1:T(8,128)(2,1)}), bf16[2,4,64,2048]{3,2,0,1:T(8,128)(2,1)}, u32[]{:S(2)}, u32[]{:S(2)}) %all-to-all-start.14) | async-done | bytes 2097184 | tf_op jit(solution)/shard_map/all_to_all | solution.py:188
  851.9 12.7 %all-to-all-done.16 = f32[32,1,2048]{2,1,0:T(1,128)S(1)} async-done(((f32[32,1,2048]{2,1,0:T(1,128)}), f32[32,1,2048]{2,1,0:T(1,128)S(1)}, u32[]{:S(2)}, u32[]{:S(2)}) %all-to-all-start.16) | async-done | bytes 262176 | tf_op jit(solution)/shard_map/all_to_all | solution.py:205
  886.2 96.1 %reduce-scatter.8.cloned.1.call-done = bf16[5,256,512]{2,1,0:T(8,128)(2,1)} async-done(((bf16[5,2048,512]{2,1,0:T(8,128)(2,1)}), bf16[5,256,512]{2,1,0:T(8,128)(2,1)}) %reduce-scatter.8.cloned.1.call-update) | async-done | bytes 1310736 | tf_op jit(solution)/shard_map/reduce_scatter | solution.py:197
  (611 shorter events, 421.6 us)
Async XLA Ops:
  7.2 153.5 %all-gather.5.cloned.1.call-start = ((), (), s32[]{:S(2)}) async-start(), calls=%async_computation.22 | async-start | bytes 9437184 | tf_op jit(solution)/shard_map/all_gather | solution.py:193
  32.5 207.8 %all-gather.7.cloned.1.call-start = ((), (), s32[]{:S(2)}) async-start(), calls=%async_computation.23 | async-start | bytes 2359296 | tf_op jit(solution)/shard_map/all_gather | solution.py:193
  33.3 316.4 %all-gather.9.cloned.1.call-start = ((), (), s32[]{:S(2)}) async-start(), calls=%async_computation.24 | async-start | bytes 10616832 | tf_op jit(solution)/shard_map/all_gather | solution.py:193
  45.8 16.0 %all-to-all-start = ((bf16[32,2,960]{2,1,0:T(2,128)(2,1)}), bf16[32,2,960]{2,1,0:T(2,128)(2,1)S(1)}, u32[]{:S(2)}, u32[]{:S(2)}) async-start(bf16[32,2,960]{2,1,0:T(2,128)(2,1)} %reshape.737), calls=%async_computation | async-start | bytes 262144 | tf_op jit(solution)/shard_map/all_to_all | solution.py:205
  61.9 6.1 all-to-all-start.9
  75.6 30.2 %all-to-all-start.1 = ((bf16[2,4,64,2048]{3,2,0,1:T(8,128)(2,1)}), bf16[2,4,64,2048]{3,2,0,1:T(8,128)(2,1)}, u32[]{:S(2)}, u32[]{:S(2)}) async-start(bf16[2,4,64,2048]{3,2,0,1:T(8,128)(2,1)} %broadcast_in_dim.43), calls=%async_computation.1 | async-start | bytes 4194304 | tf_op jit(solution)/shard_map/all_to_all | solution.py:176
  80.1 388.3 %all-gather.11.cloned.1.call-start = ((), (), s32[]{:S(2)}) async-start(), calls=%async_computation.25 | async-start | bytes 8847360 | tf_op jit(solution)/shard_map/all_gather | solution.py:193
  244.8 29.4 %all-to-all-start.5 = ((bf16[2,4,64,2048]{3,2,0,1:T(8,128)(2,1)}), bf16[2,4,64,2048]{3,2,0,1:T(8,128)(2,1)S(1)}, u32[]{:S(2)}, u32[]{:S(2)}) async-start(bf16[2,4,64,2048]{3,2,0,1:T(8,128)(2,1)} %copy.399), calls=%async_computation.5 | async-start | bytes 4194304 | tf_op jit(solution)/shard_map/all_to_all | solution.py:188
  248.5 315.0 %copy-start.130 = (f32[2,64]{1,0:T(2,128)}, f32[2,64]{1,0:T(2,128)S(1)}, u32[]{:S(2)}) copy-start(f32[2,64]{1,0:T(2,128)S(1)} %convert_element_type.252) | copy-start | bytes 1540
  277.1 30.6 %all-to-all-start.8 = ((bf16[2,4,64,2048]{3,2,0,1:T(8,128)(2,1)}), bf16[2,4,64,2048]{3,2,0,1:T(8,128)(2,1)}, u32[]{:S(2)}, u32[]{:S(2)}) async-start(bf16[2,4,64,2048]{3,2,0,1:T(8,128)(2,1)} %broadcast_in_dim.48), calls=%async_computation.8 | async-start | bytes 4194304 | tf_op jit(solution)/shard_map/all_to_all | solution.py:176
  284.5 279.1 %copy-start.105 = (f32[2,64]{1,0:T(2,128)}, f32[2,64]{1,0:T(2,128)S(1)}, u32[]{:S(2)}) copy-start(f32[2,64]{1,0:T(2,128)S(1)} %fusion.160) | copy-start | bytes 1540
  309.3 45.9 %all-to-all-start.6 = ((bf16[2,4,64,2048]{3,2,0,1:T(8,128)(2,1)}), bf16[2,4,64,2048]{3,2,0,1:T(8,128)(2,1)}, u32[]{:S(2)}, u32[]{:S(2)}) async-start(bf16[2,4,64,2048]{3,2,0,1:T(8,128)(2,1)} %broadcast_in_dim.47), calls=%async_computation.6 | async-start | bytes 4194304 | tf_op jit(solution)/shard_map/all_to_all | solution.py:176
  313.8 415.1 %reduce-scatter.6.cloned.1.call-start = ((), (), s32[]{:S(2)}) async-start(), calls=%async_computation.27 | async-start | bytes 8847360 | tf_op jit(solution)/shard_map/reduce_scatter | solution.py:197
  499.6 30.2 %all-to-all-start.10 = ((bf16[2,4,64,2048]{3,2,0,1:T(8,128)(2,1)}), bf16[2,4,64,2048]{3,2,0,1:T(8,128)(2,1)}, u32[]{:S(2)}, u32[]{:S(2)}) async-start(bf16[2,4,64,2048]{3,2,0,1:T(8,128)(2,1)} %copy.408), calls=%async_computation.10 | async-start | bytes 4194304 | tf_op jit(solution)/shard_map/all_to_all | solution.py:188
  529.8 30.3 %all-to-all-start.11 = ((bf16[2,4,64,2048]{3,2,0,1:T(8,128)(2,1)}), bf16[2,4,64,2048]{3,2,0,1:T(8,128)(2,1)}, u32[]{:S(2)}, u32[]{:S(2)}) async-start(bf16[2,4,64,2048]{3,2,0,1:T(8,128)(2,1)} %copy.409), calls=%async_computation.11 | async-start | bytes 4194304 | tf_op jit(solution)/shard_map/all_to_all | solution.py:188
  565.8 29.3 %all-to-all-start.12 = ((bf16[2,4,64,2048]{3,2,0,1:T(8,128)(2,1)}), bf16[2,4,64,2048]{3,2,0,1:T(8,128)(2,1)S(1)}, u32[]{:S(2)}, u32[]{:S(2)}) async-start(bf16[2,4,64,2048]{3,2,0,1:T(8,128)(2,1)} %broadcast_in_dim.50), calls=%async_computation.12 | async-start | bytes 4194304 | tf_op jit(solution)/shard_map/all_to_all | solution.py:176
  569.4 225.0 %reduce-scatter.4.cloned.1.call-start = ((), (), s32[]{:S(2)}) async-start(), calls=%async_computation.26 | async-start | bytes 10616832 | tf_op jit(solution)/shard_map/reduce_scatter | solution.py:197
  599.6 18.9 %all-to-all-start.13 = ((f32[512,4,2,1,64]{0,4,2,3,1:T(8,128)}), f32[512,4,2,1,64]{0,4,2,3,1:T(8,128)}, u32[]{:S(2)}, u32[]{:S(2)}) async-start(f32[512,4,2,1,64]{0,4,2,3,1:T(8,128)} %convolution_bitcast_fusion.1), calls=%async_computation.13 | async-start | bytes 2097152 | tf_op jit(solution)/shard_map/all_to_all | solution.py:205
  604.1 378.2 %reduce-scatter.8.cloned.1.call-start = ((), (), s32[]{:S(2)}) async-start(), calls=%async_computation.28 | async-start | bytes 11796480 | tf_op jit(solution)/shard_map/reduce_scatter | solution.py:197
  807.8 30.2 %all-to-all-start.14 = ((bf16[2,4,64,2048]{3,2,0,1:T(8,128)(2,1)}), bf16[2,4,64,2048]{3,2,0,1:T(8,128)(2,1)}, u32[]{:S(2)}, u32[]{:S(2)}) async-start(bf16[2,4,64,2048]{3,2,0,1:T(8,128)(2,1)} %copy.446), calls=%async_computation.14 | async-start | bytes 4194304 | tf_op jit(solution)/shard_map/all_to_all | solution.py:188
  845.4 19.3 %all-to-all-start.16 = ((f32[32,1,2048]{2,1,0:T(1,128)}), f32[32,1,2048]{2,1,0:T(1,128)S(1)}, u32[]{:S(2)}, u32[]{:S(2)}) async-start(f32[32,1,2048]{2,1,0:T(1,128)} %copy.455), calls=%async_computation.19 | async-start | bytes 524288 | tf_op jit(solution)/shard_map/all_to_all | solution.py:205
  869.8 5.8 all-to-all-start.17
  875.6 6.6 all-to-all-start.18
  984.6 17.9 %all-to-all-start.15 = ((bf16[4,4,64,1,512]{4,2,0,3,1:T(8,128)(2,1)}), bf16[4,4,64,1,512]{4,2,0,3,1:T(8,128)(2,1)S(1)}, u32[]{:S(2)}, u32[]{:S(2)}) async-start(bf16[4,4,64,1,512]{4,2,0,3,1:T(8,128)(2,1)} %copy.447), calls=%async_computation.18 | async-start | bytes 2097152 | tf_op jit(solution)/shard_map/all_to_all | solution.py:205
  (153 other events, 2449.6 us)
Sparse Core Ops, SparseCore 0:
  32.7 127.9 all-gather.4
  162.8 47.4 all-gather.6
  213.1 136.5 all-gather.8
  351.7 116.5 all-gather.10
  490.1 138.1 reduce-scatter.5
  631.8 162.5 reduce-scatter.3
  797.9 184.2 reduce-scatter.7

commit v12 on v11

--- a/solution.py
+++ b/solution.py
@@ -257,13 +257,16 @@
         head_scale = head_gain.astype(jnp.float32)
         reset_len = slot if group_start.shape[1] == 1 else 0
 
-        out_rows = fsdp_gather(out_weight, 0)
         column_owned = jnp.stack([query_weight, key_weight, value_weight, gate_weight])
         column_swapped = exchange(
             column_owned.reshape(4, rows, tp, cols_here), TP_AXES, 2, 1
         ).reshape(4, group_rows, cols_here)
-        column_all = fsdp_gather(column_swapped, 1)
-        query_cols, key_cols, value_cols, gate_cols = (column_all[index] for index in range(4))
+        mixer_stack = jnp.concatenate(
+            [column_swapped, out_weight.reshape(1, group_rows, cols_here)], axis=0
+        )
+        weight_all = fsdp_gather(mixer_stack, 1)
+        query_cols, key_cols, value_cols, gate_cols = (weight_all[index] for index in range(4))
+        out_rows = weight_all[4].reshape(fsdp * rows, width)
         small_pack = jnp.concatenate(
             [
                 conv_weight.reshape(-1),

time: 1020 us -> 1000 us (0.980)
  waiting for transfers between devices: 517 us -> 478 us
  blocking collectives: 41.7 us -> 10.8 us
  local copies, waits for them, and re-layouts: 137 us -> 160 us
  matrix products: 180 us -> 193 us
    all_gather x4 -> x3, waiting for transfers between devices: 177 us -> 122 us  [fsdp_gather(): return lax.all_gather(value, FSDP_AXES, axis=axis, tiled=True)]
    all_to_all x3 -> x1, blocking collectives: 35.6 us -> 4.68 us  [exchange(): return lax.all_to_all(value, axes, split_axis, concat_axis, tiled=True)]
    all_to_all x7 -> x9, waiting for transfers between devices: 36.7 us -> 55.1 us  [exchange(): return lax.all_to_all(value, axes, split_axis, concat_axis, tiled=True)]
    reduce_scatter x3, waiting for transfers between devices: 161 us -> 148 us  [fsdp_scatter_low(): lax.psum_scatter(value.astype(jnp.bfloat16), FSDP_AXES, scatter_dimension...]
    all_to_all x4, waiting for transfers between devices: 70.6 us -> 83.2 us  [tp_gather(): moved = lax.all_to_all(spread, TP_AXES, axis, axis, tiled=True)]
    all_to_all x7 -> x9, starting transfers between devices: 27.4 us -> 36.8 us  [exchange(): return lax.all_to_all(value, axes, split_axis, concat_axis, tiled=True)]
    unnamed x321 -> x309, local copies, waits for them, and re-layouts: 21.8 us -> 25.1 us
  transfers between devices with their start and end apart: 22 -> 23, of which waited for: 19 -> 21; matrix products, arithmetic and copies ran while one was open for 32% -> 37% of each run, Pallas kernels for 0% -> 0%
where the time goes in v12:
time: 1000 us; the launch traced here: 995 us
  waiting for transfers between devices  478 us (48%)
  matrix products  193 us (19%)
  local copies, waits for them, and re-layouts  160 us (16%)
  starting transfers between devices  72.6 us (7%)
  other arithmetic  65.2 us (7%)
  between operations  17 us (2%)
  blocking collectives  10.8 us (1%)
    reduce_scatter x3, waiting for transfers between devices, fsdp_scatter_low(): lax.psum_scatter(value.astype(jnp.bfloat16), FSDP_AXES, scatter_dimension...  148 us
    all_gather x3, waiting for transfers between devices, fsdp_gather(): return lax.all_gather(value, FSDP_AXES, axis=axis, tiled=True)  122 us
    all_to_all x4, waiting for transfers between devices, tp_gather(): moved = lax.all_to_all(spread, TP_AXES, axis, axis, tiled=True)  83.2 us
    dot_general x42, matrix products, outer_product_result(): return jnp.einsum(form, first, second, precision=lax.Precision.HIGHEST)  81.8 us
    all_to_all x4, waiting for transfers between devices, tp_scatter_low(): moved = lax.all_to_all(staged, TP_AXES, axis, axis, tiled=True)  69 us
    all_to_all x9, waiting for transfers between devices, exchange(): return lax.all_to_all(value, axes, split_axis, concat_axis, tiled=True)  55.1 us
    dot_general x12, matrix products, matmul_rows(): return jnp.dot(left, right, preferred_element_type=jnp.float32)  43.5 us
    dot_general x12, matrix products, back_product(): jnp.einsum('tg,fg->tf', gradient, weight, preferred_element_type=jnp.floa...  38.8 us
  transfers between devices with their start and end apart: 23, of which 21 were waited for; matrix products, arithmetic and copies ran while one was open for 37% of the time, Pallas kernels for 0%

profile of v12, /device:TPU:0, one launch (start us, length us, event | category | flops | bytes accessed | tf_op | source)
XLA Modules:
  0.0 995.3 jit_solution(14704298235586604302)
XLA Ops:
  18.3 14.3 %all-to-all-done.2 = bf16[4,64,4,512]{3,1,0,2:T(8,128)(2,1)S(1)} async-done(((bf16[4,64,4,512]{3,1,0,2:T(8,128)(2,1)}), bf16[4,64,4,512]{3,1,0,2:T(8,128)(2,1)S(1)}, u32[]{:S(2)}, u32[]{:S(2)}) %all-to-all-start.2) | async-done | bytes 1048608 | tf_op jit(solution)/shard_map/all_to_all | solution.py:205
  36.2 4.7 all_to_all.177
  45.6 5.6 all-to-all-start
  52.5 9.7 all-to-all-done
  67.9 6.1 all_to_all.178
  83.2 22.6 %all-to-all-done.1 = bf16[2,4,64,2048]{3,2,0,1:T(8,128)(2,1)} async-done(((bf16[2,4,64,2048]{3,2,0,1:T(8,128)(2,1)}), bf16[2,4,64,2048]{3,2,0,1:T(8,128)(2,1)}, u32[]{:S(2)}, u32[]{:S(2)}) %all-to-all-start.1) | async-done | bytes 2097184 | tf_op jit(solution)/shard_map/all_to_all | solution.py:176
  108.5 80.0 %all-gather.4.cloned.1.call-done = bf16[5,2048,512]{2,1,0:T(8,128)(2,1)} async-done(((bf16[5,256,512]{2,1,0:T(8,128)(2,1)}), bf16[5,2048,512]{2,1,0:T(8,128)(2,1)}) %all-gather.4.cloned.1.call-update) | async-done | bytes 10485776 | tf_op jit(solution)/shard_map/all_gather | solution.py:193
  277.5 6.3 all-to-all-done.4
  295.1 23.6 %all-to-all-done.5 = bf16[2,4,64,2048]{3,2,0,1:T(8,128)(2,1)S(1)} async-done(((bf16[2,4,64,2048]{3,2,0,1:T(8,128)(2,1)}), bf16[2,4,64,2048]{3,2,0,1:T(8,128)(2,1)S(1)}, u32[]{:S(2)}, u32[]{:S(2)}) %all-to-all-start.5) | async-done | bytes 2097184 | tf_op jit(solution)/shard_map/all_to_all | solution.py:188
  328.8 23.1 %all-to-all-done.8 = bf16[2,4,64,2048]{3,2,0,1:T(8,128)(2,1)} async-done(((bf16[2,4,64,2048]{3,2,0,1:T(8,128)(2,1)}), bf16[2,4,64,2048]{3,2,0,1:T(8,128)(2,1)}, u32[]{:S(2)}, u32[]{:S(2)}) %all-to-all-start.8) | async-done | bytes 2097184 | tf_op jit(solution)/shard_map/all_to_all | solution.py:176
  361.6 5.5 fusion.10
  367.1 16.7 %all-to-all-done.6 = bf16[2,4,64,2048]{3,2,0,1:T(8,128)(2,1)} async-done(((bf16[2,4,64,2048]{3,2,0,1:T(8,128)(2,1)}), bf16[2,4,64,2048]{3,2,0,1:T(8,128)(2,1)}, u32[]{:S(2)}, u32[]{:S(2)}) %all-to-all-start.6) | async-done | bytes 2097184 | tf_op jit(solution)/shard_map/all_to_all | solution.py:176
  400.1 4.7 pad_maximum_fusion
  404.8 41.7 %all-gather.8.cloned.1.call-done = bf16[3,2048,640]{2,1,0:T(8,128)(2,1)} async-done(((bf16[3,256,640]{2,1,0:T(8,128)(2,1)}), bf16[3,2048,640]{2,1,0:T(8,128)(2,1)}) %all-gather.8.cloned.1.call-update) | async-done | bytes 7864336 | tf_op jit(solution)/shard_map/all_gather | solution.py:193
  498.8 8.9 all-to-all-done.10
  515.3 22.7 %all-to-all-done.11 = bf16[2,4,64,2048]{3,2,0,1:T(8,128)(2,1)} async-done(((bf16[2,4,64,2048]{3,2,0,1:T(8,128)(2,1)}), bf16[2,4,64,2048]{3,2,0,1:T(8,128)(2,1)}, u32[]{:S(2)}, u32[]{:S(2)}) %all-to-all-start.11) | async-done | bytes 2097184 | tf_op jit(solution)/shard_map/all_to_all | solution.py:188
  553.1 20.8 %all-to-all-done.12 = bf16[2,4,64,2048]{3,2,0,1:T(8,128)(2,1)} async-done(((bf16[2,4,64,2048]{3,2,0,1:T(8,128)(2,1)}), bf16[2,4,64,2048]{3,2,0,1:T(8,128)(2,1)}, u32[]{:S(2)}, u32[]{:S(2)}) %all-to-all-start.12) | async-done | bytes 2097184 | tf_op jit(solution)/shard_map/all_to_all | solution.py:176
  592.2 4.8 stack_reshape.3
  718.4 54.0 %reduce-scatter.4.cloned.1.call-done = bf16[3,256,768]{2,1,0:T(8,128)(2,1)} async-done(((bf16[3,2048,768]{2,1,0:T(8,128)(2,1)}), bf16[3,256,768]{2,1,0:T(8,128)(2,1)}) %reduce-scatter.4.cloned.1.call-update) | async-done | bytes 1179664 | tf_op jit(solution)/shard_map/reduce_scatter | solution.py:197
  796.3 7.7 dynamic_update_slice.7
  805.8 13.8 %all-to-all-done.14 = bf16[2,4,64,2048]{3,2,0,1:T(8,128)(2,1)} async-done(((bf16[2,4,64,2048]{3,2,0,1:T(8,128)(2,1)}), bf16[2,4,64,2048]{3,2,0,1:T(8,128)(2,1)}, u32[]{:S(2)}, u32[]{:S(2)}) %all-to-all-start.14) | async-done | bytes 2097184 | tf_op jit(solution)/shard_map/all_to_all | solution.py:188
  833.9 12.5 %all-to-all-done.16 = f32[32,1,2048]{2,1,0:T(1,128)S(1)} async-done(((f32[32,1,2048]{2,1,0:T(1,128)}), f32[32,1,2048]{2,1,0:T(1,128)S(1)}, u32[]{:S(2)}, u32[]{:S(2)}) %all-to-all-start.16) | async-done | bytes 262176 | tf_op jit(solution)/shard_map/all_to_all | solution.py:205
  866.2 94.0 %reduce-scatter.8.cloned.1.call-done = bf16[5,256,512]{2,1,0:T(8,128)(2,1)} async-done(((bf16[5,2048,512]{2,1,0:T(8,128)(2,1)}), bf16[5,256,512]{2,1,0:T(8,128)(2,1)}) %reduce-scatter.8.cloned.1.call-update) | async-done | bytes 1310736 | tf_op jit(solution)/shard_map/reduce_scatter | solution.py:197
  974.6 6.7 all-to-all-done.15
  (601 shorter events, 467.8 us)
Async XLA Ops:
  13.9 18.7 %all-to-all-start.2 = ((bf16[4,64,4,512]{3,1,0,2:T(8,128)(2,1)}), bf16[4,64,4,512]{3,1,0,2:T(8,128)(2,1)S(1)}, u32[]{:S(2)}, u32[]{:S(2)}) async-start(bf16[4,64,4,512]{3,1,0,2:T(8,128)(2,1)} %copy.379), calls=%async_computation.2 | async-start | bytes 2097152 | tf_op jit(solution)/shard_map/all_to_all | solution.py:205
  18.1 170.5 %all-gather.4.cloned.1.call-start = ((), (), s32[]{:S(2)}) async-start(), calls=%async_computation.22 | async-start | bytes 11796480 | tf_op jit(solution)/shard_map/all_gather | solution.py:193
  33.9 327.8 %all-gather.6.cloned.1.call-start = ((), (), s32[]{:S(2)}) async-start(), calls=%async_computation.23 | async-start | bytes 10616832 | tf_op jit(solution)/shard_map/all_gather | solution.py:193
  45.6 16.6 %all-to-all-start = ((bf16[32,2,960]{2,1,0:T(2,128)(2,1)}), bf16[32,2,960]{2,1,0:T(2,128)(2,1)S(1)}, u32[]{:S(2)}, u32[]{:S(2)}) async-start(bf16[32,2,960]{2,1,0:T(2,128)(2,1)} %reshape.743), calls=%async_computation | async-start | bytes 262144 | tf_op jit(solution)/shard_map/all_to_all | solution.py:205
  62.2 5.6 all-to-all-start.9
  75.6 30.2 %all-to-all-start.1 = ((bf16[2,4,64,2048]{3,2,0,1:T(8,128)(2,1)}), bf16[2,4,64,2048]{3,2,0,1:T(8,128)(2,1)}, u32[]{:S(2)}, u32[]{:S(2)}) async-start(bf16[2,4,64,2048]{3,2,0,1:T(8,128)(2,1)} %broadcast_in_dim.43), calls=%async_computation.1 | async-start | bytes 4194304 | tf_op jit(solution)/shard_map/all_to_all | solution.py:176
  80.1 366.4 %all-gather.8.cloned.1.call-start = ((), (), s32[]{:S(2)}) async-start(), calls=%async_computation.24 | async-start | bytes 8847360 | tf_op jit(solution)/shard_map/all_gather | solution.py:193
  270.7 13.1 %all-to-all-start.4 = ((bf16[512,1,2,4,64]{0,4,2,1,3:T(8,128)(2,1)}), bf16[512,1,2,4,64]{0,4,2,1,3:T(8,128)(2,1)}, u32[]{:S(2)}, u32[]{:S(2)}) async-start(bf16[512,1,2,4,64]{0,4,2,1,3:T(8,128)(2,1)} %copy.400), calls=%async_computation.4 | async-start | bytes 1048576 | tf_op jit(solution)/shard_map/all_to_all | solution.py:205
  289.3 29.4 %all-to-all-start.5 = ((bf16[2,4,64,2048]{3,2,0,1:T(8,128)(2,1)}), bf16[2,4,64,2048]{3,2,0,1:T(8,128)(2,1)S(1)}, u32[]{:S(2)}, u32[]{:S(2)}) async-start(bf16[2,4,64,2048]{3,2,0,1:T(8,128)(2,1)} %copy.402), calls=%async_computation.5 | async-start | bytes 4194304 | tf_op jit(solution)/shard_map/all_to_all | solution.py:188
  293.1 248.4 %copy-start.127 = (f32[2,64]{1,0:T(2,128)}, f32[2,64]{1,0:T(2,128)S(1)}, u32[]{:S(2)}) copy-start(f32[2,64]{1,0:T(2,128)S(1)} %convert_element_type.252) | copy-start | bytes 1540
  321.7 30.2 %all-to-all-start.8 = ((bf16[2,4,64,2048]{3,2,0,1:T(8,128)(2,1)}), bf16[2,4,64,2048]{3,2,0,1:T(8,128)(2,1)}, u32[]{:S(2)}, u32[]{:S(2)}) async-start(bf16[2,4,64,2048]{3,2,0,1:T(8,128)(2,1)} %broadcast_in_dim.48), calls=%async_computation.8 | async-start | bytes 4194304 | tf_op jit(solution)/shard_map/all_to_all | solution.py:176
  353.6 30.2 %all-to-all-start.6 = ((bf16[2,4,64,2048]{3,2,0,1:T(8,128)(2,1)}), bf16[2,4,64,2048]{3,2,0,1:T(8,128)(2,1)}, u32[]{:S(2)}, u32[]{:S(2)}) async-start(bf16[2,4,64,2048]{3,2,0,1:T(8,128)(2,1)} %broadcast_in_dim.47), calls=%async_computation.6 | async-start | bytes 4194304 | tf_op jit(solution)/shard_map/all_to_all | solution.py:176
  358.0 360.4 %reduce-scatter.6.cloned.1.call-start = ((), (), s32[]{:S(2)}) async-start(), calls=%async_computation.26 | async-start | bytes 8847360 | tf_op jit(solution)/shard_map/reduce_scatter | solution.py:197
  477.5 30.2 %all-to-all-start.10 = ((bf16[2,4,64,2048]{3,2,0,1:T(8,128)(2,1)}), bf16[2,4,64,2048]{3,2,0,1:T(8,128)(2,1)}, u32[]{:S(2)}, u32[]{:S(2)}) async-start(bf16[2,4,64,2048]{3,2,0,1:T(8,128)(2,1)} %copy.411), calls=%async_computation.10 | async-start | bytes 4194304 | tf_op jit(solution)/shard_map/all_to_all | solution.py:188
  507.7 30.3 %all-to-all-start.11 = ((bf16[2,4,64,2048]{3,2,0,1:T(8,128)(2,1)}), bf16[2,4,64,2048]{3,2,0,1:T(8,128)(2,1)}, u32[]{:S(2)}, u32[]{:S(2)}) async-start(bf16[2,4,64,2048]{3,2,0,1:T(8,128)(2,1)} %copy.412), calls=%async_computation.11 | async-start | bytes 4194304 | tf_op jit(solution)/shard_map/all_to_all | solution.py:188
  543.7 30.2 %all-to-all-start.12 = ((bf16[2,4,64,2048]{3,2,0,1:T(8,128)(2,1)}), bf16[2,4,64,2048]{3,2,0,1:T(8,128)(2,1)}, u32[]{:S(2)}, u32[]{:S(2)}) async-start(bf16[2,4,64,2048]{3,2,0,1:T(8,128)(2,1)} %broadcast_in_dim.50), calls=%async_computation.12 | async-start | bytes 4194304 | tf_op jit(solution)/shard_map/all_to_all | solution.py:176
  548.2 224.2 %reduce-scatter.4.cloned.1.call-start = ((), (), s32[]{:S(2)}) async-start(), calls=%async_computation.25 | async-start | bytes 10616832 | tf_op jit(solution)/shard_map/reduce_scatter | solution.py:197
  579.4 18.9 %all-to-all-start.13 = ((f32[512,4,2,1,64]{0,4,2,3,1:T(8,128)}), f32[512,4,2,1,64]{0,4,2,3,1:T(8,128)}, u32[]{:S(2)}, u32[]{:S(2)}) async-start(f32[512,4,2,1,64]{0,4,2,3,1:T(8,128)} %convolution_bitcast_fusion.1), calls=%async_computation.13 | async-start | bytes 2097152 | tf_op jit(solution)/shard_map/all_to_all | solution.py:205
  583.8 376.4 %reduce-scatter.8.cloned.1.call-start = ((), (), s32[]{:S(2)}) async-start(), calls=%async_computation.27 | async-start | bytes 11796480 | tf_op jit(solution)/shard_map/reduce_scatter | solution.py:197
  789.4 30.2 %all-to-all-start.14 = ((bf16[2,4,64,2048]{3,2,0,1:T(8,128)(2,1)}), bf16[2,4,64,2048]{3,2,0,1:T(8,128)(2,1)}, u32[]{:S(2)}, u32[]{:S(2)}) async-start(bf16[2,4,64,2048]{3,2,0,1:T(8,128)(2,1)} %copy.449), calls=%async_computation.14 | async-start | bytes 4194304 | tf_op jit(solution)/shard_map/all_to_all | solution.py:188
  826.9 19.5 %all-to-all-start.16 = ((f32[32,1,2048]{2,1,0:T(1,128)}), f32[32,1,2048]{2,1,0:T(1,128)S(1)}, u32[]{:S(2)}, u32[]{:S(2)}) async-start(f32[32,1,2048]{2,1,0:T(1,128)} %copy.458), calls=%async_computation.19 | async-start | bytes 524288 | tf_op jit(solution)/shard_map/all_to_all | solution.py:205
  851.6 6.0 all-to-all-start.17
  857.6 5.6 all-to-all-start.18
  962.5 18.8 %all-to-all-start.15 = ((bf16[4,4,64,1,512]{4,2,0,3,1:T(8,128)(2,1)}), bf16[4,4,64,1,512]{4,2,0,3,1:T(8,128)(2,1)}, u32[]{:S(2)}, u32[]{:S(2)}) async-start(bf16[4,4,64,1,512]{4,2,0,3,1:T(8,128)(2,1)} %copy.450), calls=%async_computation.18 | async-start | bytes 2097152 | tf_op jit(solution)/shard_map/all_to_all | solution.py:205
  (148 other events, 2879.2 us)
Sparse Core Ops, SparseCore 0:
  34.0 154.5 all-gather.3
  191.3 136.2 all-gather.5
  329.8 116.5 all-gather.7
  468.2 138.1 reduce-scatter.5
  609.8 162.5 reduce-scatter.3
  775.8 184.3 reduce-scatter.7

commit v13 on v12

--- a/solution.py
+++ b/solution.py
@@ -301,8 +301,13 @@
             3, owned_rows, inner, hidden_here
         )
         lanes = hidden_here // 128 if hidden_here % 128 == 0 else 0
-        first = (lanes + 1) // 2 * 128 if lanes > 1 else hidden_here // 2
-        bounds = ((0, first), (first, hidden_here - first))
+        if lanes >= 3:
+            sizes = [(lanes + 2) // 3 * 128, (lanes + 2) // 3 * 128]
+            sizes.append(hidden_here - sum(sizes))
+        else:
+            sizes = [hidden_here // 2, hidden_here - hidden_here // 2]
+        starts_at = [sum(sizes[:index]) for index in range(len(sizes))]
+        bounds = tuple(zip(starts_at, sizes))
         ff_chunks = []
         for offset, size in bounds:
             swapped = exchange(ff_owned[..., offset : offset + size], INNER_AXES, 2, 1)

time: 1000 us -> 1050 us (1.050)
  waiting for transfers between devices: 478 us -> 524 us
    reduce_scatter x3 -> x4, waiting for transfers between devices: 148 us -> 175 us  [fsdp_scatter_low(): lax.psum_scatter(value.astype(jnp.bfloat16), FSDP_AXES, scatter_dimension...]
    all_gather x3 -> x4, waiting for transfers between devices: 122 us -> 138 us  [fsdp_gather(): return lax.all_gather(value, FSDP_AXES, axis=axis, tiled=True)]
    all_to_all x9 -> x11, starting transfers between devices: 36.8 us -> 43.8 us  [exchange(): return lax.all_to_all(value, axes, split_axis, concat_axis, tiled=True)]
    unnamed x309 -> x395, local copies, waits for them, and re-layouts: 25.1 us -> 29.2 us
    dot_general x12 -> x15, matrix products: 43.5 us -> 40.5 us  [matmul_rows(): return jnp.dot(left, right, preferred_element_type=jnp.float32)]
    dot_general x12 -> x15, matrix products: 38.8 us -> 40.5 us  [back_product(): jnp.einsum('tg,fg->tf', gradient, weight, preferred_element_type=jnp.floa...]
    all_to_all x9 -> x11, waiting for transfers between devices: 55.1 us -> 55.5 us  [exchange(): return lax.all_to_all(value, axes, split_axis, concat_axis, tiled=True)]
    dot_general x12 -> x15, matrix products: 28.3 us -> 28.1 us  [left_product(): jnp.einsum('tf,tg->fg', first, second, preferred_element_type=jnp.float32)]
  transfers between devices with their start and end apart: 23 -> 27, of which waited for: 21 -> 22; matrix products, arithmetic and copies ran while one was open for 37% -> 35% of each run, Pallas kernels for 0% -> 0%
where the time goes in v13:
time: 1050 us; the launch traced here: 1040 us
  waiting for transfers between devices  524 us (50%)
  matrix products  186 us (18%)
  local copies, waits for them, and re-layouts  159 us (15%)
  starting transfers between devices  78.3 us (7%)
  other arithmetic  66.3 us (6%)
  between operations  17.5 us (2%)
  blocking collectives  10.8 us (1%)
    reduce_scatter x4, waiting for transfers between devices, fsdp_scatter_low(): lax.psum_scatter(value.astype(jnp.bfloat16), FSDP_AXES, scatter_dimension...  175 us
    all_gather x4, waiting for transfers between devices, fsdp_gather(): return lax.all_gather(value, FSDP_AXES, axis=axis, tiled=True)  138 us
    all_to_all x4, waiting for transfers between devices, tp_gather(): moved = lax.all_to_all(spread, TP_AXES, axis, axis, tiled=True)  86.6 us
    dot_general x42, matrix products, outer_product_result(): return jnp.einsum(form, first, second, precision=lax.Precision.HIGHEST)  77.2 us
    all_to_all x4, waiting for transfers between devices, tp_scatter_low(): moved = lax.all_to_all(staged, TP_AXES, axis, axis, tiled=True)  67.3 us
    all_to_all x11, waiting for transfers between devices, exchange(): return lax.all_to_all(value, axes, split_axis, concat_axis, tiled=True)  55.5 us
    all_to_all x11, starting transfers between devices, exchange(): return lax.all_to_all(value, axes, split_axis, concat_axis, tiled=True)  43.8 us
    dot_general x15, matrix products, back_product(): jnp.einsum('tg,fg->tf', gradient, weight, preferred_element_type=jnp.floa...  40.5 us
  transfers between devices with their start and end apart: 27, of which 22 were waited for; matrix products, arithmetic and copies ran while one was open for 35% of the time, Pallas kernels for 0%

profile of v13, /device:TPU:0, one launch (start us, length us, event | category | flops | bytes accessed | tf_op | source)
XLA Modules:
  0.0 1041.9 jit_solution(8603922078049094823)
XLA Ops:
  18.3 14.3 %all-to-all-done.2 = bf16[4,64,4,512]{3,1,0,2:T(8,128)(2,1)S(1)} async-done(((bf16[4,64,4,512]{3,1,0,2:T(8,128)(2,1)}), bf16[4,64,4,512]{3,1,0,2:T(8,128)(2,1)S(1)}, u32[]{:S(2)}, u32[]{:S(2)}) %all-to-all-start.2) | async-done | bytes 1048608 | tf_op jit(solution)/shard_map/all_to_all | solution.py:205
  46.1 5.6 all-to-all-start
  52.9 10.5 %all-to-all-done = bf16[32,2,960]{2,1,0:T(2,128)(2,1)S(1)} async-done(((bf16[32,2,960]{2,1,0:T(2,128)(2,1)}), bf16[32,2,960]{2,1,0:T(2,128)(2,1)S(1)}, u32[]{:S(2)}, u32[]{:S(2)}) %all-to-all-start) | async-done | bytes 122912 | tf_op jit(solution)/shard_map/all_to_all | solution.py:205
  68.8 6.3 all_to_all.208
  84.6 22.4 %all-to-all-done.1 = bf16[2,4,64,2048]{3,2,0,1:T(8,128)(2,1)} async-done(((bf16[2,4,64,2048]{3,2,0,1:T(8,128)(2,1)}), bf16[2,4,64,2048]{3,2,0,1:T(8,128)(2,1)}, u32[]{:S(2)}, u32[]{:S(2)}) %all-to-all-start.1) | async-done | bytes 2097184 | tf_op jit(solution)/shard_map/all_to_all | solution.py:176
  109.7 78.9 %all-gather.5.cloned.1.call-done = bf16[5,2048,512]{2,1,0:T(8,128)(2,1)} async-done(((bf16[5,256,512]{2,1,0:T(8,128)(2,1)}), bf16[5,2048,512]{2,1,0:T(8,128)(2,1)}) %all-gather.5.cloned.1.call-update) | async-done | bytes 10485776 | tf_op jit(solution)/shard_map/all_gather | solution.py:193
  250.1 5.0 slice_bitcast_fusion.18
  289.4 24.7 %all-to-all-done.5 = bf16[2,4,64,2048]{3,2,0,1:T(8,128)(2,1)S(1)} async-done(((bf16[2,4,64,2048]{3,2,0,1:T(8,128)(2,1)}), bf16[2,4,64,2048]{3,2,0,1:T(8,128)(2,1)S(1)}, u32[]{:S(2)}, u32[]{:S(2)}) %all-to-all-start.5) | async-done | bytes 2097184 | tf_op jit(solution)/shard_map/all_to_all | solution.py:188
  316.7 4.6 all-to-all-start.8
  323.9 23.2 %all-to-all-done.8 = bf16[2,4,64,2048]{3,2,0,1:T(8,128)(2,1)} async-done(((bf16[2,4,64,2048]{3,2,0,1:T(8,128)(2,1)}), bf16[2,4,64,2048]{3,2,0,1:T(8,128)(2,1)}, u32[]{:S(2)}, u32[]{:S(2)}) %all-to-all-start.8) | async-done | bytes 2097184 | tf_op jit(solution)/shard_map/all_to_all | solution.py:176
  360.1 17.9 %all-to-all-done.6 = bf16[2,4,64,2048]{3,2,0,1:T(8,128)(2,1)S(1)} async-done(((bf16[2,4,64,2048]{3,2,0,1:T(8,128)(2,1)}), bf16[2,4,64,2048]{3,2,0,1:T(8,128)(2,1)S(1)}, u32[]{:S(2)}, u32[]{:S(2)}) %all-to-all-start.6) | async-done | bytes 2097184 | tf_op jit(solution)/shard_map/all_to_all | solution.py:176
  408.2 59.5 %all-gather.11.cloned.1.call-done = bf16[3,2048,384]{2,1,0:T(8,128)(2,1)} async-done(((bf16[3,256,384]{2,1,0:T(8,128)(2,1)}), bf16[3,2048,384]{2,1,0:T(8,128)(2,1)}) %all-gather.11.cloned.1.call-update) | async-done | bytes 4718608 | tf_op jit(solution)/shard_map/all_gather | solution.py:193
  493.9 4.8 all-to-all-start.11
  510.4 4.6 add_convert_fusion.1
  518.1 6.3 all-to-all-done.11
  531.2 22.5 %all-to-all-done.12 = bf16[2,4,64,2048]{3,2,0,1:T(8,128)(2,1)S(1)} async-done(((bf16[2,4,64,2048]{3,2,0,1:T(8,128)(2,1)}), bf16[2,4,64,2048]{3,2,0,1:T(8,128)(2,1)S(1)}, u32[]{:S(2)}, u32[]{:S(2)}) %all-to-all-start.12) | async-done | bytes 2097184 | tf_op jit(solution)/shard_map/all_to_all | solution.py:188
  565.5 23.1 %all-to-all-done.13 = bf16[2,4,64,2048]{3,2,0,1:T(8,128)(2,1)} async-done(((bf16[2,4,64,2048]{3,2,0,1:T(8,128)(2,1)}), bf16[2,4,64,2048]{3,2,0,1:T(8,128)(2,1)}, u32[]{:S(2)}, u32[]{:S(2)}) %all-to-all-start.13) | async-done | bytes 2097184 | tf_op jit(solution)/shard_map/all_to_all | solution.py:176
  606.4 4.7 stack_reshape.3
  730.7 88.1 %reduce-scatter.7.cloned.1.call-done = bf16[3,256,512]{2,1,0:T(8,128)(2,1)} async-done(((bf16[3,2048,512]{2,1,0:T(8,128)(2,1)}), bf16[3,256,512]{2,1,0:T(8,128)(2,1)}) %reduce-scatter.7.cloned.1.call-update) | async-done | bytes 786448 | tf_op jit(solution)/shard_map/reduce_scatter | solution.py:197
  842.7 7.7 dynamic_update_slice.7
  852.2 13.8 %all-to-all-done.15 = bf16[2,4,64,2048]{3,2,0,1:T(8,128)(2,1)} async-done(((bf16[2,4,64,2048]{3,2,0,1:T(8,128)(2,1)}), bf16[2,4,64,2048]{3,2,0,1:T(8,128)(2,1)}, u32[]{:S(2)}, u32[]{:S(2)}) %all-to-all-start.15) | async-done | bytes 2097184 | tf_op jit(solution)/shard_map/all_to_all | solution.py:188
  881.8 14.2 %all-to-all-done.17 = f32[32,1,2048]{2,1,0:T(1,128)S(1)} async-done(((f32[32,1,2048]{2,1,0:T(1,128)}), f32[32,1,2048]{2,1,0:T(1,128)S(1)}, u32[]{:S(2)}, u32[]{:S(2)}) %all-to-all-start.17) | async-done | bytes 262176 | tf_op jit(solution)/shard_map/all_to_all | solution.py:205
  919.8 87.0 %reduce-scatter.11.cloned.1.call-done = bf16[5,256,512]{2,1,0:T(8,128)(2,1)} async-done(((bf16[5,2048,512]{2,1,0:T(8,128)(2,1)}), bf16[5,256,512]{2,1,0:T(8,128)(2,1)}) %reduce-scatter.11.cloned.1.call-update) | async-done | bytes 1310736 | tf_op jit(solution)/shard_map/reduce_scatter | solution.py:197
  1021.2 6.7 all-to-all-done.16
  (712 shorter events, 468.1 us)
Async XLA Ops:
  13.9 18.7 %all-to-all-start.2 = ((bf16[4,64,4,512]{3,1,0,2:T(8,128)(2,1)}), bf16[4,64,4,512]{3,1,0,2:T(8,128)(2,1)S(1)}, u32[]{:S(2)}, u32[]{:S(2)}) async-start(bf16[4,64,4,512]{3,1,0,2:T(8,128)(2,1)} %copy.457), calls=%async_computation.2 | async-start | bytes 2097152 | tf_op jit(solution)/shard_map/all_to_all | solution.py:205
  18.1 170.4 %all-gather.5.cloned.1.call-start = ((), (), s32[]{:S(2)}) async-start(), calls=%async_computation.25 | async-start | bytes 11796480 | tf_op jit(solution)/shard_map/all_gather | solution.py:193
  33.9 321.7 %all-gather.7.cloned.1.call-start = ((), (), s32[]{:S(2)}) async-start(), calls=%async_computation.26 | async-start | bytes 7077888 | tf_op jit(solution)/shard_map/all_gather | solution.py:193
  46.1 17.3 %all-to-all-start = ((bf16[32,2,960]{2,1,0:T(2,128)(2,1)}), bf16[32,2,960]{2,1,0:T(2,128)(2,1)S(1)}, u32[]{:S(2)}, u32[]{:S(2)}) async-start(bf16[32,2,960]{2,1,0:T(2,128)(2,1)} %reshape.757), calls=%async_computation | async-start | bytes 262144 | tf_op jit(solution)/shard_map/all_to_all | solution.py:205
  63.3 5.5 all-to-all-start.9
  76.7 30.2 %all-to-all-start.1 = ((bf16[2,4,64,2048]{3,2,0,1:T(8,128)(2,1)}), bf16[2,4,64,2048]{3,2,0,1:T(8,128)(2,1)}, u32[]{:S(2)}, u32[]{:S(2)}) async-start(bf16[2,4,64,2048]{3,2,0,1:T(8,128)(2,1)} %broadcast_in_dim.43), calls=%async_computation.1 | async-start | bytes 4194304 | tf_op jit(solution)/shard_map/all_to_all | solution.py:176
  81.2 311.7 %all-gather.9.cloned.1.call-start = ((), (), s32[]{:S(2)}) async-start(), calls=%async_computation.27 | async-start | bytes 7077888 | tf_op jit(solution)/shard_map/all_gather | solution.py:193
  263.9 13.0 %all-to-all-start.4 = ((bf16[512,1,2,4,64]{0,4,2,1,3:T(8,128)(2,1)}), bf16[512,1,2,4,64]{0,4,2,1,3:T(8,128)(2,1)}, u32[]{:S(2)}, u32[]{:S(2)}) async-start(bf16[512,1,2,4,64]{0,4,2,1,3:T(8,128)(2,1)} %copy.478), calls=%async_computation.4 | async-start | bytes 1048576 | tf_op jit(solution)/shard_map/all_to_all | solution.py:205
  276.9 7.5 all-to-all-start.10
  284.5 29.6 %all-to-all-start.5 = ((bf16[2,4,64,2048]{3,2,0,1:T(8,128)(2,1)}), bf16[2,4,64,2048]{3,2,0,1:T(8,128)(2,1)S(1)}, u32[]{:S(2)}, u32[]{:S(2)}) async-start(bf16[2,4,64,2048]{3,2,0,1:T(8,128)(2,1)} %copy.480), calls=%async_computation.5 | async-start | bytes 4194304 | tf_op jit(solution)/shard_map/all_to_all | solution.py:188
  316.7 30.4 %all-to-all-start.8 = ((bf16[2,4,64,2048]{3,2,0,1:T(8,128)(2,1)}), bf16[2,4,64,2048]{3,2,0,1:T(8,128)(2,1)}, u32[]{:S(2)}, u32[]{:S(2)}) async-start(bf16[2,4,64,2048]{3,2,0,1:T(8,128)(2,1)} %broadcast_in_dim.48), calls=%async_computation.8 | async-start | bytes 4194304 | tf_op jit(solution)/shard_map/all_to_all | solution.py:176
  321.3 146.4 %all-gather.11.cloned.1.call-start = ((), (), s32[]{:S(2)}) async-start(), calls=%async_computation.28 | async-start | bytes 5308416 | tf_op jit(solution)/shard_map/all_gather | solution.py:193
  348.7 29.3 %all-to-all-start.6 = ((bf16[2,4,64,2048]{3,2,0,1:T(8,128)(2,1)}), bf16[2,4,64,2048]{3,2,0,1:T(8,128)(2,1)S(1)}, u32[]{:S(2)}, u32[]{:S(2)}) async-start(bf16[2,4,64,2048]{3,2,0,1:T(8,128)(2,1)} %broadcast_in_dim.47), calls=%async_computation.6 | async-start | bytes 4194304 | tf_op jit(solution)/shard_map/all_to_all | solution.py:176
  352.3 378.3 %reduce-scatter.9.cloned.1.call-start = ((), (), s32[]{:S(2)}) async-start(), calls=%async_computation.31 | async-start | bytes 5308416 | tf_op jit(solution)/shard_map/reduce_scatter | solution.py:197
  482.6 248.1 %reduce-scatter.5.cloned.1.call-start = ((), (), s32[]{:S(2)}) async-start(), calls=%async_computation.29 | async-start | bytes 7077888 | tf_op jit(solution)/shard_map/reduce_scatter | solution.py:197
  493.9 30.5 %all-to-all-start.11 = ((bf16[2,4,64,2048]{3,2,0,1:T(8,128)(2,1)}), bf16[2,4,64,2048]{3,2,0,1:T(8,128)(2,1)}, u32[]{:S(2)}, u32[]{:S(2)}) async-start(bf16[2,4,64,2048]{3,2,0,1:T(8,128)(2,1)} %copy.505), calls=%async_computation.11 | async-start | bytes 4194304 | tf_op jit(solution)/shard_map/all_to_all | solution.py:188
  524.4 29.3 %all-to-all-start.12 = ((bf16[2,4,64,2048]{3,2,0,1:T(8,128)(2,1)}), bf16[2,4,64,2048]{3,2,0,1:T(8,128)(2,1)S(1)}, u32[]{:S(2)}, u32[]{:S(2)}) async-start(bf16[2,4,64,2048]{3,2,0,1:T(8,128)(2,1)} %copy.506), calls=%async_computation.12 | async-start | bytes 4194304 | tf_op jit(solution)/shard_map/all_to_all | solution.py:188
  558.3 30.3 %all-to-all-start.13 = ((bf16[2,4,64,2048]{3,2,0,1:T(8,128)(2,1)}), bf16[2,4,64,2048]{3,2,0,1:T(8,128)(2,1)}, u32[]{:S(2)}, u32[]{:S(2)}) async-start(bf16[2,4,64,2048]{3,2,0,1:T(8,128)(2,1)} %broadcast_in_dim.50), calls=%async_computation.13 | async-start | bytes 4194304 | tf_op jit(solution)/shard_map/all_to_all | solution.py:176
  594.0 18.9 %all-to-all-start.14 = ((f32[512,4,2,1,64]{0,4,2,3,1:T(8,128)}), f32[512,4,2,1,64]{0,4,2,3,1:T(8,128)}, u32[]{:S(2)}, u32[]{:S(2)}) async-start(f32[512,4,2,1,64]{0,4,2,3,1:T(8,128)} %convolution_bitcast_fusion.1), calls=%async_computation.14 | async-start | bytes 2097152 | tf_op jit(solution)/shard_map/all_to_all | solution.py:205
  598.4 220.4 %reduce-scatter.7.cloned.1.call-start = ((), (), s32[]{:S(2)}) async-start(), calls=%async_computation.30 | async-start | bytes 7077888 | tf_op jit(solution)/shard_map/reduce_scatter | solution.py:197
  601.2 405.6 %reduce-scatter.11.cloned.1.call-start = ((), (), s32[]{:S(2)}) async-start(), calls=%async_computation.32 | async-start | bytes 11796480 | tf_op jit(solution)/shard_map/reduce_scatter | solution.py:197
  835.8 30.2 %all-to-all-start.15 = ((bf16[2,4,64,2048]{3,2,0,1:T(8,128)(2,1)}), bf16[2,4,64,2048]{3,2,0,1:T(8,128)(2,1)}, u32[]{:S(2)}, u32[]{:S(2)}) async-start(bf16[2,4,64,2048]{3,2,0,1:T(8,128)(2,1)} %copy.543), calls=%async_computation.15 | async-start | bytes 4194304 | tf_op jit(solution)/shard_map/all_to_all | solution.py:188
  874.6 21.3 %all-to-all-start.17 = ((f32[32,1,2048]{2,1,0:T(1,128)}), f32[32,1,2048]{2,1,0:T(1,128)S(1)}, u32[]{:S(2)}, u32[]{:S(2)}) async-start(f32[32,1,2048]{2,1,0:T(1,128)} %copy.552), calls=%async_computation.21 | async-start | bytes 524288 | tf_op jit(solution)/shard_map/all_to_all | solution.py:205
  1009.2 18.8 %all-to-all-start.16 = ((bf16[4,4,64,1,512]{4,2,0,3,1:T(8,128)(2,1)}), bf16[4,4,64,1,512]{4,2,0,3,1:T(8,128)(2,1)}, u32[]{:S(2)}, u32[]{:S(2)}) async-start(bf16[4,4,64,1,512]{4,2,0,3,1:T(8,128)(2,1)} %copy.544), calls=%async_computation.20 | async-start | bytes 2097152 | tf_op jit(solution)/shard_map/all_to_all | solution.py:205
  (195 other events, 3430.2 us)
Sparse Core Ops, SparseCore 0:
  34.0 154.5 all-gather.4
  190.7 97.2 all-gather.6
  290.2 97.2 all-gather.8
  389.5 78.1 all-gather.10
  482.7 93.3 reduce-scatter.8
  579.5 118.0 reduce-scatter.4
  701.3 117.4 reduce-scatter.6
  822.4 184.3 reduce-scatter.10

commit v14 on v12

--- a/solution.py
+++ b/solution.py
@@ -301,7 +301,7 @@
             3, owned_rows, inner, hidden_here
         )
         lanes = hidden_here // 128 if hidden_here % 128 == 0 else 0
-        first = (lanes + 1) // 2 * 128 if lanes > 1 else hidden_here // 2
+        first = (lanes - lanes * 3 // 11) * 128 if lanes > 1 else hidden_here // 2
         bounds = ((0, first), (first, hidden_here - first))
         ff_chunks = []
         for offset, size in bounds:

time: 1000 us -> 997 us (level)
  local copies, waits for them, and re-layouts: 160 us -> 150 us
    all_to_all x4 -> x5, starting transfers between devices: 17.8 us -> 21.7 us  [tp_gather(): moved = lax.all_to_all(spread, TP_AXES, axis, axis, tiled=True)]
    all_to_all x4 -> x5, waiting for transfers between devices: 83.2 us -> 81.5 us  [tp_gather(): moved = lax.all_to_all(spread, TP_AXES, axis, axis, tiled=True)]
    unnamed x309 -> x357, local copies, waits for them, and re-layouts: 25.1 us -> 24.2 us
  transfers between devices with their start and end apart: 23 -> 24, of which waited for: 21 -> 22; matrix products, arithmetic and copies ran while one was open for 37% -> 36% of each run, Pallas kernels for 0% -> 0%
where the time goes in v14:
time: 997 us; the launch traced here: 988 us
  waiting for transfers between devices  485 us (49%)
  matrix products  185 us (19%)
  local copies, waits for them, and re-layouts  150 us (15%)
  starting transfers between devices  78.8 us (8%)
  other arithmetic  66.8 us (7%)
  between operations  17.3 us (2%)
    reduce_scatter x3, waiting for transfers between devices, fsdp_scatter_low(): lax.psum_scatter(value.astype(jnp.bfloat16), FSDP_AXES, scatter_dimension...  151 us
    all_gather x3, waiting for transfers between devices, fsdp_gather(): return lax.all_gather(value, FSDP_AXES, axis=axis, tiled=True)  126 us
    all_to_all x5, waiting for transfers between devices, tp_gather(): moved = lax.all_to_all(spread, TP_AXES, axis, axis, tiled=True)  81.5 us
    dot_general x42, matrix products, outer_product_result(): return jnp.einsum(form, first, second, precision=lax.Precision.HIGHEST)  77.2 us
    all_to_all x4, waiting for transfers between devices, tp_scatter_low(): moved = lax.all_to_all(staged, TP_AXES, axis, axis, tiled=True)  68.8 us
    all_to_all x9, waiting for transfers between devices, exchange(): return lax.all_to_all(value, axes, split_axis, concat_axis, tiled=True)  57.6 us
    dot_general x12, matrix products, matmul_rows(): return jnp.dot(left, right, preferred_element_type=jnp.float32)  42.7 us
    dot_general x12, matrix products, back_product(): jnp.einsum('tg,fg->tf', gradient, weight, preferred_element_type=jnp.floa...  38.6 us
  transfers between devices with their start and end apart: 24, of which 22 were waited for; matrix products, arithmetic and copies ran while one was open for 36% of the time, Pallas kernels for 0%

profile of v14, /device:TPU:0, one launch (start us, length us, event | category | flops | bytes accessed | tf_op | source)
XLA Modules:
  0.0 988.3 jit_solution(13365876568593133635)
XLA Ops:
  18.3 14.3 %all-to-all-done.2 = bf16[4,64,4,512]{3,1,0,2:T(8,128)(2,1)S(1)} async-done(((bf16[4,64,4,512]{3,1,0,2:T(8,128)(2,1)}), bf16[4,64,4,512]{3,1,0,2:T(8,128)(2,1)S(1)}, u32[]{:S(2)}, u32[]{:S(2)}) %all-to-all-start.2) | async-done | bytes 1048608 | tf_op jit(solution)/shard_map/all_to_all | solution.py:205
  47.0 5.6 all-to-all-start
  52.8 11.0 %all-to-all-done = bf16[32,2,960]{2,1,0:T(2,128)(2,1)S(1)} async-done(((bf16[32,2,960]{2,1,0:T(2,128)(2,1)}), bf16[32,2,960]{2,1,0:T(2,128)(2,1)S(1)}, u32[]{:S(2)}, u32[]{:S(2)}) %all-to-all-start) | async-done | bytes 122912 | tf_op jit(solution)/shard_map/all_to_all | solution.py:205
  80.0 23.8 %all-to-all-done.1 = bf16[2,4,64,2048]{3,2,0,1:T(8,128)(2,1)} async-done(((bf16[2,4,64,2048]{3,2,0,1:T(8,128)(2,1)}), bf16[2,4,64,2048]{3,2,0,1:T(8,128)(2,1)}, u32[]{:S(2)}, u32[]{:S(2)}) %all-to-all-start.1) | async-done | bytes 2097184 | tf_op jit(solution)/shard_map/all_to_all | solution.py:176
  106.5 82.1 %all-gather.4.cloned.1.call-done = bf16[5,2048,512]{2,1,0:T(8,128)(2,1)} async-done(((bf16[5,256,512]{2,1,0:T(8,128)(2,1)}), bf16[5,2048,512]{2,1,0:T(8,128)(2,1)}) %all-gather.4.cloned.1.call-update) | async-done | bytes 10485776 | tf_op jit(solution)/shard_map/all_gather | solution.py:193
  294.0 23.4 %all-to-all-done.5 = bf16[2,4,64,2048]{3,2,0,1:T(8,128)(2,1)} async-done(((bf16[2,4,64,2048]{3,2,0,1:T(8,128)(2,1)}), bf16[2,4,64,2048]{3,2,0,1:T(8,128)(2,1)}, u32[]{:S(2)}, u32[]{:S(2)}) %all-to-all-start.5) | async-done | bytes 2097184 | tf_op jit(solution)/shard_map/all_to_all | solution.py:188
  327.9 21.3 %all-to-all-done.8 = bf16[2,4,64,2048]{3,2,0,1:T(8,128)(2,1)} async-done(((bf16[2,4,64,2048]{3,2,0,1:T(8,128)(2,1)}), bf16[2,4,64,2048]{3,2,0,1:T(8,128)(2,1)}, u32[]{:S(2)}, u32[]{:S(2)}) %all-to-all-start.8) | async-done | bytes 2097184 | tf_op jit(solution)/shard_map/all_to_all | solution.py:176
  359.6 5.8 all-gather.6.cloned.1.call-done
  365.4 6.5 fusion.4
  371.9 10.1 %all-to-all-done.6 = bf16[2,4,64,2048]{3,2,0,1:T(8,128)(2,1)} async-done(((bf16[2,4,64,2048]{3,2,0,1:T(8,128)(2,1)}), bf16[2,4,64,2048]{3,2,0,1:T(8,128)(2,1)}, u32[]{:S(2)}, u32[]{:S(2)}) %all-to-all-start.6) | async-done | bytes 2097184 | tf_op jit(solution)/shard_map/all_to_all | solution.py:176
  383.8 5.3 fusion.3
  389.2 5.5 fusion.11
  402.4 5.4 pad_maximum_fusion
  407.8 37.9 %all-gather.8.cloned.1.call-done = bf16[3,2048,384]{2,1,0:T(8,128)(2,1)} async-done(((bf16[3,256,384]{2,1,0:T(8,128)(2,1)}), bf16[3,2048,384]{2,1,0:T(8,128)(2,1)}) %all-gather.8.cloned.1.call-update) | async-done | bytes 4718608 | tf_op jit(solution)/shard_map/all_gather | solution.py:193
  492.2 8.9 all-to-all-done.10
  508.7 22.7 %all-to-all-done.11 = bf16[2,4,64,2048]{3,2,0,1:T(8,128)(2,1)} async-done(((bf16[2,4,64,2048]{3,2,0,1:T(8,128)(2,1)}), bf16[2,4,64,2048]{3,2,0,1:T(8,128)(2,1)}, u32[]{:S(2)}, u32[]{:S(2)}) %all-to-all-start.11) | async-done | bytes 2097184 | tf_op jit(solution)/shard_map/all_to_all | solution.py:188
  544.2 23.2 %all-to-all-done.12 = bf16[2,4,64,2048]{3,2,0,1:T(8,128)(2,1)} async-done(((bf16[2,4,64,2048]{3,2,0,1:T(8,128)(2,1)}), bf16[2,4,64,2048]{3,2,0,1:T(8,128)(2,1)}, u32[]{:S(2)}, u32[]{:S(2)}) %all-to-all-start.12) | async-done | bytes 2097184 | tf_op jit(solution)/shard_map/all_to_all | solution.py:176
  585.8 5.9 all-to-all-done.13
  706.0 59.3 %reduce-scatter.4.cloned.1.call-done = bf16[3,256,1024]{2,1,0:T(8,128)(2,1)} async-done(((bf16[3,2048,1024]{2,1,0:T(8,128)(2,1)}), bf16[3,256,1024]{2,1,0:T(8,128)(2,1)}) %reduce-scatter.4.cloned.1.call-update) | async-done | bytes 1572880 | tf_op jit(solution)/shard_map/reduce_scatter | solution.py:197
  789.3 7.7 dynamic_update_slice.7
  798.8 13.8 %all-to-all-done.14 = bf16[2,4,64,2048]{3,2,0,1:T(8,128)(2,1)} async-done(((bf16[2,4,64,2048]{3,2,0,1:T(8,128)(2,1)}), bf16[2,4,64,2048]{3,2,0,1:T(8,128)(2,1)}, u32[]{:S(2)}, u32[]{:S(2)}) %all-to-all-start.14) | async-done | bytes 2097184 | tf_op jit(solution)/shard_map/all_to_all | solution.py:188
  826.8 12.5 %all-to-all-done.16 = f32[32,1,2048]{2,1,0:T(1,128)S(1)} async-done(((f32[32,1,2048]{2,1,0:T(1,128)}), f32[32,1,2048]{2,1,0:T(1,128)S(1)}, u32[]{:S(2)}, u32[]{:S(2)}) %all-to-all-start.16) | async-done | bytes 262176 | tf_op jit(solution)/shard_map/all_to_all | solution.py:205
  861.3 91.8 %reduce-scatter.8.cloned.1.call-done = bf16[5,256,512]{2,1,0:T(8,128)(2,1)} async-done(((bf16[5,2048,512]{2,1,0:T(8,128)(2,1)}), bf16[5,256,512]{2,1,0:T(8,128)(2,1)}) %reduce-scatter.8.cloned.1.call-update) | async-done | bytes 1310736 | tf_op jit(solution)/shard_map/reduce_scatter | solution.py:197
  967.5 6.7 all-to-all-done.15
  (650 shorter events, 460.4 us)
Async XLA Ops:
  13.9 18.7 %all-to-all-start.2 = ((bf16[4,64,4,512]{3,1,0,2:T(8,128)(2,1)}), bf16[4,64,4,512]{3,1,0,2:T(8,128)(2,1)S(1)}, u32[]{:S(2)}, u32[]{:S(2)}) async-start(bf16[4,64,4,512]{3,1,0,2:T(8,128)(2,1)} %copy.379), calls=%async_computation.2 | async-start | bytes 2097152 | tf_op jit(solution)/shard_map/all_to_all | solution.py:205
  18.1 170.4 %all-gather.4.cloned.1.call-start = ((), (), s32[]{:S(2)}) async-start(), calls=%async_computation.22 | async-start | bytes 11796480 | tf_op jit(solution)/shard_map/all_gather | solution.py:193
  33.9 331.5 %all-gather.6.cloned.1.call-start = ((), (), s32[]{:S(2)}) async-start(), calls=%async_computation.23 | async-start | bytes 14155776 | tf_op jit(solution)/shard_map/all_gather | solution.py:193
  47.0 16.8 %all-to-all-start = ((bf16[32,2,960]{2,1,0:T(2,128)(2,1)}), bf16[32,2,960]{2,1,0:T(2,128)(2,1)S(1)}, u32[]{:S(2)}, u32[]{:S(2)}) async-start(bf16[32,2,960]{2,1,0:T(2,128)(2,1)} %reshape.743), calls=%async_computation | async-start | bytes 262144 | tf_op jit(solution)/shard_map/all_to_all | solution.py:205
  64.4 6.9 all-to-all-start.3
  72.9 30.9 %all-to-all-start.1 = ((bf16[2,4,64,2048]{3,2,0,1:T(8,128)(2,1)}), bf16[2,4,64,2048]{3,2,0,1:T(8,128)(2,1)}, u32[]{:S(2)}, u32[]{:S(2)}) async-start(bf16[2,4,64,2048]{3,2,0,1:T(8,128)(2,1)} %broadcast_in_dim.43), calls=%async_computation.1 | async-start | bytes 4194304 | tf_op jit(solution)/shard_map/all_to_all | solution.py:176
  264.1 13.1 %all-to-all-start.4 = ((bf16[512,1,2,4,64]{0,4,2,1,3:T(8,128)(2,1)}), bf16[512,1,2,4,64]{0,4,2,1,3:T(8,128)(2,1)}, u32[]{:S(2)}, u32[]{:S(2)}) async-start(bf16[512,1,2,4,64]{0,4,2,1,3:T(8,128)(2,1)} %copy.400), calls=%async_computation.4 | async-start | bytes 1048576 | tf_op jit(solution)/shard_map/all_to_all | solution.py:205
  277.2 9.8 all-to-all-start.9
  287.0 30.3 %all-to-all-start.5 = ((bf16[2,4,64,2048]{3,2,0,1:T(8,128)(2,1)}), bf16[2,4,64,2048]{3,2,0,1:T(8,128)(2,1)}, u32[]{:S(2)}, u32[]{:S(2)}) async-start(bf16[2,4,64,2048]{3,2,0,1:T(8,128)(2,1)} %copy.402), calls=%async_computation.5 | async-start | bytes 4194304 | tf_op jit(solution)/shard_map/all_to_all | solution.py:188
  291.6 154.1 %all-gather.8.cloned.1.call-start = ((), (), s32[]{:S(2)}) async-start(), calls=%async_computation.24 | async-start | bytes 5308416 | tf_op jit(solution)/shard_map/all_gather | solution.py:193
  318.9 30.2 %all-to-all-start.8 = ((bf16[2,4,64,2048]{3,2,0,1:T(8,128)(2,1)}), bf16[2,4,64,2048]{3,2,0,1:T(8,128)(2,1)}, u32[]{:S(2)}, u32[]{:S(2)}) async-start(bf16[2,4,64,2048]{3,2,0,1:T(8,128)(2,1)} %broadcast_in_dim.48), calls=%async_computation.8 | async-start | bytes 4194304 | tf_op jit(solution)/shard_map/all_to_all | solution.py:176
  351.8 30.2 %all-to-all-start.6 = ((bf16[2,4,64,2048]{3,2,0,1:T(8,128)(2,1)}), bf16[2,4,64,2048]{3,2,0,1:T(8,128)(2,1)}, u32[]{:S(2)}, u32[]{:S(2)}) async-start(bf16[2,4,64,2048]{3,2,0,1:T(8,128)(2,1)} %broadcast_in_dim.47), calls=%async_computation.6 | async-start | bytes 4194304 | tf_op jit(solution)/shard_map/all_to_all | solution.py:176
  356.3 349.7 %reduce-scatter.6.cloned.1.call-start = ((), (), s32[]{:S(2)}) async-start(), calls=%async_computation.26 | async-start | bytes 5308416 | tf_op jit(solution)/shard_map/reduce_scatter | solution.py:197
  460.7 304.6 %reduce-scatter.4.cloned.1.call-start = ((), (), s32[]{:S(2)}) async-start(), calls=%async_computation.25 | async-start | bytes 14155776 | tf_op jit(solution)/shard_map/reduce_scatter | solution.py:197
  470.5 30.7 %all-to-all-start.10 = ((bf16[2,4,64,2048]{3,2,0,1:T(8,128)(2,1)}), bf16[2,4,64,2048]{3,2,0,1:T(8,128)(2,1)}, u32[]{:S(2)}, u32[]{:S(2)}) async-start(bf16[2,4,64,2048]{3,2,0,1:T(8,128)(2,1)} %copy.411), calls=%async_computation.10 | async-start | bytes 4194304 | tf_op jit(solution)/shard_map/all_to_all | solution.py:188
  501.1 30.2 %all-to-all-start.11 = ((bf16[2,4,64,2048]{3,2,0,1:T(8,128)(2,1)}), bf16[2,4,64,2048]{3,2,0,1:T(8,128)(2,1)}, u32[]{:S(2)}, u32[]{:S(2)}) async-start(bf16[2,4,64,2048]{3,2,0,1:T(8,128)(2,1)} %copy.412), calls=%async_computation.11 | async-start | bytes 4194304 | tf_op jit(solution)/shard_map/all_to_all | solution.py:188
  537.2 30.2 %all-to-all-start.12 = ((bf16[2,4,64,2048]{3,2,0,1:T(8,128)(2,1)}), bf16[2,4,64,2048]{3,2,0,1:T(8,128)(2,1)}, u32[]{:S(2)}, u32[]{:S(2)}) async-start(bf16[2,4,64,2048]{3,2,0,1:T(8,128)(2,1)} %broadcast_in_dim.50), calls=%async_computation.12 | async-start | bytes 4194304 | tf_op jit(solution)/shard_map/all_to_all | solution.py:176
  572.8 18.9 %all-to-all-start.13 = ((f32[512,4,2,1,64]{0,4,2,3,1:T(8,128)}), f32[512,4,2,1,64]{0,4,2,3,1:T(8,128)}, u32[]{:S(2)}, u32[]{:S(2)}) async-start(f32[512,4,2,1,64]{0,4,2,3,1:T(8,128)} %convolution_bitcast_fusion.1), calls=%async_computation.13 | async-start | bytes 2097152 | tf_op jit(solution)/shard_map/all_to_all | solution.py:205
  577.2 375.9 %reduce-scatter.8.cloned.1.call-start = ((), (), s32[]{:S(2)}) async-start(), calls=%async_computation.27 | async-start | bytes 11796480 | tf_op jit(solution)/shard_map/reduce_scatter | solution.py:197
  782.4 30.2 %all-to-all-start.14 = ((bf16[2,4,64,2048]{3,2,0,1:T(8,128)(2,1)}), bf16[2,4,64,2048]{3,2,0,1:T(8,128)(2,1)}, u32[]{:S(2)}, u32[]{:S(2)}) async-start(bf16[2,4,64,2048]{3,2,0,1:T(8,128)(2,1)} %copy.449), calls=%async_computation.14 | async-start | bytes 4194304 | tf_op jit(solution)/shard_map/all_to_all | solution.py:188
  819.9 19.5 %all-to-all-start.16 = ((f32[32,1,2048]{2,1,0:T(1,128)}), f32[32,1,2048]{2,1,0:T(1,128)S(1)}, u32[]{:S(2)}, u32[]{:S(2)}) async-start(f32[32,1,2048]{2,1,0:T(1,128)} %copy.458), calls=%async_computation.19 | async-start | bytes 524288 | tf_op jit(solution)/shard_map/all_to_all | solution.py:205
  844.8 6.6 all-to-all-start.17
  851.4 6.2 all-to-all-start.18
  955.5 18.8 %all-to-all-start.15 = ((bf16[4,4,64,1,512]{4,2,0,3,1:T(8,128)(2,1)}), bf16[4,4,64,1,512]{4,2,0,3,1:T(8,128)(2,1)}, u32[]{:S(2)}, u32[]{:S(2)}) async-start(bf16[4,4,64,1,512]{4,2,0,3,1:T(8,128)(2,1)} %copy.450), calls=%async_computation.18 | async-start | bytes 2097152 | tf_op jit(solution)/shard_map/all_to_all | solution.py:205
  (173 other events, 3441.2 us)
Sparse Core Ops, SparseCore 0:
  34.0 154.5 all-gather.3
  190.7 174.6 all-gather.5
  367.6 78.0 all-gather.7
  460.8 93.4 reduce-scatter.5
  557.7 207.5 reduce-scatter.3
  768.8 184.2 reduce-scatter.7

commit v15 on v14

--- a/solution.py
+++ b/solution.py
@@ -197,6 +197,15 @@
     return lax.psum_scatter(
         value.astype(jnp.bfloat16), FSDP_AXES, scatter_dimension=axis, tiled=True
     )
+
+
+def fsdp_scatter_direct(value, fsdp, axis):
+    shape = list(value.shape)
+    staged = value.astype(jnp.bfloat16).reshape(
+        shape[:axis] + [fsdp, shape[axis] // fsdp] + shape[axis + 1 :]
+    )
+    moved = lax.all_to_all(staged, FSDP_AXES, axis, axis, tiled=True)
+    return jnp.sum(moved.astype(jnp.float32), axis=axis)
 
 
 def exchange(value, axes, split_axis, concat_axis):
@@ -405,7 +414,13 @@
             ]
         )
         ff_reduced, mixer_sums = lax.optimization_barrier((ff_reduced, mixer_sums))
-        mixer_reduced = fsdp_scatter_low(mixer_sums, 1)
+        mixer_reduced = jnp.concatenate(
+            [
+                fsdp_scatter_low(mixer_sums[:3], 1),
+                fsdp_scatter_direct(mixer_sums[3:], fsdp, 1).astype(jnp.bfloat16),
+            ],
+            axis=0,
+        )
         ff_back = jnp.concatenate(
             [
                 exchange(

time: 997 us -> 1020 us (1.023)
  blocking collectives: 5 us -> 17.8 us
    all_to_all x0 -> x1, waiting for transfers between devices: none -> 108 us  [fsdp_scatter_direct(): moved = lax.all_to_all(staged, FSDP_AXES, axis, axis, tiled=True)]
    reduce_scatter x3, waiting for transfers between devices: 151 us -> 51 us  [fsdp_scatter_low(): lax.psum_scatter(value.astype(jnp.bfloat16), FSDP_AXES, scatter_dimension...]
    all_to_all x1 -> x3, blocking collectives: 5 us -> 17.8 us  [exchange(): return lax.all_to_all(value, axes, split_axis, concat_axis, tiled=True)]
    all_to_all x9 -> x7, starting transfers between devices: 38.4 us -> 30.2 us  [exchange(): return lax.all_to_all(value, axes, split_axis, concat_axis, tiled=True)]
    all_to_all x9 -> x7, waiting for transfers between devices: 57.6 us -> 49.6 us  [exchange(): return lax.all_to_all(value, axes, split_axis, concat_axis, tiled=True)]
  transfers between devices with their start and end apart: 24 -> 23, of which waited for: 22 -> 20; matrix products, arithmetic and copies ran while one was open for 36% -> 36% of each run, Pallas kernels for 0% -> 0%
where the time goes in v15:
time: 1020 us; the launch traced here: 1010 us
  waiting for transfers between devices  486 us (48%)
  matrix products  188 us (18%)
  local copies, waits for them, and re-layouts  159 us (16%)
  starting transfers between devices  75.2 us (7%)
  other arithmetic  68.5 us (7%)
  blocking collectives  17.8 us (2%)
  between operations  17.3 us (2%)
    all_gather x3, waiting for transfers between devices, fsdp_gather(): return lax.all_gather(value, FSDP_AXES, axis=axis, tiled=True)  126 us
    all_to_all x1, waiting for transfers between devices, fsdp_scatter_direct(): moved = lax.all_to_all(staged, FSDP_AXES, axis, axis, tiled=True)  108 us
    all_to_all x5, waiting for transfers between devices, tp_gather(): moved = lax.all_to_all(spread, TP_AXES, axis, axis, tiled=True)  81.5 us
    dot_general x42, matrix products, outer_product_result(): return jnp.einsum(form, first, second, precision=lax.Precision.HIGHEST)  80.1 us
    all_to_all x4, waiting for transfers between devices, tp_scatter_low(): moved = lax.all_to_all(staged, TP_AXES, axis, axis, tiled=True)  70 us
    reduce_scatter x3, waiting for transfers between devices, fsdp_scatter_low(): lax.psum_scatter(value.astype(jnp.bfloat16), FSDP_AXES, scatter_dimension...  51 us
    all_to_all x7, waiting for transfers between devices, exchange(): return lax.all_to_all(value, axes, split_axis, concat_axis, tiled=True)  49.6 us
    dot_general x12, matrix products, matmul_rows(): return jnp.dot(left, right, preferred_element_type=jnp.float32)  42.6 us
  transfers between devices with their start and end apart: 23, of which 20 were waited for; matrix products, arithmetic and copies ran while one was open for 36% of the time, Pallas kernels for 0%

profile of v15, /device:TPU:0, one launch (start us, length us, event | category | flops | bytes accessed | tf_op | source)
XLA Modules:
  0.0 1012.6 jit_solution(14573575256640384795)
XLA Ops:
  18.3 14.3 %all-to-all-done.2 = bf16[4,64,4,512]{3,1,0,2:T(8,128)(2,1)S(1)} async-done(((bf16[4,64,4,512]{3,1,0,2:T(8,128)(2,1)}), bf16[4,64,4,512]{3,1,0,2:T(8,128)(2,1)S(1)}, u32[]{:S(2)}, u32[]{:S(2)}) %all-to-all-start.2) | async-done | bytes 1048608 | tf_op jit(solution)/shard_map/all_to_all | solution.py:214
  47.0 5.6 all-to-all-start
  52.8 11.0 %all-to-all-done = bf16[32,2,960]{2,1,0:T(2,128)(2,1)S(1)} async-done(((bf16[32,2,960]{2,1,0:T(2,128)(2,1)}), bf16[32,2,960]{2,1,0:T(2,128)(2,1)S(1)}, u32[]{:S(2)}, u32[]{:S(2)}) %all-to-all-start) | async-done | bytes 122912 | tf_op jit(solution)/shard_map/all_to_all | solution.py:214
  79.6 23.8 %all-to-all-done.1 = bf16[2,4,64,2048]{3,2,0,1:T(8,128)(2,1)} async-done(((bf16[2,4,64,2048]{3,2,0,1:T(8,128)(2,1)}), bf16[2,4,64,2048]{3,2,0,1:T(8,128)(2,1)}, u32[]{:S(2)}, u32[]{:S(2)}) %all-to-all-start.1) | async-done | bytes 2097184 | tf_op jit(solution)/shard_map/all_to_all | solution.py:176
  106.1 82.4 %all-gather.4.cloned.1.call-done = bf16[5,2048,512]{2,1,0:T(8,128)(2,1)} async-done(((bf16[5,256,512]{2,1,0:T(8,128)(2,1)}), bf16[5,2048,512]{2,1,0:T(8,128)(2,1)}) %all-gather.4.cloned.1.call-update) | async-done | bytes 10485776 | tf_op jit(solution)/shard_map/all_gather | solution.py:193
  293.9 23.4 %all-to-all-done.5 = bf16[2,4,64,2048]{3,2,0,1:T(8,128)(2,1)} async-done(((bf16[2,4,64,2048]{3,2,0,1:T(8,128)(2,1)}), bf16[2,4,64,2048]{3,2,0,1:T(8,128)(2,1)}, u32[]{:S(2)}, u32[]{:S(2)}) %all-to-all-start.5) | async-done | bytes 2097184 | tf_op jit(solution)/shard_map/all_to_all | solution.py:188
  327.9 21.3 %all-to-all-done.8 = bf16[2,4,64,2048]{3,2,0,1:T(8,128)(2,1)} async-done(((bf16[2,4,64,2048]{3,2,0,1:T(8,128)(2,1)}), bf16[2,4,64,2048]{3,2,0,1:T(8,128)(2,1)}, u32[]{:S(2)}, u32[]{:S(2)}) %all-to-all-start.8) | async-done | bytes 2097184 | tf_op jit(solution)/shard_map/all_to_all | solution.py:176
  359.9 5.5 all-gather.6.cloned.1.call-done
  365.4 6.5 fusion.4
  371.9 10.1 %all-to-all-done.6 = bf16[2,4,64,2048]{3,2,0,1:T(8,128)(2,1)} async-done(((bf16[2,4,64,2048]{3,2,0,1:T(8,128)(2,1)}), bf16[2,4,64,2048]{3,2,0,1:T(8,128)(2,1)}, u32[]{:S(2)}, u32[]{:S(2)}) %all-to-all-start.6) | async-done | bytes 2097184 | tf_op jit(solution)/shard_map/all_to_all | solution.py:176
  389.1 5.5 fusion.11
  407.8 37.9 %all-gather.8.cloned.1.call-done = bf16[3,2048,384]{2,1,0:T(8,128)(2,1)} async-done(((bf16[3,256,384]{2,1,0:T(8,128)(2,1)}), bf16[3,2048,384]{2,1,0:T(8,128)(2,1)}) %all-gather.8.cloned.1.call-update) | async-done | bytes 4718608 | tf_op jit(solution)/shard_map/all_gather | solution.py:193
  492.0 8.9 all-to-all-done.10
  508.5 22.7 %all-to-all-done.11 = bf16[2,4,64,2048]{3,2,0,1:T(8,128)(2,1)} async-done(((bf16[2,4,64,2048]{3,2,0,1:T(8,128)(2,1)}), bf16[2,4,64,2048]{3,2,0,1:T(8,128)(2,1)}, u32[]{:S(2)}, u32[]{:S(2)}) %all-to-all-start.11) | async-done | bytes 2097184 | tf_op jit(solution)/shard_map/all_to_all | solution.py:188
  544.2 23.2 %all-to-all-done.12 = bf16[2,4,64,2048]{3,2,0,1:T(8,128)(2,1)} async-done(((bf16[2,4,64,2048]{3,2,0,1:T(8,128)(2,1)}), bf16[2,4,64,2048]{3,2,0,1:T(8,128)(2,1)}, u32[]{:S(2)}, u32[]{:S(2)}) %all-to-all-start.12) | async-done | bytes 2097184 | tf_op jit(solution)/shard_map/all_to_all | solution.py:176
  585.9 5.7 all-to-all-done.13
  714.3 51.0 %reduce-scatter.4.cloned.1.call-done = bf16[3,256,1024]{2,1,0:T(8,128)(2,1)} async-done(((bf16[3,2048,1024]{2,1,0:T(8,128)(2,1)}), bf16[3,256,1024]{2,1,0:T(8,128)(2,1)}) %reduce-scatter.4.cloned.1.call-update) | async-done | bytes 1572880 | tf_op jit(solution)/shard_map/reduce_scatter | solution.py:197
  765.3 5.8 slice.293
  793.0 7.7 dynamic_update_slice.7
  801.9 15.0 %all-to-all-done.14 = bf16[2,4,64,2048]{3,2,0,1:T(8,128)(2,1)} async-done(((bf16[2,4,64,2048]{3,2,0,1:T(8,128)(2,1)}), bf16[2,4,64,2048]{3,2,0,1:T(8,128)(2,1)}, u32[]{:S(2)}, u32[]{:S(2)}) %all-to-all-start.14) | async-done | bytes 2097184 | tf_op jit(solution)/shard_map/all_to_all | solution.py:188
  830.4 7.6 all-to-all-done.17
  842.9 7.9 all_to_all.184
  866.7 107.8 %all-to-all-done.15 = bf16[2,8,256,512]{3,2,0,1:T(8,128)(2,1)} async-done(((bf16[2,8,256,512]{3,2,0,1:T(8,128)(2,1)}), bf16[2,8,256,512]{3,2,0,1:T(8,128)(2,1)}, u32[]{:S(2)}, u32[]{:S(2)}) %all-to-all-start.15) | async-done | bytes 4194336 | tf_op jit(solution)/shard_map/all_to_all | solution.py:207
  991.8 6.7 all-to-all-done.16
  (653 shorter events, 477.9 us)
Async XLA Ops:
  13.9 18.7 %all-to-all-start.2 = ((bf16[4,64,4,512]{3,1,0,2:T(8,128)(2,1)}), bf16[4,64,4,512]{3,1,0,2:T(8,128)(2,1)S(1)}, u32[]{:S(2)}, u32[]{:S(2)}) async-start(bf16[4,64,4,512]{3,1,0,2:T(8,128)(2,1)} %copy.381), calls=%async_computation.2 | async-start | bytes 2097152 | tf_op jit(solution)/shard_map/all_to_all | solution.py:214
  18.1 170.4 %all-gather.4.cloned.1.call-start = ((), (), s32[]{:S(2)}) async-start(), calls=%async_computation.23 | async-start | bytes 11796480 | tf_op jit(solution)/shard_map/all_gather | solution.py:193
  33.9 331.5 %all-gather.6.cloned.1.call-start = ((), (), s32[]{:S(2)}) async-start(), calls=%async_computation.24 | async-start | bytes 14155776 | tf_op jit(solution)/shard_map/all_gather | solution.py:193
  47.0 16.8 %all-to-all-start = ((bf16[32,2,960]{2,1,0:T(2,128)(2,1)}), bf16[32,2,960]{2,1,0:T(2,128)(2,1)S(1)}, u32[]{:S(2)}, u32[]{:S(2)}) async-start(bf16[32,2,960]{2,1,0:T(2,128)(2,1)} %reshape.747), calls=%async_computation | async-start | bytes 262144 | tf_op jit(solution)/shard_map/all_to_all | solution.py:214
  64.4 6.9 all-to-all-start.3
  72.9 30.5 %all-to-all-start.1 = ((bf16[2,4,64,2048]{3,2,0,1:T(8,128)(2,1)}), bf16[2,4,64,2048]{3,2,0,1:T(8,128)(2,1)}, u32[]{:S(2)}, u32[]{:S(2)}) async-start(bf16[2,4,64,2048]{3,2,0,1:T(8,128)(2,1)} %broadcast_in_dim.43), calls=%async_computation.1 | async-start | bytes 4194304 | tf_op jit(solution)/shard_map/all_to_all | solution.py:176
  78.2 165.7 %copy-start.95 = (f32[64,64]{1,0:T(8,128)}, f32[64,64]{1,0:T(8,128)S(1)}, u32[]{:S(2)}) copy-start(f32[64,64]{1,0:T(8,128)S(1)} %fusion.134) | copy-start | bytes 49156
  264.1 13.1 %all-to-all-start.4 = ((bf16[512,1,2,4,64]{0,4,2,1,3:T(8,128)(2,1)}), bf16[512,1,2,4,64]{0,4,2,1,3:T(8,128)(2,1)}, u32[]{:S(2)}, u32[]{:S(2)}) async-start(bf16[512,1,2,4,64]{0,4,2,1,3:T(8,128)(2,1)} %copy.402), calls=%async_computation.4 | async-start | bytes 1048576 | tf_op jit(solution)/shard_map/all_to_all | solution.py:214
  277.2 9.8 all-to-all-start.9
  287.0 30.3 %all-to-all-start.5 = ((bf16[2,4,64,2048]{3,2,0,1:T(8,128)(2,1)}), bf16[2,4,64,2048]{3,2,0,1:T(8,128)(2,1)}, u32[]{:S(2)}, u32[]{:S(2)}) async-start(bf16[2,4,64,2048]{3,2,0,1:T(8,128)(2,1)} %copy.404), calls=%async_computation.5 | async-start | bytes 4194304 | tf_op jit(solution)/shard_map/all_to_all | solution.py:188
  291.5 154.1 %all-gather.8.cloned.1.call-start = ((), (), s32[]{:S(2)}) async-start(), calls=%async_computation.25 | async-start | bytes 5308416 | tf_op jit(solution)/shard_map/all_gather | solution.py:193
  318.9 30.3 %all-to-all-start.8 = ((bf16[2,4,64,2048]{3,2,0,1:T(8,128)(2,1)}), bf16[2,4,64,2048]{3,2,0,1:T(8,128)(2,1)}, u32[]{:S(2)}, u32[]{:S(2)}) async-start(bf16[2,4,64,2048]{3,2,0,1:T(8,128)(2,1)} %broadcast_in_dim.48), calls=%async_computation.8 | async-start | bytes 4194304 | tf_op jit(solution)/shard_map/all_to_all | solution.py:176
  351.8 30.2 %all-to-all-start.6 = ((bf16[2,4,64,2048]{3,2,0,1:T(8,128)(2,1)}), bf16[2,4,64,2048]{3,2,0,1:T(8,128)(2,1)}, u32[]{:S(2)}, u32[]{:S(2)}) async-start(bf16[2,4,64,2048]{3,2,0,1:T(8,128)(2,1)} %broadcast_in_dim.47), calls=%async_computation.6 | async-start | bytes 4194304 | tf_op jit(solution)/shard_map/all_to_all | solution.py:176
  356.3 358.1 %reduce-scatter.6.cloned.1.call-start = ((), (), s32[]{:S(2)}) async-start(), calls=%async_computation.27 | async-start | bytes 5308416 | tf_op jit(solution)/shard_map/reduce_scatter | solution.py:197
  460.7 304.7 %reduce-scatter.4.cloned.1.call-start = ((), (), s32[]{:S(2)}) async-start(), calls=%async_computation.26 | async-start | bytes 14155776 | tf_op jit(solution)/shard_map/reduce_scatter | solution.py:197
  470.5 30.5 %all-to-all-start.10 = ((bf16[2,4,64,2048]{3,2,0,1:T(8,128)(2,1)}), bf16[2,4,64,2048]{3,2,0,1:T(8,128)(2,1)}, u32[]{:S(2)}, u32[]{:S(2)}) async-start(bf16[2,4,64,2048]{3,2,0,1:T(8,128)(2,1)} %copy.413), calls=%async_computation.10 | async-start | bytes 4194304 | tf_op jit(solution)/shard_map/all_to_all | solution.py:188
  500.9 30.2 %all-to-all-start.11 = ((bf16[2,4,64,2048]{3,2,0,1:T(8,128)(2,1)}), bf16[2,4,64,2048]{3,2,0,1:T(8,128)(2,1)}, u32[]{:S(2)}, u32[]{:S(2)}) async-start(bf16[2,4,64,2048]{3,2,0,1:T(8,128)(2,1)} %copy.414), calls=%async_computation.11 | async-start | bytes 4194304 | tf_op jit(solution)/shard_map/all_to_all | solution.py:188
  537.1 30.2 %all-to-all-start.12 = ((bf16[2,4,64,2048]{3,2,0,1:T(8,128)(2,1)}), bf16[2,4,64,2048]{3,2,0,1:T(8,128)(2,1)}, u32[]{:S(2)}, u32[]{:S(2)}) async-start(bf16[2,4,64,2048]{3,2,0,1:T(8,128)(2,1)} %broadcast_in_dim.50), calls=%async_computation.12 | async-start | bytes 4194304 | tf_op jit(solution)/shard_map/all_to_all | solution.py:176
  572.7 18.9 %all-to-all-start.13 = ((f32[512,4,2,1,64]{0,4,2,3,1:T(8,128)}), f32[512,4,2,1,64]{0,4,2,3,1:T(8,128)}, u32[]{:S(2)}, u32[]{:S(2)}) async-start(f32[512,4,2,1,64]{0,4,2,3,1:T(8,128)} %convolution_bitcast_fusion.1), calls=%async_computation.13 | async-start | bytes 2097152 | tf_op jit(solution)/shard_map/all_to_all | solution.py:214
  577.1 400.4 %reduce-scatter.8.cloned.1.call-start = ((), (), s32[]{:S(2)}) async-start(), calls=%async_computation.28 | async-start | bytes 7077888 | tf_op jit(solution)/shard_map/reduce_scatter | solution.py:197
  786.7 30.2 %all-to-all-start.14 = ((bf16[2,4,64,2048]{3,2,0,1:T(8,128)(2,1)}), bf16[2,4,64,2048]{3,2,0,1:T(8,128)(2,1)}, u32[]{:S(2)}, u32[]{:S(2)}) async-start(bf16[2,4,64,2048]{3,2,0,1:T(8,128)(2,1)} %copy.451), calls=%async_computation.14 | async-start | bytes 4194304 | tf_op jit(solution)/shard_map/all_to_all | solution.py:188
  820.6 17.4 %all-to-all-start.17 = ((f32[32,1,2048]{2,1,0:T(1,128)}), f32[32,1,2048]{2,1,0:T(1,128)S(1)}, u32[]{:S(2)}, u32[]{:S(2)}) async-start(f32[32,1,2048]{2,1,0:T(1,128)} %copy.461), calls=%async_computation.20 | async-start | bytes 524288 | tf_op jit(solution)/shard_map/all_to_all | solution.py:214
  850.8 123.7 %all-to-all-start.15 = ((bf16[2,8,256,512]{3,2,0,1:T(8,128)(2,1)}), bf16[2,8,256,512]{3,2,0,1:T(8,128)(2,1)}, u32[]{:S(2)}, u32[]{:S(2)}) async-start(bf16[2,8,256,512]{3,2,0,1:T(8,128)(2,1)} %copy.452), calls=%async_computation.18 | async-start | bytes 8388608 | tf_op jit(solution)/shard_map/all_to_all | solution.py:207
  979.8 18.8 %all-to-all-start.16 = ((bf16[4,4,64,1,512]{4,2,0,3,1:T(8,128)(2,1)}), bf16[4,4,64,1,512]{4,2,0,3,1:T(8,128)(2,1)}, u32[]{:S(2)}, u32[]{:S(2)}) async-start(bf16[4,4,64,1,512]{4,2,0,3,1:T(8,128)(2,1)} %copy.453), calls=%async_computation.19 | async-start | bytes 2097152 | tf_op jit(solution)/shard_map/all_to_all | solution.py:214
  (171 other events, 3270.7 us)
Sparse Core Ops, SparseCore 0:
  34.0 154.5 all-gather.3
  190.7 174.6 all-gather.5
  367.6 78.0 all-gather.7
  460.8 93.5 reduce-scatter.5
  557.8 207.4 reduce-scatter.3
  771.3 145.5 reduce-scatter.7

commit v16 on v14

--- a/solution.py
+++ b/solution.py
@@ -301,7 +301,7 @@
             3, owned_rows, inner, hidden_here
         )
         lanes = hidden_here // 128 if hidden_here % 128 == 0 else 0
-        first = (lanes - lanes * 3 // 11) * 128 if lanes > 1 else hidden_here // 2
+        first = (lanes - lanes * 2 // 11) * 128 if lanes > 1 else hidden_here // 2
         bounds = ((0, first), (first, hidden_here - first))
         ff_chunks = []
         for offset, size in bounds:

time: 997 us -> 994 us (level)
  matrix products: 185 us -> 173 us
    all_gather x3, waiting for transfers between devices: 126 us -> 112 us  [fsdp_gather(): return lax.all_gather(value, FSDP_AXES, axis=axis, tiled=True)]
    unnamed x357 -> x361, local copies, waits for them, and re-layouts: 24.2 us -> 28.7 us
  transfers between devices with their start and end apart: 24 -> 24, of which waited for: 22 -> 21; matrix products, arithmetic and copies ran while one was open for 36% -> 36% of each run, Pallas kernels for 0% -> 0%
where the time goes in v16:
time: 994 us; the launch traced here: 985 us
  waiting for transfers between devices  487 us (49%)
  matrix products  173 us (17%)
  local copies, waits for them, and re-layouts  156 us (16%)
  starting transfers between devices  78 us (8%)
  other arithmetic  67.8 us (7%)
  between operations  17.5 us (2%)
    reduce_scatter x3, waiting for transfers between devices, fsdp_scatter_low(): lax.psum_scatter(value.astype(jnp.bfloat16), FSDP_AXES, scatter_dimension...  153 us
    all_gather x3, waiting for transfers between devices, fsdp_gather(): return lax.all_gather(value, FSDP_AXES, axis=axis, tiled=True)  112 us
    all_to_all x5, waiting for transfers between devices, tp_gather(): moved = lax.all_to_all(spread, TP_AXES, axis, axis, tiled=True)  90.6 us
    dot_general x42, matrix products, outer_product_result(): return jnp.einsum(form, first, second, precision=lax.Precision.HIGHEST)  77.2 us
    all_to_all x4, waiting for transfers between devices, tp_scatter_low(): moved = lax.all_to_all(staged, TP_AXES, axis, axis, tiled=True)  73.4 us
    all_to_all x9, waiting for transfers between devices, exchange(): return lax.all_to_all(value, axes, split_axis, concat_axis, tiled=True)  57.5 us
    all_to_all x9, starting transfers between devices, exchange(): return lax.all_to_all(value, axes, split_axis, concat_axis, tiled=True)  37.9 us
    dot_general x12, matrix products, back_product(): jnp.einsum('tg,fg->tf', gradient, weight, preferred_element_type=jnp.floa...  34.6 us
  transfers between devices with their start and end apart: 24, of which 21 were waited for; matrix products, arithmetic and copies ran while one was open for 36% of the time, Pallas kernels for 0%

profile of v16, /device:TPU:0, one launch (start us, length us, event | category | flops | bytes accessed | tf_op | source)
XLA Modules:
  0.0 985.3 jit_solution(4549090030086300961)
XLA Ops:
  18.3 14.3 %all-to-all-done.2 = bf16[4,64,4,512]{3,1,0,2:T(8,128)(2,1)S(1)} async-done(((bf16[4,64,4,512]{3,1,0,2:T(8,128)(2,1)}), bf16[4,64,4,512]{3,1,0,2:T(8,128)(2,1)S(1)}, u32[]{:S(2)}, u32[]{:S(2)}) %all-to-all-start.2) | async-done | bytes 1048608 | tf_op jit(solution)/shard_map/all_to_all | solution.py:205
  37.1 5.2 all_to_all.177
  47.8 5.6 all-to-all-start
  53.7 10.8 %all-to-all-done = bf16[32,2,960]{2,1,0:T(2,128)(2,1)S(1)} async-done(((bf16[32,2,960]{2,1,0:T(2,128)(2,1)}), bf16[32,2,960]{2,1,0:T(2,128)(2,1)S(1)}, u32[]{:S(2)}, u32[]{:S(2)}) %all-to-all-start) | async-done | bytes 122912 | tf_op jit(solution)/shard_map/all_to_all | solution.py:205
  80.3 23.8 %all-to-all-done.1 = bf16[2,4,64,2048]{3,2,0,1:T(8,128)(2,1)} async-done(((bf16[2,4,64,2048]{3,2,0,1:T(8,128)(2,1)}), bf16[2,4,64,2048]{3,2,0,1:T(8,128)(2,1)}, u32[]{:S(2)}, u32[]{:S(2)}) %all-to-all-start.1) | async-done | bytes 2097184 | tf_op jit(solution)/shard_map/all_to_all | solution.py:176
  106.8 81.7 %all-gather.4.cloned.1.call-done = bf16[5,2048,512]{2,1,0:T(8,128)(2,1)} async-done(((bf16[5,256,512]{2,1,0:T(8,128)(2,1)}), bf16[5,2048,512]{2,1,0:T(8,128)(2,1)}) %all-gather.4.cloned.1.call-update) | async-done | bytes 10485776 | tf_op jit(solution)/shard_map/all_gather | solution.py:193
  291.9 25.0 %all-to-all-done.5 = bf16[2,4,64,2048]{3,2,0,1:T(8,128)(2,1)} async-done(((bf16[2,4,64,2048]{3,2,0,1:T(8,128)(2,1)}), bf16[2,4,64,2048]{3,2,0,1:T(8,128)(2,1)}, u32[]{:S(2)}, u32[]{:S(2)}) %all-to-all-start.5) | async-done | bytes 2097184 | tf_op jit(solution)/shard_map/all_to_all | solution.py:188
  329.3 19.6 %all-to-all-done.8 = bf16[2,4,64,2048]{3,2,0,1:T(8,128)(2,1)} async-done(((bf16[2,4,64,2048]{3,2,0,1:T(8,128)(2,1)}), bf16[2,4,64,2048]{3,2,0,1:T(8,128)(2,1)}, u32[]{:S(2)}, u32[]{:S(2)}) %all-to-all-start.8) | async-done | bytes 2097184 | tf_op jit(solution)/shard_map/all_to_all | solution.py:176
  360.2 21.5 %all-to-all-done.6 = bf16[2,4,64,2048]{3,2,0,1:T(8,128)(2,1)} async-done(((bf16[2,4,64,2048]{3,2,0,1:T(8,128)(2,1)}), bf16[2,4,64,2048]{3,2,0,1:T(8,128)(2,1)}, u32[]{:S(2)}, u32[]{:S(2)}) %all-to-all-start.6) | async-done | bytes 2097184 | tf_op jit(solution)/shard_map/all_to_all | solution.py:176
  384.9 6.0 fusion.7
  409.2 6.4 pad_maximum_fusion
  415.7 30.4 %all-gather.8.cloned.1.call-done = bf16[3,2048,256]{2,1,0:T(8,128)(2,1)} async-done(((bf16[3,256,256]{2,1,0:T(8,128)(2,1)}), bf16[3,2048,256]{2,1,0:T(8,128)(2,1)}) %all-gather.8.cloned.1.call-update) | async-done | bytes 3145744 | tf_op jit(solution)/shard_map/all_gather | solution.py:193
  457.0 5.2 fusion.8
  470.3 5.3 fusion.3
  484.1 11.9 %all-to-all-done.10 = bf16[2,4,64,2048]{3,2,0,1:T(8,128)(2,1)} async-done(((bf16[2,4,64,2048]{3,2,0,1:T(8,128)(2,1)}), bf16[2,4,64,2048]{3,2,0,1:T(8,128)(2,1)}, u32[]{:S(2)}, u32[]{:S(2)}) %all-to-all-start.10) | async-done | bytes 2097184 | tf_op jit(solution)/shard_map/all_to_all | solution.py:188
  503.6 22.7 %all-to-all-done.11 = bf16[2,4,64,2048]{3,2,0,1:T(8,128)(2,1)} async-done(((bf16[2,4,64,2048]{3,2,0,1:T(8,128)(2,1)}), bf16[2,4,64,2048]{3,2,0,1:T(8,128)(2,1)}, u32[]{:S(2)}, u32[]{:S(2)}) %all-to-all-start.11) | async-done | bytes 2097184 | tf_op jit(solution)/shard_map/all_to_all | solution.py:188
  538.9 23.2 %all-to-all-done.12 = bf16[2,4,64,2048]{3,2,0,1:T(8,128)(2,1)} async-done(((bf16[2,4,64,2048]{3,2,0,1:T(8,128)(2,1)}), bf16[2,4,64,2048]{3,2,0,1:T(8,128)(2,1)}, u32[]{:S(2)}, u32[]{:S(2)}) %all-to-all-start.12) | async-done | bytes 2097184 | tf_op jit(solution)/shard_map/all_to_all | solution.py:176
  580.4 5.9 all-to-all-done.13
  701.0 61.1 %reduce-scatter.4.cloned.1.call-done = bf16[3,256,1152]{2,1,0:T(8,128)(2,1)} async-done(((bf16[3,2048,1152]{2,1,0:T(8,128)(2,1)}), bf16[3,256,1152]{2,1,0:T(8,128)(2,1)}) %reduce-scatter.4.cloned.1.call-update) | async-done | bytes 1769488 | tf_op jit(solution)/shard_map/reduce_scatter | solution.py:197
  786.0 7.7 dynamic_update_slice.7
  795.5 13.8 %all-to-all-done.14 = bf16[2,4,64,2048]{3,2,0,1:T(8,128)(2,1)} async-done(((bf16[2,4,64,2048]{3,2,0,1:T(8,128)(2,1)}), bf16[2,4,64,2048]{3,2,0,1:T(8,128)(2,1)}, u32[]{:S(2)}, u32[]{:S(2)}) %all-to-all-start.14) | async-done | bytes 2097184 | tf_op jit(solution)/shard_map/all_to_all | solution.py:188
  823.7 12.5 %all-to-all-done.16 = f32[32,1,2048]{2,1,0:T(1,128)S(1)} async-done(((f32[32,1,2048]{2,1,0:T(1,128)}), f32[32,1,2048]{2,1,0:T(1,128)S(1)}, u32[]{:S(2)}, u32[]{:S(2)}) %all-to-all-start.16) | async-done | bytes 262176 | tf_op jit(solution)/shard_map/all_to_all | solution.py:205
  858.0 91.9 %reduce-scatter.8.cloned.1.call-done = bf16[5,256,512]{2,1,0:T(8,128)(2,1)} async-done(((bf16[5,2048,512]{2,1,0:T(8,128)(2,1)}), bf16[5,256,512]{2,1,0:T(8,128)(2,1)}) %reduce-scatter.8.cloned.1.call-update) | async-done | bytes 1310736 | tf_op jit(solution)/shard_map/reduce_scatter | solution.py:197
  964.3 6.7 all-to-all-done.15
  (654 shorter events, 449.6 us)
Async XLA Ops:
  13.9 18.7 %all-to-all-start.2 = ((bf16[4,64,4,512]{3,1,0,2:T(8,128)(2,1)}), bf16[4,64,4,512]{3,1,0,2:T(8,128)(2,1)S(1)}, u32[]{:S(2)}, u32[]{:S(2)}) async-start(bf16[4,64,4,512]{3,1,0,2:T(8,128)(2,1)} %copy.379), calls=%async_computation.2 | async-start | bytes 2097152 | tf_op jit(solution)/shard_map/all_to_all | solution.py:205
  18.1 170.4 %all-gather.4.cloned.1.call-start = ((), (), s32[]{:S(2)}) async-start(), calls=%async_computation.22 | async-start | bytes 11796480 | tf_op jit(solution)/shard_map/all_gather | solution.py:193
  33.9 351.1 %all-gather.6.cloned.1.call-start = ((), (), s32[]{:S(2)}) async-start(), calls=%async_computation.23 | async-start | bytes 15925248 | tf_op jit(solution)/shard_map/all_gather | solution.py:193
  47.8 16.6 %all-to-all-start = ((bf16[32,2,960]{2,1,0:T(2,128)(2,1)}), bf16[32,2,960]{2,1,0:T(2,128)(2,1)S(1)}, u32[]{:S(2)}, u32[]{:S(2)}) async-start(bf16[32,2,960]{2,1,0:T(2,128)(2,1)} %reshape.743), calls=%async_computation | async-start | bytes 262144 | tf_op jit(solution)/shard_map/all_to_all | solution.py:205
  65.1 6.9 all-to-all-start.3
  73.5 30.5 %all-to-all-start.1 = ((bf16[2,4,64,2048]{3,2,0,1:T(8,128)(2,1)}), bf16[2,4,64,2048]{3,2,0,1:T(8,128)(2,1)}, u32[]{:S(2)}, u32[]{:S(2)}) async-start(bf16[2,4,64,2048]{3,2,0,1:T(8,128)(2,1)} %broadcast_in_dim.43), calls=%async_computation.1 | async-start | bytes 4194304 | tf_op jit(solution)/shard_map/all_to_all | solution.py:176
  264.0 13.3 %all-to-all-start.4 = ((bf16[512,1,2,4,64]{0,4,2,1,3:T(8,128)(2,1)}), bf16[512,1,2,4,64]{0,4,2,1,3:T(8,128)(2,1)}, u32[]{:S(2)}, u32[]{:S(2)}) async-start(bf16[512,1,2,4,64]{0,4,2,1,3:T(8,128)(2,1)} %copy.400), calls=%async_computation.4 | async-start | bytes 1048576 | tf_op jit(solution)/shard_map/all_to_all | solution.py:205
  277.4 9.0 all-to-all-start.9
  286.4 30.6 %all-to-all-start.5 = ((bf16[2,4,64,2048]{3,2,0,1:T(8,128)(2,1)}), bf16[2,4,64,2048]{3,2,0,1:T(8,128)(2,1)}, u32[]{:S(2)}, u32[]{:S(2)}) async-start(bf16[2,4,64,2048]{3,2,0,1:T(8,128)(2,1)} %copy.402), calls=%async_computation.5 | async-start | bytes 4194304 | tf_op jit(solution)/shard_map/all_to_all | solution.py:188
  318.6 30.3 %all-to-all-start.8 = ((bf16[2,4,64,2048]{3,2,0,1:T(8,128)(2,1)}), bf16[2,4,64,2048]{3,2,0,1:T(8,128)(2,1)}, u32[]{:S(2)}, u32[]{:S(2)}) async-start(bf16[2,4,64,2048]{3,2,0,1:T(8,128)(2,1)} %broadcast_in_dim.48), calls=%async_computation.8 | async-start | bytes 4194304 | tf_op jit(solution)/shard_map/all_to_all | solution.py:176
  351.6 30.2 %all-to-all-start.6 = ((bf16[2,4,64,2048]{3,2,0,1:T(8,128)(2,1)}), bf16[2,4,64,2048]{3,2,0,1:T(8,128)(2,1)}, u32[]{:S(2)}, u32[]{:S(2)}) async-start(bf16[2,4,64,2048]{3,2,0,1:T(8,128)(2,1)} %broadcast_in_dim.47), calls=%async_computation.6 | async-start | bytes 4194304 | tf_op jit(solution)/shard_map/all_to_all | solution.py:176
  356.0 90.0 %all-gather.8.cloned.1.call-start = ((), (), s32[]{:S(2)}) async-start(), calls=%async_computation.24 | async-start | bytes 3538944 | tf_op jit(solution)/shard_map/all_gather | solution.py:193
  357.0 344.0 %reduce-scatter.6.cloned.1.call-start = ((), (), s32[]{:S(2)}) async-start(), calls=%async_computation.26 | async-start | bytes 3538944 | tf_op jit(solution)/shard_map/reduce_scatter | solution.py:197
  456.4 305.7 %reduce-scatter.4.cloned.1.call-start = ((), (), s32[]{:S(2)}) async-start(), calls=%async_computation.25 | async-start | bytes 15925248 | tf_op jit(solution)/shard_map/reduce_scatter | solution.py:197
  465.6 30.4 %all-to-all-start.10 = ((bf16[2,4,64,2048]{3,2,0,1:T(8,128)(2,1)}), bf16[2,4,64,2048]{3,2,0,1:T(8,128)(2,1)}, u32[]{:S(2)}, u32[]{:S(2)}) async-start(bf16[2,4,64,2048]{3,2,0,1:T(8,128)(2,1)} %copy.411), calls=%async_computation.10 | async-start | bytes 4194304 | tf_op jit(solution)/shard_map/all_to_all | solution.py:188
  496.0 30.2 %all-to-all-start.11 = ((bf16[2,4,64,2048]{3,2,0,1:T(8,128)(2,1)}), bf16[2,4,64,2048]{3,2,0,1:T(8,128)(2,1)}, u32[]{:S(2)}, u32[]{:S(2)}) async-start(bf16[2,4,64,2048]{3,2,0,1:T(8,128)(2,1)} %copy.412), calls=%async_computation.11 | async-start | bytes 4194304 | tf_op jit(solution)/shard_map/all_to_all | solution.py:188
  531.9 30.2 %all-to-all-start.12 = ((bf16[2,4,64,2048]{3,2,0,1:T(8,128)(2,1)}), bf16[2,4,64,2048]{3,2,0,1:T(8,128)(2,1)}, u32[]{:S(2)}, u32[]{:S(2)}) async-start(bf16[2,4,64,2048]{3,2,0,1:T(8,128)(2,1)} %broadcast_in_dim.50), calls=%async_computation.12 | async-start | bytes 4194304 | tf_op jit(solution)/shard_map/all_to_all | solution.py:176
  567.4 18.9 %all-to-all-start.13 = ((f32[512,4,2,1,64]{0,4,2,3,1:T(8,128)}), f32[512,4,2,1,64]{0,4,2,3,1:T(8,128)}, u32[]{:S(2)}, u32[]{:S(2)}) async-start(f32[512,4,2,1,64]{0,4,2,3,1:T(8,128)} %convolution_bitcast_fusion.1), calls=%async_computation.13 | async-start | bytes 2097152 | tf_op jit(solution)/shard_map/all_to_all | solution.py:205
  571.8 378.1 %reduce-scatter.8.cloned.1.call-start = ((), (), s32[]{:S(2)}) async-start(), calls=%async_computation.27 | async-start | bytes 11796480 | tf_op jit(solution)/shard_map/reduce_scatter | solution.py:197
  779.1 30.2 %all-to-all-start.14 = ((bf16[2,4,64,2048]{3,2,0,1:T(8,128)(2,1)}), bf16[2,4,64,2048]{3,2,0,1:T(8,128)(2,1)}, u32[]{:S(2)}, u32[]{:S(2)}) async-start(bf16[2,4,64,2048]{3,2,0,1:T(8,128)(2,1)} %copy.449), calls=%async_computation.14 | async-start | bytes 4194304 | tf_op jit(solution)/shard_map/all_to_all | solution.py:188
  816.6 19.6 %all-to-all-start.16 = ((f32[32,1,2048]{2,1,0:T(1,128)}), f32[32,1,2048]{2,1,0:T(1,128)S(1)}, u32[]{:S(2)}, u32[]{:S(2)}) async-start(f32[32,1,2048]{2,1,0:T(1,128)} %copy.458), calls=%async_computation.19 | async-start | bytes 524288 | tf_op jit(solution)/shard_map/all_to_all | solution.py:205
  841.7 6.8 all-to-all-start.17
  848.5 5.9 all-to-all-start.18
  952.3 18.8 %all-to-all-start.15 = ((bf16[4,4,64,1,512]{4,2,0,3,1:T(8,128)(2,1)}), bf16[4,4,64,1,512]{4,2,0,3,1:T(8,128)(2,1)}, u32[]{:S(2)}, u32[]{:S(2)}) async-start(bf16[4,4,64,1,512]{4,2,0,3,1:T(8,128)(2,1)} %copy.450), calls=%async_computation.18 | async-start | bytes 2097152 | tf_op jit(solution)/shard_map/all_to_all | solution.py:205
  (175 other events, 3372.2 us)
Sparse Core Ops, SparseCore 0:
  34.0 154.4 all-gather.3
  190.7 193.7 all-gather.5
  387.3 58.6 all-gather.7
  456.5 73.4 reduce-scatter.5
  533.5 228.5 reduce-scatter.3
  765.5 184.3 reduce-scatter.7

commit v17 on v16

--- a/solution.py
+++ b/solution.py
@@ -395,14 +395,23 @@
         value_low = value_back.astype(jnp.bfloat16)
         gate_low = gate_lin_back.astype(jnp.bfloat16)
         beta_low = beta_back.astype(jnp.bfloat16)
-        mixer_sums = jnp.stack(
+        column_sums = jnp.stack(
             [
                 left_product(normed_group, query_low),
                 left_product(normed_group, key_low),
                 left_product(normed_group, value_low),
                 left_product(normed_group, gate_low),
-                left_product(gated_rows, mixed_group).reshape(width, cols_here),
             ]
+        ).astype(jnp.bfloat16)
+        column_rows = exchange(
+            column_sums.reshape(4, fsdp, tp, rows, 1, cols_here), TP_AXES, 2, 4
+        ).reshape(4, fsdp * rows, width)
+        mixer_sums = jnp.concatenate(
+            [
+                column_rows,
+                left_product(gated_rows, mixed_group).astype(jnp.bfloat16)[None],
+            ],
+            axis=0,
         )
         ff_reduced, mixer_sums = lax.optimization_barrier((ff_reduced, mixer_sums))
         mixer_reduced = fsdp_scatter_low(mixer_sums, 1)
@@ -450,11 +459,10 @@
         )
         small_width = small_terms.shape[1]
         small_out = jnp.sum(exchange(small_terms, ALL_AXES, 0, 0), axis=0)
-        column_back = exchange(
-            mixer_reduced[:4].reshape(4, tp, rows, 1, cols_here), TP_AXES, 1, 3
-        ).reshape(4, rows, width).astype(jnp.float32)
-        query_grad, key_grad, value_grad, gate_grad = (column_back[index] for index in range(4))
-        out_grad = mixer_reduced[4].reshape(rows, width).astype(jnp.float32)
+        mixer_grads = mixer_reduced.astype(jnp.float32)
+        query_grad, key_grad, value_grad, gate_grad, out_grad = (
+            mixer_grads[index] for index in range(5)
+        )
         conv_grad = small_out[:conv_size].reshape(conv_weight.shape)
         beta_grad = small_out[conv_size : conv_size + beta_size].reshape(beta_weight.shape)
         mixer_gain_grad = small_out[conv_size + beta_size : conv_size + beta_size + rows]

time: 994 us -> 1050 us (1.056)
  local copies, waits for them, and re-layouts: 156 us -> 183 us
  waiting for transfers between devices: 487 us -> 506 us
    all_to_all x9, waiting for transfers between devices: 57.5 us -> 138 us  [exchange(): return lax.all_to_all(value, axes, split_axis, concat_axis, tiled=True)]
    reduce_scatter x3, waiting for transfers between devices: 153 us -> 85.9 us  [fsdp_scatter_low(): lax.psum_scatter(value.astype(jnp.bfloat16), FSDP_AXES, scatter_dimension...]
    reshape x1, local copies, waits for them, and re-layouts: 1.17 us -> 14.3 us  [on_device(): column_rows = exchange(column_sums.reshape(4, fsdp, tp, rows, 1, cols_her...]
    all_to_all x7 -> x8, local copies, waits for them, and re-layouts: 7.85 us -> 19.1 us  [exchange(): return lax.all_to_all(value, axes, split_axis, concat_axis, tiled=True)]
    unnamed x361 -> x351, local copies, waits for them, and re-layouts: 28.7 us -> 25.7 us
  transfers between devices with their start and end apart: 24 -> 24, of which waited for: 21 -> 21; matrix products, arithmetic and copies ran while one was open for 36% -> 38% of each run, Pallas kernels for 0% -> 0%
where the time goes in v17:
time: 1050 us; the launch traced here: 1040 us
  waiting for transfers between devices  506 us (48%)
  local copies, waits for them, and re-layouts  183 us (17%)
  matrix products  171 us (16%)
  starting transfers between devices  79 us (8%)
  other arithmetic  75.7 us (7%)
  between operations  17.6 us (2%)
    all_to_all x9, waiting for transfers between devices, exchange(): return lax.all_to_all(value, axes, split_axis, concat_axis, tiled=True)  138 us
    all_gather x3, waiting for transfers between devices, fsdp_gather(): return lax.all_gather(value, FSDP_AXES, axis=axis, tiled=True)  115 us
    all_to_all x5, waiting for transfers between devices, tp_gather(): moved = lax.all_to_all(spread, TP_AXES, axis, axis, tiled=True)  88.7 us
    reduce_scatter x3, waiting for transfers between devices, fsdp_scatter_low(): lax.psum_scatter(value.astype(jnp.bfloat16), FSDP_AXES, scatter_dimension...  85.9 us
    dot_general x42, matrix products, outer_product_result(): return jnp.einsum(form, first, second, precision=lax.Precision.HIGHEST)  78.8 us
    all_to_all x4, waiting for transfers between devices, tp_scatter_low(): moved = lax.all_to_all(staged, TP_AXES, axis, axis, tiled=True)  76.9 us
    all_to_all x9, starting transfers between devices, exchange(): return lax.all_to_all(value, axes, split_axis, concat_axis, tiled=True)  38.7 us
    dot_general x12, matrix products, back_product(): jnp.einsum('tg,fg->tf', gradient, weight, preferred_element_type=jnp.floa...  34.7 us
  transfers between devices with their start and end apart: 24, of which 21 were waited for; matrix products, arithmetic and copies ran while one was open for 38% of the time, Pallas kernels for 0%

profile of v17, /device:TPU:0, one launch (start us, length us, event | category | flops | bytes accessed | tf_op | source)
XLA Modules:
  0.0 1036.2 jit_solution(8597009537587788689)
XLA Ops:
  18.3 14.3 %all-to-all-done.2 = bf16[4,64,4,512]{3,1,0,2:T(8,128)(2,1)S(1)} async-done(((bf16[4,64,4,512]{3,1,0,2:T(8,128)(2,1)}), bf16[4,64,4,512]{3,1,0,2:T(8,128)(2,1)S(1)}, u32[]{:S(2)}, u32[]{:S(2)}) %all-to-all-start.2) | async-done | bytes 1048608 | tf_op jit(solution)/shard_map/all_to_all | solution.py:205
  47.9 5.6 all-to-all-start
  53.7 10.7 %all-to-all-done = bf16[32,2,960]{2,1,0:T(2,128)(2,1)S(1)} async-done(((bf16[32,2,960]{2,1,0:T(2,128)(2,1)}), bf16[32,2,960]{2,1,0:T(2,128)(2,1)S(1)}, u32[]{:S(2)}, u32[]{:S(2)}) %all-to-all-start) | async-done | bytes 122912 | tf_op jit(solution)/shard_map/all_to_all | solution.py:205
  80.3 23.8 %all-to-all-done.1 = bf16[2,4,64,2048]{3,2,0,1:T(8,128)(2,1)} async-done(((bf16[2,4,64,2048]{3,2,0,1:T(8,128)(2,1)}), bf16[2,4,64,2048]{3,2,0,1:T(8,128)(2,1)}, u32[]{:S(2)}, u32[]{:S(2)}) %all-to-all-start.1) | async-done | bytes 2097184 | tf_op jit(solution)/shard_map/all_to_all | solution.py:176
  106.8 81.7 %all-gather.4.cloned.1.call-done = bf16[5,2048,512]{2,1,0:T(8,128)(2,1)} async-done(((bf16[5,256,512]{2,1,0:T(8,128)(2,1)}), bf16[5,2048,512]{2,1,0:T(8,128)(2,1)}) %all-gather.4.cloned.1.call-update) | async-done | bytes 10485776 | tf_op jit(solution)/shard_map/all_gather | solution.py:193
  288.6 25.0 %all-to-all-done.5 = bf16[2,4,64,2048]{3,2,0,1:T(8,128)(2,1)} async-done(((bf16[2,4,64,2048]{3,2,0,1:T(8,128)(2,1)}), bf16[2,4,64,2048]{3,2,0,1:T(8,128)(2,1)}, u32[]{:S(2)}, u32[]{:S(2)}) %all-to-all-start.5) | async-done | bytes 2097184 | tf_op jit(solution)/shard_map/all_to_all | solution.py:188
  326.0 19.6 %all-to-all-done.8 = bf16[2,4,64,2048]{3,2,0,1:T(8,128)(2,1)} async-done(((bf16[2,4,64,2048]{3,2,0,1:T(8,128)(2,1)}), bf16[2,4,64,2048]{3,2,0,1:T(8,128)(2,1)}, u32[]{:S(2)}, u32[]{:S(2)}) %all-to-all-start.8) | async-done | bytes 2097184 | tf_op jit(solution)/shard_map/all_to_all | solution.py:176
  356.9 21.5 %all-to-all-done.6 = bf16[2,4,64,2048]{3,2,0,1:T(8,128)(2,1)} async-done(((bf16[2,4,64,2048]{3,2,0,1:T(8,128)(2,1)}), bf16[2,4,64,2048]{3,2,0,1:T(8,128)(2,1)}, u32[]{:S(2)}, u32[]{:S(2)}) %all-to-all-start.6) | async-done | bytes 2097184 | tf_op jit(solution)/shard_map/all_to_all | solution.py:176
  384.6 6.0 fusion.7
  408.9 6.4 pad_maximum_fusion
  415.3 30.8 %all-gather.8.cloned.1.call-done = bf16[3,2048,256]{2,1,0:T(8,128)(2,1)} async-done(((bf16[3,256,256]{2,1,0:T(8,128)(2,1)}), bf16[3,2048,256]{2,1,0:T(8,128)(2,1)}) %all-gather.8.cloned.1.call-update) | async-done | bytes 3145744 | tf_op jit(solution)/shard_map/all_gather | solution.py:193
  483.7 11.9 %all-to-all-done.10 = bf16[2,4,64,2048]{3,2,0,1:T(8,128)(2,1)} async-done(((bf16[2,4,64,2048]{3,2,0,1:T(8,128)(2,1)}), bf16[2,4,64,2048]{3,2,0,1:T(8,128)(2,1)}, u32[]{:S(2)}, u32[]{:S(2)}) %all-to-all-start.10) | async-done | bytes 2097184 | tf_op jit(solution)/shard_map/all_to_all | solution.py:188
  503.7 22.1 %all-to-all-done.11 = bf16[2,4,64,2048]{3,2,0,1:T(8,128)(2,1)} async-done(((bf16[2,4,64,2048]{3,2,0,1:T(8,128)(2,1)}), bf16[2,4,64,2048]{3,2,0,1:T(8,128)(2,1)}, u32[]{:S(2)}, u32[]{:S(2)}) %all-to-all-start.11) | async-done | bytes 2097184 | tf_op jit(solution)/shard_map/all_to_all | solution.py:188
  540.3 21.4 %all-to-all-done.12 = bf16[2,4,64,2048]{3,2,0,1:T(8,128)(2,1)} async-done(((bf16[2,4,64,2048]{3,2,0,1:T(8,128)(2,1)}), bf16[2,4,64,2048]{3,2,0,1:T(8,128)(2,1)}, u32[]{:S(2)}, u32[]{:S(2)}) %all-to-all-start.12) | async-done | bytes 2097184 | tf_op jit(solution)/shard_map/all_to_all | solution.py:176
  579.9 6.3 all-to-all-done.13
  700.3 8.2 copy.471
  708.6 5.6 all-to-all-start.15
  718.7 88.7 %all-to-all-done.15 = bf16[4,8,4,64,1,512]{5,3,1,4,0,2:T(8,128)(2,1)} async-done(((bf16[4,8,4,64,1,512]{5,3,1,4,0,2:T(8,128)(2,1)}), bf16[4,8,4,64,1,512]{5,3,1,4,0,2:T(8,128)(2,1)}, u32[]{:S(2)}, u32[]{:S(2)}) %all-to-all-start.15) | async-done | bytes 8388640 | tf_op jit(solution)/shard_map/all_to_all | solution.py:205
  807.4 11.1 %copy.472 = bf16[4,8,1,64,4,1,512]{6,4,3,1,0,5,2:T(4,128)(2,1)} copy(bf16[4,8,1,64,4,1,512]{6,3,1,0,4,5,2:T(8,128)(2,1)} %bitcast.98) | data formatting | bytes 16777216 | tf_op jit(solution)/shard_map/all_to_all | solution.py:205
  818.5 14.3 %reshape.784 = bf16[4,512,2048]{2,1,0:T(8,128)(2,1)} reshape(bf16[4,8,1,64,4,1,512]{6,4,3,1,0,5,2:T(4,128)(2,1)} %copy.472) | data formatting | bytes 16777216 | tf_op jit(solution)/shard_map/reshape | solution.py:408
  832.8 8.9 pad_maximum_fusion.1
  871.1 17.9 %all-to-all-done.14 = bf16[2,4,64,2048]{3,2,0,1:T(8,128)(2,1)} async-done(((bf16[2,4,64,2048]{3,2,0,1:T(8,128)(2,1)}), bf16[2,4,64,2048]{3,2,0,1:T(8,128)(2,1)}, u32[]{:S(2)}, u32[]{:S(2)}) %all-to-all-start.14) | async-done | bytes 2097184 | tf_op jit(solution)/shard_map/all_to_all | solution.py:188
  903.1 12.5 %all-to-all-done.16 = f32[32,1,2048]{2,1,0:T(1,128)S(1)} async-done(((f32[32,1,2048]{2,1,0:T(1,128)}), f32[32,1,2048]{2,1,0:T(1,128)S(1)}, u32[]{:S(2)}, u32[]{:S(2)}) %all-to-all-start.16) | async-done | bytes 262176 | tf_op jit(solution)/shard_map/all_to_all | solution.py:205
  939.9 85.9 %reduce-scatter.8.cloned.1.call-done = bf16[5,64,2048]{2,1,0:T(8,128)(2,1)} async-done(((bf16[5,512,2048]{2,1,0:T(8,128)(2,1)}), bf16[5,64,2048]{2,1,0:T(8,128)(2,1)}) %reduce-scatter.8.cloned.1.call-update) | async-done | bytes 1310736 | tf_op jit(solution)/shard_map/reduce_scatter | solution.py:197
  (639 shorter events, 458.3 us)
Async XLA Ops:
  13.9 18.7 %all-to-all-start.2 = ((bf16[4,64,4,512]{3,1,0,2:T(8,128)(2,1)}), bf16[4,64,4,512]{3,1,0,2:T(8,128)(2,1)S(1)}, u32[]{:S(2)}, u32[]{:S(2)}) async-start(bf16[4,64,4,512]{3,1,0,2:T(8,128)(2,1)} %copy.395), calls=%async_computation.2 | async-start | bytes 2097152 | tf_op jit(solution)/shard_map/all_to_all | solution.py:205
  18.1 170.4 %all-gather.4.cloned.1.call-start = ((), (), s32[]{:S(2)}) async-start(), calls=%async_computation.22 | async-start | bytes 11796480 | tf_op jit(solution)/shard_map/all_gather | solution.py:193
  33.9 350.7 %all-gather.6.cloned.1.call-start = ((), (), s32[]{:S(2)}) async-start(), calls=%async_computation.23 | async-start | bytes 15925248 | tf_op jit(solution)/shard_map/all_gather | solution.py:193
  47.9 16.6 %all-to-all-start = ((bf16[32,2,960]{2,1,0:T(2,128)(2,1)}), bf16[32,2,960]{2,1,0:T(2,128)(2,1)S(1)}, u32[]{:S(2)}, u32[]{:S(2)}) async-start(bf16[32,2,960]{2,1,0:T(2,128)(2,1)} %reshape.826), calls=%async_computation | async-start | bytes 262144 | tf_op jit(solution)/shard_map/all_to_all | solution.py:205
  65.1 6.9 all-to-all-start.3
  73.6 30.6 %all-to-all-start.1 = ((bf16[2,4,64,2048]{3,2,0,1:T(8,128)(2,1)}), bf16[2,4,64,2048]{3,2,0,1:T(8,128)(2,1)}, u32[]{:S(2)}, u32[]{:S(2)}) async-start(bf16[2,4,64,2048]{3,2,0,1:T(8,128)(2,1)} %broadcast_in_dim.45), calls=%async_computation.1 | async-start | bytes 4194304 | tf_op jit(solution)/shard_map/all_to_all | solution.py:176
  261.1 13.0 %all-to-all-start.4 = ((bf16[512,1,2,4,64]{0,4,2,1,3:T(8,128)(2,1)}), bf16[512,1,2,4,64]{0,4,2,1,3:T(8,128)(2,1)}, u32[]{:S(2)}, u32[]{:S(2)}) async-start(bf16[512,1,2,4,64]{0,4,2,1,3:T(8,128)(2,1)} %copy.416), calls=%async_computation.4 | async-start | bytes 1048576 | tf_op jit(solution)/shard_map/all_to_all | solution.py:205
  274.2 9.0 all-to-all-start.9
  283.2 30.3 %all-to-all-start.5 = ((bf16[2,4,64,2048]{3,2,0,1:T(8,128)(2,1)}), bf16[2,4,64,2048]{3,2,0,1:T(8,128)(2,1)}, u32[]{:S(2)}, u32[]{:S(2)}) async-start(bf16[2,4,64,2048]{3,2,0,1:T(8,128)(2,1)} %copy.418), calls=%async_computation.5 | async-start | bytes 4194304 | tf_op jit(solution)/shard_map/all_to_all | solution.py:188
  315.2 30.3 %all-to-all-start.8 = ((bf16[2,4,64,2048]{3,2,0,1:T(8,128)(2,1)}), bf16[2,4,64,2048]{3,2,0,1:T(8,128)(2,1)}, u32[]{:S(2)}, u32[]{:S(2)}) async-start(bf16[2,4,64,2048]{3,2,0,1:T(8,128)(2,1)} %broadcast_in_dim.50), calls=%async_computation.8 | async-start | bytes 4194304 | tf_op jit(solution)/shard_map/all_to_all | solution.py:176
  348.2 30.2 %all-to-all-start.6 = ((bf16[2,4,64,2048]{3,2,0,1:T(8,128)(2,1)}), bf16[2,4,64,2048]{3,2,0,1:T(8,128)(2,1)}, u32[]{:S(2)}, u32[]{:S(2)}) async-start(bf16[2,4,64,2048]{3,2,0,1:T(8,128)(2,1)} %broadcast_in_dim.49), calls=%async_computation.6 | async-start | bytes 4194304 | tf_op jit(solution)/shard_map/all_to_all | solution.py:176
  352.6 93.4 %all-gather.8.cloned.1.call-start = ((), (), s32[]{:S(2)}) async-start(), calls=%async_computation.24 | async-start | bytes 3538944 | tf_op jit(solution)/shard_map/all_gather | solution.py:193
  353.6 488.1 %reduce-scatter.6.cloned.1.call-start = ((), (), s32[]{:S(2)}) async-start(), calls=%async_computation.26 | async-start | bytes 3538944 | tf_op jit(solution)/shard_map/reduce_scatter | solution.py:197
  465.2 30.4 %all-to-all-start.10 = ((bf16[2,4,64,2048]{3,2,0,1:T(8,128)(2,1)}), bf16[2,4,64,2048]{3,2,0,1:T(8,128)(2,1)}, u32[]{:S(2)}, u32[]{:S(2)}) async-start(bf16[2,4,64,2048]{3,2,0,1:T(8,128)(2,1)} %copy.427), calls=%async_computation.10 | async-start | bytes 4194304 | tf_op jit(solution)/shard_map/all_to_all | solution.py:188
  495.6 30.2 %all-to-all-start.11 = ((bf16[2,4,64,2048]{3,2,0,1:T(8,128)(2,1)}), bf16[2,4,64,2048]{3,2,0,1:T(8,128)(2,1)}, u32[]{:S(2)}, u32[]{:S(2)}) async-start(bf16[2,4,64,2048]{3,2,0,1:T(8,128)(2,1)} %copy.428), calls=%async_computation.11 | async-start | bytes 4194304 | tf_op jit(solution)/shard_map/all_to_all | solution.py:188
  500.1 341.7 %reduce-scatter.4.cloned.1.call-start = ((), (), s32[]{:S(2)}) async-start(), calls=%async_computation.25 | async-start | bytes 15925248 | tf_op jit(solution)/shard_map/reduce_scatter | solution.py:197
  531.5 30.2 %all-to-all-start.12 = ((bf16[2,4,64,2048]{3,2,0,1:T(8,128)(2,1)}), bf16[2,4,64,2048]{3,2,0,1:T(8,128)(2,1)}, u32[]{:S(2)}, u32[]{:S(2)}) async-start(bf16[2,4,64,2048]{3,2,0,1:T(8,128)(2,1)} %broadcast_in_dim.52), calls=%async_computation.12 | async-start | bytes 4194304 | tf_op jit(solution)/shard_map/all_to_all | solution.py:176
  567.3 18.9 %all-to-all-start.13 = ((f32[512,4,2,1,64]{0,4,2,3,1:T(8,128)}), f32[512,4,2,1,64]{0,4,2,3,1:T(8,128)}, u32[]{:S(2)}, u32[]{:S(2)}) async-start(f32[512,4,2,1,64]{0,4,2,3,1:T(8,128)} %convolution_bitcast_fusion.1), calls=%async_computation.13 | async-start | bytes 2097152 | tf_op jit(solution)/shard_map/all_to_all | solution.py:205
  708.6 98.8 %all-to-all-start.15 = ((bf16[4,8,4,64,1,512]{5,3,1,4,0,2:T(8,128)(2,1)}), bf16[4,8,4,64,1,512]{5,3,1,4,0,2:T(8,128)(2,1)}, u32[]{:S(2)}, u32[]{:S(2)}) async-start(bf16[4,8,4,64,1,512]{5,3,1,4,0,2:T(8,128)(2,1)} %copy.471), calls=%async_computation.17 | async-start | bytes 16777216 | tf_op jit(solution)/shard_map/all_to_all | solution.py:205
  714.2 311.6 %reduce-scatter.8.cloned.1.call-start = ((), (), s32[]{:S(2)}) async-start(), calls=%async_computation.27 | async-start | bytes 11796480 | tf_op jit(solution)/shard_map/reduce_scatter | solution.py:197
  858.4 30.6 %all-to-all-start.14 = ((bf16[2,4,64,2048]{3,2,0,1:T(8,128)(2,1)}), bf16[2,4,64,2048]{3,2,0,1:T(8,128)(2,1)}, u32[]{:S(2)}, u32[]{:S(2)}) async-start(bf16[2,4,64,2048]{3,2,0,1:T(8,128)(2,1)} %copy.465), calls=%async_computation.14 | async-start | bytes 4194304 | tf_op jit(solution)/shard_map/all_to_all | solution.py:188
  896.4 19.3 %all-to-all-start.16 = ((f32[32,1,2048]{2,1,0:T(1,128)}), f32[32,1,2048]{2,1,0:T(1,128)S(1)}, u32[]{:S(2)}, u32[]{:S(2)}) async-start(f32[32,1,2048]{2,1,0:T(1,128)} %copy.476), calls=%async_computation.19 | async-start | bytes 524288 | tf_op jit(solution)/shard_map/all_to_all | solution.py:205
  921.1 6.8 all-to-all-start.17
  927.9 5.9 all-to-all-start.18
  (171 other events, 3461.9 us)
Sparse Core Ops, SparseCore 0:
  34.0 154.4 all-gather.3
  190.7 193.7 all-gather.5
  387.3 58.6 all-gather.7
  456.5 73.4 reduce-scatter.5
  533.6 228.5 reduce-scatter.3
  841.9 183.8 reduce-scatter.7

commit v18 on v16

--- a/solution.py
+++ b/solution.py
@@ -301,7 +301,7 @@
             3, owned_rows, inner, hidden_here
         )
         lanes = hidden_here // 128 if hidden_here % 128 == 0 else 0
-        first = (lanes - lanes * 2 // 11) * 128 if lanes > 1 else hidden_here // 2
+        first = (lanes - 1) * 128 if lanes > 1 else hidden_here // 2
         bounds = ((0, first), (first, hidden_here - first))
         ff_chunks = []
         for offset, size in bounds:

time: 994 us -> 1010 us (1.016)
  waiting for transfers between devices: 487 us -> 511 us
    reduce_scatter x3, waiting for transfers between devices: 153 us -> 167 us  [fsdp_scatter_low(): lax.psum_scatter(value.astype(jnp.bfloat16), FSDP_AXES, scatter_dimension...]
    unnamed x361 -> x359, local copies, waits for them, and re-layouts: 28.7 us -> 27.3 us
  transfers between devices with their start and end apart: 24 -> 24, of which waited for: 21 -> 21; matrix products, arithmetic and copies ran while one was open for 36% -> 35% of each run, Pallas kernels for 0% -> 0%
where the time goes in v18:
time: 1010 us; the launch traced here: 999 us
  waiting for transfers between devices  511 us (51%)
  matrix products  172 us (17%)
  local copies, waits for them, and re-layouts  152 us (15%)
  starting transfers between devices  75.4 us (7%)
  other arithmetic  65.2 us (6%)
  between operations  17.5 us (2%)
    reduce_scatter x3, waiting for transfers between devices, fsdp_scatter_low(): lax.psum_scatter(value.astype(jnp.bfloat16), FSDP_AXES, scatter_dimension...  167 us
    all_gather x3, waiting for transfers between devices, fsdp_gather(): return lax.all_gather(value, FSDP_AXES, axis=axis, tiled=True)  117 us
    all_to_all x5, waiting for transfers between devices, tp_gather(): moved = lax.all_to_all(spread, TP_AXES, axis, axis, tiled=True)  94.2 us
    dot_general x42, matrix products, outer_product_result(): return jnp.einsum(form, first, second, precision=lax.Precision.HIGHEST)  77.2 us
    all_to_all x4, waiting for transfers between devices, tp_scatter_low(): moved = lax.all_to_all(staged, TP_AXES, axis, axis, tiled=True)  75.3 us
    all_to_all x9, waiting for transfers between devices, exchange(): return lax.all_to_all(value, axes, split_axis, concat_axis, tiled=True)  57.2 us
    all_to_all x9, starting transfers between devices, exchange(): return lax.all_to_all(value, axes, split_axis, concat_axis, tiled=True)  37 us
    dot_general x12, matrix products, back_product(): jnp.einsum('tg,fg->tf', gradient, weight, preferred_element_type=jnp.floa...  34 us
  transfers between devices with their start and end apart: 24, of which 21 were waited for; matrix products, arithmetic and copies ran while one was open for 35% of the time, Pallas kernels for 0%

profile of v18, /device:TPU:0, one launch (start us, length us, event | category | flops | bytes accessed | tf_op | source)
XLA Modules:
  0.0 998.8 jit_solution(2848675889399177403)
XLA Ops:
  18.3 14.3 %all-to-all-done.2 = bf16[4,64,4,512]{3,1,0,2:T(8,128)(2,1)S(1)} async-done(((bf16[4,64,4,512]{3,1,0,2:T(8,128)(2,1)}), bf16[4,64,4,512]{3,1,0,2:T(8,128)(2,1)S(1)}, u32[]{:S(2)}, u32[]{:S(2)}) %all-to-all-start.2) | async-done | bytes 1048608 | tf_op jit(solution)/shard_map/all_to_all | solution.py:205
  37.2 5.3 all_to_all.177
  48.1 5.6 all-to-all-start
  54.0 10.8 %all-to-all-done = bf16[32,2,960]{2,1,0:T(2,128)(2,1)S(1)} async-done(((bf16[32,2,960]{2,1,0:T(2,128)(2,1)}), bf16[32,2,960]{2,1,0:T(2,128)(2,1)S(1)}, u32[]{:S(2)}, u32[]{:S(2)}) %all-to-all-start) | async-done | bytes 122912 | tf_op jit(solution)/shard_map/all_to_all | solution.py:205
  80.6 23.8 %all-to-all-done.1 = bf16[2,4,64,2048]{3,2,0,1:T(8,128)(2,1)} async-done(((bf16[2,4,64,2048]{3,2,0,1:T(8,128)(2,1)}), bf16[2,4,64,2048]{3,2,0,1:T(8,128)(2,1)}, u32[]{:S(2)}, u32[]{:S(2)}) %all-to-all-start.1) | async-done | bytes 2097184 | tf_op jit(solution)/shard_map/all_to_all | solution.py:176
  107.1 81.5 %all-gather.4.cloned.1.call-done = bf16[5,2048,512]{2,1,0:T(8,128)(2,1)} async-done(((bf16[5,256,512]{2,1,0:T(8,128)(2,1)}), bf16[5,2048,512]{2,1,0:T(8,128)(2,1)}) %all-gather.4.cloned.1.call-update) | async-done | bytes 10485776 | tf_op jit(solution)/shard_map/all_gather | solution.py:193
  290.2 25.4 %all-to-all-done.5 = bf16[2,4,64,2048]{3,2,0,1:T(8,128)(2,1)S(1)} async-done(((bf16[2,4,64,2048]{3,2,0,1:T(8,128)(2,1)}), bf16[2,4,64,2048]{3,2,0,1:T(8,128)(2,1)S(1)}, u32[]{:S(2)}, u32[]{:S(2)}) %all-to-all-start.5) | async-done | bytes 2097184 | tf_op jit(solution)/shard_map/all_to_all | solution.py:188
  324.8 23.1 %all-to-all-done.8 = bf16[2,4,64,2048]{3,2,0,1:T(8,128)(2,1)} async-done(((bf16[2,4,64,2048]{3,2,0,1:T(8,128)(2,1)}), bf16[2,4,64,2048]{3,2,0,1:T(8,128)(2,1)}, u32[]{:S(2)}, u32[]{:S(2)}) %all-to-all-start.8) | async-done | bytes 2097184 | tf_op jit(solution)/shard_map/all_to_all | solution.py:176
  358.1 21.6 %all-to-all-done.6 = bf16[2,4,64,2048]{3,2,0,1:T(8,128)(2,1)} async-done(((bf16[2,4,64,2048]{3,2,0,1:T(8,128)(2,1)}), bf16[2,4,64,2048]{3,2,0,1:T(8,128)(2,1)}, u32[]{:S(2)}, u32[]{:S(2)}) %all-to-all-start.6) | async-done | bytes 2097184 | tf_op jit(solution)/shard_map/all_to_all | solution.py:176
  381.5 22.2 %all-gather.6.cloned.1.call-done = bf16[3,2048,1280]{2,1,0:T(8,128)(2,1)} async-done(((bf16[3,256,1280]{2,1,0:T(8,128)(2,1)}), bf16[3,2048,1280]{2,1,0:T(8,128)(2,1)}) %all-gather.6.cloned.1.call-update) | async-done | bytes 15728656 | tf_op jit(solution)/shard_map/all_gather | solution.py:193
  403.7 6.1 fusion.7
  428.4 6.9 pad_maximum_fusion
  435.3 13.6 %all-gather.8.cloned.1.call-done = bf16[3,2048,128]{2,1,0:T(8,128)(2,1)} async-done(((bf16[3,256,128]{2,1,0:T(8,128)(2,1)}), bf16[3,2048,128]{2,1,0:T(8,128)(2,1)}) %all-gather.8.cloned.1.call-update) | async-done | bytes 1572880 | tf_op jit(solution)/shard_map/all_gather | solution.py:193
  470.0 5.4 fusion.3
  484.0 11.6 %all-to-all-done.10 = bf16[2,4,64,2048]{3,2,0,1:T(8,128)(2,1)S(1)} async-done(((bf16[2,4,64,2048]{3,2,0,1:T(8,128)(2,1)}), bf16[2,4,64,2048]{3,2,0,1:T(8,128)(2,1)S(1)}, u32[]{:S(2)}, u32[]{:S(2)}) %all-to-all-start.10) | async-done | bytes 2097184 | tf_op jit(solution)/shard_map/all_to_all | solution.py:188
  501.5 24.4 %all-to-all-done.11 = bf16[2,4,64,2048]{3,2,0,1:T(8,128)(2,1)} async-done(((bf16[2,4,64,2048]{3,2,0,1:T(8,128)(2,1)}), bf16[2,4,64,2048]{3,2,0,1:T(8,128)(2,1)}, u32[]{:S(2)}, u32[]{:S(2)}) %all-to-all-start.11) | async-done | bytes 2097184 | tf_op jit(solution)/shard_map/all_to_all | solution.py:188
  538.8 23.2 %all-to-all-done.12 = bf16[2,4,64,2048]{3,2,0,1:T(8,128)(2,1)} async-done(((bf16[2,4,64,2048]{3,2,0,1:T(8,128)(2,1)}), bf16[2,4,64,2048]{3,2,0,1:T(8,128)(2,1)}, u32[]{:S(2)}, u32[]{:S(2)}) %all-to-all-start.12) | async-done | bytes 2097184 | tf_op jit(solution)/shard_map/all_to_all | solution.py:176
  580.4 5.9 all-to-all-done.13
  700.5 74.7 %reduce-scatter.4.cloned.1.call-done = bf16[3,256,1280]{2,1,0:T(8,128)(2,1)} async-done(((bf16[3,2048,1280]{2,1,0:T(8,128)(2,1)}), bf16[3,256,1280]{2,1,0:T(8,128)(2,1)}) %reduce-scatter.4.cloned.1.call-update) | async-done | bytes 1966096 | tf_op jit(solution)/shard_map/reduce_scatter | solution.py:197
  799.1 7.7 dynamic_update_slice.7
  808.6 13.8 %all-to-all-done.14 = bf16[2,4,64,2048]{3,2,0,1:T(8,128)(2,1)} async-done(((bf16[2,4,64,2048]{3,2,0,1:T(8,128)(2,1)}), bf16[2,4,64,2048]{3,2,0,1:T(8,128)(2,1)}, u32[]{:S(2)}, u32[]{:S(2)}) %all-to-all-start.14) | async-done | bytes 2097184 | tf_op jit(solution)/shard_map/all_to_all | solution.py:188
  836.6 12.8 %all-to-all-done.16 = f32[32,1,2048]{2,1,0:T(1,128)S(1)} async-done(((f32[32,1,2048]{2,1,0:T(1,128)}), f32[32,1,2048]{2,1,0:T(1,128)S(1)}, u32[]{:S(2)}, u32[]{:S(2)}) %all-to-all-start.16) | async-done | bytes 262176 | tf_op jit(solution)/shard_map/all_to_all | solution.py:205
  871.6 91.8 %reduce-scatter.8.cloned.1.call-done = bf16[5,256,512]{2,1,0:T(8,128)(2,1)} async-done(((bf16[5,2048,512]{2,1,0:T(8,128)(2,1)}), bf16[5,256,512]{2,1,0:T(8,128)(2,1)}) %reduce-scatter.8.cloned.1.call-update) | async-done | bytes 1310736 | tf_op jit(solution)/shard_map/reduce_scatter | solution.py:197
  977.9 6.7 all-to-all-done.15
  (652 shorter events, 443.0 us)
Async XLA Ops:
  13.9 18.7 %all-to-all-start.2 = ((bf16[4,64,4,512]{3,1,0,2:T(8,128)(2,1)}), bf16[4,64,4,512]{3,1,0,2:T(8,128)(2,1)S(1)}, u32[]{:S(2)}, u32[]{:S(2)}) async-start(bf16[4,64,4,512]{3,1,0,2:T(8,128)(2,1)} %copy.379), calls=%async_computation.2 | async-start | bytes 2097152 | tf_op jit(solution)/shard_map/all_to_all | solution.py:205
  18.1 170.4 %all-gather.4.cloned.1.call-start = ((), (), s32[]{:S(2)}) async-start(), calls=%async_computation.22 | async-start | bytes 11796480 | tf_op jit(solution)/shard_map/all_gather | solution.py:193
  33.9 369.9 %all-gather.6.cloned.1.call-start = ((), (), s32[]{:S(2)}) async-start(), calls=%async_computation.23 | async-start | bytes 17694720 | tf_op jit(solution)/shard_map/all_gather | solution.py:193
  48.1 16.6 %all-to-all-start = ((bf16[32,2,960]{2,1,0:T(2,128)(2,1)}), bf16[32,2,960]{2,1,0:T(2,128)(2,1)S(1)}, u32[]{:S(2)}, u32[]{:S(2)}) async-start(bf16[32,2,960]{2,1,0:T(2,128)(2,1)} %reshape.743), calls=%async_computation | async-start | bytes 262144 | tf_op jit(solution)/shard_map/all_to_all | solution.py:205
  65.3 6.9 all-to-all-start.3
  73.8 30.5 %all-to-all-start.1 = ((bf16[2,4,64,2048]{3,2,0,1:T(8,128)(2,1)}), bf16[2,4,64,2048]{3,2,0,1:T(8,128)(2,1)}, u32[]{:S(2)}, u32[]{:S(2)}) async-start(bf16[2,4,64,2048]{3,2,0,1:T(8,128)(2,1)} %broadcast_in_dim.43), calls=%async_computation.1 | async-start | bytes 4194304 | tf_op jit(solution)/shard_map/all_to_all | solution.py:176
  263.9 13.2 %all-to-all-start.4 = ((bf16[512,1,2,4,64]{0,4,2,1,3:T(8,128)(2,1)}), bf16[512,1,2,4,64]{0,4,2,1,3:T(8,128)(2,1)}, u32[]{:S(2)}, u32[]{:S(2)}) async-start(bf16[512,1,2,4,64]{0,4,2,1,3:T(8,128)(2,1)} %copy.400), calls=%async_computation.4 | async-start | bytes 1048576 | tf_op jit(solution)/shard_map/all_to_all | solution.py:205
  277.1 9.0 all-to-all-start.9
  286.1 29.6 %all-to-all-start.5 = ((bf16[2,4,64,2048]{3,2,0,1:T(8,128)(2,1)}), bf16[2,4,64,2048]{3,2,0,1:T(8,128)(2,1)S(1)}, u32[]{:S(2)}, u32[]{:S(2)}) async-start(bf16[2,4,64,2048]{3,2,0,1:T(8,128)(2,1)} %copy.402), calls=%async_computation.5 | async-start | bytes 4194304 | tf_op jit(solution)/shard_map/all_to_all | solution.py:188
  317.7 30.2 %all-to-all-start.8 = ((bf16[2,4,64,2048]{3,2,0,1:T(8,128)(2,1)}), bf16[2,4,64,2048]{3,2,0,1:T(8,128)(2,1)}, u32[]{:S(2)}, u32[]{:S(2)}) async-start(bf16[2,4,64,2048]{3,2,0,1:T(8,128)(2,1)} %broadcast_in_dim.48), calls=%async_computation.8 | async-start | bytes 4194304 | tf_op jit(solution)/shard_map/all_to_all | solution.py:176
  349.6 30.2 %all-to-all-start.6 = ((bf16[2,4,64,2048]{3,2,0,1:T(8,128)(2,1)}), bf16[2,4,64,2048]{3,2,0,1:T(8,128)(2,1)}, u32[]{:S(2)}, u32[]{:S(2)}) async-start(bf16[2,4,64,2048]{3,2,0,1:T(8,128)(2,1)} %broadcast_in_dim.47), calls=%async_computation.6 | async-start | bytes 4194304 | tf_op jit(solution)/shard_map/all_to_all | solution.py:176
  354.0 94.9 %all-gather.8.cloned.1.call-start = ((), (), s32[]{:S(2)}) async-start(), calls=%async_computation.24 | async-start | bytes 1769472 | tf_op jit(solution)/shard_map/all_gather | solution.py:193
  354.9 345.6 %reduce-scatter.6.cloned.1.call-start = ((), (), s32[]{:S(2)}) async-start(), calls=%async_computation.26 | async-start | bytes 1769472 | tf_op jit(solution)/shard_map/reduce_scatter | solution.py:197
  456.8 318.4 %reduce-scatter.4.cloned.1.call-start = ((), (), s32[]{:S(2)}) async-start(), calls=%async_computation.25 | async-start | bytes 17694720 | tf_op jit(solution)/shard_map/reduce_scatter | solution.py:197
  466.2 29.4 %all-to-all-start.10 = ((bf16[2,4,64,2048]{3,2,0,1:T(8,128)(2,1)}), bf16[2,4,64,2048]{3,2,0,1:T(8,128)(2,1)S(1)}, u32[]{:S(2)}, u32[]{:S(2)}) async-start(bf16[2,4,64,2048]{3,2,0,1:T(8,128)(2,1)} %copy.411), calls=%async_computation.10 | async-start | bytes 4194304 | tf_op jit(solution)/shard_map/all_to_all | solution.py:188
  495.7 30.2 %all-to-all-start.11 = ((bf16[2,4,64,2048]{3,2,0,1:T(8,128)(2,1)}), bf16[2,4,64,2048]{3,2,0,1:T(8,128)(2,1)}, u32[]{:S(2)}, u32[]{:S(2)}) async-start(bf16[2,4,64,2048]{3,2,0,1:T(8,128)(2,1)} %copy.412), calls=%async_computation.11 | async-start | bytes 4194304 | tf_op jit(solution)/shard_map/all_to_all | solution.py:188
  531.5 30.5 %all-to-all-start.12 = ((bf16[2,4,64,2048]{3,2,0,1:T(8,128)(2,1)}), bf16[2,4,64,2048]{3,2,0,1:T(8,128)(2,1)}, u32[]{:S(2)}, u32[]{:S(2)}) async-start(bf16[2,4,64,2048]{3,2,0,1:T(8,128)(2,1)} %broadcast_in_dim.50), calls=%async_computation.12 | async-start | bytes 4194304 | tf_op jit(solution)/shard_map/all_to_all | solution.py:176
  567.3 18.9 %all-to-all-start.13 = ((f32[512,4,2,1,64]{0,4,2,3,1:T(8,128)}), f32[512,4,2,1,64]{0,4,2,3,1:T(8,128)}, u32[]{:S(2)}, u32[]{:S(2)}) async-start(f32[512,4,2,1,64]{0,4,2,3,1:T(8,128)} %convolution_bitcast_fusion.1), calls=%async_computation.13 | async-start | bytes 2097152 | tf_op jit(solution)/shard_map/all_to_all | solution.py:205
  571.7 391.7 %reduce-scatter.8.cloned.1.call-start = ((), (), s32[]{:S(2)}) async-start(), calls=%async_computation.27 | async-start | bytes 11796480 | tf_op jit(solution)/shard_map/reduce_scatter | solution.py:197
  792.1 30.2 %all-to-all-start.14 = ((bf16[2,4,64,2048]{3,2,0,1:T(8,128)(2,1)}), bf16[2,4,64,2048]{3,2,0,1:T(8,128)(2,1)}, u32[]{:S(2)}, u32[]{:S(2)}) async-start(bf16[2,4,64,2048]{3,2,0,1:T(8,128)(2,1)} %copy.449), calls=%async_computation.14 | async-start | bytes 4194304 | tf_op jit(solution)/shard_map/all_to_all | solution.py:188
  829.6 19.7 %all-to-all-start.16 = ((f32[32,1,2048]{2,1,0:T(1,128)}), f32[32,1,2048]{2,1,0:T(1,128)S(1)}, u32[]{:S(2)}, u32[]{:S(2)}) async-start(f32[32,1,2048]{2,1,0:T(1,128)} %copy.458), calls=%async_computation.19 | async-start | bytes 524288 | tf_op jit(solution)/shard_map/all_to_all | solution.py:205
  855.0 6.7 all-to-all-start.17
  861.7 5.8 all-to-all-start.18
  965.8 18.8 %all-to-all-start.15 = ((bf16[4,4,64,1,512]{4,2,0,3,1:T(8,128)(2,1)}), bf16[4,4,64,1,512]{4,2,0,3,1:T(8,128)(2,1)}, u32[]{:S(2)}, u32[]{:S(2)}) async-start(bf16[4,4,64,1,512]{4,2,0,3,1:T(8,128)(2,1)} %copy.450), calls=%async_computation.18 | async-start | bytes 2097152 | tf_op jit(solution)/shard_map/all_to_all | solution.py:205
  (174 other events, 3454.9 us)
Sparse Core Ops, SparseCore 0:
  34.0 154.5 all-gather.3
  190.7 212.9 all-gather.5
  406.5 42.3 all-gather.7
  456.9 64.2 reduce-scatter.5
  525.1 250.0 reduce-scatter.3
  779.1 184.2 reduce-scatter.7

commit v19 on v18

--- a/solution.py
+++ b/solution.py
@@ -261,10 +261,28 @@
         column_swapped = exchange(
             column_owned.reshape(4, rows, tp, cols_here), TP_AXES, 2, 1
         ).reshape(4, group_rows, cols_here)
+        owned_rows, hidden_half = swiglu_gate.shape
+        hidden_here = hidden_half // inner
+        ff_owned = jnp.stack([swiglu_gate, swiglu_up, swiglu_down.T]).reshape(
+            3, owned_rows, inner, hidden_here
+        )
+        lanes = hidden_here // 128 if hidden_here % 128 == 0 else 0
+        first = (lanes - lanes * 2 // 11) * 128 if lanes > 1 else hidden_here // 2
+        order = ((first, hidden_here - first), (0, first))
+        ff_swapped = [
+            exchange(ff_owned[..., offset : offset + size], INNER_AXES, 2, 1).reshape(
+                3, inner * owned_rows, size
+            )
+            for offset, size in order
+        ]
+        small_chunk = fsdp_gather(ff_swapped[0], 1)
         mixer_stack = jnp.concatenate(
             [column_swapped, out_weight.reshape(1, group_rows, cols_here)], axis=0
         )
+        small_chunk, mixer_stack = lax.optimization_barrier((small_chunk, mixer_stack))
         weight_all = fsdp_gather(mixer_stack, 1)
+        weight_all, large_swapped = lax.optimization_barrier((weight_all, ff_swapped[1]))
+        ff_chunks = [small_chunk, fsdp_gather(large_swapped, 1)]
         query_cols, key_cols, value_cols, gate_cols = (weight_all[index] for index in range(4))
         out_rows = weight_all[4].reshape(fsdp * rows, width)
         small_pack = jnp.concatenate(
@@ -294,19 +312,6 @@
             conv_full.astype(jnp.float32), position * cols_here, cols_here, axis=2
         )
         beta_here = lax.dynamic_slice_in_dim(beta_full, position * heads_here, heads_here, axis=1)
-
-        owned_rows, hidden_half = swiglu_gate.shape
-        hidden_here = hidden_half // inner
-        ff_owned = jnp.stack([swiglu_gate, swiglu_up, swiglu_down.T]).reshape(
-            3, owned_rows, inner, hidden_here
-        )
-        lanes = hidden_here // 128 if hidden_here % 128 == 0 else 0
-        first = (lanes - 1) * 128 if lanes > 1 else hidden_here // 2
-        bounds = ((0, first), (first, hidden_here - first))
-        ff_chunks = []
-        for offset, size in bounds:
-            swapped = exchange(ff_owned[..., offset : offset + size], INNER_AXES, 2, 1)
-            ff_chunks.append(fsdp_gather(swapped.reshape(3, inner * owned_rows, size), 1))
 
         inputs = tokens.astype(jnp.float32).reshape(micro_count * slot, width)
         normed, norm_back = jax.vjp(rms_norm, inputs, gain_mixer.astype(jnp.float32))
@@ -411,7 +416,7 @@
                 exchange(
                     piece.reshape(3, inner, owned_rows, 1, size), INNER_AXES, 1, 3
                 ).reshape(3, owned_rows, inner, size)
-                for piece, (offset, size) in zip(ff_reduced, bounds)
+                for piece, (offset, size) in sorted(zip(ff_reduced, order), key=lambda pair: pair[1][0])
             ],
             axis=3,
         ).reshape(3, owned_rows, hidden_half).astype(jnp.float32)

time: 1010 us -> 1020 us (level)
    all_gather x3, waiting for transfers between devices: 117 us -> 183 us  [fsdp_gather(): return lax.all_gather(value, FSDP_AXES, axis=axis, tiled=True)]
    reduce_scatter x3, waiting for transfers between devices: 167 us -> 117 us  [fsdp_scatter_low(): lax.psum_scatter(value.astype(jnp.bfloat16), FSDP_AXES, scatter_dimension...]
    all_to_all x9 -> x8, starting transfers between devices: 37 us -> 29.7 us  [exchange(): return lax.all_to_all(value, axes, split_axis, concat_axis, tiled=True)]
    all_to_all x9 -> x8, waiting for transfers between devices: 57.2 us -> 55.9 us  [exchange(): return lax.all_to_all(value, axes, split_axis, concat_axis, tiled=True)]
    unnamed x359 -> x339, local copies, waits for them, and re-layouts: 27.3 us -> 27.1 us
  transfers between devices with their start and end apart: 24 -> 23, of which waited for: 21 -> 21; matrix products, arithmetic and copies ran while one was open for 35% -> 36% of each run, Pallas kernels for 0% -> 0%
where the time goes in v19:
time: 1020 us; the launch traced here: 1010 us
  waiting for transfers between devices  520 us (51%)
  matrix products  177 us (17%)
  local copies, waits for them, and re-layouts  151 us (15%)
  starting transfers between devices  69.7 us (7%)
  other arithmetic  63.5 us (6%)
  between operations  17.4 us (2%)
    all_gather x3, waiting for transfers between devices, fsdp_gather(): return lax.all_gather(value, FSDP_AXES, axis=axis, tiled=True)  183 us
    reduce_scatter x3, waiting for transfers between devices, fsdp_scatter_low(): lax.psum_scatter(value.astype(jnp.bfloat16), FSDP_AXES, scatter_dimension...  117 us
    all_to_all x5, waiting for transfers between devices, tp_gather(): moved = lax.all_to_all(spread, TP_AXES, axis, axis, tiled=True)  91.8 us
    dot_general x42, matrix products, outer_product_result(): return jnp.einsum(form, first, second, precision=lax.Precision.HIGHEST)  75.7 us
    all_to_all x4, waiting for transfers between devices, tp_scatter_low(): moved = lax.all_to_all(staged, TP_AXES, axis, axis, tiled=True)  72.1 us
    all_to_all x8, waiting for transfers between devices, exchange(): return lax.all_to_all(value, axes, split_axis, concat_axis, tiled=True)  55.9 us
    dot_general x12, matrix products, back_product(): jnp.einsum('tg,fg->tf', gradient, weight, preferred_element_type=jnp.floa...  39 us
    dot_general x12, matrix products, matmul_rows(): return jnp.dot(left, right, preferred_element_type=jnp.float32)  34.8 us
  transfers between devices with their start and end apart: 23, of which 21 were waited for; matrix products, arithmetic and copies ran while one was open for 36% of the time, Pallas kernels for 0%

profile of v19, /device:TPU:0, one launch (start us, length us, event | category | flops | bytes accessed | tf_op | source)
XLA Modules:
  0.0 1008.3 jit_solution(7302924860546734517)
XLA Ops:
  25.6 13.5 %all-to-all-done.3 = bf16[4,64,4,512]{3,1,0,2:T(8,128)(2,1)S(1)} async-done(((bf16[4,64,4,512]{3,1,0,2:T(8,128)(2,1)}), bf16[4,64,4,512]{3,1,0,2:T(8,128)(2,1)S(1)}, u32[]{:S(2)}, u32[]{:S(2)}) %all-to-all-start.3) | async-done | bytes 1048608 | tf_op jit(solution)/shard_map/all_to_all | solution.py:205
  40.4 38.4 %all-gather.4.cloned.1.call-done = bf16[3,2048,256]{2,1,0:T(8,128)(2,1)} async-done(((bf16[3,256,256]{2,1,0:T(8,128)(2,1)}), bf16[3,2048,256]{2,1,0:T(8,128)(2,1)}) %all-gather.4.cloned.1.call-update) | async-done | bytes 3145744 | tf_op jit(solution)/shard_map/all_gather | solution.py:193
  79.1 5.2 all_to_all.178
  86.5 144.6 %all-gather.6.cloned.1.call-done = bf16[5,2048,512]{2,1,0:T(8,128)(2,1)} async-done(((bf16[5,256,512]{2,1,0:T(8,128)(2,1)}), bf16[5,2048,512]{2,1,0:T(8,128)(2,1)}) %all-gather.6.cloned.1.call-update) | async-done | bytes 10485776 | tf_op jit(solution)/shard_map/all_gather | solution.py:193
  237.3 8.4 all-to-all-done
  261.1 24.3 %all-to-all-done.1 = bf16[2,4,64,2048]{3,2,0,1:T(8,128)(2,1)} async-done(((bf16[2,4,64,2048]{3,2,0,1:T(8,128)(2,1)}), bf16[2,4,64,2048]{3,2,0,1:T(8,128)(2,1)}, u32[]{:S(2)}, u32[]{:S(2)}) %all-to-all-start.1) | async-done | bytes 2097184 | tf_op jit(solution)/shard_map/all_to_all | solution.py:176
  366.5 6.2 all-to-all-done.6
  382.3 25.5 %all-to-all-done.7 = bf16[2,4,64,2048]{3,2,0,1:T(8,128)(2,1)} async-done(((bf16[2,4,64,2048]{3,2,0,1:T(8,128)(2,1)}), bf16[2,4,64,2048]{3,2,0,1:T(8,128)(2,1)}, u32[]{:S(2)}, u32[]{:S(2)}) %all-to-all-start.7) | async-done | bytes 2097184 | tf_op jit(solution)/shard_map/all_to_all | solution.py:188
  418.4 21.3 %all-to-all-done.9 = bf16[2,4,64,2048]{3,2,0,1:T(8,128)(2,1)} async-done(((bf16[2,4,64,2048]{3,2,0,1:T(8,128)(2,1)}), bf16[2,4,64,2048]{3,2,0,1:T(8,128)(2,1)}, u32[]{:S(2)}, u32[]{:S(2)}) %all-to-all-start.9) | async-done | bytes 2097184 | tf_op jit(solution)/shard_map/all_to_all | solution.py:176
  452.7 19.9 %all-to-all-done.8 = bf16[2,4,64,2048]{3,2,0,1:T(8,128)(2,1)} async-done(((bf16[2,4,64,2048]{3,2,0,1:T(8,128)(2,1)}), bf16[2,4,64,2048]{3,2,0,1:T(8,128)(2,1)}, u32[]{:S(2)}, u32[]{:S(2)}) %all-to-all-start.8) | async-done | bytes 2097184 | tf_op jit(solution)/shard_map/all_to_all | solution.py:176
  482.3 6.0 fusion.13
  507.8 6.4 pad_maximum_fusion
  531.2 5.2 fusion.11
  536.4 5.0 fusion.7
  545.0 11.9 %all-to-all-done.10 = bf16[2,4,64,2048]{3,2,0,1:T(8,128)(2,1)} async-done(((bf16[2,4,64,2048]{3,2,0,1:T(8,128)(2,1)}), bf16[2,4,64,2048]{3,2,0,1:T(8,128)(2,1)}, u32[]{:S(2)}, u32[]{:S(2)}) %all-to-all-start.10) | async-done | bytes 2097184 | tf_op jit(solution)/shard_map/all_to_all | solution.py:188
  564.8 22.5 %all-to-all-done.11 = bf16[2,4,64,2048]{3,2,0,1:T(8,128)(2,1)} async-done(((bf16[2,4,64,2048]{3,2,0,1:T(8,128)(2,1)}), bf16[2,4,64,2048]{3,2,0,1:T(8,128)(2,1)}, u32[]{:S(2)}, u32[]{:S(2)}) %all-to-all-start.11) | async-done | bytes 2097184 | tf_op jit(solution)/shard_map/all_to_all | solution.py:188
  599.9 23.2 %all-to-all-done.12 = bf16[2,4,64,2048]{3,2,0,1:T(8,128)(2,1)} async-done(((bf16[2,4,64,2048]{3,2,0,1:T(8,128)(2,1)}), bf16[2,4,64,2048]{3,2,0,1:T(8,128)(2,1)}, u32[]{:S(2)}, u32[]{:S(2)}) %all-to-all-start.12) | async-done | bytes 2097184 | tf_op jit(solution)/shard_map/all_to_all | solution.py:176
  641.1 6.2 all-to-all-done.13
  761.4 23.7 %reduce-scatter.6.cloned.1.call-done = bf16[3,256,1152]{2,1,0:T(8,128)(2,1)} async-done(((bf16[3,2048,1152]{2,1,0:T(8,128)(2,1)}), bf16[3,256,1152]{2,1,0:T(8,128)(2,1)}) %reduce-scatter.6.cloned.1.call-update) | async-done | bytes 1769488 | tf_op jit(solution)/shard_map/reduce_scatter | solution.py:197
  811.8 7.7 dynamic_update_slice.7
  820.2 12.2 %all-to-all-done.14 = bf16[2,4,64,2048]{3,2,0,1:T(8,128)(2,1)} async-done(((bf16[2,4,64,2048]{3,2,0,1:T(8,128)(2,1)}), bf16[2,4,64,2048]{3,2,0,1:T(8,128)(2,1)}, u32[]{:S(2)}, u32[]{:S(2)}) %all-to-all-start.14) | async-done | bytes 2097184 | tf_op jit(solution)/shard_map/all_to_all | solution.py:188
  846.7 12.5 %all-to-all-done.16 = f32[32,1,2048]{2,1,0:T(1,128)S(1)} async-done(((f32[32,1,2048]{2,1,0:T(1,128)}), f32[32,1,2048]{2,1,0:T(1,128)S(1)}, u32[]{:S(2)}, u32[]{:S(2)}) %all-to-all-start.16) | async-done | bytes 262176 | tf_op jit(solution)/shard_map/all_to_all | solution.py:205
  879.9 93.0 %reduce-scatter.8.cloned.1.call-done = bf16[5,256,512]{2,1,0:T(8,128)(2,1)} async-done(((bf16[5,2048,512]{2,1,0:T(8,128)(2,1)}), bf16[5,256,512]{2,1,0:T(8,128)(2,1)}) %reduce-scatter.8.cloned.1.call-update) | async-done | bytes 1310736 | tf_op jit(solution)/shard_map/reduce_scatter | solution.py:197
  987.3 6.7 all-to-all-done.15
  (630 shorter events, 441.4 us)
Async XLA Ops:
  7.2 71.6 %all-gather.4.cloned.1.call-start = ((), (), s32[]{:S(2)}) async-start(), calls=%async_computation.22 | async-start | bytes 3538944 | tf_op jit(solution)/shard_map/all_gather | solution.py:193
  20.3 18.9 %all-to-all-start.3 = ((bf16[4,64,4,512]{3,1,0,2:T(8,128)(2,1)}), bf16[4,64,4,512]{3,1,0,2:T(8,128)(2,1)S(1)}, u32[]{:S(2)}, u32[]{:S(2)}) async-start(bf16[4,64,4,512]{3,1,0,2:T(8,128)(2,1)} %copy.383), calls=%async_computation.3 | async-start | bytes 2097152 | tf_op jit(solution)/shard_map/all_to_all | solution.py:205
  24.5 206.6 %all-gather.6.cloned.1.call-start = ((), (), s32[]{:S(2)}) async-start(), calls=%async_computation.23 | async-start | bytes 11796480 | tf_op jit(solution)/shard_map/all_gather | solution.py:193
  78.8 403.4 %all-gather.8.cloned.1.call-start = ((), (), s32[]{:S(2)}) async-start(), calls=%async_computation.24 | async-start | bytes 15925248 | tf_op jit(solution)/shard_map/all_gather | solution.py:193
  234.3 11.4 %all-to-all-start = ((bf16[32,2,960]{2,1,0:T(2,128)(2,1)}), bf16[32,2,960]{2,1,0:T(2,128)(2,1)S(1)}, u32[]{:S(2)}, u32[]{:S(2)}) async-start(bf16[32,2,960]{2,1,0:T(2,128)(2,1)} %reshape.743), calls=%async_computation | async-start | bytes 262144 | tf_op jit(solution)/shard_map/all_to_all | solution.py:205
  246.3 6.9 all-to-all-start.5
  254.8 30.5 %all-to-all-start.1 = ((bf16[2,4,64,2048]{3,2,0,1:T(8,128)(2,1)}), bf16[2,4,64,2048]{3,2,0,1:T(8,128)(2,1)}, u32[]{:S(2)}, u32[]{:S(2)}) async-start(bf16[2,4,64,2048]{3,2,0,1:T(8,128)(2,1)} %broadcast_in_dim.43), calls=%async_computation.1 | async-start | bytes 4194304 | tf_op jit(solution)/shard_map/all_to_all | solution.py:176
  360.4 12.3 %all-to-all-start.6 = ((bf16[512,1,2,4,64]{0,4,2,1,3:T(8,128)(2,1)}), bf16[512,1,2,4,64]{0,4,2,1,3:T(8,128)(2,1)S(1)}, u32[]{:S(2)}, u32[]{:S(2)}) async-start(bf16[512,1,2,4,64]{0,4,2,1,3:T(8,128)(2,1)} %copy.406), calls=%async_computation.6 | async-start | bytes 1048576 | tf_op jit(solution)/shard_map/all_to_all | solution.py:205
  377.3 30.6 %all-to-all-start.7 = ((bf16[2,4,64,2048]{3,2,0,1:T(8,128)(2,1)}), bf16[2,4,64,2048]{3,2,0,1:T(8,128)(2,1)}, u32[]{:S(2)}, u32[]{:S(2)}) async-start(bf16[2,4,64,2048]{3,2,0,1:T(8,128)(2,1)} %copy.408), calls=%async_computation.7 | async-start | bytes 4194304 | tf_op jit(solution)/shard_map/all_to_all | solution.py:188
  382.2 208.7 %copy-start.143 = (f32[2,64]{1,0:T(2,128)}, f32[2,64]{1,0:T(2,128)S(1)}, u32[]{:S(2)}) copy-start(f32[2,64]{1,0:T(2,128)S(1)} %convert_element_type.252) | copy-start | bytes 1540
  409.5 30.2 %all-to-all-start.9 = ((bf16[2,4,64,2048]{3,2,0,1:T(8,128)(2,1)}), bf16[2,4,64,2048]{3,2,0,1:T(8,128)(2,1)}, u32[]{:S(2)}, u32[]{:S(2)}) async-start(bf16[2,4,64,2048]{3,2,0,1:T(8,128)(2,1)} %broadcast_in_dim.48), calls=%async_computation.9 | async-start | bytes 4194304 | tf_op jit(solution)/shard_map/all_to_all | solution.py:176
  442.4 30.2 %all-to-all-start.8 = ((bf16[2,4,64,2048]{3,2,0,1:T(8,128)(2,1)}), bf16[2,4,64,2048]{3,2,0,1:T(8,128)(2,1)}, u32[]{:S(2)}, u32[]{:S(2)}) async-start(bf16[2,4,64,2048]{3,2,0,1:T(8,128)(2,1)} %broadcast_in_dim.47), calls=%async_computation.8 | async-start | bytes 4194304 | tf_op jit(solution)/shard_map/all_to_all | solution.py:176
  446.8 314.6 %reduce-scatter.4.cloned.1.call-start = ((), (), s32[]{:S(2)}) async-start(), calls=%async_computation.25 | async-start | bytes 3538944 | tf_op jit(solution)/shard_map/reduce_scatter | solution.py:197
  482.2 302.9 %reduce-scatter.6.cloned.1.call-start = ((), (), s32[]{:S(2)}) async-start(), calls=%async_computation.26 | async-start | bytes 15925248 | tf_op jit(solution)/shard_map/reduce_scatter | solution.py:197
  526.7 30.2 %all-to-all-start.10 = ((bf16[2,4,64,2048]{3,2,0,1:T(8,128)(2,1)}), bf16[2,4,64,2048]{3,2,0,1:T(8,128)(2,1)}, u32[]{:S(2)}, u32[]{:S(2)}) async-start(bf16[2,4,64,2048]{3,2,0,1:T(8,128)(2,1)} %copy.411), calls=%async_computation.10 | async-start | bytes 4194304 | tf_op jit(solution)/shard_map/all_to_all | solution.py:188
  556.9 30.4 %all-to-all-start.11 = ((bf16[2,4,64,2048]{3,2,0,1:T(8,128)(2,1)}), bf16[2,4,64,2048]{3,2,0,1:T(8,128)(2,1)}, u32[]{:S(2)}, u32[]{:S(2)}) async-start(bf16[2,4,64,2048]{3,2,0,1:T(8,128)(2,1)} %copy.412), calls=%async_computation.11 | async-start | bytes 4194304 | tf_op jit(solution)/shard_map/all_to_all | solution.py:188
  592.9 30.2 %all-to-all-start.12 = ((bf16[2,4,64,2048]{3,2,0,1:T(8,128)(2,1)}), bf16[2,4,64,2048]{3,2,0,1:T(8,128)(2,1)}, u32[]{:S(2)}, u32[]{:S(2)}) async-start(bf16[2,4,64,2048]{3,2,0,1:T(8,128)(2,1)} %broadcast_in_dim.50), calls=%async_computation.12 | async-start | bytes 4194304 | tf_op jit(solution)/shard_map/all_to_all | solution.py:176
  628.4 18.9 %all-to-all-start.13 = ((f32[512,4,2,1,64]{0,4,2,3,1:T(8,128)}), f32[512,4,2,1,64]{0,4,2,3,1:T(8,128)}, u32[]{:S(2)}, u32[]{:S(2)}) async-start(f32[512,4,2,1,64]{0,4,2,3,1:T(8,128)} %convolution_bitcast_fusion.1), calls=%async_computation.13 | async-start | bytes 2097152 | tf_op jit(solution)/shard_map/all_to_all | solution.py:205
  632.8 340.1 %reduce-scatter.8.cloned.1.call-start = ((), (), s32[]{:S(2)}) async-start(), calls=%async_computation.27 | async-start | bytes 11796480 | tf_op jit(solution)/shard_map/reduce_scatter | solution.py:197
  802.1 30.2 %all-to-all-start.14 = ((bf16[2,4,64,2048]{3,2,0,1:T(8,128)(2,1)}), bf16[2,4,64,2048]{3,2,0,1:T(8,128)(2,1)}, u32[]{:S(2)}, u32[]{:S(2)}) async-start(bf16[2,4,64,2048]{3,2,0,1:T(8,128)(2,1)} %copy.449), calls=%async_computation.14 | async-start | bytes 4194304 | tf_op jit(solution)/shard_map/all_to_all | solution.py:188
  839.6 19.6 %all-to-all-start.16 = ((f32[32,1,2048]{2,1,0:T(1,128)}), f32[32,1,2048]{2,1,0:T(1,128)S(1)}, u32[]{:S(2)}, u32[]{:S(2)}) async-start(f32[32,1,2048]{2,1,0:T(1,128)} %copy.458), calls=%async_computation.19 | async-start | bytes 524288 | tf_op jit(solution)/shard_map/all_to_all | solution.py:205
  863.7 5.4 all-to-all-start.18
  869.1 6.3 all-to-all-start.17
  975.3 18.8 %all-to-all-start.15 = ((bf16[4,4,64,1,512]{4,2,0,3,1:T(8,128)(2,1)}), bf16[4,4,64,1,512]{4,2,0,3,1:T(8,128)(2,1)}, u32[]{:S(2)}, u32[]{:S(2)}) async-start(bf16[4,4,64,1,512]{4,2,0,3,1:T(8,128)(2,1)} %copy.450), calls=%async_computation.18 | async-start | bytes 2097152 | tf_op jit(solution)/shard_map/all_to_all | solution.py:205
  (163 other events, 2537.2 us)
Sparse Core Ops, SparseCore 0:
  15.6 63.2 all-gather.3
  81.6 149.4 all-gather.5
  233.3 193.7 all-gather.7
  482.3 70.6 reduce-scatter.3
  556.6 228.4 reduce-scatter.5
  788.6 184.2 reduce-scatter.7

commit v20 on v19

--- a/solution.py
+++ b/solution.py
@@ -275,14 +275,14 @@
             )
             for offset, size in order
         ]
-        small_chunk = fsdp_gather(ff_swapped[0], 1)
         mixer_stack = jnp.concatenate(
             [column_swapped, out_weight.reshape(1, group_rows, cols_here)], axis=0
         )
-        small_chunk, mixer_stack = lax.optimization_barrier((small_chunk, mixer_stack))
         weight_all = fsdp_gather(mixer_stack, 1)
-        weight_all, large_swapped = lax.optimization_barrier((weight_all, ff_swapped[1]))
-        ff_chunks = [small_chunk, fsdp_gather(large_swapped, 1)]
+        weight_all, small_swapped, large_swapped = lax.optimization_barrier(
+            (weight_all, ff_swapped[0], ff_swapped[1])
+        )
+        ff_chunks = [fsdp_gather(small_swapped, 1), fsdp_gather(large_swapped, 1)]
         query_cols, key_cols, value_cols, gate_cols = (weight_all[index] for index in range(4))
         out_rows = weight_all[4].reshape(fsdp * rows, width)
         small_pack = jnp.concatenate(

time: 1020 us -> 984 us (0.965)
  waiting for transfers between devices: 520 us -> 486 us
    all_gather x3, waiting for transfers between devices: 183 us -> 139 us  [fsdp_gather(): return lax.all_gather(value, FSDP_AXES, axis=axis, tiled=True)]
    all_to_all x8 -> x10, starting transfers between devices: 29.7 us -> 37 us  [exchange(): return lax.all_to_all(value, axes, split_axis, concat_axis, tiled=True)]
    unnamed x339 -> x335, local copies, waits for them, and re-layouts: 27.1 us -> 24.1 us
    all_to_all x8 -> x10, waiting for transfers between devices: 55.9 us -> 58.4 us  [exchange(): return lax.all_to_all(value, axes, split_axis, concat_axis, tiled=True)]
  transfers between devices with their start and end apart: 23 -> 25, of which waited for: 21 -> 23; matrix products, arithmetic and copies ran while one was open for 36% -> 37% of each run, Pallas kernels for 0% -> 0%
where the time goes in v20:
time: 984 us; the launch traced here: 976 us
  waiting for transfers between devices  486 us (49%)
  matrix products  177 us (18%)
  local copies, waits for them, and re-layouts  154 us (16%)
  starting transfers between devices  77.1 us (8%)
  other arithmetic  63.3 us (6%)
  between operations  17.4 us (2%)
    all_gather x3, waiting for transfers between devices, fsdp_gather(): return lax.all_gather(value, FSDP_AXES, axis=axis, tiled=True)  139 us
    reduce_scatter x3, waiting for transfers between devices, fsdp_scatter_low(): lax.psum_scatter(value.astype(jnp.bfloat16), FSDP_AXES, scatter_dimension...  122 us
    all_to_all x5, waiting for transfers between devices, tp_gather(): moved = lax.all_to_all(spread, TP_AXES, axis, axis, tiled=True)  94.3 us
    dot_general x42, matrix products, outer_product_result(): return jnp.einsum(form, first, second, precision=lax.Precision.HIGHEST)  75.7 us
    all_to_all x4, waiting for transfers between devices, tp_scatter_low(): moved = lax.all_to_all(staged, TP_AXES, axis, axis, tiled=True)  72.1 us
    all_to_all x10, waiting for transfers between devices, exchange(): return lax.all_to_all(value, axes, split_axis, concat_axis, tiled=True)  58.4 us
    dot_general x12, matrix products, back_product(): jnp.einsum('tg,fg->tf', gradient, weight, preferred_element_type=jnp.floa...  39.2 us
    all_to_all x10, starting transfers between devices, exchange(): return lax.all_to_all(value, axes, split_axis, concat_axis, tiled=True)  37 us
  transfers between devices with their start and end apart: 25, of which 23 were waited for; matrix products, arithmetic and copies ran while one was open for 37% of the time, Pallas kernels for 0%

profile of v20, /device:TPU:0, one launch (start us, length us, event | category | flops | bytes accessed | tf_op | source)
XLA Modules:
  0.0 975.6 jit_solution(16318195159370536724)
XLA Ops:
  18.3 14.3 %all-to-all-done.2 = bf16[4,64,4,512]{3,1,0,2:T(8,128)(2,1)S(1)} async-done(((bf16[4,64,4,512]{3,1,0,2:T(8,128)(2,1)}), bf16[4,64,4,512]{3,1,0,2:T(8,128)(2,1)S(1)}, u32[]{:S(2)}, u32[]{:S(2)}) %all-to-all-start.2) | async-done | bytes 1048608 | tf_op jit(solution)/shard_map/all_to_all | solution.py:205
  50.3 135.6 %all-gather.4.cloned.1.call-done = bf16[5,2048,512]{2,1,0:T(8,128)(2,1)} async-done(((bf16[5,256,512]{2,1,0:T(8,128)(2,1)}), bf16[5,2048,512]{2,1,0:T(8,128)(2,1)}) %all-gather.4.cloned.1.call-update) | async-done | bytes 10485776 | tf_op jit(solution)/shard_map/all_gather | solution.py:193
  192.9 8.4 all-to-all-done
  216.7 24.3 %all-to-all-done.1 = bf16[2,4,64,2048]{3,2,0,1:T(8,128)(2,1)} async-done(((bf16[2,4,64,2048]{3,2,0,1:T(8,128)(2,1)}), bf16[2,4,64,2048]{3,2,0,1:T(8,128)(2,1)}, u32[]{:S(2)}, u32[]{:S(2)}) %all-to-all-start.1) | async-done | bytes 2097184 | tf_op jit(solution)/shard_map/all_to_all | solution.py:176
  321.7 6.2 all-to-all-done.6
  332.5 4.8 all-to-all-start.7
  337.5 25.5 %all-to-all-done.7 = bf16[2,4,64,2048]{3,2,0,1:T(8,128)(2,1)} async-done(((bf16[2,4,64,2048]{3,2,0,1:T(8,128)(2,1)}), bf16[2,4,64,2048]{3,2,0,1:T(8,128)(2,1)}, u32[]{:S(2)}, u32[]{:S(2)}) %all-to-all-start.7) | async-done | bytes 2097184 | tf_op jit(solution)/shard_map/all_to_all | solution.py:188
  373.6 21.3 %all-to-all-done.9 = bf16[2,4,64,2048]{3,2,0,1:T(8,128)(2,1)} async-done(((bf16[2,4,64,2048]{3,2,0,1:T(8,128)(2,1)}), bf16[2,4,64,2048]{3,2,0,1:T(8,128)(2,1)}, u32[]{:S(2)}, u32[]{:S(2)}) %all-to-all-start.9) | async-done | bytes 2097184 | tf_op jit(solution)/shard_map/all_to_all | solution.py:176
  405.3 22.5 %all-to-all-done.8 = bf16[2,4,64,2048]{3,2,0,1:T(8,128)(2,1)} async-done(((bf16[2,4,64,2048]{3,2,0,1:T(8,128)(2,1)}), bf16[2,4,64,2048]{3,2,0,1:T(8,128)(2,1)}, u32[]{:S(2)}, u32[]{:S(2)}) %all-to-all-start.8) | async-done | bytes 2097184 | tf_op jit(solution)/shard_map/all_to_all | solution.py:176
  444.1 6.0 fusion.13
  469.3 6.4 pad_maximum_fusion
  479.8 4.9 fusion.5
  492.7 5.2 fusion.11
  498.0 5.0 fusion.7
  506.7 11.7 %all-to-all-done.10 = bf16[2,4,64,2048]{3,2,0,1:T(8,128)(2,1)} async-done(((bf16[2,4,64,2048]{3,2,0,1:T(8,128)(2,1)}), bf16[2,4,64,2048]{3,2,0,1:T(8,128)(2,1)}, u32[]{:S(2)}, u32[]{:S(2)}) %all-to-all-start.10) | async-done | bytes 2097184 | tf_op jit(solution)/shard_map/all_to_all | solution.py:188
  526.1 22.7 %all-to-all-done.11 = bf16[2,4,64,2048]{3,2,0,1:T(8,128)(2,1)} async-done(((bf16[2,4,64,2048]{3,2,0,1:T(8,128)(2,1)}), bf16[2,4,64,2048]{3,2,0,1:T(8,128)(2,1)}, u32[]{:S(2)}, u32[]{:S(2)}) %all-to-all-start.11) | async-done | bytes 2097184 | tf_op jit(solution)/shard_map/all_to_all | solution.py:188
  561.6 23.1 %all-to-all-done.12 = bf16[2,4,64,2048]{3,2,0,1:T(8,128)(2,1)} async-done(((bf16[2,4,64,2048]{3,2,0,1:T(8,128)(2,1)}), bf16[2,4,64,2048]{3,2,0,1:T(8,128)(2,1)}, u32[]{:S(2)}, u32[]{:S(2)}) %all-to-all-start.12) | async-done | bytes 2097184 | tf_op jit(solution)/shard_map/all_to_all | solution.py:176
  602.8 6.2 all-to-all-done.13
  723.3 29.1 %reduce-scatter.6.cloned.1.call-done = bf16[3,256,1152]{2,1,0:T(8,128)(2,1)} async-done(((bf16[3,2048,1152]{2,1,0:T(8,128)(2,1)}), bf16[3,256,1152]{2,1,0:T(8,128)(2,1)}) %reduce-scatter.6.cloned.1.call-update) | async-done | bytes 1769488 | tf_op jit(solution)/shard_map/reduce_scatter | solution.py:197
  779.1 7.7 dynamic_update_slice.7
  787.5 12.2 %all-to-all-done.14 = bf16[2,4,64,2048]{3,2,0,1:T(8,128)(2,1)} async-done(((bf16[2,4,64,2048]{3,2,0,1:T(8,128)(2,1)}), bf16[2,4,64,2048]{3,2,0,1:T(8,128)(2,1)}, u32[]{:S(2)}, u32[]{:S(2)}) %all-to-all-start.14) | async-done | bytes 2097184 | tf_op jit(solution)/shard_map/all_to_all | solution.py:188
  814.0 12.5 %all-to-all-done.16 = f32[32,1,2048]{2,1,0:T(1,128)S(1)} async-done(((f32[32,1,2048]{2,1,0:T(1,128)}), f32[32,1,2048]{2,1,0:T(1,128)S(1)}, u32[]{:S(2)}, u32[]{:S(2)}) %all-to-all-start.16) | async-done | bytes 262176 | tf_op jit(solution)/shard_map/all_to_all | solution.py:205
  847.2 93.0 %reduce-scatter.8.cloned.1.call-done = bf16[5,256,512]{2,1,0:T(8,128)(2,1)} async-done(((bf16[5,2048,512]{2,1,0:T(8,128)(2,1)}), bf16[5,256,512]{2,1,0:T(8,128)(2,1)}) %reduce-scatter.8.cloned.1.call-update) | async-done | bytes 1310736 | tf_op jit(solution)/shard_map/reduce_scatter | solution.py:197
  954.6 6.7 all-to-all-done.15
  (628 shorter events, 442.9 us)
Async XLA Ops:
  13.9 18.7 %all-to-all-start.2 = ((bf16[4,64,4,512]{3,1,0,2:T(8,128)(2,1)}), bf16[4,64,4,512]{3,1,0,2:T(8,128)(2,1)S(1)}, u32[]{:S(2)}, u32[]{:S(2)}) async-start(bf16[4,64,4,512]{3,1,0,2:T(8,128)(2,1)} %copy.379), calls=%async_computation.2 | async-start | bytes 2097152 | tf_op jit(solution)/shard_map/all_to_all | solution.py:205
  18.1 167.8 %all-gather.4.cloned.1.call-start = ((), (), s32[]{:S(2)}) async-start(), calls=%async_computation.22 | async-start | bytes 11796480 | tf_op jit(solution)/shard_map/all_gather | solution.py:193
  41.7 6.4 all-to-all-start.4
  45.5 385.4 %all-gather.6.cloned.1.call-start = ((), (), s32[]{:S(2)}) async-start(), calls=%async_computation.23 | async-start | bytes 3538944 | tf_op jit(solution)/shard_map/all_gather | solution.py:193
  185.9 258.2 %all-gather.8.cloned.1.call-start = ((), (), s32[]{:S(2)}) async-start(), calls=%async_computation.24 | async-start | bytes 15925248 | tf_op jit(solution)/shard_map/all_gather | solution.py:193
  189.9 11.4 %all-to-all-start = ((bf16[32,2,960]{2,1,0:T(2,128)(2,1)}), bf16[32,2,960]{2,1,0:T(2,128)(2,1)S(1)}, u32[]{:S(2)}, u32[]{:S(2)}) async-start(bf16[32,2,960]{2,1,0:T(2,128)(2,1)} %reshape.743), calls=%async_computation | async-start | bytes 262144 | tf_op jit(solution)/shard_map/all_to_all | solution.py:205
  201.9 6.9 all-to-all-start.5
  210.4 30.5 %all-to-all-start.1 = ((bf16[2,4,64,2048]{3,2,0,1:T(8,128)(2,1)}), bf16[2,4,64,2048]{3,2,0,1:T(8,128)(2,1)}, u32[]{:S(2)}, u32[]{:S(2)}) async-start(bf16[2,4,64,2048]{3,2,0,1:T(8,128)(2,1)} %broadcast_in_dim.43), calls=%async_computation.1 | async-start | bytes 4194304 | tf_op jit(solution)/shard_map/all_to_all | solution.py:176
  315.6 12.3 %all-to-all-start.6 = ((bf16[512,1,2,4,64]{0,4,2,1,3:T(8,128)(2,1)}), bf16[512,1,2,4,64]{0,4,2,1,3:T(8,128)(2,1)S(1)}, u32[]{:S(2)}, u32[]{:S(2)}) async-start(bf16[512,1,2,4,64]{0,4,2,1,3:T(8,128)(2,1)} %copy.406), calls=%async_computation.6 | async-start | bytes 1048576 | tf_op jit(solution)/shard_map/all_to_all | solution.py:205
  332.5 30.6 %all-to-all-start.7 = ((bf16[2,4,64,2048]{3,2,0,1:T(8,128)(2,1)}), bf16[2,4,64,2048]{3,2,0,1:T(8,128)(2,1)}, u32[]{:S(2)}, u32[]{:S(2)}) async-start(bf16[2,4,64,2048]{3,2,0,1:T(8,128)(2,1)} %copy.408), calls=%async_computation.7 | async-start | bytes 4194304 | tf_op jit(solution)/shard_map/all_to_all | solution.py:188
  364.7 30.3 %all-to-all-start.9 = ((bf16[2,4,64,2048]{3,2,0,1:T(8,128)(2,1)}), bf16[2,4,64,2048]{3,2,0,1:T(8,128)(2,1)}, u32[]{:S(2)}, u32[]{:S(2)}) async-start(bf16[2,4,64,2048]{3,2,0,1:T(8,128)(2,1)} %broadcast_in_dim.48), calls=%async_computation.9 | async-start | bytes 4194304 | tf_op jit(solution)/shard_map/all_to_all | solution.py:176
  397.6 30.2 %all-to-all-start.8 = ((bf16[2,4,64,2048]{3,2,0,1:T(8,128)(2,1)}), bf16[2,4,64,2048]{3,2,0,1:T(8,128)(2,1)}, u32[]{:S(2)}, u32[]{:S(2)}) async-start(bf16[2,4,64,2048]{3,2,0,1:T(8,128)(2,1)} %broadcast_in_dim.47), calls=%async_computation.8 | async-start | bytes 4194304 | tf_op jit(solution)/shard_map/all_to_all | solution.py:176
  402.0 321.3 %reduce-scatter.4.cloned.1.call-start = ((), (), s32[]{:S(2)}) async-start(), calls=%async_computation.25 | async-start | bytes 3538944 | tf_op jit(solution)/shard_map/reduce_scatter | solution.py:197
  441.1 311.3 %reduce-scatter.6.cloned.1.call-start = ((), (), s32[]{:S(2)}) async-start(), calls=%async_computation.26 | async-start | bytes 15925248 | tf_op jit(solution)/shard_map/reduce_scatter | solution.py:197
  488.2 30.3 %all-to-all-start.10 = ((bf16[2,4,64,2048]{3,2,0,1:T(8,128)(2,1)}), bf16[2,4,64,2048]{3,2,0,1:T(8,128)(2,1)}, u32[]{:S(2)}, u32[]{:S(2)}) async-start(bf16[2,4,64,2048]{3,2,0,1:T(8,128)(2,1)} %copy.411), calls=%async_computation.10 | async-start | bytes 4194304 | tf_op jit(solution)/shard_map/all_to_all | solution.py:188
  518.5 30.4 %all-to-all-start.11 = ((bf16[2,4,64,2048]{3,2,0,1:T(8,128)(2,1)}), bf16[2,4,64,2048]{3,2,0,1:T(8,128)(2,1)}, u32[]{:S(2)}, u32[]{:S(2)}) async-start(bf16[2,4,64,2048]{3,2,0,1:T(8,128)(2,1)} %copy.412), calls=%async_computation.11 | async-start | bytes 4194304 | tf_op jit(solution)/shard_map/all_to_all | solution.py:188
  554.5 30.3 %all-to-all-start.12 = ((bf16[2,4,64,2048]{3,2,0,1:T(8,128)(2,1)}), bf16[2,4,64,2048]{3,2,0,1:T(8,128)(2,1)}, u32[]{:S(2)}, u32[]{:S(2)}) async-start(bf16[2,4,64,2048]{3,2,0,1:T(8,128)(2,1)} %broadcast_in_dim.50), calls=%async_computation.12 | async-start | bytes 4194304 | tf_op jit(solution)/shard_map/all_to_all | solution.py:176
  590.0 19.0 %all-to-all-start.13 = ((f32[512,4,2,1,64]{0,4,2,3,1:T(8,128)}), f32[512,4,2,1,64]{0,4,2,3,1:T(8,128)}, u32[]{:S(2)}, u32[]{:S(2)}) async-start(f32[512,4,2,1,64]{0,4,2,3,1:T(8,128)} %convolution_bitcast_fusion.1), calls=%async_computation.13 | async-start | bytes 2097152 | tf_op jit(solution)/shard_map/all_to_all | solution.py:205
  594.5 345.7 %reduce-scatter.8.cloned.1.call-start = ((), (), s32[]{:S(2)}) async-start(), calls=%async_computation.27 | async-start | bytes 11796480 | tf_op jit(solution)/shard_map/reduce_scatter | solution.py:197
  769.4 30.2 %all-to-all-start.14 = ((bf16[2,4,64,2048]{3,2,0,1:T(8,128)(2,1)}), bf16[2,4,64,2048]{3,2,0,1:T(8,128)(2,1)}, u32[]{:S(2)}, u32[]{:S(2)}) async-start(bf16[2,4,64,2048]{3,2,0,1:T(8,128)(2,1)} %copy.449), calls=%async_computation.14 | async-start | bytes 4194304 | tf_op jit(solution)/shard_map/all_to_all | solution.py:188
  807.0 19.5 %all-to-all-start.16 = ((f32[32,1,2048]{2,1,0:T(1,128)}), f32[32,1,2048]{2,1,0:T(1,128)S(1)}, u32[]{:S(2)}, u32[]{:S(2)}) async-start(f32[32,1,2048]{2,1,0:T(1,128)} %copy.458), calls=%async_computation.19 | async-start | bytes 524288 | tf_op jit(solution)/shard_map/all_to_all | solution.py:205
  831.0 5.4 all-to-all-start.18
  836.4 6.3 all-to-all-start.17
  942.6 18.8 %all-to-all-start.15 = ((bf16[4,4,64,1,512]{4,2,0,3,1:T(8,128)(2,1)}), bf16[4,4,64,1,512]{4,2,0,3,1:T(8,128)(2,1)}, u32[]{:S(2)}, u32[]{:S(2)}) async-start(bf16[4,4,64,1,512]{4,2,0,3,1:T(8,128)(2,1)} %copy.450), calls=%async_computation.18 | async-start | bytes 2097152 | tf_op jit(solution)/shard_map/all_to_all | solution.py:205
  (163 other events, 2708.4 us)
Sparse Core Ops, SparseCore 0:
  34.0 151.8 all-gather.3
  188.7 58.9 all-gather.5
  249.8 194.2 all-gather.7
  447.6 72.9 reduce-scatter.3
  524.0 228.3 reduce-scatter.5
  755.9 184.2 reduce-scatter.7

commit v21 on v20

--- a/solution.py
+++ b/solution.py
@@ -267,7 +267,7 @@
             3, owned_rows, inner, hidden_here
         )
         lanes = hidden_here // 128 if hidden_here % 128 == 0 else 0
-        first = (lanes - lanes * 2 // 11) * 128 if lanes > 1 else hidden_here // 2
+        first = (lanes - lanes * 3 // 11) * 128 if lanes > 1 else hidden_here // 2
         order = ((first, hidden_here - first), (0, first))
         ff_swapped = [
             exchange(ff_owned[..., offset : offset + size], INNER_AXES, 2, 1).reshape(

time: 984 us -> 984 us (level)
    unnamed x335 -> x365, local copies, waits for them, and re-layouts: 24.1 us -> 22.8 us
  transfers between devices with their start and end apart: 25 -> 25, of which waited for: 23 -> 22; matrix products, arithmetic and copies ran while one was open for 37% -> 38% of each run, Pallas kernels for 0% -> 0%
where the time goes in v21:
time: 984 us; the launch traced here: 975 us
  waiting for transfers between devices  483 us (49%)
  matrix products  179 us (18%)
  local copies, waits for them, and re-layouts  152 us (15%)
  starting transfers between devices  77.6 us (8%)
  other arithmetic  65.1 us (7%)
  between operations  17.4 us (2%)
    all_gather x3, waiting for transfers between devices, fsdp_gather(): return lax.all_gather(value, FSDP_AXES, axis=axis, tiled=True)  136 us
    reduce_scatter x3, waiting for transfers between devices, fsdp_scatter_low(): lax.psum_scatter(value.astype(jnp.bfloat16), FSDP_AXES, scatter_dimension...  122 us
    all_to_all x5, waiting for transfers between devices, tp_gather(): moved = lax.all_to_all(spread, TP_AXES, axis, axis, tiled=True)  93.9 us
    dot_general x42, matrix products, outer_product_result(): return jnp.einsum(form, first, second, precision=lax.Precision.HIGHEST)  75.8 us
    all_to_all x4, waiting for transfers between devices, tp_scatter_low(): moved = lax.all_to_all(staged, TP_AXES, axis, axis, tiled=True)  72 us
    all_to_all x10, waiting for transfers between devices, exchange(): return lax.all_to_all(value, axes, split_axis, concat_axis, tiled=True)  58.2 us
    dot_general x12, matrix products, back_product(): jnp.einsum('tg,fg->tf', gradient, weight, preferred_element_type=jnp.floa...  40.6 us
    all_to_all x10, starting transfers between devices, exchange(): return lax.all_to_all(value, axes, split_axis, concat_axis, tiled=True)  36.9 us
  transfers between devices with their start and end apart: 25, of which 22 were waited for; matrix products, arithmetic and copies ran while one was open for 38% of the time, Pallas kernels for 0%

profile of v21, /device:TPU:0, one launch (start us, length us, event | category | flops | bytes accessed | tf_op | source)
XLA Modules:
  0.0 974.8 jit_solution(1460841816422158312)
XLA Ops:
  18.3 14.3 %all-to-all-done.2 = bf16[4,64,4,512]{3,1,0,2:T(8,128)(2,1)S(1)} async-done(((bf16[4,64,4,512]{3,1,0,2:T(8,128)(2,1)}), bf16[4,64,4,512]{3,1,0,2:T(8,128)(2,1)S(1)}, u32[]{:S(2)}, u32[]{:S(2)}) %all-to-all-start.2) | async-done | bytes 1048608 | tf_op jit(solution)/shard_map/all_to_all | solution.py:205
  49.8 136.2 %all-gather.4.cloned.1.call-done = bf16[5,2048,512]{2,1,0:T(8,128)(2,1)} async-done(((bf16[5,256,512]{2,1,0:T(8,128)(2,1)}), bf16[5,2048,512]{2,1,0:T(8,128)(2,1)}) %all-gather.4.cloned.1.call-update) | async-done | bytes 10485776 | tf_op jit(solution)/shard_map/all_gather | solution.py:193
  192.9 8.6 all-to-all-done
  210.6 5.1 all-to-all-start.1
  217.7 23.8 %all-to-all-done.1 = bf16[2,4,64,2048]{3,2,0,1:T(8,128)(2,1)} async-done(((bf16[2,4,64,2048]{3,2,0,1:T(8,128)(2,1)}), bf16[2,4,64,2048]{3,2,0,1:T(8,128)(2,1)}, u32[]{:S(2)}, u32[]{:S(2)}) %all-to-all-start.1) | async-done | bytes 2097184 | tf_op jit(solution)/shard_map/all_to_all | solution.py:176
  321.8 6.2 all-to-all-done.6
  332.5 5.0 all-to-all-start.7
  337.7 25.5 %all-to-all-done.7 = bf16[2,4,64,2048]{3,2,0,1:T(8,128)(2,1)} async-done(((bf16[2,4,64,2048]{3,2,0,1:T(8,128)(2,1)}), bf16[2,4,64,2048]{3,2,0,1:T(8,128)(2,1)}, u32[]{:S(2)}, u32[]{:S(2)}) %all-to-all-start.7) | async-done | bytes 2097184 | tf_op jit(solution)/shard_map/all_to_all | solution.py:188
  373.8 21.3 %all-to-all-done.9 = bf16[2,4,64,2048]{3,2,0,1:T(8,128)(2,1)} async-done(((bf16[2,4,64,2048]{3,2,0,1:T(8,128)(2,1)}), bf16[2,4,64,2048]{3,2,0,1:T(8,128)(2,1)}, u32[]{:S(2)}, u32[]{:S(2)}) %all-to-all-start.9) | async-done | bytes 2097184 | tf_op jit(solution)/shard_map/all_to_all | solution.py:176
  405.4 22.6 %all-to-all-done.8 = bf16[2,4,64,2048]{3,2,0,1:T(8,128)(2,1)} async-done(((bf16[2,4,64,2048]{3,2,0,1:T(8,128)(2,1)}), bf16[2,4,64,2048]{3,2,0,1:T(8,128)(2,1)}, u32[]{:S(2)}, u32[]{:S(2)}) %all-to-all-start.8) | async-done | bytes 2097184 | tf_op jit(solution)/shard_map/all_to_all | solution.py:176
  450.5 5.7 fusion.10
  471.1 5.4 pad_maximum_fusion
  476.5 4.9 fusion.2
  490.2 5.0 fusion.8
  504.4 11.6 %all-to-all-done.10 = bf16[2,4,64,2048]{3,2,0,1:T(8,128)(2,1)} async-done(((bf16[2,4,64,2048]{3,2,0,1:T(8,128)(2,1)}), bf16[2,4,64,2048]{3,2,0,1:T(8,128)(2,1)}, u32[]{:S(2)}, u32[]{:S(2)}) %all-to-all-start.10) | async-done | bytes 2097184 | tf_op jit(solution)/shard_map/all_to_all | solution.py:188
  523.6 22.7 %all-to-all-done.11 = bf16[2,4,64,2048]{3,2,0,1:T(8,128)(2,1)} async-done(((bf16[2,4,64,2048]{3,2,0,1:T(8,128)(2,1)}), bf16[2,4,64,2048]{3,2,0,1:T(8,128)(2,1)}, u32[]{:S(2)}, u32[]{:S(2)}) %all-to-all-start.11) | async-done | bytes 2097184 | tf_op jit(solution)/shard_map/all_to_all | solution.py:188
  559.1 23.2 %all-to-all-done.12 = bf16[2,4,64,2048]{3,2,0,1:T(8,128)(2,1)} async-done(((bf16[2,4,64,2048]{3,2,0,1:T(8,128)(2,1)}), bf16[2,4,64,2048]{3,2,0,1:T(8,128)(2,1)}, u32[]{:S(2)}, u32[]{:S(2)}) %all-to-all-start.12) | async-done | bytes 2097184 | tf_op jit(solution)/shard_map/all_to_all | solution.py:176
  600.6 5.9 all-to-all-done.13
  722.5 29.3 %reduce-scatter.6.cloned.1.call-done = bf16[3,256,1024]{2,1,0:T(8,128)(2,1)} async-done(((bf16[3,2048,1024]{2,1,0:T(8,128)(2,1)}), bf16[3,256,1024]{2,1,0:T(8,128)(2,1)}) %reduce-scatter.6.cloned.1.call-update) | async-done | bytes 1572880 | tf_op jit(solution)/shard_map/reduce_scatter | solution.py:197
  778.5 7.7 dynamic_update_slice.7
  786.9 12.2 %all-to-all-done.14 = bf16[2,4,64,2048]{3,2,0,1:T(8,128)(2,1)} async-done(((bf16[2,4,64,2048]{3,2,0,1:T(8,128)(2,1)}), bf16[2,4,64,2048]{3,2,0,1:T(8,128)(2,1)}, u32[]{:S(2)}, u32[]{:S(2)}) %all-to-all-start.14) | async-done | bytes 2097184 | tf_op jit(solution)/shard_map/all_to_all | solution.py:188
  813.4 12.5 %all-to-all-done.16 = f32[32,1,2048]{2,1,0:T(1,128)S(1)} async-done(((f32[32,1,2048]{2,1,0:T(1,128)}), f32[32,1,2048]{2,1,0:T(1,128)S(1)}, u32[]{:S(2)}, u32[]{:S(2)}) %all-to-all-start.16) | async-done | bytes 262176 | tf_op jit(solution)/shard_map/all_to_all | solution.py:205
  846.6 93.1 %reduce-scatter.8.cloned.1.call-done = bf16[5,256,512]{2,1,0:T(8,128)(2,1)} async-done(((bf16[5,2048,512]{2,1,0:T(8,128)(2,1)}), bf16[5,256,512]{2,1,0:T(8,128)(2,1)}) %reduce-scatter.8.cloned.1.call-update) | async-done | bytes 1310736 | tf_op jit(solution)/shard_map/reduce_scatter | solution.py:197
  954.1 6.7 all-to-all-done.15
  (658 shorter events, 443.0 us)
Async XLA Ops:
  13.9 18.7 %all-to-all-start.2 = ((bf16[4,64,4,512]{3,1,0,2:T(8,128)(2,1)}), bf16[4,64,4,512]{3,1,0,2:T(8,128)(2,1)S(1)}, u32[]{:S(2)}, u32[]{:S(2)}) async-start(bf16[4,64,4,512]{3,1,0,2:T(8,128)(2,1)} %copy.379), calls=%async_computation.2 | async-start | bytes 2097152 | tf_op jit(solution)/shard_map/all_to_all | solution.py:205
  18.1 167.8 %all-gather.4.cloned.1.call-start = ((), (), s32[]{:S(2)}) async-start(), calls=%async_computation.22 | async-start | bytes 11796480 | tf_op jit(solution)/shard_map/all_gather | solution.py:193
  42.0 6.2 all-to-all-start.4
  45.7 385.4 %all-gather.6.cloned.1.call-start = ((), (), s32[]{:S(2)}) async-start(), calls=%async_computation.23 | async-start | bytes 5308416 | tf_op jit(solution)/shard_map/all_gather | solution.py:193
  185.9 264.6 %all-gather.8.cloned.1.call-start = ((), (), s32[]{:S(2)}) async-start(), calls=%async_computation.24 | async-start | bytes 14155776 | tf_op jit(solution)/shard_map/all_gather | solution.py:193
  189.9 11.6 %all-to-all-start = ((bf16[32,2,960]{2,1,0:T(2,128)(2,1)}), bf16[32,2,960]{2,1,0:T(2,128)(2,1)S(1)}, u32[]{:S(2)}, u32[]{:S(2)}) async-start(bf16[32,2,960]{2,1,0:T(2,128)(2,1)} %reshape.743), calls=%async_computation | async-start | bytes 262144 | tf_op jit(solution)/shard_map/all_to_all | solution.py:205
  202.1 6.9 all-to-all-start.5
  210.6 30.9 %all-to-all-start.1 = ((bf16[2,4,64,2048]{3,2,0,1:T(8,128)(2,1)}), bf16[2,4,64,2048]{3,2,0,1:T(8,128)(2,1)}, u32[]{:S(2)}, u32[]{:S(2)}) async-start(bf16[2,4,64,2048]{3,2,0,1:T(8,128)(2,1)} %broadcast_in_dim.43), calls=%async_computation.1 | async-start | bytes 4194304 | tf_op jit(solution)/shard_map/all_to_all | solution.py:176
  315.7 12.3 %all-to-all-start.6 = ((bf16[512,1,2,4,64]{0,4,2,1,3:T(8,128)(2,1)}), bf16[512,1,2,4,64]{0,4,2,1,3:T(8,128)(2,1)S(1)}, u32[]{:S(2)}, u32[]{:S(2)}) async-start(bf16[512,1,2,4,64]{0,4,2,1,3:T(8,128)(2,1)} %copy.406), calls=%async_computation.6 | async-start | bytes 1048576 | tf_op jit(solution)/shard_map/all_to_all | solution.py:205
  332.5 30.8 %all-to-all-start.7 = ((bf16[2,4,64,2048]{3,2,0,1:T(8,128)(2,1)}), bf16[2,4,64,2048]{3,2,0,1:T(8,128)(2,1)}, u32[]{:S(2)}, u32[]{:S(2)}) async-start(bf16[2,4,64,2048]{3,2,0,1:T(8,128)(2,1)} %copy.408), calls=%async_computation.7 | async-start | bytes 4194304 | tf_op jit(solution)/shard_map/all_to_all | solution.py:188
  364.9 30.2 %all-to-all-start.9 = ((bf16[2,4,64,2048]{3,2,0,1:T(8,128)(2,1)}), bf16[2,4,64,2048]{3,2,0,1:T(8,128)(2,1)}, u32[]{:S(2)}, u32[]{:S(2)}) async-start(bf16[2,4,64,2048]{3,2,0,1:T(8,128)(2,1)} %broadcast_in_dim.48), calls=%async_computation.9 | async-start | bytes 4194304 | tf_op jit(solution)/shard_map/all_to_all | solution.py:176
  397.7 30.2 %all-to-all-start.8 = ((bf16[2,4,64,2048]{3,2,0,1:T(8,128)(2,1)}), bf16[2,4,64,2048]{3,2,0,1:T(8,128)(2,1)}, u32[]{:S(2)}, u32[]{:S(2)}) async-start(bf16[2,4,64,2048]{3,2,0,1:T(8,128)(2,1)} %broadcast_in_dim.47), calls=%async_computation.8 | async-start | bytes 4194304 | tf_op jit(solution)/shard_map/all_to_all | solution.py:176
  402.2 320.3 %reduce-scatter.4.cloned.1.call-start = ((), (), s32[]{:S(2)}) async-start(), calls=%async_computation.25 | async-start | bytes 5308416 | tf_op jit(solution)/shard_map/reduce_scatter | solution.py:197
  445.7 306.1 %reduce-scatter.6.cloned.1.call-start = ((), (), s32[]{:S(2)}) async-start(), calls=%async_computation.26 | async-start | bytes 14155776 | tf_op jit(solution)/shard_map/reduce_scatter | solution.py:197
  485.7 30.3 %all-to-all-start.10 = ((bf16[2,4,64,2048]{3,2,0,1:T(8,128)(2,1)}), bf16[2,4,64,2048]{3,2,0,1:T(8,128)(2,1)}, u32[]{:S(2)}, u32[]{:S(2)}) async-start(bf16[2,4,64,2048]{3,2,0,1:T(8,128)(2,1)} %copy.411), calls=%async_computation.10 | async-start | bytes 4194304 | tf_op jit(solution)/shard_map/all_to_all | solution.py:188
  515.9 30.4 %all-to-all-start.11 = ((bf16[2,4,64,2048]{3,2,0,1:T(8,128)(2,1)}), bf16[2,4,64,2048]{3,2,0,1:T(8,128)(2,1)}, u32[]{:S(2)}, u32[]{:S(2)}) async-start(bf16[2,4,64,2048]{3,2,0,1:T(8,128)(2,1)} %copy.412), calls=%async_computation.11 | async-start | bytes 4194304 | tf_op jit(solution)/shard_map/all_to_all | solution.py:188
  552.0 30.2 %all-to-all-start.12 = ((bf16[2,4,64,2048]{3,2,0,1:T(8,128)(2,1)}), bf16[2,4,64,2048]{3,2,0,1:T(8,128)(2,1)}, u32[]{:S(2)}, u32[]{:S(2)}) async-start(bf16[2,4,64,2048]{3,2,0,1:T(8,128)(2,1)} %broadcast_in_dim.50), calls=%async_computation.12 | async-start | bytes 4194304 | tf_op jit(solution)/shard_map/all_to_all | solution.py:176
  587.6 18.9 %all-to-all-start.13 = ((f32[512,4,2,1,64]{0,4,2,3,1:T(8,128)}), f32[512,4,2,1,64]{0,4,2,3,1:T(8,128)}, u32[]{:S(2)}, u32[]{:S(2)}) async-start(f32[512,4,2,1,64]{0,4,2,3,1:T(8,128)} %convolution_bitcast_fusion.1), calls=%async_computation.13 | async-start | bytes 2097152 | tf_op jit(solution)/shard_map/all_to_all | solution.py:205
  592.0 347.7 %reduce-scatter.8.cloned.1.call-start = ((), (), s32[]{:S(2)}) async-start(), calls=%async_computation.27 | async-start | bytes 11796480 | tf_op jit(solution)/shard_map/reduce_scatter | solution.py:197
  768.8 30.2 %all-to-all-start.14 = ((bf16[2,4,64,2048]{3,2,0,1:T(8,128)(2,1)}), bf16[2,4,64,2048]{3,2,0,1:T(8,128)(2,1)}, u32[]{:S(2)}, u32[]{:S(2)}) async-start(bf16[2,4,64,2048]{3,2,0,1:T(8,128)(2,1)} %copy.449), calls=%async_computation.14 | async-start | bytes 4194304 | tf_op jit(solution)/shard_map/all_to_all | solution.py:188
  806.4 19.5 %all-to-all-start.16 = ((f32[32,1,2048]{2,1,0:T(1,128)}), f32[32,1,2048]{2,1,0:T(1,128)S(1)}, u32[]{:S(2)}, u32[]{:S(2)}) async-start(f32[32,1,2048]{2,1,0:T(1,128)} %copy.458), calls=%async_computation.19 | async-start | bytes 524288 | tf_op jit(solution)/shard_map/all_to_all | solution.py:205
  830.5 5.6 all-to-all-start.18
  836.1 6.2 all-to-all-start.17
  942.0 18.8 %all-to-all-start.15 = ((bf16[4,4,64,1,512]{4,2,0,3,1:T(8,128)(2,1)}), bf16[4,4,64,1,512]{4,2,0,3,1:T(8,128)(2,1)}, u32[]{:S(2)}, u32[]{:S(2)}) async-start(bf16[4,4,64,1,512]{4,2,0,3,1:T(8,128)(2,1)} %copy.450), calls=%async_computation.18 | async-start | bytes 2097152 | tf_op jit(solution)/shard_map/all_to_all | solution.py:205
  (178 other events, 2580.1 us)
Sparse Core Ops, SparseCore 0:
  34.0 151.8 all-gather.3
  188.1 78.9 all-gather.5
  269.3 174.5 all-gather.7
  447.4 93.4 reduce-scatter.3
  544.3 207.4 reduce-scatter.5
  755.2 184.3 reduce-scatter.7
